TPU v7x, 128 devices: a whole 4x4x4 slice. The times are simulated.
128 devices in a mesh: dp: 16 (over z_lo, y, core), tensor: 8 (over z_hi, x).
Axes of the slice: x: 4, y: 4, z: 4 (z_hi: 2, z_lo: 2; z = z_hi * 2 + z_lo), core: 2. Of those that a mesh axis runs over, the one named last changes fastest.
Arguments:
- hidden: bfloat16 [16384, 2048], P(('dp', 'tensor')), may hold values from -6 to 6
- routes: int32 [16384, 2], P('dp'), may hold values from 0 to 63, all different within a row; in each aligned block of 1024 rows (0 to 1023, 1024 to 2047, ...) at most 40 rows name the same one
- prefix: int32 [16], P('dp'), may hold values from 1 to 512
- attn_gain: bfloat16 [2048], P('dp'), may hold values from 0.5 to 1.5
- query_proj: bfloat16 [2048, 3072], P('dp', 'tensor'), may hold values from -0.125 to 0.125
- latent_proj: bfloat16 [2048, 576], P('dp'), may hold values from -0.125 to 0.125
- latent_gain: bfloat16 [512], P('dp'), may hold values from 0.5 to 1.5
- expand_proj: bfloat16 [512, 4096], P('dp', 'tensor'), may hold values from -0.25 to 0.25
- output_proj: bfloat16 [2048, 2048], P('tensor', 'dp'), may hold values from -1 to 1
- second_gain: bfloat16 [2048], P('dp'), may hold values from 0.5 to 1.5
- router_proj: bfloat16 [2048, 64], P('dp'), may hold values from -0.09375 to 0.09375
- expert_gate: bfloat16 [64, 1408, 2048], P('dp', 'tensor'), may hold values from -0.125 to 0.125
- expert_up: bfloat16 [64, 1408, 2048], P('dp', 'tensor'), may hold values from -0.125 to 0.125
- expert_down: bfloat16 [64, 1408, 2048], P('dp', 'tensor'), may hold values from -0.15625 to 0.15625
- shared_gate: bfloat16 [2048, 2816], P('dp', 'tensor'), may hold values from -0.125 to 0.125
- shared_up: bfloat16 [2048, 2816], P('dp', 'tensor'), may hold values from -0.125 to 0.125
- shared_down: bfloat16 [2816, 2048], P('tensor', 'dp'), may hold values from -0.109375 to 0.109375
- out_grad: bfloat16 [16384, 2048], P(('dp', 'tensor')), may hold values from -6 to 6
Outputs:
- output: bfloat16 [16384, 2048], P(('dp', 'tensor'))
- hidden_grad: float32 [16384, 2048], P(('dp', 'tensor'))
- attn_gain_grad: float32 [2048], P(('dp', 'tensor'))
- query_proj_grad: float32 [2048, 3072], P('dp', 'tensor')
- latent_proj_grad: float32 [2048, 576], P(('dp', 'tensor'))
- latent_gain_grad: float32 [512], P(('dp', 'tensor'))
- expand_proj_grad: float32 [512, 4096], P('dp', 'tensor')
- output_proj_grad: float32 [2048, 2048], P('tensor', 'dp')
- second_gain_grad: float32 [2048], P(('dp', 'tensor'))
- router_proj_grad: float32 [2048, 64], P(('dp', 'tensor'))
- expert_gate_grad: float32 [64, 1408, 2048], P('dp', 'tensor')
- expert_up_grad: float32 [64, 1408, 2048], P('dp', 'tensor')
- expert_down_grad: float32 [64, 1408, 2048], P('dp', 'tensor')
- shared_gate_grad: float32 [2048, 2816], P('dp', 'tensor')
- shared_up_grad: float32 [2048, 2816], P('dp', 'tensor')
- shared_down_grad: float32 [2816, 2048], P('tensor', 'dp')
Inputs may be any that keep to these rules, and one draw needn't show every extreme that they name: `routes`: each row names 2 different experts. Within the rows of one sequence no expert is named more than 40 times, a bound that some block reaches.
All inputs are finite; a program needn't handle non-finite values.
Results may differ from a plain program's by a relative error of at most 0.029.
Values may be sent and summed in bfloat16 or wider, within the bound.
No kernel may reach another device: no remote copies, remote signals or barrier semaphores. Data moves between devices by JAX's collectives and lax.ppermute only.
A program may use at most 320 MiB of HBM per device.

v0:
```python
import math

import jax
import jax.numpy as jnp
from jax import lax
from jax.sharding import PartitionSpec as P

D = 2048
DN = 128
DR = 64
DV = 128
KVR = 512


EPS = 1e-06
HIGH = lax.Precision.HIGHEST
MASKED = -1e30


def norm_scale(values):
    return lax.rsqrt(jnp.mean(values * values, -1, keepdims=True) + EPS)


def norm_back(values, scales, gains, upstream):
    weighted = gains * upstream
    return scales * weighted - values * scales**3 * jnp.mean(values * weighted, -1, keepdims=True)


def rope_tables(positions, rope_width):
    half_width = rope_width // 2
    frequency = 10000.0 ** (-2.0 * jnp.arange(half_width).astype(jnp.float32) / rope_width)
    angles = positions.astype(jnp.float32)[:, None] * frequency[None, :]
    return (jnp.cos(angles), jnp.sin(angles))


def rotate(vectors, cosines, sine_values):
    half_width = vectors.shape[-1] // 2
    front_half = vectors[..., :half_width]
    back_half = vectors[..., half_width:]
    return jnp.concatenate(
        [
            front_half * cosines - back_half * sine_values,
            back_half * cosines + front_half * sine_values,
        ],
        -1,
    )


def rotate_back(gradients, cosines, sine_values):
    half_width = gradients.shape[-1] // 2
    front_half = gradients[..., :half_width]
    back_half = gradients[..., half_width:]
    return jnp.concatenate(
        [
            front_half * cosines + back_half * sine_values,
            back_half * cosines - front_half * sine_values,
        ],
        -1,
    )


def round_trip(values):
    return lax.optimization_barrier(values.astype(jnp.bfloat16)).astype(jnp.float32)


def block_scores(query_block, keys_nope, key_rope, rows_start, prefix_len, score_scale):
    raw_scores = jnp.einsum(
        "qhd,khd->hqk", query_block[..., :DN], keys_nope, preferred_element_type=jnp.float32
    )
    raw_scores = raw_scores + jnp.einsum(
        "qhr,kr->hqk", query_block[..., DN:], key_rope, preferred_element_type=jnp.float32
    )
    query_places = rows_start + jnp.arange(query_block.shape[0])
    key_places = jnp.arange(keys_nope.shape[0])
    visible = (key_places[None, :] <= query_places[:, None]) | (key_places[None, :] < prefix_len)
    return jnp.where(visible[None], raw_scores * score_scale, MASKED)


def silu_back(act_grad, gate_pre, up_pre, sigmoid_gate):
    up_grad = (act_grad * gate_pre * sigmoid_gate).astype(jnp.bfloat16)
    gate_grad = (act_grad * up_pre * sigmoid_gate * (1.0 + gate_pre * (1.0 - sigmoid_gate))).astype(
        jnp.bfloat16
    )
    return (gate_grad, up_grad)


def shards(
    hidden,
    routes,
    prefix,
    attn_gain,
    query_proj,
    latent_proj,
    latent_gain,
    expand_proj,
    output_proj,
    second_gain,
    router_proj,
    expert_gate,
    expert_up,
    expert_down,
    shared_gate,
    shared_up,
    shared_down,
    out_grad,
):
    tok_dev = hidden.shape[0]
    tensor_size = lax.axis_size("tensor")
    tensor_rank = lax.axis_index("tensor")
    dp_size = lax.axis_size("dp")
    seq_len = tok_dev * tensor_size
    start_row = tensor_rank * tok_dev
    (
        attn_gains,
        query_weights,
        latent_weights,
        kv_gains,
        expand_weights,
        output_weights,
        second_gains,
        router_weights,
        gate_shared,
        up_shared,
        down_shared,
    ) = (
        lax.all_gather(attn_gain, "dp", axis=0, tiled=True),
        lax.all_gather(query_proj, "dp", axis=0, tiled=True),
        lax.all_gather(latent_proj, "dp", axis=0, tiled=True),
        lax.all_gather(latent_gain, "dp", axis=0, tiled=True),
        lax.all_gather(expand_proj, "dp", axis=0, tiled=True),
        lax.all_gather(output_proj, "dp", axis=1, tiled=True),
        lax.all_gather(second_gain, "dp", axis=0, tiled=True),
        lax.all_gather(router_proj, "dp", axis=0, tiled=True),
        lax.all_gather(shared_gate, "dp", axis=0, tiled=True),
        lax.all_gather(shared_up, "dp", axis=0, tiled=True),
        lax.all_gather(shared_down, "dp", axis=1, tiled=True),
    )
    hidden_f = hidden.astype(jnp.float32)
    scale_one = norm_scale(hidden_f)
    gain_one = attn_gains.astype(jnp.float32)
    normed_own = (hidden_f * scale_one * gain_one).astype(jnp.bfloat16)
    latent_raw = jnp.dot(normed_own, latent_weights, preferred_element_type=jnp.float32)
    compressed = latent_raw[:, :KVR]
    scale_kv = norm_scale(compressed)
    gain_kv = kv_gains.astype(jnp.float32)
    own_cosines, own_sines = rope_tables(start_row + jnp.arange(tok_dev), DR)
    latent_packed = jnp.concatenate(
        [compressed * scale_kv * gain_kv, rotate(latent_raw[:, KVR:], own_cosines, own_sines)], -1
    ).astype(jnp.bfloat16)
    normed_all, latent_seq, grad_seq = (
        lax.all_gather(normed_own, "tensor", axis=0, tiled=True),
        lax.all_gather(latent_packed, "tensor", axis=0, tiled=True),
        lax.all_gather(out_grad, "tensor", axis=0, tiled=True),
    )
    head_count = query_weights.shape[1] // (DN + DR)
    all_cosines, all_sines = rope_tables(jnp.arange(seq_len), DR)
    query_raw = jnp.dot(normed_all, query_weights, preferred_element_type=jnp.float32).reshape(
        seq_len, head_count, DN + DR
    )
    query_low = jnp.concatenate(
        [
            query_raw[..., :DN],
            rotate(query_raw[..., DN:], all_cosines[:, None, :], all_sines[:, None, :]),
        ],
        -1,
    ).astype(jnp.bfloat16)
    compressed_seq = latent_seq[:, :KVR]
    key_rope = latent_seq[:, KVR:]
    expanded = jnp.dot(compressed_seq, expand_weights, preferred_element_type=jnp.float32).reshape(
        seq_len, head_count, DN + DV
    )
    keys_nope = expanded[..., :DN].astype(jnp.bfloat16)
    values_low = expanded[..., DN:].astype(jnp.bfloat16)
    score_scale = 1.0 / math.sqrt(DN + DR)
    block_rows = min(512, seq_len)
    prefix_len = prefix[0]
    lse_list = []
    mixed_list = []
    for rows_start in range(0, seq_len, block_rows):
        query_block = query_low[rows_start : rows_start + block_rows]
        masked = block_scores(query_block, keys_nope, key_rope, rows_start, prefix_len, score_scale)
        top_score = jnp.max(masked, -1, keepdims=True)
        exp_scores = jnp.exp(masked - top_score)
        totals = jnp.sum(exp_scores, -1, keepdims=True)
        prob_low = (exp_scores / totals).astype(jnp.bfloat16)
        lse_list.append(top_score + jnp.log(totals))
        mixed_list.append(
            jnp.einsum(
                "hqk,khv->qhv", prob_low, values_low, preferred_element_type=jnp.float32
            ).astype(jnp.bfloat16)
        )
    mixed_all = jnp.concatenate(mixed_list, 0).reshape(seq_len, head_count * DV)
    attn_part = jnp.dot(mixed_all, output_weights, preferred_element_type=jnp.float32)
    attn_own = lax.psum_scatter(
        attn_part.astype(jnp.bfloat16), "tensor", scatter_dimension=0, tiled=True
    ).astype(jnp.float32)
    residual_own = hidden_f + attn_own
    residual_all = lax.all_gather(
        residual_own.astype(jnp.bfloat16), "tensor", axis=0, tiled=True
    ).astype(residual_own.dtype)
    scale_two = norm_scale(residual_all)
    gain_two = second_gains.astype(jnp.float32)
    normed_two = (residual_all * scale_two * gain_two).astype(jnp.bfloat16)
    logits = jnp.dot(normed_two, router_weights, preferred_element_type=jnp.float32)
    experts = router_weights.shape[1]
    top_count = routes.shape[1]
    chosen_hot = routes[:, :, None] == jnp.arange(experts)[None, None, :]
    chosen_logits = jnp.sum(jnp.where(chosen_hot, logits[:, None, :], 0.0), -1)
    gate_values = jax.nn.softmax(chosen_logits, axis=-1)
    flat_hot = chosen_hot.reshape(seq_len * top_count, experts).astype(jnp.int32)
    earlier = jnp.cumsum(flat_hot, 0) - flat_hot
    slot_pos = jnp.sum(earlier * flat_hot, -1)
    expert_ids = routes.reshape(-1)
    exp_dev = expert_gate.shape[0]
    capacity = tensor_size * (5 * seq_len * top_count // (4 * experts * tensor_size))
    slot_index = expert_ids * capacity + slot_pos
    token_ids = jnp.arange(seq_len * top_count) // top_count
    slot_token = jnp.full((experts * capacity,), seq_len, jnp.int32).at[slot_index].set(token_ids)
    slot_gate = (
        jnp.zeros((experts * capacity,), jnp.float32).at[slot_index].set(gate_values.reshape(-1))
    )
    padded_normed = jnp.concatenate([normed_two, jnp.zeros((1, D), jnp.bfloat16)], 0)
    padded_grad = jnp.concatenate([grad_seq, jnp.zeros((1, D), jnp.bfloat16)], 0)
    send_rows = jnp.take(padded_normed, slot_token, axis=0).reshape(dp_size, exp_dev, capacity, D)
    send_grads = (
        (jnp.take(padded_grad, slot_token, axis=0).astype(jnp.float32) * slot_gate[:, None])
        .astype(jnp.bfloat16)
        .reshape(dp_size, exp_dev, capacity, D)
    )
    recv_rows, recv_grads = (
        lax.all_to_all(send_rows, "dp", split_axis=0, concat_axis=0, tiled=True),
        lax.all_to_all(send_grads, "dp", split_axis=0, concat_axis=0, tiled=True),
    )
    gate_pre = jnp.einsum(
        "sjcd,jfd->sjcf", recv_rows, expert_gate, preferred_element_type=jnp.float32
    )
    up_pre = jnp.einsum("sjcd,jfd->sjcf", recv_rows, expert_up, preferred_element_type=jnp.float32)
    sigmoid_gate = jax.nn.sigmoid(gate_pre)
    expert_act = (gate_pre * sigmoid_gate * up_pre).astype(jnp.bfloat16)
    expert_out = jnp.einsum(
        "sjcf,jfd->sjcd", expert_act, expert_down, preferred_element_type=jnp.float32
    )
    act_grad = jnp.einsum(
        "sjcd,jfd->sjcf", recv_grads, expert_down, preferred_element_type=jnp.float32
    )
    gate_low_grad, up_low_grad = silu_back(act_grad, gate_pre, up_pre, sigmoid_gate)
    expert_down_grad = jnp.einsum(
        "sjcf,sjcd->jfd", expert_act, recv_grads, preferred_element_type=jnp.float32
    )
    expert_gate_grad = jnp.einsum(
        "sjcf,sjcd->jfd", gate_low_grad, recv_rows, preferred_element_type=jnp.float32
    )
    expert_up_grad = jnp.einsum(
        "sjcf,sjcd->jfd", up_low_grad, recv_rows, preferred_element_type=jnp.float32
    )
    row_grads = jnp.einsum(
        "sjcf,jfd->sjcd", gate_low_grad, expert_gate, preferred_element_type=jnp.float32
    )
    row_grads = row_grads + jnp.einsum(
        "sjcf,jfd->sjcd", up_low_grad, expert_up, preferred_element_type=jnp.float32
    )
    back_out, back_rows = (
        lax.all_to_all(
            expert_out.astype(jnp.bfloat16), "dp", split_axis=0, concat_axis=0, tiled=True
        ).astype(expert_out.dtype),
        lax.all_to_all(
            row_grads.astype(jnp.bfloat16), "dp", split_axis=0, concat_axis=0, tiled=True
        ).astype(row_grads.dtype),
    )
    table_rows = experts * capacity
    out_table = jnp.concatenate(
        [back_out.reshape(table_rows, D), jnp.zeros((1, D), jnp.float32)], 0
    )
    back_table = jnp.concatenate(
        [back_rows.reshape(table_rows, D), jnp.zeros((1, D), jnp.float32)], 0
    )
    picked_out = jnp.take(out_table, slot_index, axis=0).reshape(seq_len, top_count, D)
    picked_back = jnp.take(back_table, slot_index, axis=0).reshape(seq_len, top_count, D)
    shared_pre_gate = jnp.dot(normed_two, gate_shared, preferred_element_type=jnp.float32)
    shared_pre_up = jnp.dot(normed_two, up_shared, preferred_element_type=jnp.float32)
    shared_sigmoid = jax.nn.sigmoid(shared_pre_gate)
    shared_act = (shared_pre_gate * shared_sigmoid * shared_pre_up).astype(jnp.bfloat16)
    shared_out = jnp.dot(shared_act, down_shared, preferred_element_type=jnp.float32)
    shared_act_grad = jnp.dot(grad_seq, down_shared.T, preferred_element_type=jnp.float32)
    shared_gate_low, shared_up_low = silu_back(
        shared_act_grad, shared_pre_gate, shared_pre_up, shared_sigmoid
    )
    shared_down_grad = jnp.dot(shared_act.T, grad_seq, preferred_element_type=jnp.float32)
    shared_gate_grad = jnp.dot(normed_two.T, shared_gate_low, preferred_element_type=jnp.float32)
    shared_up_grad = jnp.dot(normed_two.T, shared_up_low, preferred_element_type=jnp.float32)
    shared_back = jnp.dot(shared_gate_low, gate_shared.T, preferred_element_type=jnp.float32)
    shared_back = shared_back + jnp.dot(
        shared_up_low, up_shared.T, preferred_element_type=jnp.float32
    )
    grad_seq_f = grad_seq.astype(jnp.float32)
    feed_part = shared_out + jnp.sum(gate_values[:, :, None] * picked_out, 1)
    gate_part = jnp.sum(grad_seq_f[:, None, :] * picked_out, -1)
    feed_own = lax.psum_scatter(
        feed_part.astype(jnp.bfloat16), "tensor", scatter_dimension=0, tiled=True
    ).astype(jnp.float32)
    output = (residual_own + feed_own).astype(jnp.bfloat16)
    normed_two_grad, gate_grads = (
        lax.psum((jnp.sum(picked_back, 1) + shared_back).astype(jnp.bfloat16), "tensor").astype(
            jnp.float32
        ),
        lax.psum(gate_part.astype(jnp.bfloat16), "tensor").astype(jnp.float32),
    )
    weighted_total = jnp.sum(gate_values * gate_grads, -1, keepdims=True)
    chosen_grads = gate_values * (gate_grads - weighted_total)
    logit_grads = jnp.sum(jnp.where(chosen_hot, chosen_grads[:, :, None], 0.0), 1)
    normed_two_grad = normed_two_grad + jnp.dot(
        logit_grads, router_weights.astype(jnp.float32).T, precision=HIGH
    )
    residual_grad = grad_seq_f + norm_back(residual_all, scale_two, gain_two, normed_two_grad)
    own_two_grad = lax.dynamic_slice_in_dim(normed_two_grad, start_row, tok_dev, 0)
    own_scale_two = lax.dynamic_slice_in_dim(scale_two, start_row, tok_dev, 0)
    second_gain_grad = jnp.sum(own_two_grad * residual_own * own_scale_two, 0)
    own_normed_two = lax.dynamic_slice_in_dim(normed_two, start_row, tok_dev, 0).astype(jnp.float32)
    router_grad = jnp.dot(
        own_normed_two.T,
        lax.dynamic_slice_in_dim(logit_grads, start_row, tok_dev, 0),
        precision=HIGH,
    )
    branch_grad = residual_grad.astype(jnp.bfloat16)
    output_grad_w = jnp.dot(mixed_all.T, branch_grad, preferred_element_type=jnp.float32)
    mixed_grad = (
        jnp.dot(branch_grad, output_weights.T, preferred_element_type=jnp.float32)
        .astype(jnp.bfloat16)
        .reshape(seq_len, head_count, DV)
    )
    keys_nope_grad = jnp.zeros((seq_len, head_count, DN), jnp.float32)
    key_rope_grad = jnp.zeros((seq_len, DR), jnp.float32)
    values_grad = jnp.zeros((seq_len, head_count, DV), jnp.float32)
    query_grad_list = []
    for block_index, rows_start in enumerate(range(0, seq_len, block_rows)):
        query_block = query_low[rows_start : rows_start + block_rows]
        masked = block_scores(query_block, keys_nope, key_rope, rows_start, prefix_len, score_scale)
        prob_full = jnp.exp(masked - lse_list[block_index])
        prob_low = prob_full.astype(jnp.bfloat16)
        mixed_block = mixed_grad[rows_start : rows_start + block_rows]
        prob_grads = jnp.einsum(
            "qhv,khv->hqk", mixed_block, values_low, preferred_element_type=jnp.float32
        )
        row_delta = jnp.sum(prob_full * prob_grads, -1, keepdims=True)
        score_grads = (prob_full * (prob_grads - row_delta)).astype(jnp.bfloat16)
        query_nope_grad = (
            jnp.einsum("hqk,khd->qhd", score_grads, keys_nope, preferred_element_type=jnp.float32)
            * score_scale
        )
        query_rope_grad = (
            jnp.einsum("hqk,kr->qhr", score_grads, key_rope, preferred_element_type=jnp.float32)
            * score_scale
        )
        keys_nope_grad = (
            keys_nope_grad
            + jnp.einsum(
                "hqk,qhd->khd",
                score_grads,
                query_block[..., :DN],
                preferred_element_type=jnp.float32,
            )
            * score_scale
        )
        key_rope_grad = (
            key_rope_grad
            + jnp.einsum(
                "hqk,qhr->kr",
                score_grads,
                query_block[..., DN:],
                preferred_element_type=jnp.float32,
            )
            * score_scale
        )
        values_grad = values_grad + jnp.einsum(
            "hqk,qhv->khv", prob_low, mixed_block, preferred_element_type=jnp.float32
        )
        block_cosines = all_cosines[rows_start : rows_start + block_rows, None, :]
        block_sines = all_sines[rows_start : rows_start + block_rows, None, :]
        query_grad_list.append(
            jnp.concatenate(
                [
                    query_nope_grad,
                    rotate_back(round_trip(query_rope_grad), block_cosines, block_sines),
                ],
                -1,
            ).astype(jnp.bfloat16)
        )
    query_grads = jnp.concatenate(query_grad_list, 0).reshape(seq_len, head_count * (DN + DR))
    query_grad_w = jnp.dot(normed_all.T, query_grads, preferred_element_type=jnp.float32)
    normed_grad_part = jnp.dot(query_grads, query_weights.T, preferred_element_type=jnp.float32)
    expand_grads = jnp.concatenate(
        [keys_nope_grad.astype(jnp.bfloat16), values_grad.astype(jnp.bfloat16)], -1
    ).reshape(seq_len, head_count * (DN + DV))
    expand_grad_w = jnp.dot(compressed_seq.T, expand_grads, preferred_element_type=jnp.float32)
    compressed_grad_part = jnp.dot(
        expand_grads, expand_weights.T, preferred_element_type=jnp.float32
    )
    latent_grad_part = jnp.concatenate([compressed_grad_part, key_rope_grad], -1)
    normed_grad_own, latent_grad_own = (
        lax.psum_scatter(
            normed_grad_part.astype(jnp.bfloat16), "tensor", scatter_dimension=0, tiled=True
        ).astype(jnp.float32),
        lax.psum_scatter(
            latent_grad_part.astype(jnp.bfloat16), "tensor", scatter_dimension=0, tiled=True
        ).astype(jnp.float32),
    )
    compressed_grad = latent_grad_own[:, :KVR]
    kv_gain_grad = jnp.sum(compressed_grad * compressed * scale_kv, 0)
    raw_grad = jnp.concatenate(
        [
            norm_back(compressed, scale_kv, gain_kv, compressed_grad),
            rotate_back(latent_grad_own[:, KVR:], own_cosines, own_sines),
        ],
        -1,
    ).astype(jnp.bfloat16)
    latent_grad_w = jnp.dot(normed_own.T, raw_grad, preferred_element_type=jnp.float32)
    normed_grad = normed_grad_own + jnp.dot(
        raw_grad, latent_weights.T, preferred_element_type=jnp.float32
    )
    attn_gain_grad = jnp.sum(normed_grad * hidden_f * scale_one, 0)
    hidden_grad = lax.dynamic_slice_in_dim(residual_grad, start_row, tok_dev, 0) + norm_back(
        hidden_f, scale_one, gain_one, normed_grad
    )
    (
        query_proj_grad,
        expand_proj_grad,
        output_proj_grad,
        shared_gate_out,
        shared_up_out,
        shared_down_out,
    ) = (
        lax.psum_scatter(
            query_grad_w.astype(jnp.bfloat16), "dp", scatter_dimension=0, tiled=True
        ).astype(jnp.float32),
        lax.psum_scatter(
            expand_grad_w.astype(jnp.bfloat16), "dp", scatter_dimension=0, tiled=True
        ).astype(jnp.float32),
        lax.psum_scatter(
            output_grad_w.astype(jnp.bfloat16), "dp", scatter_dimension=1, tiled=True
        ).astype(jnp.float32),
        lax.psum_scatter(
            shared_gate_grad.astype(jnp.bfloat16), "dp", scatter_dimension=0, tiled=True
        ).astype(jnp.float32),
        lax.psum_scatter(
            shared_up_grad.astype(jnp.bfloat16), "dp", scatter_dimension=0, tiled=True
        ).astype(jnp.float32),
        lax.psum_scatter(
            shared_down_grad.astype(jnp.bfloat16), "dp", scatter_dimension=1, tiled=True
        ).astype(jnp.float32),
    )
    attn_gain_out, latent_proj_grad, latent_gain_out, second_gain_out, router_out = (
        lax.psum_scatter(attn_gain_grad, ("dp", "tensor"), scatter_dimension=0, tiled=True),
        lax.psum_scatter(latent_grad_w, ("dp", "tensor"), scatter_dimension=0, tiled=True),
        lax.psum_scatter(kv_gain_grad, ("dp", "tensor"), scatter_dimension=0, tiled=True),
        lax.psum_scatter(second_gain_grad, ("dp", "tensor"), scatter_dimension=0, tiled=True),
        lax.psum_scatter(router_grad, ("dp", "tensor"), scatter_dimension=0, tiled=True),
    )
    return (
        output,
        hidden_grad,
        attn_gain_out,
        query_proj_grad,
        latent_proj_grad,
        latent_gain_out,
        expand_proj_grad,
        output_proj_grad,
        second_gain_out,
        router_out,
        expert_gate_grad,
        expert_up_grad,
        expert_down_grad,
        shared_gate_out,
        shared_up_out,
        shared_down_out,
    )


def solution(mesh):
    return jax.shard_map(
        shards,
        mesh=mesh,
        in_specs=(
            P(("dp", "tensor"), None),
            P("dp", None),
            P("dp"),
            P("dp"),
            P("dp", "tensor"),
            P("dp", None),
            P("dp"),
            P("dp", "tensor"),
            P("tensor", "dp"),
            P("dp"),
            P("dp", None),
            P("dp", "tensor", None),
            P("dp", "tensor", None),
            P("dp", "tensor", None),
            P("dp", "tensor"),
            P("dp", "tensor"),
            P("tensor", "dp"),
            P(("dp", "tensor"), None),
        ),
        out_specs=(
            P(("dp", "tensor"), None),
            P(("dp", "tensor"), None),
            P(("dp", "tensor")),
            P("dp", "tensor"),
            P(("dp", "tensor"), None),
            P(("dp", "tensor")),
            P("dp", "tensor"),
            P("tensor", "dp"),
            P(("dp", "tensor")),
            P(("dp", "tensor"), None),
            P("dp", "tensor", None),
            P("dp", "tensor", None),
            P("dp", "tensor", None),
            P("dp", "tensor"),
            P("dp", "tensor"),
            P("tensor", "dp"),
        ),
        check_vma=False,
    )
```

profile of v0, /device:TPU:0, one launch (start us, length us, event | category | flops | bytes accessed | tf_op | source)
XLA Modules:
  0.0 3478.9 jit_solution(13352248595725869544)
XLA Ops:
  8.0 20.6 all-gather
  31.4 27.8 all-reduce.4
  91.2 24.5 all-gather.15.cloned.1.call-done
  118.8 30.5 all-gather.19.cloned.1.call-done
  149.3 74.4 %all-gather.17.cloned.1.call-done = bf16[1024,2048]{1,0:T(8,128)(2,1)} async-done(((bf16[128,2048]{1,0:T(8,128)(2,1)}), bf16[1024,2048]{1,0:T(8,128)(2,1)}) %all-gather.17.cloned.1.call-update) | async-done | bytes 4194320 | tf_op jit(solution)/shard_map/all_gather | solution.py:151
  261.8 85.3 %reduce-scatter.23.cloned.1.call-done = bf16[128,2048]{1,0:T(8,128)(2,1)} async-done(((bf16[1024,2048]{1,0:T(8,128)(2,1)}), bf16[128,2048]{1,0:T(8,128)(2,1)}) %reduce-scatter.23.cloned.1.call-update) | async-done | bytes 524304 | tf_op jit(solution)/shard_map/reduce_scatter | solution.py:194
  369.4 31.8 reduce-window.6
  429.7 22.9 gather_fusion
  458.8 122.7 %all_to_all.20 = bf16[16,4,40,2048]{3,2,1,0:T(8,128)(2,1)} all-to-all(bf16[16,4,40,2048]{3,2,1,0:T(8,128)(2,1)S(1)} %bitcast.232), channel_id=1, replica_groups=mesh['dp'=16,'tensor'=8] {'dp'}, dimensions={0} | all-to-all | bytes 20971520 | tf_op jit(solution)/shard_map/all_to_all | solution.py:231
  622.2 153.1 %all_gather.58 = bf16[2048,64]{0,1:T(8,128)(2,1)S(1)} all-gather(bf16[128,64]{0,1:T(8,128)(2,1)S(1)} %copy-done.84), channel_id=1, replica_groups=mesh['dp'=16,'tensor'=8] {'dp'}, dimensions={0}, use_global_device_ids=true | all-gather | bytes 278528 | tf_op jit(solution)/shard_map/all_gather | solution.py:133
  786.1 20.5 mul.623
  811.4 23.0 gather_fusion.2
  850.2 23.5 gather_fusion.1
  892.3 22.4 psum.15
  930.9 126.5 %all_to_all.21 = bf16[16,4,40,2048]{3,2,1,0:T(8,128)(2,1)} all-to-all(bf16[16,4,40,2048]{3,2,1,0:T(8,128)(2,1)S(1)} %bitcast.231), channel_id=1, replica_groups=mesh['dp'=16,'tensor'=8] {'dp'}, dimensions={0} | all-to-all | bytes 20971520 | tf_op jit(solution)/shard_map/all_to_all | solution.py:232
  1110.0 111.0 %all-gather.25.cloned.1.call-done = bf16[2048,352]{0,1:T(8,128)(2,1)} async-done(((bf16[128,352]{0,1:T(8,128)(2,1)}), bf16[2048,352]{0,1:T(8,128)(2,1)}) %all-gather.25.cloned.1.call-update) | async-done | bytes 1441808 | tf_op jit(solution)/shard_map/all_gather | solution.py:134
  1226.3 42.2 %all-gather.27.cloned.1.call-done = bf16[2048,352]{0,1:T(8,128)(2,1)} async-done(((bf16[128,352]{0,1:T(8,128)(2,1)}), bf16[2048,352]{0,1:T(8,128)(2,1)}) %all-gather.27.cloned.1.call-update) | async-done | bytes 1441808 | tf_op jit(solution)/shard_map/all_gather | solution.py:135
  1273.9 30.4 all-gather.29.cloned.1.call-done
  1329.2 23.5 gather_fusion.3
  1384.5 24.8 reduce_sum.201
  1420.3 109.0 %all-reduce.11.cloned.1.call-done = bf16[1024,2048]{1,0:T(8,128)(2,1)} async-done(((bf16[1024,2048]{1,0:T(8,128)(2,1)}), bf16[1024,2048]{1,0:T(8,128)(2,1)}) %all-reduce.11.cloned.1.call-update) | async-done | bytes 4194320 | tf_op jit(solution)/shard_map/psum | solution.py:303
  1628.2 29.3 multiply_reduce_fusion.1
  1699.6 61.6 %reduce-scatter.43.cloned.1.call-done = bf16[128,352]{1,0:T(8,128)(2,1)} async-done(((bf16[2048,352]{1,0:T(8,128)(2,1)}), bf16[128,352]{1,0:T(8,128)(2,1)}) %reduce-scatter.43.cloned.1.call-update) | async-done | bytes 90128
  1763.0 61.6 %reduce-scatter.45.cloned.1.call-done = bf16[128,352]{1,0:T(8,128)(2,1)} async-done(((bf16[2048,352]{1,0:T(8,128)(2,1)}), bf16[128,352]{1,0:T(8,128)(2,1)}) %reduce-scatter.45.cloned.1.call-update) | async-done | bytes 90128
  1849.5 36.3 %reduce-scatter.33.cloned.1.call-done = bf16[32,512]{1,0:T(8,128)(2,1)} async-done(((bf16[512,512]{1,0:T(8,128)(2,1)}), bf16[32,512]{1,0:T(8,128)(2,1)}) %reduce-scatter.33.cloned.1.call-update) | async-done | bytes 32784 | tf_op jit(solution)/shard_map/reduce_scatter | solution.py:435
  1887.2 60.9 %reduce-scatter.39.cloned.1.call-done = bf16[128,256]{1,0:T(8,128)(2,1)} async-done(((bf16[2048,256]{1,0:T(8,128)(2,1)}), bf16[128,256]{1,0:T(8,128)(2,1)}) %reduce-scatter.39.cloned.1.call-update) | async-done | bytes 65552
  1949.7 62.0 %reduce-scatter.29.cloned.1.call-done = bf16[128,384]{1,0:T(8,128)(2,1)} async-done(((bf16[2048,384]{1,0:T(8,128)(2,1)}), bf16[128,384]{1,0:T(8,128)(2,1)}) %reduce-scatter.29.cloned.1.call-update) | async-done | bytes 98320 | tf_op jit(solution)/shard_map/reduce_scatter | solution.py:432
  2013.5 85.9 %reduce-scatter.25.cloned.1.call-done = bf16[128,2048]{1,0:T(8,128)(2,1)} async-done(((bf16[1024,2048]{1,0:T(8,128)(2,1)}), bf16[128,2048]{1,0:T(8,128)(2,1)}) %reduce-scatter.25.cloned.1.call-update) | async-done | bytes 524304 | tf_op jit(solution)/shard_map/reduce_scatter | solution.py:298
  2099.3 88.0 %reduce-scatter.27.cloned.1.call-done = bf16[128,2048]{1,0:T(8,128)(2,1)} async-done(((bf16[1024,2048]{1,0:T(8,128)(2,1)}), bf16[128,2048]{1,0:T(8,128)(2,1)}) %reduce-scatter.27.cloned.1.call-update) | async-done | bytes 524304 | tf_op jit(solution)/shard_map/reduce_scatter | solution.py:400
  2192.4 66.0 %all-reduce.8 = (f32[2048]{0:T(1024)S(1)}, f32[512]{0:T(512)S(1)}, f32[2048]{0:T(1024)S(1)}) all-reduce(f32[2048]{0:T(1024)} %get-tuple-element.18, f32[512]{0:T(512)} %get-tuple-element.20, f32[2048]{0:T(1024)} %get-tuple-element.22), channel_id=6, replica_groups=mesh['dp'=16,'tensor'=8] {'dp','tensor'}, use_global_device_ids=true, to_apply=%region_32.35.clone | all-reduce | flops 4608 | bytes 36864
  2263.7 564.6 %reduce-scatter.35.cloned.1.call-done = f32[16,64]{1,0:T(8,128)} async-done(((f32[2048,64]{1,0:T(8,128)}), f32[16,64]{1,0:T(8,128)}) %reduce-scatter.35.cloned.1.call-update) | async-done | bytes 4112 | tf_op jit(solution)/shard_map/reduce_scatter | solution.py:456
  2828.3 643.9 %reduce-scatter.31.cloned.1.call-done = f32[16,576]{1,0:T(8,128)} async-done(((f32[2048,576]{1,0:T(8,128)}), f32[16,576]{1,0:T(8,128)}) %reduce-scatter.31.cloned.1.call-update) | async-done | bytes 36880 | tf_op jit(solution)/shard_map/reduce_scatter | solution.py:453
  (437 shorter events, 551.5 us)
Async XLA Ops:
  7.2 593.7 %copy-start = (bf16[4,176,2048]{2,1,0:T(8,128)(2,1)S(1)}, bf16[4,176,2048]{2,1,0:T(8,128)(2,1)}, u32[]{:S(2)}) copy-start(bf16[4,176,2048]{2,1,0:T(8,128)(2,1)} %param.35) | copy-start | bytes 8650756
  7.2 55.6 %all-gather.13.cloned.1.call-start = ((), (), s32[]{:S(2)}) async-start(), calls=%async_computation.16 | async-start | bytes 2506752 | tf_op jit(solution)/shard_map/all_gather | solution.py:128
  7.9 107.8 %all-gather.15.cloned.1.call-start = ((), (), s32[]{:S(2)}) async-start(), calls=%async_computation.17 | async-start | bytes 1327104 | tf_op jit(solution)/shard_map/all_gather | solution.py:152
  67.1 82.2 %all-gather.19.cloned.1.call-start = ((), (), s32[]{:S(2)}) async-start(), calls=%async_computation.19 | async-start | bytes 1671168 | tf_op jit(solution)/shard_map/all_gather | solution.py:127
  67.8 155.9 %all-gather.17.cloned.1.call-start = ((), (), s32[]{:S(2)}) async-start(), calls=%async_computation.18 | async-start | bytes 4718592 | tf_op jit(solution)/shard_map/all_gather | solution.py:151
  68.4 188.6 %all-gather.21.cloned.1.call-start = ((), (), s32[]{:S(2)}) async-start(), calls=%async_computation.20 | async-start | bytes 1114112 | tf_op jit(solution)/shard_map/all_gather | solution.py:131
  69.0 278.2 %reduce-scatter.23.cloned.1.call-start = ((), (), s32[]{:S(2)}) async-start(), calls=%async_computation.21 | async-start | bytes 4718592 | tf_op jit(solution)/shard_map/reduce_scatter | solution.py:194
  89.2 146.4 %copy-start.45 = (f32[1024,32]{0,1:T(8,128)}, f32[1024,32]{0,1:T(8,128)S(1)}, u32[]{:S(2)}) copy-start(f32[1024,32]{0,1:T(8,128)S(1)} %get-tuple-element.52) | copy-start | bytes 393220
  261.7 158.6 %all-gather.23.cloned.1.call-start = ((), (), s32[]{:S(2)}) async-start(), calls=%async_computation.22 | async-start | bytes 4718592 | tf_op jit(solution)/shard_map/all_gather | solution.py:198
  458.8 122.7 %copy-start.32 = (bf16[4,176,2048]{2,1,0:T(8,128)(2,1)S(1)}, bf16[4,176,2048]{2,1,0:T(8,128)(2,1)}, u32[]{:S(2)}) copy-start(bf16[4,176,2048]{2,1,0:T(8,128)(2,1)} %param.33) | copy-start | bytes 8650756
  616.5 221.6 %all-to-all-start.1 = ((bf16[16,4,40,2048]{3,2,1,0:T(8,128)(2,1)}), bf16[16,4,40,2048]{3,2,1,0:T(8,128)(2,1)}, u32[]{:S(2)}, u32[]{:S(2)}) async-start(bf16[16,4,40,2048]{3,2,1,0:T(8,128)(2,1)} %copy.110), calls=%async_computation.2 | async-start | bytes 20971520 | tf_op jit(solution)/shard_map/all_to_all | solution.py:263
  621.5 154.1 %all-gather.31.cloned.1.call-start = ((), (), s32[]{:S(2)}) async-start(), calls=%async_computation.27 | async-start | bytes 4718592 | tf_op jit(solution)/shard_map/all_gather | solution.py:153
  1102.8 213.8 %all-to-all-start.3 = ((bf16[16,4,40,2048]{3,2,1,0:T(8,128)(2,1)}), bf16[16,4,40,2048]{3,2,1,0:T(8,128)(2,1)}, u32[]{:S(2)}, u32[]{:S(2)}) async-start(bf16[16,4,40,2048]{3,2,1,0:T(8,128)(2,1)} %copy.113), calls=%async_computation.5 | async-start | bytes 20971520 | tf_op jit(solution)/shard_map/all_to_all | solution.py:266
  1107.6 113.3 %all-gather.25.cloned.1.call-start = ((), (), s32[]{:S(2)}) async-start(), calls=%async_computation.23 | async-start | bytes 1531904 | tf_op jit(solution)/shard_map/all_gather | solution.py:134
  1108.3 160.2 %all-gather.27.cloned.1.call-start = ((), (), s32[]{:S(2)}) async-start(), calls=%async_computation.24 | async-start | bytes 1531904 | tf_op jit(solution)/shard_map/all_gather | solution.py:135
  1108.9 195.4 %all-gather.29.cloned.1.call-start = ((), (), s32[]{:S(2)}) async-start(), calls=%async_computation.25 | async-start | bytes 1531904 | tf_op jit(solution)/shard_map/all_gather | solution.py:136
  1109.7 419.7 %all-reduce.11.cloned.1.call-start = ((), (), s32[]{:S(2)}) async-start(), calls=%async_computation.28 | async-start | bytes 8388608 | tf_op jit(solution)/shard_map/psum | solution.py:303
  1419.6 255.0 %reduce-scatter.37.cloned.1.call-start = ((), (), s32[]{:S(2)}) async-start(), calls=%async_computation.34 | async-start | bytes 1474560
  1561.1 136.9 %reduce-scatter.41.cloned.1.call-start = ((), (), s32[]{:S(2)}) async-start(), calls=%async_computation.36 | async-start | bytes 1671168
  1569.0 192.2 %reduce-scatter.43.cloned.1.call-start = ((), (), s32[]{:S(2)}) async-start(), calls=%async_computation.37 | async-start | bytes 1671168
  1576.7 247.8 %reduce-scatter.45.cloned.1.call-start = ((), (), s32[]{:S(2)}) async-start(), calls=%async_computation.38 | async-start | bytes 1671168
  1584.5 301.3 %reduce-scatter.33.cloned.1.call-start = ((), (), s32[]{:S(2)}) async-start(), calls=%async_computation.32 | async-start | bytes 557056 | tf_op jit(solution)/shard_map/reduce_scatter | solution.py:435
  1587.6 360.4 %reduce-scatter.39.cloned.1.call-start = ((), (), s32[]{:S(2)}) async-start(), calls=%async_computation.35 | async-start | bytes 1114112
  1596.4 415.3 %reduce-scatter.29.cloned.1.call-start = ((), (), s32[]{:S(2)}) async-start(), calls=%async_computation.30 | async-start | bytes 1671168 | tf_op jit(solution)/shard_map/reduce_scatter | solution.py:432
  1607.6 491.7 %reduce-scatter.25.cloned.1.call-start = ((), (), s32[]{:S(2)}) async-start(), calls=%async_computation.26 | async-start | bytes 4718592 | tf_op jit(solution)/shard_map/reduce_scatter | solution.py:298
  1665.4 521.9 %reduce-scatter.27.cloned.1.call-start = ((), (), s32[]{:S(2)}) async-start(), calls=%async_computation.29 | async-start | bytes 4718592 | tf_op jit(solution)/shard_map/reduce_scatter | solution.py:400
  1671.4 1156.9 %reduce-scatter.35.cloned.1.call-start = ((), (), s32[]{:S(2)}) async-start(), calls=%async_computation.33 | async-start | bytes 1056768 | tf_op jit(solution)/shard_map/reduce_scatter | solution.py:456
  1674.3 1797.8 %reduce-scatter.31.cloned.1.call-start = ((), (), s32[]{:S(2)}) async-start(), calls=%async_computation.31 | async-start | bytes 5283840 | tf_op jit(solution)/shard_map/reduce_scatter | solution.py:453
  1680.0 146.2 %copy-start.44 = (bf16[16,4,40,176]{3,2,0,1:T(8,128)(2,1)S(1)}, bf16[16,4,40,176]{3,2,0,1:T(8,128)(2,1)}, u32[]{:S(2)}) copy-start(bf16[16,4,40,176]{3,2,0,1:T(8,128)(2,1)} %copy-done.43) | copy-start | bytes 2703364
  1844.5 342.8 %copy-start.15 = (bf16[128,2048]{1,0:T(8,128)(2,1)S(1)}, bf16[128,2048]{1,0:T(8,128)(2,1)}, u32[]{:S(2)}) copy-start(bf16[128,2048]{1,0:T(8,128)(2,1)} %param.22) | copy-start | bytes 1572868
  1844.5 342.8 %copy-start.62 = (f32[16,1,128]{2,1,0:T(1,128)S(1)}, f32[16,1,128]{2,1,0:T(1,128)}, u32[]{:S(2)}) copy-start(f32[16,1,128]{2,1,0:T(1,128)} %copy-done.61) | copy-start | bytes 24580
  2011.7 1460.4 %copy-start.1 = (bf16[4,176,2048]{2,1,0:T(8,128)(2,1)S(1)}, bf16[4,176,2048]{2,1,0:T(8,128)(2,1)}, u32[]{:S(2)}) copy-start(bf16[4,176,2048]{2,1,0:T(8,128)(2,1)} %param.35) | copy-start | bytes 8650756
  (98 other events, 1648.9 us)
Sparse Core Ops, SparseCore 0:
  9.7 40.7 all-gather.12
  67.2 48.4 all-gather.14
  117.4 31.8 all-gather.18
  152.0 71.6 all-gather.16
  225.2 31.7 all-gather.20
  261.9 85.1 reduce-scatter.22
  350.0 70.2 all-gather.22
  624.7 150.8 all-gather.30
  1110.1 110.8 all-gather.24
  1222.4 46.0 all-gather.26
  1270.1 34.1 all-gather.28
  1419.7 109.6 all-reduce.10
  1561.2 72.4 reduce-scatter.36
  1636.7 61.2 reduce-scatter.40
  1700.2 61.0 reduce-scatter.42
  1763.6 60.8 reduce-scatter.44
  1826.7 59.0 reduce-scatter.32
  1888.1 59.8 reduce-scatter.38
  1950.4 61.2 reduce-scatter.28
  2015.9 83.3 reduce-scatter.24
  2103.7 83.5 reduce-scatter.26
  2190.3 637.8 reduce-scatter.34
  2831.2 640.8 reduce-scatter.30
where the time goes:
time: 3490 us; the launch traced here: 3480 us
  waiting for transfers between devices  2210 us (63%)
  blocking collectives  577 us (17%)
  local copies, waits for them, and re-layouts  254 us (7%)
  matrix products  220 us (6%)
  other arithmetic  190 us (5%)
    reduce_scatter x1, waiting for transfers between devices, shards(): lax.psum_scatter(latent_grad_w, ('dp', 'tensor'), scatter_dimension=0, ti...  644 us
    reduce_scatter x1, waiting for transfers between devices, shards(): lax.psum_scatter(router_grad, ('dp', 'tensor'), scatter_dimension=0, tile...  565 us
    unnamed x28, waiting for transfers between devices  206 us
    all_gather x1, blocking collectives, shards(): lax.all_gather(router_proj, 'dp', axis=0, tiled=True)  153 us
    all_to_all x1, blocking collectives, shards(): lax.all_to_all(send_grads, 'dp', split_axis=0, concat_axis=0, tiled=True)  127 us
    all_to_all x1, blocking collectives, shards(): lax.all_to_all(send_rows, 'dp', split_axis=0, concat_axis=0, tiled=True)  123 us
    all_gather x1, waiting for transfers between devices, shards(): lax.all_gather(shared_gate, 'dp', axis=0, tiled=True)  111 us
    psum x1, waiting for transfers between devices, shards(): lax.psum((jnp.sum(picked_back, 1) + shared_back).astype(jnp.bfloat16), 't...  109 us
  transfers between devices with their start and end apart: 25, of which 21 were waited for; matrix products, arithmetic and copies ran while one was open for 9% of the time, Pallas kernels for 0%

commit v1 on v0

--- a/solution.py
+++ b/solution.py
@@ -3,6 +3,8 @@
 import jax
 import jax.numpy as jnp
 from jax import lax
+from jax.experimental import pallas as pl
+from jax.experimental.pallas import tpu as pltpu
 from jax.sharding import PartitionSpec as P
 
 D = 2048
@@ -82,6 +84,150 @@
         jnp.bfloat16
     )
     return (gate_grad, up_grad)
+
+
+def dispatch_kernel(tok_ref, rows_hbm, grads_hbm, col_ref, out_ref, rows_buf, grads_buf, sems):
+    block = rows_buf.shape[0]
+    tile_rows = rows_buf.shape[1]
+    last = rows_hbm.shape[0] - 1
+    base = pl.program_id(0) * block
+
+    def start(r, carry):
+        tok = jnp.minimum(tok_ref[base + r], last)
+        pltpu.make_async_copy(rows_hbm.at[tok], rows_buf.at[r], sems.at[0, r]).start()
+        pltpu.make_async_copy(grads_hbm.at[tok], grads_buf.at[r], sems.at[1, r]).start()
+        return carry
+
+    lax.fori_loop(0, block, start, 0)
+
+    def finish(r, carry):
+        pltpu.make_async_copy(rows_hbm.at[0], rows_buf.at[r], sems.at[0, r]).wait()
+        pltpu.make_async_copy(grads_hbm.at[0], grads_buf.at[r], sems.at[1, r]).wait()
+        return carry
+
+    lax.fori_loop(0, block, finish, 0)
+    rows = rows_buf[...]
+    out_ref[:, :tile_rows, :] = jnp.where(col_ref[0] > 0, rows, jnp.zeros_like(rows))
+    out_ref[:, tile_rows:, :] = (grads_buf[...].astype(jnp.float32) * col_ref[1]).astype(
+        out_ref.dtype
+    )
+
+
+def dispatch_rows(slot_token, rows, grads, valid, gate, block=128):
+    slots = slot_token.shape[0]
+    count, width = rows.shape
+    tile_rows = width // 128
+    cols = jnp.broadcast_to(jnp.stack([valid, gate])[:, :, None, None], (2, slots, 1, 128))
+    out = pl.pallas_call(
+        dispatch_kernel,
+        out_shape=jax.ShapeDtypeStruct((slots, 2 * tile_rows, 128), rows.dtype),
+        grid_spec=pltpu.PrefetchScalarGridSpec(
+            num_scalar_prefetch=1,
+            grid=(slots // block,),
+            in_specs=[
+                pl.BlockSpec(memory_space=pl.ANY),
+                pl.BlockSpec(memory_space=pl.ANY),
+                pl.BlockSpec((2, block, 1, 128), lambda i, tok: (0, i, 0, 0)),
+            ],
+            out_specs=pl.BlockSpec((block, 2 * tile_rows, 128), lambda i, tok: (i, 0, 0)),
+            scratch_shapes=[
+                pltpu.VMEM((block, tile_rows, 128), rows.dtype),
+                pltpu.VMEM((block, tile_rows, 128), grads.dtype),
+                pltpu.SemaphoreType.DMA((2, block)),
+            ],
+        ),
+        cost_estimate=pl.CostEstimate(
+            flops=slots * width, transcendentals=0, bytes_accessed=4 * slots * 2 * width
+        ),
+    )(slot_token, rows.reshape(count, tile_rows, 128), grads.reshape(count, tile_rows, 128), cols)
+    return out
+
+
+def combine_kernel(
+    slot_ref, table_hbm, gate_ref, grad_ref, shared_out_ref, shared_back_ref,
+    feed_ref, back_ref, part_ref, picked, sems,
+):
+    top = picked.shape[0]
+    block = picked.shape[1]
+    tile_rows = grad_ref.shape[1]
+    last = table_hbm.shape[0] - 1
+    base = pl.program_id(0) * block
+
+    def start(r, carry):
+        for k in range(top):
+            slot = jnp.clip(slot_ref[(base + r) * top + k], 0, last)
+            pltpu.make_async_copy(table_hbm.at[slot], picked.at[k, r], sems.at[k, r]).start()
+        return carry
+
+    lax.fori_loop(0, block, start, 0)
+
+    def finish(r, carry):
+        for k in range(top):
+            pltpu.make_async_copy(table_hbm.at[0], picked.at[k, r], sems.at[k, r]).wait()
+        return carry
+
+    lax.fori_loop(0, block, finish, 0)
+    grad = grad_ref[...].astype(jnp.float32)
+    weighted = None
+    backs = None
+    lanes = lax.broadcasted_iota(jnp.int32, part_ref.shape, 2)
+    parts = jnp.zeros(part_ref.shape, jnp.float32)
+    for k in range(top):
+        out_k = picked[k, :, :tile_rows, :].astype(jnp.float32)
+        term = gate_ref[k] * out_k
+        weighted = term if weighted is None else weighted + term
+        back_k = picked[k, :, tile_rows:, :].astype(jnp.float32)
+        backs = back_k if backs is None else backs + back_k
+        dot_k = jnp.sum(jnp.sum(grad * out_k, 2, keepdims=True), 1, keepdims=True)
+        parts = jnp.where(lanes == k, dot_k, parts)
+    feed_ref[...] = (shared_out_ref[...] + weighted).astype(feed_ref.dtype)
+    back_ref[...] = (backs + shared_back_ref[...]).astype(back_ref.dtype)
+    part_ref[...] = parts
+
+
+def combine_rows(slot_index, table, gate_values, grad, shared_out, shared_back, block=128):
+    tokens, top = gate_values.shape
+    width = grad.shape[1]
+    tile_rows = width // 128
+    gates = jnp.broadcast_to(gate_values.T[:, :, None, None], (top, tokens, 1, 128))
+    row_spec = pl.BlockSpec((block, tile_rows, 128), lambda i, s: (i, 0, 0))
+    feed, back, parts = pl.pallas_call(
+        combine_kernel,
+        out_shape=(
+            jax.ShapeDtypeStruct((tokens, tile_rows, 128), jnp.bfloat16),
+            jax.ShapeDtypeStruct((tokens, tile_rows, 128), jnp.bfloat16),
+            jax.ShapeDtypeStruct((tokens, 1, 128), jnp.float32),
+        ),
+        grid_spec=pltpu.PrefetchScalarGridSpec(
+            num_scalar_prefetch=1,
+            grid=(tokens // block,),
+            in_specs=[
+                pl.BlockSpec(memory_space=pl.ANY),
+                pl.BlockSpec((top, block, 1, 128), lambda i, s: (0, i, 0, 0)),
+                row_spec,
+                row_spec,
+                row_spec,
+            ],
+            out_specs=[row_spec, row_spec, pl.BlockSpec((block, 1, 128), lambda i, s: (i, 0, 0))],
+            scratch_shapes=[
+                pltpu.VMEM((top, block, 2 * tile_rows, 128), table.dtype),
+                pltpu.SemaphoreType.DMA((top, block)),
+            ],
+        ),
+        cost_estimate=pl.CostEstimate(
+            flops=8 * tokens * top * width,
+            transcendentals=0,
+            bytes_accessed=tokens * (top * 4 * width + 2 * width + 8 * width + 4 * width),
+        ),
+    )(
+        slot_index.reshape(-1),
+        table.reshape(table.shape[0], 2 * tile_rows, 128),
+        gates,
+        grad.reshape(tokens, tile_rows, 128),
+        shared_out.reshape(tokens, tile_rows, 128),
+        shared_back.reshape(tokens, tile_rows, 128),
+    )
+    return feed.reshape(tokens, width), back.reshape(tokens, width), parts[:, 0, :top]
 
 
 def shards(
@@ -110,50 +256,67 @@
     dp_size = lax.axis_size("dp")
     seq_len = tok_dev * tensor_size
     start_row = tensor_rank * tok_dev
-    (
-        attn_gains,
-        query_weights,
-        latent_weights,
-        kv_gains,
-        expand_weights,
-        output_weights,
-        second_gains,
-        router_weights,
-        gate_shared,
-        up_shared,
-        down_shared,
-    ) = (
-        lax.all_gather(attn_gain, "dp", axis=0, tiled=True),
-        lax.all_gather(query_proj, "dp", axis=0, tiled=True),
-        lax.all_gather(latent_proj, "dp", axis=0, tiled=True),
-        lax.all_gather(latent_gain, "dp", axis=0, tiled=True),
-        lax.all_gather(expand_proj, "dp", axis=0, tiled=True),
-        lax.all_gather(output_proj, "dp", axis=1, tiled=True),
-        lax.all_gather(second_gain, "dp", axis=0, tiled=True),
-        lax.all_gather(router_proj, "dp", axis=0, tiled=True),
-        lax.all_gather(shared_gate, "dp", axis=0, tiled=True),
-        lax.all_gather(shared_up, "dp", axis=0, tiled=True),
-        lax.all_gather(shared_down, "dp", axis=1, tiled=True),
-    )
-    hidden_f = hidden.astype(jnp.float32)
-    scale_one = norm_scale(hidden_f)
+    rows_dp = attn_gain.shape[0]
+    kv_rows = latent_gain.shape[0]
+    head_cols = query_proj.shape[1]
+    latent_cols = latent_proj.shape[1]
+    expand_cols = expand_proj.shape[1]
+    expand_flat_cols = kv_rows * expand_cols // rows_dp
+    first_pack = jnp.concatenate(
+        [
+            query_proj,
+            latent_proj,
+            expand_proj.reshape(rows_dp, expand_flat_cols),
+            attn_gain[:, None],
+            jnp.pad(latent_gain, (0, rows_dp - kv_rows))[:, None],
+        ],
+        1,
+    )
+    first_all = lax.all_gather(first_pack, "dp", axis=0, tiled=True)
+    cut = [0]
+    for width in (head_cols, latent_cols, expand_flat_cols, 1, 1):
+        cut.append(cut[-1] + width)
+    query_weights = first_all[:, cut[0] : cut[1]]
+    latent_weights = first_all[:, cut[1] : cut[2]]
+    expand_weights = first_all[:, cut[2] : cut[3]].reshape(dp_size * kv_rows, expand_cols)
+    attn_gains = first_all[:, cut[3]]
+    kv_gains = first_all[:, cut[4]].reshape(dp_size, rows_dp)[:, :kv_rows].reshape(-1)
+    out_cols = output_proj.shape[0]
+    experts = router_proj.shape[1]
+    shared_cols = shared_gate.shape[1]
+    second_pack = jnp.concatenate([output_proj.T, second_gain[:, None], router_proj], 1)
+    second_all = lax.all_gather(second_pack, "dp", axis=0, tiled=True)
+    output_weights_t = second_all[:, :out_cols]
+    second_gains = second_all[:, out_cols]
+    router_weights = second_all[:, out_cols + 1 :]
+    shared_local = jnp.concatenate([shared_gate, shared_up, shared_down.T], 1)
+
+    hidden_all = lax.all_gather(hidden, "tensor", axis=0, tiled=True)
+    grad_seq = lax.all_gather(out_grad, "tensor", axis=0, tiled=True)
+    hidden_all_f = hidden_all.astype(jnp.float32)
+    scale_one_all = norm_scale(hidden_all_f)
     gain_one = attn_gains.astype(jnp.float32)
-    normed_own = (hidden_f * scale_one * gain_one).astype(jnp.bfloat16)
-    latent_raw = jnp.dot(normed_own, latent_weights, preferred_element_type=jnp.float32)
-    compressed = latent_raw[:, :KVR]
-    scale_kv = norm_scale(compressed)
+    normed_all = (hidden_all_f * scale_one_all * gain_one).astype(jnp.bfloat16)
+    hidden_f = lax.dynamic_slice_in_dim(hidden_all_f, start_row, tok_dev, 0)
+    scale_one = lax.dynamic_slice_in_dim(scale_one_all, start_row, tok_dev, 0)
+    normed_own = lax.dynamic_slice_in_dim(normed_all, start_row, tok_dev, 0)
+    latent_raw_all = jnp.dot(normed_all, latent_weights, preferred_element_type=jnp.float32)
+    compressed_all = latent_raw_all[:, :KVR]
+    scale_kv_all = norm_scale(compressed_all)
     gain_kv = kv_gains.astype(jnp.float32)
-    own_cosines, own_sines = rope_tables(start_row + jnp.arange(tok_dev), DR)
-    latent_packed = jnp.concatenate(
-        [compressed * scale_kv * gain_kv, rotate(latent_raw[:, KVR:], own_cosines, own_sines)], -1
+    all_cosines, all_sines = rope_tables(jnp.arange(seq_len), DR)
+    latent_seq = jnp.concatenate(
+        [
+            compressed_all * scale_kv_all * gain_kv,
+            rotate(latent_raw_all[:, KVR:], all_cosines, all_sines),
+        ],
+        -1,
     ).astype(jnp.bfloat16)
-    normed_all, latent_seq, grad_seq = (
-        lax.all_gather(normed_own, "tensor", axis=0, tiled=True),
-        lax.all_gather(latent_packed, "tensor", axis=0, tiled=True),
-        lax.all_gather(out_grad, "tensor", axis=0, tiled=True),
-    )
+    compressed = lax.dynamic_slice_in_dim(compressed_all, start_row, tok_dev, 0)
+    scale_kv = lax.dynamic_slice_in_dim(scale_kv_all, start_row, tok_dev, 0)
+    own_cosines = lax.dynamic_slice_in_dim(all_cosines, start_row, tok_dev, 0)
+    own_sines = lax.dynamic_slice_in_dim(all_sines, start_row, tok_dev, 0)
     head_count = query_weights.shape[1] // (DN + DR)
-    all_cosines, all_sines = rope_tables(jnp.arange(seq_len), DR)
     query_raw = jnp.dot(normed_all, query_weights, preferred_element_type=jnp.float32).reshape(
         seq_len, head_count, DN + DR
     )
@@ -190,26 +353,25 @@
             ).astype(jnp.bfloat16)
         )
     mixed_all = jnp.concatenate(mixed_list, 0).reshape(seq_len, head_count * DV)
-    attn_part = jnp.dot(mixed_all, output_weights, preferred_element_type=jnp.float32)
-    attn_own = lax.psum_scatter(
-        attn_part.astype(jnp.bfloat16), "tensor", scatter_dimension=0, tiled=True
-    ).astype(jnp.float32)
-    residual_own = hidden_f + attn_own
-    residual_all = lax.all_gather(
-        residual_own.astype(jnp.bfloat16), "tensor", axis=0, tiled=True
-    ).astype(residual_own.dtype)
+    attn_part = jnp.einsum(
+        "tk,dk->td", mixed_all, output_weights_t, preferred_element_type=jnp.float32
+    )
+    branch_all = lax.psum(attn_part.astype(jnp.bfloat16), "tensor").astype(jnp.float32)
+    residual_all = hidden_all_f + branch_all
+    residual_own = lax.dynamic_slice_in_dim(residual_all, start_row, tok_dev, 0)
     scale_two = norm_scale(residual_all)
     gain_two = second_gains.astype(jnp.float32)
     normed_two = (residual_all * scale_two * gain_two).astype(jnp.bfloat16)
     logits = jnp.dot(normed_two, router_weights, preferred_element_type=jnp.float32)
-    experts = router_weights.shape[1]
     top_count = routes.shape[1]
     chosen_hot = routes[:, :, None] == jnp.arange(experts)[None, None, :]
     chosen_logits = jnp.sum(jnp.where(chosen_hot, logits[:, None, :], 0.0), -1)
     gate_values = jax.nn.softmax(chosen_logits, axis=-1)
-    flat_hot = chosen_hot.reshape(seq_len * top_count, experts).astype(jnp.int32)
-    earlier = jnp.cumsum(flat_hot, 0) - flat_hot
-    slot_pos = jnp.sum(earlier * flat_hot, -1)
+    assignments = seq_len * top_count
+    flat_hot = chosen_hot.reshape(assignments, experts).astype(jnp.bfloat16)
+    lower = (jnp.arange(assignments)[:, None] > jnp.arange(assignments)[None, :]).astype(jnp.bfloat16)
+    earlier = jnp.dot(lower, flat_hot, preferred_element_type=jnp.float32)
+    slot_pos = jnp.sum(earlier * flat_hot.astype(jnp.float32), -1).astype(jnp.int32)
     expert_ids = routes.reshape(-1)
     exp_dev = expert_gate.shape[0]
     capacity = tensor_size * (5 * seq_len * top_count // (4 * experts * tensor_size))
@@ -219,18 +381,20 @@
     slot_gate = (
         jnp.zeros((experts * capacity,), jnp.float32).at[slot_index].set(gate_values.reshape(-1))
     )
-    padded_normed = jnp.concatenate([normed_two, jnp.zeros((1, D), jnp.bfloat16)], 0)
-    padded_grad = jnp.concatenate([grad_seq, jnp.zeros((1, D), jnp.bfloat16)], 0)
-    send_rows = jnp.take(padded_normed, slot_token, axis=0).reshape(dp_size, exp_dev, capacity, D)
-    send_grads = (
-        (jnp.take(padded_grad, slot_token, axis=0).astype(jnp.float32) * slot_gate[:, None])
-        .astype(jnp.bfloat16)
-        .reshape(dp_size, exp_dev, capacity, D)
-    )
-    recv_rows, recv_grads = (
-        lax.all_to_all(send_rows, "dp", split_axis=0, concat_axis=0, tiled=True),
-        lax.all_to_all(send_grads, "dp", split_axis=0, concat_axis=0, tiled=True),
-    )
+    slot_valid = (slot_token < seq_len).astype(jnp.float32)
+    tile_rows = D // 128
+    send_both = dispatch_rows(slot_token, normed_two, grad_seq, slot_valid, slot_gate).reshape(
+        dp_size, exp_dev, capacity, 2 * tile_rows, 128
+    )
+    shared_local, send_both = lax.optimization_barrier((shared_local, send_both))
+    shared_all = lax.all_gather(shared_local, "dp", axis=0, tiled=True)
+    gate_shared = shared_all[:, :shared_cols]
+    up_shared = shared_all[:, shared_cols : 2 * shared_cols]
+    down_shared_t = shared_all[:, 2 * shared_cols :]
+    recv_both = lax.all_to_all(send_both, "dp", split_axis=0, concat_axis=0, tiled=True)
+    recv_both = recv_both.reshape(dp_size, exp_dev, capacity, 2 * D)
+    recv_rows = recv_both[..., :D]
+    recv_grads = recv_both[..., D:]
     gate_pre = jnp.einsum(
         "sjcd,jfd->sjcf", recv_rows, expert_gate, preferred_element_type=jnp.float32
     )
@@ -259,52 +423,59 @@
     row_grads = row_grads + jnp.einsum(
         "sjcf,jfd->sjcd", up_low_grad, expert_up, preferred_element_type=jnp.float32
     )
-    back_out, back_rows = (
-        lax.all_to_all(
-            expert_out.astype(jnp.bfloat16), "dp", split_axis=0, concat_axis=0, tiled=True
-        ).astype(expert_out.dtype),
-        lax.all_to_all(
-            row_grads.astype(jnp.bfloat16), "dp", split_axis=0, concat_axis=0, tiled=True
-        ).astype(row_grads.dtype),
-    )
-    table_rows = experts * capacity
-    out_table = jnp.concatenate(
-        [back_out.reshape(table_rows, D), jnp.zeros((1, D), jnp.float32)], 0
-    )
-    back_table = jnp.concatenate(
-        [back_rows.reshape(table_rows, D), jnp.zeros((1, D), jnp.float32)], 0
-    )
-    picked_out = jnp.take(out_table, slot_index, axis=0).reshape(seq_len, top_count, D)
-    picked_back = jnp.take(back_table, slot_index, axis=0).reshape(seq_len, top_count, D)
+    back_both = lax.all_to_all(
+        jnp.concatenate(
+            [expert_out.astype(jnp.bfloat16), row_grads.astype(jnp.bfloat16)], -1
+        ).reshape(dp_size, exp_dev, capacity, 2 * tile_rows, 128),
+        "dp",
+        split_axis=0,
+        concat_axis=0,
+        tiled=True,
+    )
     shared_pre_gate = jnp.dot(normed_two, gate_shared, preferred_element_type=jnp.float32)
     shared_pre_up = jnp.dot(normed_two, up_shared, preferred_element_type=jnp.float32)
     shared_sigmoid = jax.nn.sigmoid(shared_pre_gate)
     shared_act = (shared_pre_gate * shared_sigmoid * shared_pre_up).astype(jnp.bfloat16)
-    shared_out = jnp.dot(shared_act, down_shared, preferred_element_type=jnp.float32)
-    shared_act_grad = jnp.dot(grad_seq, down_shared.T, preferred_element_type=jnp.float32)
+    shared_out = jnp.einsum(
+        "tf,df->td", shared_act, down_shared_t, preferred_element_type=jnp.float32
+    )
+    shared_act_grad = jnp.dot(grad_seq, down_shared_t, preferred_element_type=jnp.float32)
     shared_gate_low, shared_up_low = silu_back(
         shared_act_grad, shared_pre_gate, shared_pre_up, shared_sigmoid
     )
-    shared_down_grad = jnp.dot(shared_act.T, grad_seq, preferred_element_type=jnp.float32)
+    shared_down_grad_t = jnp.dot(grad_seq.T, shared_act, preferred_element_type=jnp.float32)
     shared_gate_grad = jnp.dot(normed_two.T, shared_gate_low, preferred_element_type=jnp.float32)
     shared_up_grad = jnp.dot(normed_two.T, shared_up_low, preferred_element_type=jnp.float32)
-    shared_back = jnp.dot(shared_gate_low, gate_shared.T, preferred_element_type=jnp.float32)
-    shared_back = shared_back + jnp.dot(
-        shared_up_low, up_shared.T, preferred_element_type=jnp.float32
-    )
+    shared_back = jnp.einsum(
+        "tf,df->td", shared_gate_low, gate_shared, preferred_element_type=jnp.float32
+    )
+    shared_back = shared_back + jnp.einsum(
+        "tf,df->td", shared_up_low, up_shared, preferred_element_type=jnp.float32
+    )
+    shared_grads_in = jnp.concatenate(
+        [shared_gate_grad, shared_up_grad, shared_down_grad_t], 1
+    ).astype(jnp.bfloat16)
     grad_seq_f = grad_seq.astype(jnp.float32)
-    feed_part = shared_out + jnp.sum(gate_values[:, :, None] * picked_out, 1)
-    gate_part = jnp.sum(grad_seq_f[:, None, :] * picked_out, -1)
-    feed_own = lax.psum_scatter(
-        feed_part.astype(jnp.bfloat16), "tensor", scatter_dimension=0, tiled=True
-    ).astype(jnp.float32)
+    table_rows = experts * capacity
+    feed_part, back_part, gate_cols = combine_rows(
+        slot_index.reshape(seq_len, top_count),
+        back_both.reshape(table_rows, 2 * tile_rows, 128),
+        gate_values,
+        grad_seq,
+        shared_out,
+        shared_back,
+    )
+    gate_part = gate_cols[:, :top_count]
+    feed_own = lax.psum_scatter(feed_part, "tensor", scatter_dimension=0, tiled=True).astype(
+        jnp.float32
+    )
     output = (residual_own + feed_own).astype(jnp.bfloat16)
-    normed_two_grad, gate_grads = (
-        lax.psum((jnp.sum(picked_back, 1) + shared_back).astype(jnp.bfloat16), "tensor").astype(
-            jnp.float32
-        ),
-        lax.psum(gate_part.astype(jnp.bfloat16), "tensor").astype(jnp.float32),
-    )
+    normed_two_grad, gate_grads = lax.psum(
+        (back_part, gate_part.astype(jnp.bfloat16)),
+        "tensor",
+    )
+    normed_two_grad = normed_two_grad.astype(jnp.float32)
+    gate_grads = gate_grads.astype(jnp.float32)
     weighted_total = jnp.sum(gate_values * gate_grads, -1, keepdims=True)
     chosen_grads = gate_values * (gate_grads - weighted_total)
     logit_grads = jnp.sum(jnp.where(chosen_hot, chosen_grads[:, :, None], 0.0), 1)
@@ -312,19 +483,14 @@
         logit_grads, router_weights.astype(jnp.float32).T, precision=HIGH
     )
     residual_grad = grad_seq_f + norm_back(residual_all, scale_two, gain_two, normed_two_grad)
-    own_two_grad = lax.dynamic_slice_in_dim(normed_two_grad, start_row, tok_dev, 0)
-    own_scale_two = lax.dynamic_slice_in_dim(scale_two, start_row, tok_dev, 0)
-    second_gain_grad = jnp.sum(own_two_grad * residual_own * own_scale_two, 0)
-    own_normed_two = lax.dynamic_slice_in_dim(normed_two, start_row, tok_dev, 0).astype(jnp.float32)
-    router_grad = jnp.dot(
-        own_normed_two.T,
-        lax.dynamic_slice_in_dim(logit_grads, start_row, tok_dev, 0),
-        precision=HIGH,
-    )
     branch_grad = residual_grad.astype(jnp.bfloat16)
-    output_grad_w = jnp.dot(mixed_all.T, branch_grad, preferred_element_type=jnp.float32)
+    shared_grads_in, branch_grad = lax.optimization_barrier((shared_grads_in, branch_grad))
+    shared_pack = lax.psum_scatter(
+        shared_grads_in, "dp", scatter_dimension=0, tiled=True
+    ).astype(jnp.float32)
+    output_grad_w_t = jnp.dot(branch_grad.T, mixed_all, preferred_element_type=jnp.float32)
     mixed_grad = (
-        jnp.dot(branch_grad, output_weights.T, preferred_element_type=jnp.float32)
+        jnp.dot(branch_grad, output_weights_t, preferred_element_type=jnp.float32)
         .astype(jnp.bfloat16)
         .reshape(seq_len, head_count, DV)
     )
@@ -396,65 +562,87 @@
         expand_grads, expand_weights.T, preferred_element_type=jnp.float32
     )
     latent_grad_part = jnp.concatenate([compressed_grad_part, key_rope_grad], -1)
-    normed_grad_own, latent_grad_own = (
-        lax.psum_scatter(
-            normed_grad_part.astype(jnp.bfloat16), "tensor", scatter_dimension=0, tiled=True
-        ).astype(jnp.float32),
-        lax.psum_scatter(
-            latent_grad_part.astype(jnp.bfloat16), "tensor", scatter_dimension=0, tiled=True
-        ).astype(jnp.float32),
-    )
-    compressed_grad = latent_grad_own[:, :KVR]
-    kv_gain_grad = jnp.sum(compressed_grad * compressed * scale_kv, 0)
-    raw_grad = jnp.concatenate(
+    attn_pack = lax.psum_scatter(
+        jnp.concatenate(
+            [
+                query_grad_w,
+                output_grad_w_t,
+                expand_grad_w.reshape(dp_size * rows_dp, expand_flat_cols),
+            ],
+            1,
+        ).astype(jnp.bfloat16),
+        "dp",
+        scatter_dimension=0,
+        tiled=True,
+    ).astype(jnp.float32)
+    token_all = lax.psum(
+        jnp.concatenate([normed_grad_part, latent_grad_part], 1).astype(jnp.bfloat16), "tensor"
+    ).astype(jnp.float32)
+    compressed_grad_all = token_all[:, D : D + KVR]
+    kv_gain_full = jnp.sum(compressed_grad_all * compressed_all * scale_kv_all, 0)
+    raw_grad_all = jnp.concatenate(
         [
-            norm_back(compressed, scale_kv, gain_kv, compressed_grad),
-            rotate_back(latent_grad_own[:, KVR:], own_cosines, own_sines),
+            norm_back(compressed_all, scale_kv_all, gain_kv, compressed_grad_all),
+            rotate_back(token_all[:, D + KVR :], all_cosines, all_sines),
         ],
         -1,
     ).astype(jnp.bfloat16)
-    latent_grad_w = jnp.dot(normed_own.T, raw_grad, preferred_element_type=jnp.float32)
-    normed_grad = normed_grad_own + jnp.dot(
-        raw_grad, latent_weights.T, preferred_element_type=jnp.float32
-    )
-    attn_gain_grad = jnp.sum(normed_grad * hidden_f * scale_one, 0)
+    normed_grad_all = token_all[:, :D] + jnp.dot(
+        raw_grad_all, latent_weights.T, preferred_element_type=jnp.float32
+    )
+    normed_grad = lax.dynamic_slice_in_dim(normed_grad_all, start_row, tok_dev, 0)
     hidden_grad = lax.dynamic_slice_in_dim(residual_grad, start_row, tok_dev, 0) + norm_back(
         hidden_f, scale_one, gain_one, normed_grad
     )
-    (
-        query_proj_grad,
-        expand_proj_grad,
-        output_proj_grad,
-        shared_gate_out,
-        shared_up_out,
-        shared_down_out,
-    ) = (
-        lax.psum_scatter(
-            query_grad_w.astype(jnp.bfloat16), "dp", scatter_dimension=0, tiled=True
-        ).astype(jnp.float32),
-        lax.psum_scatter(
-            expand_grad_w.astype(jnp.bfloat16), "dp", scatter_dimension=0, tiled=True
-        ).astype(jnp.float32),
-        lax.psum_scatter(
-            output_grad_w.astype(jnp.bfloat16), "dp", scatter_dimension=1, tiled=True
-        ).astype(jnp.float32),
-        lax.psum_scatter(
-            shared_gate_grad.astype(jnp.bfloat16), "dp", scatter_dimension=0, tiled=True
-        ).astype(jnp.float32),
-        lax.psum_scatter(
-            shared_up_grad.astype(jnp.bfloat16), "dp", scatter_dimension=0, tiled=True
-        ).astype(jnp.float32),
-        lax.psum_scatter(
-            shared_down_grad.astype(jnp.bfloat16), "dp", scatter_dimension=1, tiled=True
-        ).astype(jnp.float32),
-    )
-    attn_gain_out, latent_proj_grad, latent_gain_out, second_gain_out, router_out = (
-        lax.psum_scatter(attn_gain_grad, ("dp", "tensor"), scatter_dimension=0, tiled=True),
-        lax.psum_scatter(latent_grad_w, ("dp", "tensor"), scatter_dimension=0, tiled=True),
-        lax.psum_scatter(kv_gain_grad, ("dp", "tensor"), scatter_dimension=0, tiled=True),
-        lax.psum_scatter(second_gain_grad, ("dp", "tensor"), scatter_dimension=0, tiled=True),
-        lax.psum_scatter(router_grad, ("dp", "tensor"), scatter_dimension=0, tiled=True),
-    )
+    row_per = D // (dp_size * tensor_size)
+
+    def own_rows(values):
+        split = values.reshape(values.shape[0], dp_size, tensor_size, row_per)
+        return lax.dynamic_slice_in_dim(split, tensor_rank, 1, 2).reshape(values.shape[0], -1)
+
+    latent_rows = jnp.dot(own_rows(normed_all).T, raw_grad_all, preferred_element_type=jnp.float32)
+    attn_gain_rows = jnp.sum(
+        own_rows(normed_grad_all) * own_rows(hidden_all_f) * scale_one_all, 0
+    )
+    second_gain_rows = jnp.sum(
+        own_rows(normed_two_grad) * own_rows(residual_all) * scale_two, 0
+    )
+    router_rows = jnp.dot(
+        own_rows(normed_two).astype(jnp.float32).T, logit_grads, precision=HIGH
+    )
+    kv_per = kv_gain_full.shape[0] // (dp_size * tensor_size)
+    kv_rows_own = lax.dynamic_slice_in_dim(
+        kv_gain_full.reshape(dp_size, tensor_size, kv_per), tensor_rank, 1, 1
+    ).reshape(dp_size, kv_per)
+    kv_column = jnp.pad(kv_rows_own, ((0, 0), (0, row_per - kv_per))).reshape(-1)
+    small_pack = jnp.concatenate(
+        [
+            latent_rows,
+            router_rows,
+            attn_gain_rows[:, None],
+            second_gain_rows[:, None],
+            kv_column[:, None],
+        ],
+        1,
+    )
+    small_own = lax.psum_scatter(small_pack, "dp", scatter_dimension=0, tiled=True)
+    cut = [0]
+    for width in (latent_cols, experts, 1, 1, 1):
+        cut.append(cut[-1] + width)
+    latent_proj_grad = small_own[:, cut[0] : cut[1]]
+    router_out = small_own[:, cut[1] : cut[2]]
+    attn_gain_out = small_own[:, cut[2]]
+    second_gain_out = small_own[:, cut[3]]
+    latent_gain_out = small_own[:kv_per, cut[4]]
+    cut = [0]
+    for width in (head_cols, out_cols, expand_flat_cols):
+        cut.append(cut[-1] + width)
+    query_proj_grad = attn_pack[:, cut[0] : cut[1]]
+    output_proj_grad = attn_pack[:, cut[1] : cut[2]].T
+    expand_proj_grad = attn_pack[:, cut[2] : cut[3]].reshape(kv_rows, expand_cols)
+    shared_gate_out = shared_pack[:, :shared_cols]
+    shared_up_out = shared_pack[:, shared_cols : 2 * shared_cols]
+    shared_down_out = shared_pack[:, 2 * shared_cols :].T
     return (
         output,
         hidden_grad,

time: 3490 us -> 1790 us (0.51)
  waiting for transfers between devices: 2210 us -> 909 us
  blocking collectives: 577 us -> 259 us
  other arithmetic: 190 us -> 88.6 us
  Pallas kernels: 0 us -> 93.9 us
  matrix products: 220 us -> 180 us
    reduce_scatter x7 -> x0, waiting for transfers between devices: 1570 us -> none  [the longest x1 644 us: shards(): lax.psum_scatter(latent_grad_w, ('dp', 'tensor'), scatter_dimension=0, ti...]
    all_gather x4 -> x0, blocking collectives: 211 us -> none  [the longest x1 153 us: shards(): lax.all_gather(router_proj, 'dp', axis=0, tiled=True)]
    psum x1 -> x3, waiting for transfers between devices: 109 us -> 265 us  [the longest x1 105 us: shards(): lax.psum(attn_part.astype(jnp.bfloat16), 'tensor').astype(jnp.float32)]
    pallas_call x0 -> x2, Pallas kernels: none -> 93.9 us  [the longest x1 57.5 us: dispatch_rows(): pl.pallas_call(dispatch_kernel, out_shape=jax.ShapeDtypeStruct((slots, 2...]
    unnamed x2 -> x0, blocking collectives: 93.8 us -> none
    gather x4 -> x0, local copies, waits for them, and re-layouts: 92.8 us -> none  [the longest x1 23.5 us: shards(): jnp.take(back_table, slot_index, axis=0).reshape(seq_len, top_count, D)]
    all_gather x10 -> x5, waiting for transfers between devices: 328 us -> 411 us  [the longest x1 238 us: shards(): shared_all = lax.all_gather(shared_local, 'dp', axis=0, tiled=True)]
    reduce_sum x5 -> x4, other arithmetic: 73.2 us -> 5.83 us  [the longest x1 1.91 us: norm_back(): jnp.mean(values * weighted, -1, keepdims=True)]
  transfers between devices with their start and end apart: 25 -> 13, of which waited for: 21 -> 12; matrix products, arithmetic and copies ran while one was open for 9% -> 13% of each run, Pallas kernels for 0% -> 0%
where the time goes in v1:
time: 1790 us; the launch traced here: 1770 us
  waiting for transfers between devices  909 us (51%)
  blocking collectives  259 us (14%)
  local copies, waits for them, and re-layouts  221 us (12%)
  matrix products  180 us (10%)
  Pallas kernels  93.9 us (5%)
  other arithmetic  88.6 us (5%)
    all_gather x1, waiting for transfers between devices, shards(): shared_all = lax.all_gather(shared_local, 'dp', axis=0, tiled=True)  238 us
    all_to_all x1, blocking collectives, shards(): lax.all_to_all(send_both, 'dp', split_axis=0, concat_axis=0, tiled=True)  236 us
    unnamed x16, waiting for transfers between devices  210 us
    psum x1, waiting for transfers between devices, shards(): lax.psum(attn_part.astype(jnp.bfloat16), 'tensor').astype(jnp.float32)  105 us
    psum x1, waiting for transfers between devices, shards(): lax.psum(jnp.concatenate([normed_grad_part, latent_grad_part], 1).astype(...  82 us
    psum x1, waiting for transfers between devices, shards(): lax.psum((back_part, gate_part.astype(jnp.bfloat16)), 'tensor')  77.8 us
    all_gather x1, waiting for transfers between devices, shards(): hidden_all = lax.all_gather(hidden, 'tensor', axis=0, tiled=True)  69.6 us
    unnamed x225, local copies, waits for them, and re-layouts  65.9 us
  transfers between devices with their start and end apart: 13, of which 12 were waited for; matrix products, arithmetic and copies ran while one was open for 13% of the time, Pallas kernels for 0%

profile of v1, /device:TPU:0, one launch (start us, length us, event | category | flops | bytes accessed | tf_op | source)
XLA Modules:
  0.0 1774.9 jit_solution(1199529957844971326)
XLA Ops:
  21.9 69.6 %all-gather.6.cloned.1.call-done = bf16[1024,2048]{0,1:T(8,128)(2,1)} async-done(((bf16[128,2048]{0,1:T(8,128)(2,1)}), bf16[1024,2048]{0,1:T(8,128)(2,1)}) %all-gather.6.cloned.1.call-update) | async-done | bytes 4194320 | tf_op jit(solution)/shard_map/all_gather | solution.py:294
  94.7 44.1 %all-gather.8.cloned.1.call-done = bf16[2048,1090]{0,1:T(8,128)(2,1)} async-done(((bf16[128,1090]{0,1:T(8,128)(2,1)}), bf16[2048,1090]{0,1:T(8,128)(2,1)}) %all-gather.8.cloned.1.call-update) | async-done | bytes 4464656 | tf_op jit(solution)/shard_map/all_gather | solution.py:275
  187.0 8.1 scatter_custom_fusion.tok_ref
  196.6 59.4 %all-gather.12.cloned.1.call-done = bf16[1024,2048]{0,1:T(8,128)(2,1)} async-done(((bf16[128,2048]{0,1:T(8,128)(2,1)}), bf16[1024,2048]{0,1:T(8,128)(2,1)}) %all-gather.12.cloned.1.call-update) | async-done | bytes 4194320 | tf_op jit(solution)/shard_map/all_gather | solution.py:295
  262.9 104.7 %all-reduce.6.cloned.1.call-done = bf16[1024,2048]{0,1:T(8,128)(2,1)} async-done(((bf16[1024,2048]{0,1:T(8,128)(2,1)}), bf16[1024,2048]{0,1:T(8,128)(2,1)}) %all-reduce.6.cloned.1.call-update) | async-done | bytes 4194320 | tf_op jit(solution)/shard_map/psum | solution.py:359
  388.4 8.1 scatter_custom_fusion.1
  403.9 57.5 %shard_map.297 = bf16[2560,32,128]{2,1,0:T(8,128)(2,1)} custom-call(s32[2560]{0:T(1024)} %copy-done.67, bf16[1024,16,128]{2,1,0:T(8,128)(2,1)} %copy.220.rows_hbm, bf16[1024,16,128]{2,1,0:T(8,128)(2,1)} %copy.221.grads_hbm.grad_ref, f32[2,2560,1,128]{3,2,1,0:T(1,128)} %broadcast_in_dim.73.col_ref), custom_call_target="tpu_custom_call" | custom-call | flops 5242880 | bytes 41943040 | tf_op jit(solution)/shard_map/pallas_call | solution.py:121
  461.4 236.3 %all_to_all.10 = bf16[16,4,40,32,128]{4,3,2,1,0:T(8,128)(2,1)} all-to-all(bf16[16,4,40,32,128]{4,3,2,1,0:T(8,128)(2,1)} %bitcast.248), channel_id=1, replica_groups=mesh['dp'=16,'tensor'=8] {'dp'}, dimensions={0} | all-to-all | bytes 41943040 | tf_op jit(solution)/shard_map/all_to_all | solution.py:394
  697.7 31.3 %reshape.503 = bf16[16,4,40,4096]{3,2,1,0:T(8,128)(2,1)} reshape(bf16[16,4,40,32,128]{4,3,2,1,0:T(8,128)(2,1)} %all_to_all.10) | data formatting | bytes 41943040 | tf_op jit(solution)/shard_map/reshape | solution.py:395
  729.0 17.0 fusion.167
  746.0 8.8 fusion.12
  754.8 8.6 fusion.4
  763.5 11.3 fusion.43
  774.8 12.7 fusion.33
  792.9 12.3 fusion.1
  805.2 10.4 pad_maximum_fusion
  823.1 19.0 %copy.176 = bf16[16,4,40,32,128]{4,3,2,1,0:T(8,128)(2,1)} copy(bf16[16,4,40,32,128]{4,3,2,0,1:T(8,128)(2,1)} %bitcast.250) | data formatting | bytes 41943040 | tf_op jit(solution)/shard_map/reshape | solution.py:429
  848.9 237.7 %all-gather.14.cloned.1.call-done = bf16[2048,1056]{0,1:T(8,128)(2,1)} async-done(((bf16[128,1056]{0,1:T(8,128)(2,1)}), bf16[2048,1056]{0,1:T(8,128)(2,1)}) %all-gather.14.cloned.1.call-update) | async-done | bytes 4325392 | tf_op jit(solution)/shard_map/all_gather | solution.py:390
  1114.4 23.8 %all-to-all-done.1 = bf16[16,4,40,32,128]{4,3,2,1,0:T(8,128)(2,1)} async-done(((bf16[16,4,40,32,128]{4,3,2,1,0:T(8,128)(2,1)}), bf16[16,4,40,32,128]{4,3,2,1,0:T(8,128)(2,1)}, u32[]{:S(2)}, u32[]{:S(2)}) %all-to-all-start.1) | async-done | bytes 20971552 | tf_op jit(solution)/shard_map/all_to_all | solution.py:426
  1141.8 36.4 %shard_map.298 = (bf16[1024,16,128]{2,1,0:T(8,128)(2,1)}, bf16[1024,16,128]{2,1,0:T(8,128)(2,1)}, f32[1024,1,128]{2,1,0:T(1,128)}) custom-call(s32[2048]{0:T(1024)} %multiply_add_fusion.slot_ref, bf16[2560,32,128]{2,1,0:T(8,128)(2,1)} %bitcast.37.table_hbm, f32[2,1024,1,128]{3,2,1,0:T(1,128)} %broadcast_in_dim.74.gate_ref, ...), custom_call_target="tpu_custom_call" | custom-call | flops 33554432 | bytes 46137344 | tf_op jit(solution)/shard_map/pallas_call | solution.py:194
  1196.9 22.6 %psum.30 = bf16[1024,2]{0,1:T(2,128)(2,1)S(1)} all-reduce(bf16[1024,2]{0,1:T(2,128)(2,1)S(1)} %bitcast.292), channel_id=1, replica_groups=mesh['dp'=16,'tensor'=8] {'tensor'}, use_global_device_ids=true, to_apply=%region_16.17 | all-reduce | flops 2048 | bytes 8192 | tf_op jit(solution)/shard_map/psum | solution.py:473
  1219.7 77.8 %all-reduce.8.cloned.1.call-done = bf16[1024,2048]{0,1:T(8,128)(2,1)} async-done(((bf16[1024,2048]{0,1:T(8,128)(2,1)}), bf16[1024,2048]{0,1:T(8,128)(2,1)}) %all-reduce.8.cloned.1.call-update) | async-done | bytes 4194320 | tf_op jit(solution)/shard_map/psum | solution.py:473
  1297.5 10.6 multiply_reduce_fusion
  1308.1 12.4 fusion.166
  1343.4 10.8 pad_maximum_fusion.1
  1400.1 82.0 %all-reduce.10.cloned.1.call-done = bf16[1024,2624]{0,1:T(8,128)(2,1)} async-done(((bf16[1024,2624]{0,1:T(8,128)(2,1)}), bf16[1024,2624]{0,1:T(8,128)(2,1)}) %all-reduce.10.cloned.1.call-update) | async-done | bytes 5373968 | tf_op jit(solution)/shard_map/psum | solution.py:578
  1510.0 9.4 fusion.20
  1519.4 9.3 fusion.23
  1533.7 35.0 %reduce-scatter.13.cloned.1.call-done = bf16[128,2048]{1,0:T(8,128)(2,1)} async-done(((bf16[1024,2048]{1,0:T(8,128)(2,1)}), bf16[128,2048]{1,0:T(8,128)(2,1)}) %reduce-scatter.13.cloned.1.call-update) | async-done | bytes 524304
  1580.3 54.6 %reduce-scatter.17.cloned.1.call-done = bf16[128,768]{1,0:T(8,128)(2,1)} async-done(((bf16[2048,768]{1,0:T(8,128)(2,1)}), bf16[128,768]{1,0:T(8,128)(2,1)}) %reduce-scatter.17.cloned.1.call-update) | async-done | bytes 196624
  1639.9 57.1 %reduce-scatter.15.cloned.1.call-done = f32[16,643]{1,0:T(8,128)} async-done(((f32[256,643]{1,0:T(8,128)}), f32[16,643]{1,0:T(8,128)}) %reduce-scatter.15.cloned.1.call-update) | async-done | bytes 41168
  1703.2 62.6 %reduce-scatter.19.cloned.1.call-done = bf16[128,1056]{1,0:T(8,128)(2,1)} async-done(((bf16[2048,1056]{1,0:T(8,128)(2,1)}), bf16[128,1056]{1,0:T(8,128)(2,1)}) %reduce-scatter.19.cloned.1.call-update) | async-done | bytes 270352
  (412 shorter events, 296.8 us)
Async XLA Ops:
  7.2 756.3 %copy-start = (bf16[4,176,2048]{2,1,0:T(8,128)(2,1)S(1)}, bf16[4,176,2048]{2,1,0:T(8,128)(2,1)}, u32[]{:S(2)}) copy-start(bf16[4,176,2048]{2,1,0:T(8,128)(2,1)} %param.30) | copy-start | bytes 8650756
  7.2 84.3 %all-gather.6.cloned.1.call-start = ((), (), s32[]{:S(2)}) async-start(), calls=%async_computation.6 | async-start | bytes 4718592 | tf_op jit(solution)/shard_map/all_gather | solution.py:294
  9.5 129.3 %all-gather.8.cloned.1.call-start = ((), (), s32[]{:S(2)}) async-start(), calls=%async_computation.7 | async-start | bytes 4769792 | tf_op jit(solution)/shard_map/all_gather | solution.py:275
  16.2 160.4 %all-gather.10.cloned.1.call-start = ((), (), s32[]{:S(2)}) async-start(), calls=%async_computation.8 | async-start | bytes 1427456 | tf_op jit(solution)/shard_map/all_gather | solution.py:288
  17.8 238.3 %all-gather.12.cloned.1.call-start = ((), (), s32[]{:S(2)}) async-start(), calls=%async_computation.10 | async-start | bytes 4718592 | tf_op jit(solution)/shard_map/all_gather | solution.py:295
  19.9 347.7 %all-reduce.6.cloned.1.call-start = ((), (), s32[]{:S(2)}) async-start(), calls=%async_computation.9 | async-start | bytes 8388608 | tf_op jit(solution)/shard_map/psum | solution.py:359
  20.0 144.7 %copy-start.97 = (f32[32]{0:T(128)}, f32[32]{0:T(128)S(1)}, u32[]{:S(2)}) copy-start(f32[32]{0:T(128)S(1)} %multiply_power_fusion) | copy-start | bytes 388
  20.0 144.7 %copy-start.77 = (f32[1024]{0:T(1024)}, f32[1024]{0:T(1024)S(1)}, u32[]{:S(2)}) copy-start(f32[1024]{0:T(1024)S(1)} %iota_convert_fusion) | copy-start | bytes 12292
  94.7 55.9 %copy-start.75 = (f32[1024]{0:T(1024)}, f32[1024]{0:T(1024)S(1)}, u32[]{:S(2)}) copy-start(f32[1024]{0:T(1024)S(1)} %add_rsqrt_fusion.2) | copy-start | bytes 12292
  147.8 18.8 %copy-start.89 = (f32[512]{0:T(512)}, f32[512]{0:T(512)S(1)}, u32[]{:S(2)}) copy-start(f32[512]{0:T(512)S(1)} %reshape.474) | copy-start | bytes 6148
  195.1 67.8 %copy-start.67 = (s32[2560]{0:T(1024)}, s32[2560]{0:T(1024)S(1)}, u32[]{:S(2)}) copy-start(s32[2560]{0:T(1024)S(1)} %scatter_custom_fusion.tok_ref) | copy-start | bytes 30724
  196.6 177.1 %copy-start.59 = (f32[2048,1]{0,1:T(1,128)}, f32[2048,1]{0,1:T(1,128)S(1)}, u32[]{:S(2)}) copy-start(f32[2048,1]{0,1:T(1,128)S(1)} %slice_convert_fusion.1) | copy-start | bytes 24580
  729.0 17.0 copy-start.27
  774.8 12.7 copy-start.29
  774.8 12.7 copy-start.42
  842.1 296.0 %all-to-all-start.1 = ((bf16[16,4,40,32,128]{4,3,2,1,0:T(8,128)(2,1)}), bf16[16,4,40,32,128]{4,3,2,1,0:T(8,128)(2,1)}, u32[]{:S(2)}, u32[]{:S(2)}) async-start(bf16[16,4,40,32,128]{4,3,2,1,0:T(8,128)(2,1)} %copy.176), calls=%async_computation.1 | async-start | bytes 41943040 | tf_op jit(solution)/shard_map/all_to_all | solution.py:426
  847.7 239.0 %all-gather.14.cloned.1.call-start = ((), (), s32[]{:S(2)}) async-start(), calls=%async_computation.11 | async-start | bytes 4595712 | tf_op jit(solution)/shard_map/all_gather | solution.py:390
  848.2 449.2 %all-reduce.8.cloned.1.call-start = ((), (), s32[]{:S(2)}) async-start(), calls=%async_computation.12 | async-start | bytes 8388608 | tf_op jit(solution)/shard_map/psum | solution.py:473
  1184.9 297.1 %all-reduce.10.cloned.1.call-start = ((), (), s32[]{:S(2)}) async-start(), calls=%async_computation.13 | async-start | bytes 10747904 | tf_op jit(solution)/shard_map/psum | solution.py:578
  1193.8 25.7 %copy-start.66 = (s32[1024,2]{0,1:T(2,128)S(1)}, s32[1024,2]{0,1:T(2,128)}, u32[]{:S(2)}) copy-start(s32[1024,2]{0,1:T(2,128)} %param.19) | copy-start | bytes 24580
  1193.9 103.6 %copy-start.35 = (bf16[2048,321]{0,1:T(8,128)(2,1)S(1)}, bf16[2048,321]{0,1:T(8,128)(2,1)}, u32[]{:S(2)}) copy-start(bf16[2048,321]{0,1:T(8,128)(2,1)} %all-gather.10.cloned.1.call-done) | copy-start | bytes 3944452
  1193.9 103.6 %copy-start.60 = (f32[2048,1]{0,1:T(1,128)S(1)}, f32[2048,1]{0,1:T(1,128)}, u32[]{:S(2)}) copy-start(f32[2048,1]{0,1:T(1,128)} %copy-done.59) | copy-start | bytes 24580
  1219.6 88.4 %copy-start.74 = (f32[1024]{0:T(1024)S(1)}, f32[1024]{0:T(1024)}, u32[]{:S(2)}) copy-start(f32[1024]{0:T(1024)} %copy-done.73) | copy-start | bytes 12292
  1219.7 88.4 %copy-start.91 = (f32[1024]{0:T(1024)S(1)}, f32[1024]{0:T(1024)}, u32[]{:S(2)}) copy-start(f32[1024]{0:T(1024)} %get-tuple-element.135) | copy-start | bytes 12292
  1354.2 214.5 %reduce-scatter.13.cloned.1.call-start = ((), (), s32[]{:S(2)}) async-start(), calls=%async_computation.14 | async-start | bytes 4718592
  1367.7 267.2 %reduce-scatter.17.cloned.1.call-start = ((), (), s32[]{:S(2)}) async-start(), calls=%async_computation.16 | async-start | bytes 3342336
  1388.6 308.5 %reduce-scatter.15.cloned.1.call-start = ((), (), s32[]{:S(2)}) async-start(), calls=%async_computation.15 | async-start | bytes 835584
  1501.8 263.9 %reduce-scatter.19.cloned.1.call-start = ((), (), s32[]{:S(2)}) async-start(), calls=%async_computation.17 | async-start | bytes 5013504
  1510.0 18.7 %slice-start = ((s8[10485760]{0:T(1024)(128)(4,1)}), s8[4194304]{0:T(1024)(128)(4,1)S(1)}, s32[]{:S(2)}) async-start(s8[10485760]{0:T(1024)(128)(4,1)} %bitcast.261), calls=%async_computation.18 | async-start | bytes 8388608
  1510.0 18.7 %slice-start.1 = ((s8[10485760]{0:T(1024)(128)(4,1)}), s8[4194304]{0:T(1024)(128)(4,1)S(1)}, s32[]{:S(2)}) async-start(s8[10485760]{0:T(1024)(128)(4,1)} %bitcast.261), calls=%async_computation.19 | async-start | bytes 8388608
  1533.7 38.7 %copy-start.64 = (f32[2048,1]{0,1:T(1,128)S(1)}, f32[2048,1]{0,1:T(1,128)}, u32[]{:S(2)}) copy-start(f32[2048,1]{0,1:T(1,128)} %copy-done.63) | copy-start | bytes 24580
  1574.4 193.4 %copy-start.1 = (bf16[4,176,2048]{2,1,0:T(8,128)(2,1)S(1)}, bf16[4,176,2048]{2,1,0:T(8,128)(2,1)}, u32[]{:S(2)}) copy-start(bf16[4,176,2048]{2,1,0:T(8,128)(2,1)} %param.30) | copy-start | bytes 8650756
  (83 other events, 333.1 us)
Sparse Core Ops, SparseCore 0:
  10.8 80.6 all-gather.5
  93.7 44.9 all-gather.7
  140.9 35.0 all-gather.9
  178.1 77.9 all-gather.11
  259.0 108.5 all-reduce.5
  850.4 236.2 all-gather.13
  1185.1 112.3 all-reduce.7
  1354.3 127.6 all-reduce.9
  1486.4 82.2 reduce-scatter.12
  1571.2 63.6 reduce-scatter.16
  1637.4 59.6 reduce-scatter.14
  1699.4 66.3 reduce-scatter.18

commit v2 on v1

--- a/solution.py
+++ b/solution.py
@@ -552,6 +552,7 @@
             ).astype(jnp.bfloat16)
         )
     query_grads = jnp.concatenate(query_grad_list, 0).reshape(seq_len, head_count * (DN + DR))
+    feed_own, shared_pack, query_grads = lax.optimization_barrier((feed_own, shared_pack, query_grads))
     query_grad_w = jnp.dot(normed_all.T, query_grads, preferred_element_type=jnp.float32)
     normed_grad_part = jnp.dot(query_grads, query_weights.T, preferred_element_type=jnp.float32)
     expand_grads = jnp.concatenate(

time: 1790 us -> 1760 us (0.983)
  waiting for transfers between devices: 909 us -> 884 us
    unnamed x16, waiting for transfers between devices: 210 us -> 139 us
    psum x1, waiting for transfers between devices: 82 us -> 127 us  [shards(): lax.psum(jnp.concatenate([normed_grad_part, latent_grad_part], 1).astype(...]
    unnamed x225 -> x221, local copies, waits for them, and re-layouts: 65.9 us -> 61.7 us
  transfers between devices with their start and end apart: 13 -> 13, of which waited for: 12 -> 12; matrix products, arithmetic and copies ran while one was open for 13% -> 15% of each run, Pallas kernels for 0% -> 0%
where the time goes in v2:
time: 1760 us; the launch traced here: 1750 us
  waiting for transfers between devices  884 us (50%)
  blocking collectives  259 us (15%)
  local copies, waits for them, and re-layouts  218 us (12%)
  matrix products  183 us (10%)
  Pallas kernels  93.4 us (5%)
  other arithmetic  90.6 us (5%)
    all_gather x1, waiting for transfers between devices, shards(): shared_all = lax.all_gather(shared_local, 'dp', axis=0, tiled=True)  237 us
    all_to_all x1, blocking collectives, shards(): lax.all_to_all(send_both, 'dp', split_axis=0, concat_axis=0, tiled=True)  236 us
    unnamed x16, waiting for transfers between devices  139 us
    psum x1, waiting for transfers between devices, shards(): lax.psum(jnp.concatenate([normed_grad_part, latent_grad_part], 1).astype(...  127 us
    psum x1, waiting for transfers between devices, shards(): lax.psum(attn_part.astype(jnp.bfloat16), 'tensor').astype(jnp.float32)  105 us
    psum x1, waiting for transfers between devices, shards(): lax.psum((back_part, gate_part.astype(jnp.bfloat16)), 'tensor')  78.6 us
    all_gather x1, waiting for transfers between devices, shards(): hidden_all = lax.all_gather(hidden, 'tensor', axis=0, tiled=True)  69.6 us
    unnamed x221, local copies, waits for them, and re-layouts  61.7 us
  transfers between devices with their start and end apart: 13, of which 12 were waited for; matrix products, arithmetic and copies ran while one was open for 15% of the time, Pallas kernels for 0%

profile of v2, /device:TPU:0, one launch (start us, length us, event | category | flops | bytes accessed | tf_op | source)
XLA Modules:
  0.0 1750.5 jit_solution(2430549227221558100)
XLA Ops:
  21.9 69.6 %all-gather.6.cloned.1.call-done = bf16[1024,2048]{0,1:T(8,128)(2,1)} async-done(((bf16[128,2048]{0,1:T(8,128)(2,1)}), bf16[1024,2048]{0,1:T(8,128)(2,1)}) %all-gather.6.cloned.1.call-update) | async-done | bytes 4194320 | tf_op jit(solution)/shard_map/all_gather | solution.py:294
  94.7 44.1 %all-gather.8.cloned.1.call-done = bf16[2048,1090]{0,1:T(8,128)(2,1)} async-done(((bf16[128,1090]{0,1:T(8,128)(2,1)}), bf16[2048,1090]{0,1:T(8,128)(2,1)}) %all-gather.8.cloned.1.call-update) | async-done | bytes 4464656 | tf_op jit(solution)/shard_map/all_gather | solution.py:275
  196.7 59.4 %all-gather.12.cloned.1.call-done = bf16[1024,2048]{0,1:T(8,128)(2,1)} async-done(((bf16[128,2048]{0,1:T(8,128)(2,1)}), bf16[1024,2048]{0,1:T(8,128)(2,1)}) %all-gather.12.cloned.1.call-update) | async-done | bytes 4194320 | tf_op jit(solution)/shard_map/all_gather | solution.py:295
  262.9 104.7 %all-reduce.6.cloned.1.call-done = bf16[1024,2048]{0,1:T(8,128)(2,1)} async-done(((bf16[1024,2048]{0,1:T(8,128)(2,1)}), bf16[1024,2048]{0,1:T(8,128)(2,1)}) %all-reduce.6.cloned.1.call-update) | async-done | bytes 4194320 | tf_op jit(solution)/shard_map/psum | solution.py:359
  388.4 8.1 scatter_custom_fusion.1
  403.8 57.1 %shard_map.297 = bf16[2560,32,128]{2,1,0:T(8,128)(2,1)} custom-call(s32[2560]{0:T(1024)} %copy-done.68, bf16[1024,16,128]{2,1,0:T(8,128)(2,1)} %copy.220.rows_hbm, bf16[1024,16,128]{2,1,0:T(8,128)(2,1)} %copy.221.grads_hbm.grad_ref, f32[2,2560,1,128]{3,2,1,0:T(1,128)} %broadcast_in_dim.73.col_ref), custom_call_target="tpu_custom_call" | custom-call | flops 5242880 | bytes 41943040 | tf_op jit(solution)/shard_map/pallas_call | solution.py:121
  460.8 236.3 %all_to_all.10 = bf16[16,4,40,32,128]{4,3,2,1,0:T(8,128)(2,1)} all-to-all(bf16[16,4,40,32,128]{4,3,2,1,0:T(8,128)(2,1)} %bitcast.250), channel_id=1, replica_groups=mesh['dp'=16,'tensor'=8] {'dp'}, dimensions={0} | all-to-all | bytes 41943040 | tf_op jit(solution)/shard_map/all_to_all | solution.py:394
  697.1 31.3 %reshape.503 = bf16[16,4,40,4096]{3,2,1,0:T(8,128)(2,1)} reshape(bf16[16,4,40,32,128]{4,3,2,1,0:T(8,128)(2,1)} %all_to_all.10) | data formatting | bytes 41943040 | tf_op jit(solution)/shard_map/reshape | solution.py:395
  728.4 17.1 fusion.165
  745.5 8.8 fusion.12
  754.3 8.6 fusion.4
  763.0 11.3 fusion.43
  774.3 12.4 fusion.33
  792.2 12.3 fusion.1
  804.4 10.4 pad_maximum_fusion
  822.3 19.0 %copy.176 = bf16[16,4,40,32,128]{4,3,2,1,0:T(8,128)(2,1)} copy(bf16[16,4,40,32,128]{4,3,2,0,1:T(8,128)(2,1)} %bitcast.252) | data formatting | bytes 41943040 | tf_op jit(solution)/shard_map/reshape | solution.py:429
  848.1 237.4 %all-gather.14.cloned.1.call-done = bf16[2048,1056]{0,1:T(8,128)(2,1)} async-done(((bf16[128,1056]{0,1:T(8,128)(2,1)}), bf16[2048,1056]{0,1:T(8,128)(2,1)}) %all-gather.14.cloned.1.call-update) | async-done | bytes 4325392 | tf_op jit(solution)/shard_map/all_gather | solution.py:390
  1113.3 24.0 %all-to-all-done.1 = bf16[16,4,40,32,128]{4,3,2,1,0:T(8,128)(2,1)} async-done(((bf16[16,4,40,32,128]{4,3,2,1,0:T(8,128)(2,1)}), bf16[16,4,40,32,128]{4,3,2,1,0:T(8,128)(2,1)}, u32[]{:S(2)}, u32[]{:S(2)}) %all-to-all-start.1) | async-done | bytes 20971552 | tf_op jit(solution)/shard_map/all_to_all | solution.py:426
  1140.9 36.4 %shard_map.298 = (bf16[1024,16,128]{2,1,0:T(8,128)(2,1)}, bf16[1024,16,128]{2,1,0:T(8,128)(2,1)}, f32[1024,1,128]{2,1,0:T(1,128)}) custom-call(s32[2048]{0:T(1024)} %multiply_add_fusion.slot_ref, bf16[2560,32,128]{2,1,0:T(8,128)(2,1)} %bitcast.37.table_hbm, f32[2,1024,1,128]{3,2,1,0:T(1,128)} %broadcast_in_dim.74.gate_ref, ...), custom_call_target="tpu_custom_call" | custom-call | flops 33554432 | bytes 46137344 | tf_op jit(solution)/shard_map/pallas_call | solution.py:194
  1195.1 22.9 %psum.30 = bf16[1024,2]{0,1:T(2,128)(2,1)S(1)} all-reduce(bf16[1024,2]{0,1:T(2,128)(2,1)S(1)} %bitcast.290), channel_id=1, replica_groups=mesh['dp'=16,'tensor'=8] {'tensor'}, use_global_device_ids=true, to_apply=%region_16.17 | all-reduce | flops 2048 | bytes 8192 | tf_op jit(solution)/shard_map/psum | solution.py:473
  1218.1 78.6 %all-reduce.8.cloned.1.call-done = bf16[1024,2048]{0,1:T(8,128)(2,1)} async-done(((bf16[1024,2048]{0,1:T(8,128)(2,1)}), bf16[1024,2048]{0,1:T(8,128)(2,1)}) %all-reduce.8.cloned.1.call-update) | async-done | bytes 4194320 | tf_op jit(solution)/shard_map/psum | solution.py:473
  1296.8 10.5 multiply_reduce_fusion
  1307.3 12.5 fusion.164
  1359.2 33.8 %reduce-scatter.15.cloned.1.call-done = bf16[128,1056]{1,0:T(8,128)(2,1)} async-done(((bf16[2048,1056]{1,0:T(8,128)(2,1)}), bf16[128,1056]{1,0:T(8,128)(2,1)}) %reduce-scatter.15.cloned.1.call-update) | async-done | bytes 270352
  1398.7 11.0 pad_maximum_fusion.1
  1420.3 9.6 fusion.20
  1447.9 9.6 fusion.23
  1457.5 9.0 fusion.26
  1469.0 11.2 reduce-scatter.13.cloned.1.call-done
  1483.8 126.5 %all-reduce.10.cloned.1.call-done = bf16[1024,2624]{0,1:T(8,128)(2,1)} async-done(((bf16[1024,2624]{0,1:T(8,128)(2,1)}), bf16[1024,2624]{0,1:T(8,128)(2,1)}) %all-reduce.10.cloned.1.call-update) | async-done | bytes 5373968 | tf_op jit(solution)/shard_map/psum | solution.py:579
  1638.8 36.5 %reduce-scatter.19.cloned.1.call-done = bf16[128,768]{1,0:T(8,128)(2,1)} async-done(((bf16[2048,768]{1,0:T(8,128)(2,1)}), bf16[128,768]{1,0:T(8,128)(2,1)}) %reduce-scatter.19.cloned.1.call-update) | async-done | bytes 196624
  1680.4 56.9 %reduce-scatter.17.cloned.1.call-done = f32[16,643]{1,0:T(8,128)} async-done(((f32[256,643]{1,0:T(8,128)}), f32[16,643]{1,0:T(8,128)}) %reduce-scatter.17.cloned.1.call-update) | async-done | bytes 41168
  (408 shorter events, 296.9 us)
Async XLA Ops:
  7.2 755.8 %copy-start = (bf16[4,176,2048]{2,1,0:T(8,128)(2,1)S(1)}, bf16[4,176,2048]{2,1,0:T(8,128)(2,1)}, u32[]{:S(2)}) copy-start(bf16[4,176,2048]{2,1,0:T(8,128)(2,1)} %param.30) | copy-start | bytes 8650756
  7.2 84.3 %all-gather.6.cloned.1.call-start = ((), (), s32[]{:S(2)}) async-start(), calls=%async_computation.6 | async-start | bytes 4718592 | tf_op jit(solution)/shard_map/all_gather | solution.py:294
  9.5 129.3 %all-gather.8.cloned.1.call-start = ((), (), s32[]{:S(2)}) async-start(), calls=%async_computation.7 | async-start | bytes 4769792 | tf_op jit(solution)/shard_map/all_gather | solution.py:275
  16.2 160.7 %all-gather.10.cloned.1.call-start = ((), (), s32[]{:S(2)}) async-start(), calls=%async_computation.8 | async-start | bytes 1427456 | tf_op jit(solution)/shard_map/all_gather | solution.py:288
  17.8 238.3 %all-gather.12.cloned.1.call-start = ((), (), s32[]{:S(2)}) async-start(), calls=%async_computation.10 | async-start | bytes 4718592 | tf_op jit(solution)/shard_map/all_gather | solution.py:295
  19.9 347.7 %all-reduce.6.cloned.1.call-start = ((), (), s32[]{:S(2)}) async-start(), calls=%async_computation.9 | async-start | bytes 8388608 | tf_op jit(solution)/shard_map/psum | solution.py:359
  20.0 145.0 %copy-start.98 = (f32[32]{0:T(128)}, f32[32]{0:T(128)S(1)}, u32[]{:S(2)}) copy-start(f32[32]{0:T(128)S(1)} %multiply_power_fusion) | copy-start | bytes 388
  20.0 144.9 %copy-start.78 = (f32[1024]{0:T(1024)}, f32[1024]{0:T(1024)S(1)}, u32[]{:S(2)}) copy-start(f32[1024]{0:T(1024)S(1)} %iota_convert_fusion) | copy-start | bytes 12292
  94.7 55.9 %copy-start.76 = (f32[1024]{0:T(1024)}, f32[1024]{0:T(1024)S(1)}, u32[]{:S(2)}) copy-start(f32[1024]{0:T(1024)S(1)} %add_rsqrt_fusion.2) | copy-start | bytes 12292
  147.8 19.0 %copy-start.90 = (f32[512]{0:T(512)}, f32[512]{0:T(512)S(1)}, u32[]{:S(2)}) copy-start(f32[512]{0:T(512)S(1)} %reshape.474) | copy-start | bytes 6148
  184.2 10.9 copy-start.71
  195.1 67.8 %copy-start.68 = (s32[2560]{0:T(1024)}, s32[2560]{0:T(1024)S(1)}, u32[]{:S(2)}) copy-start(s32[2560]{0:T(1024)S(1)} %scatter_custom_fusion.tok_ref) | copy-start | bytes 30724
  196.7 177.1 %copy-start.60 = (f32[2048,1]{0,1:T(1,128)}, f32[2048,1]{0,1:T(1,128)S(1)}, u32[]{:S(2)}) copy-start(f32[2048,1]{0,1:T(1,128)S(1)} %slice_convert_fusion.1) | copy-start | bytes 24580
  728.4 17.1 copy-start.27
  774.3 12.4 copy-start.29
  774.3 12.4 copy-start.43
  841.4 296.0 %all-to-all-start.1 = ((bf16[16,4,40,32,128]{4,3,2,1,0:T(8,128)(2,1)}), bf16[16,4,40,32,128]{4,3,2,1,0:T(8,128)(2,1)}, u32[]{:S(2)}, u32[]{:S(2)}) async-start(bf16[16,4,40,32,128]{4,3,2,1,0:T(8,128)(2,1)} %copy.176), calls=%async_computation.1 | async-start | bytes 41943040 | tf_op jit(solution)/shard_map/all_to_all | solution.py:426
  846.9 238.7 %all-gather.14.cloned.1.call-start = ((), (), s32[]{:S(2)}) async-start(), calls=%async_computation.11 | async-start | bytes 4595712 | tf_op jit(solution)/shard_map/all_gather | solution.py:390
  847.4 449.3 %all-reduce.8.cloned.1.call-start = ((), (), s32[]{:S(2)}) async-start(), calls=%async_computation.12 | async-start | bytes 8388608 | tf_op jit(solution)/shard_map/psum | solution.py:473
  1184.0 208.9 %reduce-scatter.15.cloned.1.call-start = ((), (), s32[]{:S(2)}) async-start(), calls=%async_computation.15 | async-start | bytes 5013504
  1192.0 26.0 %copy-start.67 = (s32[1024,2]{0,1:T(2,128)S(1)}, s32[1024,2]{0,1:T(2,128)}, u32[]{:S(2)}) copy-start(s32[1024,2]{0,1:T(2,128)} %param.19) | copy-start | bytes 24580
  1192.0 104.7 %copy-start.37 = (bf16[2048,321]{0,1:T(8,128)(2,1)S(1)}, bf16[2048,321]{0,1:T(8,128)(2,1)}, u32[]{:S(2)}) copy-start(bf16[2048,321]{0,1:T(8,128)(2,1)} %all-gather.10.cloned.1.call-done) | copy-start | bytes 3944452
  1192.1 104.7 %copy-start.61 = (f32[2048,1]{0,1:T(1,128)S(1)}, f32[2048,1]{0,1:T(1,128)}, u32[]{:S(2)}) copy-start(f32[2048,1]{0,1:T(1,128)} %copy-done.60) | copy-start | bytes 24580
  1218.1 89.2 %copy-start.75 = (f32[1024]{0:T(1024)S(1)}, f32[1024]{0:T(1024)}, u32[]{:S(2)}) copy-start(f32[1024]{0:T(1024)} %copy-done.74) | copy-start | bytes 12292
  1218.1 89.2 %copy-start.92 = (f32[1024]{0:T(1024)S(1)}, f32[1024]{0:T(1024)}, u32[]{:S(2)}) copy-start(f32[1024]{0:T(1024)} %get-tuple-element.140) | copy-start | bytes 12292
  1326.2 154.0 %reduce-scatter.13.cloned.1.call-start = ((), (), s32[]{:S(2)}) async-start(), calls=%async_computation.14 | async-start | bytes 4718592
  1339.5 270.8 %all-reduce.10.cloned.1.call-start = ((), (), s32[]{:S(2)}) async-start(), calls=%async_computation.13 | async-start | bytes 10747904 | tf_op jit(solution)/shard_map/psum | solution.py:579
  1358.4 36.5 %copy-start.53 = (bf16[1024,384]{0,1:T(8,128)(2,1)S(1)}, bf16[1024,384]{0,1:T(8,128)(2,1)}, u32[]{:S(2)}) copy-start(bf16[1024,384]{0,1:T(8,128)(2,1)} %pad_maximum_fusion.6) | copy-start | bytes 2359300
  1409.7 265.6 %reduce-scatter.19.cloned.1.call-start = ((), (), s32[]{:S(2)}) async-start(), calls=%async_computation.17 | async-start | bytes 3342336
  1447.7 289.6 %reduce-scatter.17.cloned.1.call-start = ((), (), s32[]{:S(2)}) async-start(), calls=%async_computation.16 | async-start | bytes 835584
  1616.0 10.9 copy-start.57
  1632.8 110.6 %copy-start.1 = (bf16[4,176,2048]{2,1,0:T(8,128)(2,1)S(1)}, bf16[4,176,2048]{2,1,0:T(8,128)(2,1)}, u32[]{:S(2)}) copy-start(bf16[4,176,2048]{2,1,0:T(8,128)(2,1)} %param.30) | copy-start | bytes 8650756
  (81 other events, 346.3 us)
Sparse Core Ops, SparseCore 0:
  10.8 80.6 all-gather.5
  93.7 44.9 all-gather.7
  140.9 35.0 all-gather.9
  178.0 77.9 all-gather.11
  259.0 108.5 all-reduce.5
  849.0 236.5 all-gather.13
  1184.2 112.5 all-reduce.7
  1326.3 66.6 reduce-scatter.14
  1396.8 83.2 reduce-scatter.12
  1482.5 127.7 all-reduce.9
  1612.9 62.4 reduce-scatter.18
  1677.7 59.5 reduce-scatter.16

commit v3 on v2

--- a/solution.py
+++ b/solution.py
@@ -86,31 +86,29 @@
     return (gate_grad, up_grad)
 
 
-def dispatch_kernel(tok_ref, rows_hbm, grads_hbm, col_ref, out_ref, rows_buf, grads_buf, sems):
-    block = rows_buf.shape[0]
-    tile_rows = rows_buf.shape[1]
-    last = rows_hbm.shape[0] - 1
+def dispatch_kernel(tok_ref, both_hbm, col_ref, out_ref, both_buf, sems):
+    block = both_buf.shape[0]
+    tile_rows = both_buf.shape[1] // 2
+    last = both_hbm.shape[0] - 1
     base = pl.program_id(0) * block
 
     def start(r, carry):
         tok = jnp.minimum(tok_ref[base + r], last)
-        pltpu.make_async_copy(rows_hbm.at[tok], rows_buf.at[r], sems.at[0, r]).start()
-        pltpu.make_async_copy(grads_hbm.at[tok], grads_buf.at[r], sems.at[1, r]).start()
+        pltpu.make_async_copy(both_hbm.at[tok], both_buf.at[r], sems.at[r]).start()
         return carry
 
-    lax.fori_loop(0, block, start, 0)
+    lax.fori_loop(0, block, start, 0, unroll=4)
 
     def finish(r, carry):
-        pltpu.make_async_copy(rows_hbm.at[0], rows_buf.at[r], sems.at[0, r]).wait()
-        pltpu.make_async_copy(grads_hbm.at[0], grads_buf.at[r], sems.at[1, r]).wait()
+        pltpu.make_async_copy(both_hbm.at[0], both_buf.at[r], sems.at[r]).wait()
         return carry
 
-    lax.fori_loop(0, block, finish, 0)
-    rows = rows_buf[...]
+    lax.fori_loop(0, block, finish, 0, unroll=4)
+    rows = both_buf[:, :tile_rows, :]
     out_ref[:, :tile_rows, :] = jnp.where(col_ref[0] > 0, rows, jnp.zeros_like(rows))
-    out_ref[:, tile_rows:, :] = (grads_buf[...].astype(jnp.float32) * col_ref[1]).astype(
-        out_ref.dtype
-    )
+    out_ref[:, tile_rows:, :] = (
+        both_buf[:, tile_rows:, :].astype(jnp.float32) * col_ref[1]
+    ).astype(out_ref.dtype)
 
 
 def dispatch_rows(slot_token, rows, grads, valid, gate, block=128):
@@ -118,6 +116,7 @@
     count, width = rows.shape
     tile_rows = width // 128
     cols = jnp.broadcast_to(jnp.stack([valid, gate])[:, :, None, None], (2, slots, 1, 128))
+    both = jnp.concatenate([rows, grads], 1).reshape(count, 2 * tile_rows, 128)
     out = pl.pallas_call(
         dispatch_kernel,
         out_shape=jax.ShapeDtypeStruct((slots, 2 * tile_rows, 128), rows.dtype),
@@ -126,20 +125,18 @@
             grid=(slots // block,),
             in_specs=[
                 pl.BlockSpec(memory_space=pl.ANY),
-                pl.BlockSpec(memory_space=pl.ANY),
                 pl.BlockSpec((2, block, 1, 128), lambda i, tok: (0, i, 0, 0)),
             ],
             out_specs=pl.BlockSpec((block, 2 * tile_rows, 128), lambda i, tok: (i, 0, 0)),
             scratch_shapes=[
-                pltpu.VMEM((block, tile_rows, 128), rows.dtype),
-                pltpu.VMEM((block, tile_rows, 128), grads.dtype),
-                pltpu.SemaphoreType.DMA((2, block)),
+                pltpu.VMEM((block, 2 * tile_rows, 128), rows.dtype),
+                pltpu.SemaphoreType.DMA((block,)),
             ],
         ),
         cost_estimate=pl.CostEstimate(
             flops=slots * width, transcendentals=0, bytes_accessed=4 * slots * 2 * width
         ),
-    )(slot_token, rows.reshape(count, tile_rows, 128), grads.reshape(count, tile_rows, 128), cols)
+    )(slot_token, both, cols)
     return out
 
 
@@ -563,19 +560,14 @@
         expand_grads, expand_weights.T, preferred_element_type=jnp.float32
     )
     latent_grad_part = jnp.concatenate([compressed_grad_part, key_rope_grad], -1)
-    attn_pack = lax.psum_scatter(
-        jnp.concatenate(
-            [
-                query_grad_w,
-                output_grad_w_t,
-                expand_grad_w.reshape(dp_size * rows_dp, expand_flat_cols),
-            ],
-            1,
-        ).astype(jnp.bfloat16),
-        "dp",
-        scatter_dimension=0,
-        tiled=True,
-    ).astype(jnp.float32)
+    attn_grads_in = jnp.concatenate(
+        [
+            query_grad_w,
+            output_grad_w_t,
+            expand_grad_w.reshape(dp_size * rows_dp, expand_flat_cols),
+        ],
+        1,
+    )
     token_all = lax.psum(
         jnp.concatenate([normed_grad_part, latent_grad_part], 1).astype(jnp.bfloat16), "tensor"
     ).astype(jnp.float32)
@@ -626,7 +618,18 @@
         ],
         1,
     )
-    small_own = lax.psum_scatter(small_pack, "dp", scatter_dimension=0, tiled=True)
+    attn_width = attn_grads_in.shape[1]
+    small_width = small_pack.shape[1]
+    small_count = row_per * small_width
+    small_cols = -(-small_count // rows_dp)
+    small_flat = jnp.pad(
+        small_pack.reshape(dp_size, small_count), ((0, 0), (0, small_cols * rows_dp - small_count))
+    ).reshape(dp_size * rows_dp, small_cols)
+    merged_own = lax.psum_scatter(
+        jnp.concatenate([attn_grads_in, small_flat], 1), "dp", scatter_dimension=0, tiled=True
+    )
+    attn_pack = merged_own[:, :attn_width]
+    small_own = merged_own[:, attn_width:].reshape(-1)[:small_count].reshape(row_per, small_width)
     cut = [0]
     for width in (latent_cols, experts, 1, 1, 1):
         cut.append(cut[-1] + width)

time: 1760 us -> 1730 us (0.983)
  waiting for transfers between devices: 884 us -> 844 us
    reduce_scatter x0 -> x1, waiting for transfers between devices: none -> 61.1 us  [shards(): lax.psum_scatter(jnp.concatenate([attn_grads_in, small_flat], 1), 'dp', s...]
    unnamed x16 -> x13, waiting for transfers between devices: 139 us -> 82.5 us
    psum x1, waiting for transfers between devices: 127 us -> 85.4 us  [shards(): lax.psum(jnp.concatenate([normed_grad_part, latent_grad_part], 1).astype(...]
    unnamed x221 -> x215, local copies, waits for them, and re-layouts: 61.7 us -> 53.6 us
  transfers between devices with their start and end apart: 13 -> 12, of which waited for: 12 -> 11; matrix products, arithmetic and copies ran while one was open for 15% -> 14% of each run, Pallas kernels for 0% -> 0%
where the time goes in v3:
time: 1730 us; the launch traced here: 1720 us
  waiting for transfers between devices  844 us (49%)
  blocking collectives  258 us (15%)
  local copies, waits for them, and re-layouts  219 us (13%)
  matrix products  186 us (11%)
  other arithmetic  101 us (6%)
  Pallas kernels  87.2 us (5%)
    all_to_all x1, blocking collectives, shards(): lax.all_to_all(send_both, 'dp', split_axis=0, concat_axis=0, tiled=True)  236 us
    all_gather x1, waiting for transfers between devices, shards(): shared_all = lax.all_gather(shared_local, 'dp', axis=0, tiled=True)  231 us
    psum x1, waiting for transfers between devices, shards(): lax.psum(attn_part.astype(jnp.bfloat16), 'tensor').astype(jnp.float32)  94.7 us
    psum x1, waiting for transfers between devices, shards(): lax.psum(jnp.concatenate([normed_grad_part, latent_grad_part], 1).astype(...  85.4 us
    unnamed x13, waiting for transfers between devices  82.5 us
    psum x1, waiting for transfers between devices, shards(): lax.psum((back_part, gate_part.astype(jnp.bfloat16)), 'tensor')  79.2 us
    all_gather x1, waiting for transfers between devices, shards(): hidden_all = lax.all_gather(hidden, 'tensor', axis=0, tiled=True)  71.8 us
    all_gather x1, waiting for transfers between devices, shards(): grad_seq = lax.all_gather(out_grad, 'tensor', axis=0, tiled=True)  70.4 us
  transfers between devices with their start and end apart: 12, of which 11 were waited for; matrix products, arithmetic and copies ran while one was open for 14% of the time, Pallas kernels for 0%

profile of v3, /device:TPU:0, one launch (start us, length us, event | category | flops | bytes accessed | tf_op | source)
XLA Modules:
  0.0 1717.5 jit_solution(4663136992292218643)
XLA Ops:
  19.8 71.8 %all-gather.6.cloned.1.call-done = bf16[1024,2048]{0,1:T(8,128)(2,1)} async-done(((bf16[128,2048]{0,1:T(8,128)(2,1)}), bf16[1024,2048]{0,1:T(8,128)(2,1)}) %all-gather.6.cloned.1.call-update) | async-done | bytes 4194320 | tf_op jit(solution)/shard_map/all_gather | solution.py:291
  94.7 44.1 %all-gather.8.cloned.1.call-done = bf16[2048,1090]{0,1:T(8,128)(2,1)} async-done(((bf16[128,1090]{0,1:T(8,128)(2,1)}), bf16[2048,1090]{0,1:T(8,128)(2,1)}) %all-gather.8.cloned.1.call-update) | async-done | bytes 4464656 | tf_op jit(solution)/shard_map/all_gather | solution.py:272
  191.9 8.1 scatter_custom_fusion.tok_ref
  201.5 94.7 %all-reduce.7.cloned.1.call-done = bf16[1024,2048]{0,1:T(8,128)(2,1)} async-done(((bf16[1024,2048]{0,1:T(8,128)(2,1)}), bf16[1024,2048]{0,1:T(8,128)(2,1)}) %all-reduce.7.cloned.1.call-update) | async-done | bytes 4194320 | tf_op jit(solution)/shard_map/psum | solution.py:356
  305.3 70.4 %all-gather.12.cloned.1.call-done = bf16[1024,2048]{0,1:T(8,128)(2,1)} async-done(((bf16[128,2048]{0,1:T(8,128)(2,1)}), bf16[1024,2048]{0,1:T(8,128)(2,1)}) %all-gather.12.cloned.1.call-update) | async-done | bytes 4194320 | tf_op jit(solution)/shard_map/all_gather | solution.py:292
  383.4 12.6 copy.221.both_hbm
  400.9 8.1 scatter_custom_fusion.1
  416.3 50.9 %shard_map.297 = bf16[2560,32,128]{2,1,0:T(8,128)(2,1)} custom-call(s32[2560]{0:T(1024)} %copy-done.64, bf16[1024,32,128]{2,1,0:T(8,128)(2,1)} %copy.221.both_hbm, f32[2,2560,1,128]{3,2,1,0:T(1,128)} %broadcast_in_dim.73.col_ref), custom_call_target="tpu_custom_call" | custom-call | flops 5242880 | bytes 41943040 | tf_op jit(solution)/shard_map/pallas_call | solution.py:120
  467.2 236.3 %all_to_all.10 = bf16[16,4,40,32,128]{4,3,2,1,0:T(8,128)(2,1)} all-to-all(bf16[16,4,40,32,128]{4,3,2,1,0:T(8,128)(2,1)} %bitcast.246), channel_id=1, replica_groups=mesh['dp'=16,'tensor'=8] {'dp'}, dimensions={0} | all-to-all | bytes 41943040 | tf_op jit(solution)/shard_map/all_to_all | solution.py:391
  703.5 31.3 %reshape.517 = bf16[16,4,40,4096]{3,2,1,0:T(8,128)(2,1)} reshape(bf16[16,4,40,32,128]{4,3,2,1,0:T(8,128)(2,1)} %all_to_all.10) | data formatting | bytes 41943040 | tf_op jit(solution)/shard_map/reshape | solution.py:392
  734.8 17.0 fusion.166
  751.9 8.8 fusion.12
  760.7 8.7 fusion.4
  769.4 11.3 fusion.43
  780.7 12.5 fusion.33
  798.6 12.3 fusion.1
  810.8 10.4 pad_maximum_fusion
  828.8 19.0 %copy.175 = bf16[16,4,40,32,128]{4,3,2,1,0:T(8,128)(2,1)} copy(bf16[16,4,40,32,128]{4,3,2,0,1:T(8,128)(2,1)} %bitcast.248) | data formatting | bytes 41943040 | tf_op jit(solution)/shard_map/reshape | solution.py:426
  861.4 230.9 %all-gather.14.cloned.1.call-done = bf16[2048,1056]{0,1:T(8,128)(2,1)} async-done(((bf16[128,1056]{0,1:T(8,128)(2,1)}), bf16[2048,1056]{0,1:T(8,128)(2,1)}) %all-gather.14.cloned.1.call-update) | async-done | bytes 4325392 | tf_op jit(solution)/shard_map/all_gather | solution.py:387
  1120.3 23.6 %all-to-all-done.1 = bf16[16,4,40,32,128]{4,3,2,1,0:T(8,128)(2,1)} async-done(((bf16[16,4,40,32,128]{4,3,2,1,0:T(8,128)(2,1)}), bf16[16,4,40,32,128]{4,3,2,1,0:T(8,128)(2,1)}, u32[]{:S(2)}, u32[]{:S(2)}) %all-to-all-start.1) | async-done | bytes 20971552 | tf_op jit(solution)/shard_map/all_to_all | solution.py:423
  1147.4 36.4 %shard_map.298 = (bf16[1024,16,128]{2,1,0:T(8,128)(2,1)}, bf16[1024,16,128]{2,1,0:T(8,128)(2,1)}, f32[1024,1,128]{2,1,0:T(1,128)}) custom-call(s32[2048]{0:T(1024)} %multiply_add_fusion.slot_ref, bf16[2560,32,128]{2,1,0:T(8,128)(2,1)} %bitcast.36.table_hbm, f32[2,1024,1,128]{3,2,1,0:T(1,128)} %broadcast_in_dim.74.gate_ref, ...), custom_call_target="tpu_custom_call" | custom-call | flops 33554432 | bytes 46137344 | tf_op jit(solution)/shard_map/pallas_call | solution.py:191
  1201.5 21.9 %psum.30 = bf16[1024,2]{0,1:T(2,128)(2,1)S(1)} all-reduce(bf16[1024,2]{0,1:T(2,128)(2,1)S(1)} %bitcast.289), channel_id=1, replica_groups=mesh['dp'=16,'tensor'=8] {'tensor'}, use_global_device_ids=true, to_apply=%region_16.17 | all-reduce | flops 2048 | bytes 8192 | tf_op jit(solution)/shard_map/psum | solution.py:470
  1223.5 79.2 %all-reduce.9.cloned.1.call-done = bf16[1024,2048]{0,1:T(8,128)(2,1)} async-done(((bf16[1024,2048]{0,1:T(8,128)(2,1)}), bf16[1024,2048]{0,1:T(8,128)(2,1)}) %all-reduce.9.cloned.1.call-update) | async-done | bytes 4194320 | tf_op jit(solution)/shard_map/psum | solution.py:470
  1302.7 10.5 multiply_reduce_fusion
  1313.2 12.4 fusion.165
  1351.8 46.9 %reduce-scatter.12.cloned.1.call-done = bf16[128,1056]{1,0:T(8,128)(2,1)} async-done(((bf16[2048,1056]{1,0:T(8,128)(2,1)}), bf16[128,1056]{1,0:T(8,128)(2,1)}) %reduce-scatter.12.cloned.1.call-update) | async-done | bytes 270352
  1403.7 10.5 pad_maximum_fusion.3
  1456.6 85.4 %all-reduce.11.cloned.1.call-done = bf16[1024,2624]{0,1:T(8,128)(2,1)} async-done(((bf16[1024,2624]{0,1:T(8,128)(2,1)}), bf16[1024,2624]{0,1:T(8,128)(2,1)}) %all-reduce.11.cloned.1.call-update) | async-done | bytes 5373968 | tf_op jit(solution)/shard_map/psum | solution.py:571
  1570.0 9.4 fusion.20
  1579.3 9.3 fusion.23
  1593.7 34.9 %reduce-scatter.10.cloned.1.call-done = bf16[128,2048]{1,0:T(8,128)(2,1)} async-done(((bf16[1024,2048]{1,0:T(8,128)(2,1)}), bf16[128,2048]{1,0:T(8,128)(2,1)}) %reduce-scatter.10.cloned.1.call-update) | async-done | bytes 524304
  1640.9 61.1 %reduce-scatter.8.cloned.1.call-done = f32[128,849]{0,1:T(8,128)} async-done(((f32[2048,849]{0,1:T(8,128)}), f32[128,849]{0,1:T(8,128)}) %reduce-scatter.8.cloned.1.call-update) | async-done | bytes 434704 | tf_op jit(solution)/shard_map/reduce_scatter | solution.py:628
  (409 shorter events, 300.7 us)
Async XLA Ops:
  7.2 762.2 %copy-start = (bf16[4,176,2048]{2,1,0:T(8,128)(2,1)S(1)}, bf16[4,176,2048]{2,1,0:T(8,128)(2,1)}, u32[]{:S(2)}) copy-start(bf16[4,176,2048]{2,1,0:T(8,128)(2,1)} %param.30) | copy-start | bytes 8650756
  7.2 84.3 %all-gather.6.cloned.1.call-start = ((), (), s32[]{:S(2)}) async-start(), calls=%async_computation.5 | async-start | bytes 4718592 | tf_op jit(solution)/shard_map/all_gather | solution.py:291
  9.5 129.3 %all-gather.8.cloned.1.call-start = ((), (), s32[]{:S(2)}) async-start(), calls=%async_computation.6 | async-start | bytes 4769792 | tf_op jit(solution)/shard_map/all_gather | solution.py:272
  16.2 165.2 %all-gather.10.cloned.1.call-start = ((), (), s32[]{:S(2)}) async-start(), calls=%async_computation.7 | async-start | bytes 1427456 | tf_op jit(solution)/shard_map/all_gather | solution.py:285
  17.8 278.4 %all-reduce.7.cloned.1.call-start = ((), (), s32[]{:S(2)}) async-start(), calls=%async_computation.8 | async-start | bytes 8388608 | tf_op jit(solution)/shard_map/psum | solution.py:356
  17.9 153.1 %copy-start.95 = (f32[32]{0:T(128)}, f32[32]{0:T(128)S(1)}, u32[]{:S(2)}) copy-start(f32[32]{0:T(128)S(1)} %multiply_power_fusion) | copy-start | bytes 388
  17.9 153.1 %copy-start.77 = (f32[1024]{0:T(1024)}, f32[1024]{0:T(1024)S(1)}, u32[]{:S(2)}) copy-start(f32[1024]{0:T(1024)S(1)} %iota_convert_fusion) | copy-start | bytes 12292
  94.7 55.9 %copy-start.75 = (f32[1024]{0:T(1024)}, f32[1024]{0:T(1024)S(1)}, u32[]{:S(2)}) copy-start(f32[1024]{0:T(1024)S(1)} %add_rsqrt_fusion.2) | copy-start | bytes 12292
  147.8 16.9 copy-start.83
  167.4 12.8 copy-start.16
  186.2 189.5 %all-gather.12.cloned.1.call-start = ((), (), s32[]{:S(2)}) async-start(), calls=%async_computation.9 | async-start | bytes 4718592 | tf_op jit(solution)/shard_map/all_gather | solution.py:292
  200.0 101.8 %copy-start.64 = (s32[2560]{0:T(1024)}, s32[2560]{0:T(1024)S(1)}, u32[]{:S(2)}) copy-start(s32[2560]{0:T(1024)S(1)} %scatter_custom_fusion.tok_ref) | copy-start | bytes 30724
  201.5 100.8 %copy-start.56 = (f32[2048,1]{0,1:T(1,128)}, f32[2048,1]{0,1:T(1,128)S(1)}, u32[]{:S(2)}) copy-start(f32[2048,1]{0,1:T(1,128)S(1)} %slice_convert_fusion.1) | copy-start | bytes 24580
  734.8 17.0 copy-start.28
  780.7 12.5 copy-start.42
  847.8 296.0 %all-to-all-start.1 = ((bf16[16,4,40,32,128]{4,3,2,1,0:T(8,128)(2,1)}), bf16[16,4,40,32,128]{4,3,2,1,0:T(8,128)(2,1)}, u32[]{:S(2)}, u32[]{:S(2)}) async-start(bf16[16,4,40,32,128]{4,3,2,1,0:T(8,128)(2,1)} %copy.175), calls=%async_computation.1 | async-start | bytes 41943040 | tf_op jit(solution)/shard_map/all_to_all | solution.py:423
  853.3 239.0 %all-gather.14.cloned.1.call-start = ((), (), s32[]{:S(2)}) async-start(), calls=%async_computation.10 | async-start | bytes 4595712 | tf_op jit(solution)/shard_map/all_gather | solution.py:387
  853.9 448.8 %all-reduce.9.cloned.1.call-start = ((), (), s32[]{:S(2)}) async-start(), calls=%async_computation.11 | async-start | bytes 8388608 | tf_op jit(solution)/shard_map/psum | solution.py:470
  1190.4 208.3 %reduce-scatter.12.cloned.1.call-start = ((), (), s32[]{:S(2)}) async-start(), calls=%async_computation.15 | async-start | bytes 5013504
  1198.4 25.0 %copy-start.63 = (s32[1024,2]{0,1:T(2,128)S(1)}, s32[1024,2]{0,1:T(2,128)}, u32[]{:S(2)}) copy-start(s32[1024,2]{0,1:T(2,128)} %param.19) | copy-start | bytes 24580
  1198.4 104.3 %copy-start.35 = (bf16[2048,321]{0,1:T(8,128)(2,1)S(1)}, bf16[2048,321]{0,1:T(8,128)(2,1)}, u32[]{:S(2)}) copy-start(bf16[2048,321]{0,1:T(8,128)(2,1)} %all-gather.10.cloned.1.call-done) | copy-start | bytes 3944452
  1198.4 104.3 %copy-start.57 = (f32[2048,1]{0,1:T(1,128)S(1)}, f32[2048,1]{0,1:T(1,128)}, u32[]{:S(2)}) copy-start(f32[2048,1]{0,1:T(1,128)} %copy-done.56) | copy-start | bytes 24580
  1223.5 89.7 %copy-start.71 = (f32[1024]{0:T(1024)S(1)}, f32[1024]{0:T(1024)}, u32[]{:S(2)}) copy-start(f32[1024]{0:T(1024)} %copy-done.70) | copy-start | bytes 12292
  1223.5 89.7 %copy-start.89 = (f32[1024]{0:T(1024)S(1)}, f32[1024]{0:T(1024)}, u32[]{:S(2)}) copy-start(f32[1024]{0:T(1024)} %get-tuple-element.140) | copy-start | bytes 12292
  1332.0 210.0 %all-reduce.11.cloned.1.call-start = ((), (), s32[]{:S(2)}) async-start(), calls=%async_computation.12 | async-start | bytes 10747904 | tf_op jit(solution)/shard_map/psum | solution.py:571
  1351.0 48.9 %copy-start.50 = (bf16[1024,384]{0,1:T(8,128)(2,1)S(1)}, bf16[1024,384]{0,1:T(8,128)(2,1)}, u32[]{:S(2)}) copy-start(bf16[1024,384]{0,1:T(8,128)(2,1)} %pad_maximum_fusion.7) | copy-start | bytes 2359300
  1414.2 214.3 %reduce-scatter.10.cloned.1.call-start = ((), (), s32[]{:S(2)}) async-start(), calls=%async_computation.14 | async-start | bytes 4718592
  1427.6 274.4 %reduce-scatter.8.cloned.1.call-start = ((), (), s32[]{:S(2)}) async-start(), calls=%async_computation.13 | async-start | bytes 7450624 | tf_op jit(solution)/shard_map/reduce_scatter | solution.py:628
  1570.0 18.7 %slice-start = ((s8[10485760]{0:T(1024)(128)(4,1)}), s8[4194304]{0:T(1024)(128)(4,1)S(1)}, s32[]{:S(2)}) async-start(s8[10485760]{0:T(1024)(128)(4,1)} %bitcast.259), calls=%async_computation.16 | async-start | bytes 8388608
  1570.0 18.7 %slice-start.1 = ((s8[10485760]{0:T(1024)(128)(4,1)}), s8[4194304]{0:T(1024)(128)(4,1)S(1)}, s32[]{:S(2)}) async-start(s8[10485760]{0:T(1024)(128)(4,1)} %bitcast.259), calls=%async_computation.17 | async-start | bytes 8388608
  1593.7 39.4 %copy-start.61 = (f32[2048,1]{0,1:T(1,128)S(1)}, f32[2048,1]{0,1:T(1,128)}, u32[]{:S(2)}) copy-start(f32[2048,1]{0,1:T(1,128)} %copy-done.60) | copy-start | bytes 24580
  1633.0 77.7 %copy-start.1 = (bf16[4,176,2048]{2,1,0:T(8,128)(2,1)S(1)}, bf16[4,176,2048]{2,1,0:T(8,128)(2,1)}, u32[]{:S(2)}) copy-start(bf16[4,176,2048]{2,1,0:T(8,128)(2,1)} %param.30) | copy-start | bytes 8650756
  (80 other events, 347.3 us)
Sparse Core Ops, SparseCore 0:
  10.8 80.6 all-gather.5
  93.7 44.9 all-gather.7
  140.9 35.0 all-gather.9
  186.3 109.8 all-reduce.6
  298.9 76.7 all-gather.11
  855.5 236.7 all-gather.13
  1190.5 112.1 all-reduce.8
  1332.2 66.4 reduce-scatter.11
  1414.3 127.6 all-reduce.10
  1546.3 82.2 reduce-scatter.9
  1631.2 70.7 reduce-scatter.7

commit v4 on v3

--- a/solution.py
+++ b/solution.py
@@ -289,7 +289,14 @@
     shared_local = jnp.concatenate([shared_gate, shared_up, shared_down.T], 1)
 
     hidden_all = lax.all_gather(hidden, "tensor", axis=0, tiled=True)
-    grad_seq = lax.all_gather(out_grad, "tensor", axis=0, tiled=True)
+    grad_seq = lax.all_to_all(
+        jnp.broadcast_to(out_grad[None], (tensor_size,) + out_grad.shape),
+        "tensor",
+        split_axis=0,
+        concat_axis=0,
+        tiled=True,
+    ).reshape(tensor_size * tok_dev, D)
+    grad_seq, hidden_all = lax.optimization_barrier((grad_seq, hidden_all))
     hidden_all_f = hidden_all.astype(jnp.float32)
     scale_one_all = norm_scale(hidden_all_f)
     gain_one = attn_gains.astype(jnp.float32)
@@ -467,12 +474,11 @@
         jnp.float32
     )
     output = (residual_own + feed_own).astype(jnp.bfloat16)
-    normed_two_grad, gate_grads = lax.psum(
-        (back_part, gate_part.astype(jnp.bfloat16)),
-        "tensor",
-    )
-    normed_two_grad = normed_two_grad.astype(jnp.float32)
-    gate_grads = gate_grads.astype(jnp.float32)
+    reduced_back = lax.psum(
+        jnp.concatenate([back_part, gate_cols.astype(jnp.bfloat16)], 1), "tensor"
+    ).astype(jnp.float32)
+    normed_two_grad = reduced_back[:, :D]
+    gate_grads = reduced_back[:, D : D + top_count]
     weighted_total = jnp.sum(gate_values * gate_grads, -1, keepdims=True)
     chosen_grads = gate_values * (gate_grads - weighted_total)
     logit_grads = jnp.sum(jnp.where(chosen_hot, chosen_grads[:, :, None], 0.0), 1)

time: 1730 us -> 1720 us (level)
  blocking collectives: 258 us -> 236 us
  waiting for transfers between devices: 844 us -> 824 us
    all_gather x1 -> x0, waiting for transfers between devices: 70.4 us -> none  [shards(): grad_seq = lax.all_gather(out_grad, 'tensor', axis=0, tiled=True)]
    all_to_all x0 -> x1, waiting for transfers between devices: none -> 53.9 us  [shards(): lax.all_to_all(jnp.broadcast_to(out_grad[None], (tensor_size,) + out_grad...]
    all_gather x1, waiting for transfers between devices: 71.8 us -> 46.8 us  [shards(): hidden_all = lax.all_gather(hidden, 'tensor', axis=0, tiled=True)]
    psum x1, waiting for transfers between devices: 79.2 us -> 103 us  [shards(): lax.psum(jnp.concatenate([back_part, gate_cols.astype(jnp.bfloat16)], 1),...]
    psum x1 -> x0, blocking collectives: 21.9 us -> none  [shards(): lax.psum((back_part, gate_part.astype(jnp.bfloat16)), 'tensor')]
    unnamed x215 -> x219, local copies, waits for them, and re-layouts: 53.6 us -> 54.4 us
    unnamed x13 -> x12, waiting for transfers between devices: 82.5 us -> 83.2 us
where the time goes in v4:
time: 1720 us; the launch traced here: 1700 us
  waiting for transfers between devices  824 us (48%)
  blocking collectives  236 us (14%)
  local copies, waits for them, and re-layouts  230 us (13%)
  matrix products  184 us (11%)
  other arithmetic  109 us (6%)
  Pallas kernels  86.6 us (5%)
    all_to_all x1, blocking collectives, shards(): lax.all_to_all(send_both, 'dp', split_axis=0, concat_axis=0, tiled=True)  236 us
    all_gather x1, waiting for transfers between devices, shards(): shared_all = lax.all_gather(shared_local, 'dp', axis=0, tiled=True)  231 us
    psum x1, waiting for transfers between devices, shards(): lax.psum(jnp.concatenate([back_part, gate_cols.astype(jnp.bfloat16)], 1),...  103 us
    psum x1, waiting for transfers between devices, shards(): lax.psum(attn_part.astype(jnp.bfloat16), 'tensor').astype(jnp.float32)  95 us
    psum x1, waiting for transfers between devices, shards(): lax.psum(jnp.concatenate([normed_grad_part, latent_grad_part], 1).astype(...  83.3 us
    unnamed x12, waiting for transfers between devices  83.2 us
    reduce_scatter x1, waiting for transfers between devices, shards(): lax.psum_scatter(jnp.concatenate([attn_grads_in, small_flat], 1), 'dp', s...  61 us
    unnamed x219, local copies, waits for them, and re-layouts  54.4 us
  transfers between devices with their start and end apart: 12, of which 11 were waited for; matrix products, arithmetic and copies ran while one was open for 14% of the time, Pallas kernels for 0%

profile of v4, /device:TPU:0, one launch (start us, length us, event | category | flops | bytes accessed | tf_op | source)
XLA Modules:
  0.0 1701.6 jit_solution(8075749545996622916)
XLA Ops:
  20.1 7.8 all-to-all-start
  30.7 53.9 %all-to-all-done = bf16[8,128,2048]{1,2,0:T(8,128)(2,1)} async-done(((bf16[8,128,2048]{1,2,0:T(8,128)(2,1)}), bf16[8,128,2048]{1,2,0:T(8,128)(2,1)}, u32[]{:S(2)}, u32[]{:S(2)}) %all-to-all-start) | async-done | bytes 4194336 | tf_op jit(solution)/shard_map/all_to_all | solution.py:292
  89.4 46.8 %all-gather.5.cloned.1.call-done = bf16[1024,2048]{0,1:T(8,128)(2,1)} async-done(((bf16[128,2048]{0,1:T(8,128)(2,1)}), bf16[1024,2048]{0,1:T(8,128)(2,1)}) %all-gather.5.cloned.1.call-update) | async-done | bytes 4194320 | tf_op jit(solution)/shard_map/all_gather | solution.py:291
  139.3 44.1 %all-gather.7.cloned.1.call-done = bf16[2048,1090]{0,1:T(8,128)(2,1)} async-done(((bf16[128,1090]{0,1:T(8,128)(2,1)}), bf16[2048,1090]{0,1:T(8,128)(2,1)}) %all-gather.7.cloned.1.call-update) | async-done | bytes 4464656 | tf_op jit(solution)/shard_map/all_gather | solution.py:272
  236.2 8.1 scatter_custom_fusion.tok_ref
  245.8 95.0 %all-reduce.7.cloned.1.call-done = bf16[1024,2048]{0,1:T(8,128)(2,1)} async-done(((bf16[1024,2048]{0,1:T(8,128)(2,1)}), bf16[1024,2048]{0,1:T(8,128)(2,1)}) %all-reduce.7.cloned.1.call-update) | async-done | bytes 4194320 | tf_op jit(solution)/shard_map/psum | solution.py:363
  350.0 7.8 pad_maximum_fusion.1
  357.8 12.5 copy.224.both_hbm
  375.3 8.1 scatter_custom_fusion.1
  390.7 50.2 %shard_map.297 = bf16[2560,32,128]{2,1,0:T(8,128)(2,1)} custom-call(s32[2560]{0:T(1024)} %copy-done.64, bf16[1024,32,128]{2,1,0:T(8,128)(2,1)} %copy.224.both_hbm, f32[2,2560,1,128]{3,2,1,0:T(1,128)} %broadcast_in_dim.76.col_ref), custom_call_target="tpu_custom_call" | custom-call | flops 5242880 | bytes 41943040 | tf_op jit(solution)/shard_map/pallas_call | solution.py:120
  440.9 236.3 %all_to_all.15 = bf16[16,4,40,32,128]{4,3,2,1,0:T(8,128)(2,1)} all-to-all(bf16[16,4,40,32,128]{4,3,2,1,0:T(8,128)(2,1)} %bitcast.247), channel_id=1, replica_groups=mesh['dp'=16,'tensor'=8] {'dp'}, dimensions={0} | all-to-all | bytes 41943040 | tf_op jit(solution)/shard_map/all_to_all | solution.py:398
  677.3 31.3 %reshape.522 = bf16[16,4,40,4096]{3,2,1,0:T(8,128)(2,1)} reshape(bf16[16,4,40,32,128]{4,3,2,1,0:T(8,128)(2,1)} %all_to_all.15) | data formatting | bytes 41943040 | tf_op jit(solution)/shard_map/reshape | solution.py:399
  708.6 17.1 %fusion.164 = (bf16[16,4,40,2048]{3,2,1,0:T(8,128)(2,1)}, bf16[16,4,40,2048]{3,2,1,0:T(8,128)(2,1)}) fusion(bf16[16,4,40,4096]{3,2,1,0:T(8,128)(2,1)} %reshape.522), kind=kLoop, calls=%fused_computation.287 | loop fusion | bytes 41943040 | tf_op jit(solution)/shard_map/slice | solution.py:400
  725.7 8.8 fusion.12
  734.5 8.7 fusion.4
  743.2 11.3 fusion.43
  754.5 12.4 fusion.33
  772.4 12.2 fusion.1
  784.6 10.4 pad_maximum_fusion
  802.5 19.0 %copy.178 = bf16[16,4,40,32,128]{4,3,2,1,0:T(8,128)(2,1)} copy(bf16[16,4,40,32,128]{4,3,2,0,1:T(8,128)(2,1)} %bitcast.249) | data formatting | bytes 41943040 | tf_op jit(solution)/shard_map/reshape | solution.py:433
  835.2 230.6 %all-gather.11.cloned.1.call-done = bf16[2048,1056]{0,1:T(8,128)(2,1)} async-done(((bf16[128,1056]{0,1:T(8,128)(2,1)}), bf16[2048,1056]{0,1:T(8,128)(2,1)}) %all-gather.11.cloned.1.call-update) | async-done | bytes 4325392 | tf_op jit(solution)/shard_map/all_gather | solution.py:394
  1093.6 24.0 %all-to-all-done.2 = bf16[16,4,40,32,128]{4,3,2,1,0:T(8,128)(2,1)} async-done(((bf16[16,4,40,32,128]{4,3,2,1,0:T(8,128)(2,1)}), bf16[16,4,40,32,128]{4,3,2,1,0:T(8,128)(2,1)}, u32[]{:S(2)}, u32[]{:S(2)}) %all-to-all-start.2) | async-done | bytes 20971552 | tf_op jit(solution)/shard_map/all_to_all | solution.py:430
  1121.1 36.4 %shard_map.298 = (bf16[1024,16,128]{2,1,0:T(8,128)(2,1)}, bf16[1024,16,128]{2,1,0:T(8,128)(2,1)}, f32[1024,1,128]{2,1,0:T(1,128)}) custom-call(s32[2048]{0:T(1024)} %multiply_add_fusion.slot_ref, bf16[2560,32,128]{2,1,0:T(8,128)(2,1)} %bitcast.36.table_hbm, f32[2,1024,1,128]{3,2,1,0:T(1,128)} %broadcast_in_dim.77.gate_ref, ...), custom_call_target="tpu_custom_call" | custom-call | flops 33554432 | bytes 46137344 | tf_op jit(solution)/shard_map/pallas_call | solution.py:191
  1181.0 102.5 %all-reduce.9.cloned.1.call-done = bf16[1024,2050]{0,1:T(8,128)(2,1)} async-done(((bf16[1024,2050]{0,1:T(8,128)(2,1)}), bf16[1024,2050]{0,1:T(8,128)(2,1)}) %all-reduce.9.cloned.1.call-update) | async-done | bytes 4198416 | tf_op jit(solution)/shard_map/psum | solution.py:477
  1295.8 12.4 fusion.163
  1334.3 47.4 %reduce-scatter.12.cloned.1.call-done = bf16[128,1056]{1,0:T(8,128)(2,1)} async-done(((bf16[2048,1056]{1,0:T(8,128)(2,1)}), bf16[128,1056]{1,0:T(8,128)(2,1)}) %reduce-scatter.12.cloned.1.call-update) | async-done | bytes 270352
  1387.6 10.5 pad_maximum_fusion.3
  1442.4 83.3 %all-reduce.11.cloned.1.call-done = bf16[1024,2624]{0,1:T(8,128)(2,1)} async-done(((bf16[1024,2624]{0,1:T(8,128)(2,1)}), bf16[1024,2624]{0,1:T(8,128)(2,1)}) %all-reduce.11.cloned.1.call-update) | async-done | bytes 5373968 | tf_op jit(solution)/shard_map/psum | solution.py:577
  1553.7 9.4 fusion.20
  1563.0 9.3 fusion.23
  1577.4 35.1 %reduce-scatter.10.cloned.1.call-done = bf16[128,2048]{1,0:T(8,128)(2,1)} async-done(((bf16[1024,2048]{1,0:T(8,128)(2,1)}), bf16[128,2048]{1,0:T(8,128)(2,1)}) %reduce-scatter.10.cloned.1.call-update) | async-done | bytes 524304
  1624.7 61.0 %reduce-scatter.8.cloned.1.call-done = f32[128,849]{0,1:T(8,128)} async-done(((f32[2048,849]{0,1:T(8,128)}), f32[128,849]{0,1:T(8,128)}) %reduce-scatter.8.cloned.1.call-update) | async-done | bytes 434704 | tf_op jit(solution)/shard_map/reduce_scatter | solution.py:634
  (415 shorter events, 321.1 us)
Async XLA Ops:
  7.2 736.0 %copy-start = (bf16[4,176,2048]{2,1,0:T(8,128)(2,1)S(1)}, bf16[4,176,2048]{2,1,0:T(8,128)(2,1)}, u32[]{:S(2)}) copy-start(bf16[4,176,2048]{2,1,0:T(8,128)(2,1)} %param.30) | copy-start | bytes 8650756
  7.2 128.9 %all-gather.5.cloned.1.call-start = ((), (), s32[]{:S(2)}) async-start(), calls=%async_computation.6 | async-start | bytes 4718592 | tf_op jit(solution)/shard_map/all_gather | solution.py:291
  9.5 173.9 %all-gather.7.cloned.1.call-start = ((), (), s32[]{:S(2)}) async-start(), calls=%async_computation.7 | async-start | bytes 4769792 | tf_op jit(solution)/shard_map/all_gather | solution.py:272
  20.1 64.5 %all-to-all-start = ((bf16[8,128,2048]{1,2,0:T(8,128)(2,1)}), bf16[8,128,2048]{1,2,0:T(8,128)(2,1)}, u32[]{:S(2)}, u32[]{:S(2)}) async-start(bf16[8,128,2048]{1,2,0:T(8,128)(2,1)} %broadcast_in_dim.62), calls=%async_computation | async-start | bytes 8388608 | tf_op jit(solution)/shard_map/all_to_all | solution.py:292
  27.9 198.1 %all-gather.9.cloned.1.call-start = ((), (), s32[]{:S(2)}) async-start(), calls=%async_computation.8 | async-start | bytes 1427456 | tf_op jit(solution)/shard_map/all_gather | solution.py:285
  28.7 312.2 %all-reduce.7.cloned.1.call-start = ((), (), s32[]{:S(2)}) async-start(), calls=%async_computation.9 | async-start | bytes 8388608 | tf_op jit(solution)/shard_map/psum | solution.py:363
  29.4 186.1 %copy-start.96 = (f32[32]{0:T(128)}, f32[32]{0:T(128)S(1)}, u32[]{:S(2)}) copy-start(f32[32]{0:T(128)S(1)} %multiply_power_fusion) | copy-start | bytes 388
  29.4 186.1 %copy-start.77 = (f32[1024]{0:T(1024)}, f32[1024]{0:T(1024)S(1)}, u32[]{:S(2)}) copy-start(f32[1024]{0:T(1024)S(1)} %iota_convert_fusion) | copy-start | bytes 12292
  139.3 55.9 %copy-start.75 = (f32[1024]{0:T(1024)}, f32[1024]{0:T(1024)S(1)}, u32[]{:S(2)}) copy-start(f32[1024]{0:T(1024)S(1)} %add_rsqrt_fusion.2) | copy-start | bytes 12292
  192.4 16.8 copy-start.83
  211.9 12.8 copy-start.15
  244.2 102.1 %copy-start.64 = (s32[2560]{0:T(1024)}, s32[2560]{0:T(1024)S(1)}, u32[]{:S(2)}) copy-start(s32[2560]{0:T(1024)S(1)} %scatter_custom_fusion.tok_ref) | copy-start | bytes 30724
  245.8 101.2 %copy-start.58 = (f32[2048,1]{0,1:T(1,128)}, f32[2048,1]{0,1:T(1,128)S(1)}, u32[]{:S(2)}) copy-start(f32[2048,1]{0,1:T(1,128)S(1)} %slice_convert_fusion.1) | copy-start | bytes 24580
  708.6 17.1 %copy-start.27 = (bf16[4,176,2048]{2,1,0:T(8,128)(2,1)S(1)}, bf16[4,176,2048]{2,1,0:T(8,128)(2,1)}, u32[]{:S(2)}) copy-start(bf16[4,176,2048]{2,1,0:T(8,128)(2,1)} %param.29) | copy-start | bytes 8650756
  754.5 12.4 copy-start.29
  754.5 12.4 copy-start.42
  821.6 296.0 %all-to-all-start.2 = ((bf16[16,4,40,32,128]{4,3,2,1,0:T(8,128)(2,1)}), bf16[16,4,40,32,128]{4,3,2,1,0:T(8,128)(2,1)}, u32[]{:S(2)}, u32[]{:S(2)}) async-start(bf16[16,4,40,32,128]{4,3,2,1,0:T(8,128)(2,1)} %copy.178), calls=%async_computation.2 | async-start | bytes 41943040 | tf_op jit(solution)/shard_map/all_to_all | solution.py:430
  827.1 238.7 %all-gather.11.cloned.1.call-start = ((), (), s32[]{:S(2)}) async-start(), calls=%async_computation.10 | async-start | bytes 4595712 | tf_op jit(solution)/shard_map/all_gather | solution.py:394
  827.7 455.9 %all-reduce.9.cloned.1.call-start = ((), (), s32[]{:S(2)}) async-start(), calls=%async_computation.11 | async-start | bytes 8421376 | tf_op jit(solution)/shard_map/psum | solution.py:477
  1170.6 211.2 %reduce-scatter.12.cloned.1.call-start = ((), (), s32[]{:S(2)}) async-start(), calls=%async_computation.15 | async-start | bytes 5013504
  1181.0 106.0 %copy-start.63 = (s32[1024,2]{0,1:T(2,128)S(1)}, s32[1024,2]{0,1:T(2,128)}, u32[]{:S(2)}) copy-start(s32[1024,2]{0,1:T(2,128)} %param.19) | copy-start | bytes 24580
  1181.0 106.0 %copy-start.35 = (bf16[2048,321]{0,1:T(8,128)(2,1)S(1)}, bf16[2048,321]{0,1:T(8,128)(2,1)}, u32[]{:S(2)}) copy-start(bf16[2048,321]{0,1:T(8,128)(2,1)} %all-gather.9.cloned.1.call-done) | copy-start | bytes 3944452
  1181.0 106.0 %copy-start.59 = (f32[2048,1]{0,1:T(1,128)S(1)}, f32[2048,1]{0,1:T(1,128)}, u32[]{:S(2)}) copy-start(f32[2048,1]{0,1:T(1,128)} %copy-done.58) | copy-start | bytes 24580
  1314.6 211.1 %all-reduce.11.cloned.1.call-start = ((), (), s32[]{:S(2)}) async-start(), calls=%async_computation.12 | async-start | bytes 10747904 | tf_op jit(solution)/shard_map/psum | solution.py:577
  1333.6 50.2 %copy-start.50 = (bf16[1024,384]{0,1:T(8,128)(2,1)S(1)}, bf16[1024,384]{0,1:T(8,128)(2,1)}, u32[]{:S(2)}) copy-start(bf16[1024,384]{0,1:T(8,128)(2,1)} %pad_maximum_fusion.8) | copy-start | bytes 2359300
  1398.1 214.3 %reduce-scatter.10.cloned.1.call-start = ((), (), s32[]{:S(2)}) async-start(), calls=%async_computation.14 | async-start | bytes 4718592
  1411.5 274.2 %reduce-scatter.8.cloned.1.call-start = ((), (), s32[]{:S(2)}) async-start(), calls=%async_computation.13 | async-start | bytes 7450624 | tf_op jit(solution)/shard_map/reduce_scatter | solution.py:634
  1553.7 18.7 %slice-start = ((s8[10485760]{0:T(1024)(128)(4,1)}), s8[4194304]{0:T(1024)(128)(4,1)S(1)}, s32[]{:S(2)}) async-start(s8[10485760]{0:T(1024)(128)(4,1)} %bitcast.260), calls=%async_computation.16 | async-start | bytes 8388608
  1553.7 18.7 %slice-start.1 = ((s8[10485760]{0:T(1024)(128)(4,1)}), s8[4194304]{0:T(1024)(128)(4,1)S(1)}, s32[]{:S(2)}) async-start(s8[10485760]{0:T(1024)(128)(4,1)} %bitcast.260), calls=%async_computation.17 | async-start | bytes 8388608
  1577.4 38.8 %copy-start.32 = (f32[128,1056]{0,1:T(8,128)S(1)}, f32[128,1056]{0,1:T(8,128)}, u32[]{:S(2)}) copy-start(f32[128,1056]{0,1:T(8,128)} %convert_element_type.338) | copy-start | bytes 1622020
  1577.4 39.6 %copy-start.61 = (f32[2048,1]{0,1:T(1,128)S(1)}, f32[2048,1]{0,1:T(1,128)}, u32[]{:S(2)}) copy-start(f32[2048,1]{0,1:T(1,128)} %copy-done.60) | copy-start | bytes 24580
  1616.9 77.6 %copy-start.1 = (bf16[4,176,2048]{2,1,0:T(8,128)(2,1)S(1)}, bf16[4,176,2048]{2,1,0:T(8,128)(2,1)}, u32[]{:S(2)}) copy-start(bf16[4,176,2048]{2,1,0:T(8,128)(2,1)} %param.30) | copy-start | bytes 8650756
  (82 other events, 357.4 us)
Sparse Core Ops, SparseCore 0:
  10.8 125.3 all-gather.4
  138.3 44.9 all-gather.6
  185.5 35.0 all-gather.8
  230.9 109.8 all-reduce.6
  829.2 236.5 all-gather.10
  1170.7 112.7 all-reduce.8
  1314.7 66.9 reduce-scatter.11
  1398.2 127.4 all-reduce.10
  1530.1 82.3 reduce-scatter.9
  1614.9 70.8 reduce-scatter.7

commit v5 on v4

--- a/solution.py
+++ b/solution.py
@@ -361,6 +361,7 @@
         "tk,dk->td", mixed_all, output_weights_t, preferred_element_type=jnp.float32
     )
     branch_all = lax.psum(attn_part.astype(jnp.bfloat16), "tensor").astype(jnp.float32)
+    shared_local, branch_all = lax.optimization_barrier((shared_local, branch_all))
     residual_all = hidden_all_f + branch_all
     residual_own = lax.dynamic_slice_in_dim(residual_all, start_row, tok_dev, 0)
     scale_two = norm_scale(residual_all)
@@ -390,8 +391,8 @@
     send_both = dispatch_rows(slot_token, normed_two, grad_seq, slot_valid, slot_gate).reshape(
         dp_size, exp_dev, capacity, 2 * tile_rows, 128
     )
-    shared_local, send_both = lax.optimization_barrier((shared_local, send_both))
     shared_all = lax.all_gather(shared_local, "dp", axis=0, tiled=True)
+    shared_all, send_both = lax.optimization_barrier((shared_all, send_both))
     gate_shared = shared_all[:, :shared_cols]
     up_shared = shared_all[:, shared_cols : 2 * shared_cols]
     down_shared_t = shared_all[:, 2 * shared_cols :]
@@ -473,7 +474,6 @@
     feed_own = lax.psum_scatter(feed_part, "tensor", scatter_dimension=0, tiled=True).astype(
         jnp.float32
     )
-    output = (residual_own + feed_own).astype(jnp.bfloat16)
     reduced_back = lax.psum(
         jnp.concatenate([back_part, gate_cols.astype(jnp.bfloat16)], 1), "tensor"
     ).astype(jnp.float32)
@@ -556,6 +556,7 @@
         )
     query_grads = jnp.concatenate(query_grad_list, 0).reshape(seq_len, head_count * (DN + DR))
     feed_own, shared_pack, query_grads = lax.optimization_barrier((feed_own, shared_pack, query_grads))
+    output = (residual_own + feed_own).astype(jnp.bfloat16)
     query_grad_w = jnp.dot(normed_all.T, query_grads, preferred_element_type=jnp.float32)
     normed_grad_part = jnp.dot(query_grads, query_weights.T, preferred_element_type=jnp.float32)
     expand_grads = jnp.concatenate(

time: 1720 us -> 1720 us (level)
    all_gather x1, waiting for transfers between devices: 231 us -> 0.02 us  [shards(): shared_all = lax.all_gather(shared_local, 'dp', axis=0, tiled=True)]
    all_to_all x1, waiting for transfers between devices: 24 us -> 245 us  [shards(): lax.all_to_all(jnp.concatenate([expert_out.astype(jnp.bfloat16), row_grad...]
    reduce_scatter x1, waiting for transfers between devices: 61 us -> 33.8 us  [shards(): lax.psum_scatter(jnp.concatenate([attn_grads_in, small_flat], 1), 'dp', s...]
    unnamed x12, waiting for transfers between devices: 83.2 us -> 102 us
    psum x1, waiting for transfers between devices: 103 us -> 84.9 us  [shards(): lax.psum(jnp.concatenate([back_part, gate_cols.astype(jnp.bfloat16)], 1),...]
  transfers between devices with their start and end apart: 12 -> 12, of which waited for: 11 -> 10; matrix products, arithmetic and copies ran while one was open for 14% -> 17% of each run, Pallas kernels for 0% -> 3%
where the time goes in v5:
time: 1720 us; the launch traced here: 1700 us
  waiting for transfers between devices  815 us (47%)
  blocking collectives  236 us (14%)
  local copies, waits for them, and re-layouts  235 us (14%)
  matrix products  187 us (11%)
  other arithmetic  113 us (7%)
  Pallas kernels  86.9 us (5%)
    all_to_all x1, waiting for transfers between devices, shards(): lax.all_to_all(jnp.concatenate([expert_out.astype(jnp.bfloat16), row_grad...  245 us
    all_to_all x1, blocking collectives, shards(): lax.all_to_all(send_both, 'dp', split_axis=0, concat_axis=0, tiled=True)  236 us
    psum x1, waiting for transfers between devices, shards(): lax.psum(attn_part.astype(jnp.bfloat16), 'tensor').astype(jnp.float32)  108 us
    unnamed x12, waiting for transfers between devices  102 us
    psum x1, waiting for transfers between devices, shards(): lax.psum(jnp.concatenate([normed_grad_part, latent_grad_part], 1).astype(...  97 us
    psum x1, waiting for transfers between devices, shards(): lax.psum(jnp.concatenate([back_part, gate_cols.astype(jnp.bfloat16)], 1),...  84.9 us
    unnamed x219, local copies, waits for them, and re-layouts  59.1 us
    all_to_all x1, waiting for transfers between devices, shards(): lax.all_to_all(jnp.broadcast_to(out_grad[None], (tensor_size,) + out_grad...  53.9 us
  transfers between devices with their start and end apart: 12, of which 10 were waited for; matrix products, arithmetic and copies ran while one was open for 17% of the time, Pallas kernels for 3%

profile of v5, /device:TPU:0, one launch (start us, length us, event | category | flops | bytes accessed | tf_op | source)
XLA Modules:
  0.0 1703.1 jit_solution(10224404132323398004)
XLA Ops:
  20.1 7.8 all-to-all-start
  30.6 53.9 %all-to-all-done = bf16[8,128,2048]{1,2,0:T(8,128)(2,1)} async-done(((bf16[8,128,2048]{1,2,0:T(8,128)(2,1)}), bf16[8,128,2048]{1,2,0:T(8,128)(2,1)}, u32[]{:S(2)}, u32[]{:S(2)}) %all-to-all-start) | async-done | bytes 4194336 | tf_op jit(solution)/shard_map/all_to_all | solution.py:292
  89.4 46.8 %all-gather.5.cloned.1.call-done = bf16[1024,2048]{0,1:T(8,128)(2,1)} async-done(((bf16[128,2048]{0,1:T(8,128)(2,1)}), bf16[1024,2048]{0,1:T(8,128)(2,1)}) %all-gather.5.cloned.1.call-update) | async-done | bytes 4194320 | tf_op jit(solution)/shard_map/all_gather | solution.py:291
  139.3 44.1 %all-gather.7.cloned.1.call-done = bf16[2048,1090]{0,1:T(8,128)(2,1)} async-done(((bf16[128,1090]{0,1:T(8,128)(2,1)}), bf16[2048,1090]{0,1:T(8,128)(2,1)}) %all-gather.7.cloned.1.call-update) | async-done | bytes 4464656 | tf_op jit(solution)/shard_map/all_gather | solution.py:272
  232.7 107.9 %all-reduce.7.cloned.1.call-done = bf16[1024,2048]{0,1:T(8,128)(2,1)} async-done(((bf16[1024,2048]{0,1:T(8,128)(2,1)}), bf16[1024,2048]{0,1:T(8,128)(2,1)}) %all-reduce.7.cloned.1.call-update) | async-done | bytes 4194320 | tf_op jit(solution)/shard_map/psum | solution.py:363
  350.5 8.1 scatter_custom_fusion.tok_ref
  371.4 7.8 pad_maximum_fusion.1
  379.2 12.6 copy.224.both_hbm
  396.8 8.1 scatter_custom_fusion.1
  412.1 50.5 %shard_map.297 = bf16[2560,32,128]{2,1,0:T(8,128)(2,1)} custom-call(s32[2560]{0:T(1024)} %copy-done.62, bf16[1024,32,128]{2,1,0:T(8,128)(2,1)} %copy.224.both_hbm, f32[2,2560,1,128]{3,2,1,0:T(1,128)} %broadcast_in_dim.76.col_ref), custom_call_target="tpu_custom_call" | custom-call | flops 5242880 | bytes 41943040 | tf_op jit(solution)/shard_map/pallas_call | solution.py:120
  462.6 236.3 %all_to_all.15 = bf16[16,4,40,32,128]{4,3,2,1,0:T(8,128)(2,1)} all-to-all(bf16[16,4,40,32,128]{4,3,2,1,0:T(8,128)(2,1)} %bitcast.250), channel_id=1, replica_groups=mesh['dp'=16,'tensor'=8] {'dp'}, dimensions={0} | all-to-all | bytes 41943040 | tf_op jit(solution)/shard_map/all_to_all | solution.py:399
  699.0 31.3 %reshape.522 = bf16[16,4,40,4096]{3,2,1,0:T(8,128)(2,1)} reshape(bf16[16,4,40,32,128]{4,3,2,1,0:T(8,128)(2,1)} %all_to_all.15) | data formatting | bytes 41943040 | tf_op jit(solution)/shard_map/reshape | solution.py:400
  730.2 17.2 %fusion.164 = (bf16[16,4,40,2048]{3,2,1,0:T(8,128)(2,1)}, bf16[16,4,40,2048]{3,2,1,0:T(8,128)(2,1)}) fusion(bf16[16,4,40,4096]{3,2,1,0:T(8,128)(2,1)} %reshape.522), kind=kLoop, calls=%fused_computation.287 | loop fusion | bytes 41943040 | tf_op jit(solution)/shard_map/slice | solution.py:401
  747.4 8.8 fusion.12
  756.2 8.7 fusion.4
  764.9 11.4 fusion.43
  776.3 12.5 fusion.33
  794.2 12.3 fusion.1
  806.5 10.4 pad_maximum_fusion
  824.4 19.0 %copy.178 = bf16[16,4,40,32,128]{4,3,2,1,0:T(8,128)(2,1)} copy(bf16[16,4,40,32,128]{4,3,2,0,1:T(8,128)(2,1)} %bitcast.252) | data formatting | bytes 41943040 | tf_op jit(solution)/shard_map/reshape | solution.py:434
  884.7 244.8 %all-to-all-done.2 = bf16[16,4,40,32,128]{4,3,2,1,0:T(8,128)(2,1)} async-done(((bf16[16,4,40,32,128]{4,3,2,1,0:T(8,128)(2,1)}), bf16[16,4,40,32,128]{4,3,2,1,0:T(8,128)(2,1)}, u32[]{:S(2)}, u32[]{:S(2)}) %all-to-all-start.2) | async-done | bytes 20971552 | tf_op jit(solution)/shard_map/all_to_all | solution.py:431
  1133.1 36.4 %shard_map.298 = (bf16[1024,16,128]{2,1,0:T(8,128)(2,1)}, bf16[1024,16,128]{2,1,0:T(8,128)(2,1)}, f32[1024,1,128]{2,1,0:T(1,128)}) custom-call(s32[2048]{0:T(1024)} %multiply_add_fusion.slot_ref, bf16[2560,32,128]{2,1,0:T(8,128)(2,1)} %bitcast.36.table_hbm, f32[2,1024,1,128]{3,2,1,0:T(1,128)} %broadcast_in_dim.77.gate_ref, ...), custom_call_target="tpu_custom_call" | custom-call | flops 33554432 | bytes 46137344 | tf_op jit(solution)/shard_map/pallas_call | solution.py:191
  1206.2 84.9 %all-reduce.9.cloned.1.call-done = bf16[1024,2050]{0,1:T(8,128)(2,1)} async-done(((bf16[1024,2050]{0,1:T(8,128)(2,1)}), bf16[1024,2050]{0,1:T(8,128)(2,1)}) %all-reduce.9.cloned.1.call-update) | async-done | bytes 4198416 | tf_op jit(solution)/shard_map/psum | solution.py:477
  1297.7 10.8 multiply_reduce_fusion
  1310.5 7.9 fusion.163
  1344.7 34.2 %reduce-scatter.10.cloned.1.call-done = bf16[128,2048]{1,0:T(8,128)(2,1)} async-done(((bf16[1024,2048]{1,0:T(8,128)(2,1)}), bf16[128,2048]{1,0:T(8,128)(2,1)}) %reduce-scatter.10.cloned.1.call-update) | async-done | bytes 524304
  1381.2 67.2 %reduce-scatter.12.cloned.1.call-done = bf16[128,1056]{1,0:T(8,128)(2,1)} async-done(((bf16[2048,1056]{1,0:T(8,128)(2,1)}), bf16[128,1056]{1,0:T(8,128)(2,1)}) %reduce-scatter.12.cloned.1.call-update) | async-done | bytes 270352
  1454.2 10.5 pad_maximum_fusion.3
  1495.6 97.0 %all-reduce.11.cloned.1.call-done = bf16[1024,2624]{0,1:T(8,128)(2,1)} async-done(((bf16[1024,2624]{0,1:T(8,128)(2,1)}), bf16[1024,2624]{0,1:T(8,128)(2,1)}) %all-reduce.11.cloned.1.call-update) | async-done | bytes 5373968 | tf_op jit(solution)/shard_map/psum | solution.py:578
  1618.9 9.1 fusion.20
  1628.0 9.3 fusion.23
  1653.4 33.8 %reduce-scatter.8.cloned.1.call-done = f32[128,849]{0,1:T(8,128)} async-done(((f32[2048,849]{0,1:T(8,128)}), f32[128,849]{0,1:T(8,128)}) %reduce-scatter.8.cloned.1.call-update) | async-done | bytes 434704 | tf_op jit(solution)/shard_map/reduce_scatter | solution.py:635
  (419 shorter events, 325.3 us)
Async XLA Ops:
  7.2 757.7 %copy-start = (bf16[4,176,2048]{2,1,0:T(8,128)(2,1)S(1)}, bf16[4,176,2048]{2,1,0:T(8,128)(2,1)}, u32[]{:S(2)}) copy-start(bf16[4,176,2048]{2,1,0:T(8,128)(2,1)} %param.30) | copy-start | bytes 8650756
  7.2 128.9 %all-gather.5.cloned.1.call-start = ((), (), s32[]{:S(2)}) async-start(), calls=%async_computation.6 | async-start | bytes 4718592 | tf_op jit(solution)/shard_map/all_gather | solution.py:291
  9.5 173.9 %all-gather.7.cloned.1.call-start = ((), (), s32[]{:S(2)}) async-start(), calls=%async_computation.7 | async-start | bytes 4769792 | tf_op jit(solution)/shard_map/all_gather | solution.py:272
  20.1 64.5 %all-to-all-start = ((bf16[8,128,2048]{1,2,0:T(8,128)(2,1)}), bf16[8,128,2048]{1,2,0:T(8,128)(2,1)}, u32[]{:S(2)}, u32[]{:S(2)}) async-start(bf16[8,128,2048]{1,2,0:T(8,128)(2,1)} %broadcast_in_dim.62), calls=%async_computation | async-start | bytes 8388608 | tf_op jit(solution)/shard_map/all_to_all | solution.py:292
  27.9 198.1 %all-gather.9.cloned.1.call-start = ((), (), s32[]{:S(2)}) async-start(), calls=%async_computation.8 | async-start | bytes 1427456 | tf_op jit(solution)/shard_map/all_gather | solution.py:285
  28.7 311.9 %all-reduce.7.cloned.1.call-start = ((), (), s32[]{:S(2)}) async-start(), calls=%async_computation.9 | async-start | bytes 8388608 | tf_op jit(solution)/shard_map/psum | solution.py:363
  29.4 186.1 %copy-start.92 = (f32[32]{0:T(128)}, f32[32]{0:T(128)S(1)}, u32[]{:S(2)}) copy-start(f32[32]{0:T(128)S(1)} %multiply_power_fusion) | copy-start | bytes 388
  29.4 186.1 %copy-start.73 = (f32[1024]{0:T(1024)}, f32[1024]{0:T(1024)S(1)}, u32[]{:S(2)}) copy-start(f32[1024]{0:T(1024)S(1)} %iota_convert_fusion) | copy-start | bytes 12292
  139.3 55.9 %copy-start.71 = (f32[1024]{0:T(1024)}, f32[1024]{0:T(1024)S(1)}, u32[]{:S(2)}) copy-start(f32[1024]{0:T(1024)S(1)} %add_rsqrt_fusion.2) | copy-start | bytes 12292
  192.4 16.8 copy-start.79
  230.8 231.9 %all-gather.11.cloned.1.call-start = ((), (), s32[]{:S(2)}) async-start(), calls=%async_computation.10 | async-start | bytes 4595712 | tf_op jit(solution)/shard_map/all_gather | solution.py:394
  232.7 114.5 %copy-start.58 = (s32[1024,2]{0,1:T(2,128)S(1)}, s32[1024,2]{0,1:T(2,128)}, u32[]{:S(2)}) copy-start(s32[1024,2]{0,1:T(2,128)} %param.19) | copy-start | bytes 24580
  730.2 17.2 %copy-start.26 = (bf16[4,176,2048]{2,1,0:T(8,128)(2,1)S(1)}, bf16[4,176,2048]{2,1,0:T(8,128)(2,1)}, u32[]{:S(2)}) copy-start(bf16[4,176,2048]{2,1,0:T(8,128)(2,1)} %param.29) | copy-start | bytes 8650756
  843.4 286.1 %all-to-all-start.2 = ((bf16[16,4,40,32,128]{4,3,2,1,0:T(8,128)(2,1)}), bf16[16,4,40,32,128]{4,3,2,1,0:T(8,128)(2,1)}, u32[]{:S(2)}, u32[]{:S(2)}) async-start(bf16[16,4,40,32,128]{4,3,2,1,0:T(8,128)(2,1)} %copy.178), calls=%async_computation.2 | async-start | bytes 41943040 | tf_op jit(solution)/shard_map/all_to_all | solution.py:431
  848.9 442.1 %all-reduce.9.cloned.1.call-start = ((), (), s32[]{:S(2)}) async-start(), calls=%async_computation.11 | async-start | bytes 8421376 | tf_op jit(solution)/shard_map/psum | solution.py:477
  849.6 14.6 slice-start.5
  1182.7 196.2 %reduce-scatter.10.cloned.1.call-start = ((), (), s32[]{:S(2)}) async-start(), calls=%async_computation.14 | async-start | bytes 4718592
  1196.1 252.4 %reduce-scatter.12.cloned.1.call-start = ((), (), s32[]{:S(2)}) async-start(), calls=%async_computation.15 | async-start | bytes 5013504
  1206.1 91.4 %copy-start.59 = (s32[1024,2]{0,1:T(2,128)S(1)}, s32[1024,2]{0,1:T(2,128)}, u32[]{:S(2)}) copy-start(s32[1024,2]{0,1:T(2,128)} %param.19) | copy-start | bytes 24580
  1206.1 91.5 %copy-start.34 = (bf16[2048,321]{0,1:T(8,128)(2,1)S(1)}, bf16[2048,321]{0,1:T(8,128)(2,1)}, u32[]{:S(2)}) copy-start(bf16[2048,321]{0,1:T(8,128)(2,1)} %all-gather.9.cloned.1.call-done) | copy-start | bytes 3944452
  1206.1 91.5 %copy-start.61 = (f32[2048,1]{0,1:T(1,128)S(1)}, f32[2048,1]{0,1:T(1,128)}, u32[]{:S(2)}) copy-start(f32[2048,1]{0,1:T(1,128)} %copy-done.60) | copy-start | bytes 24580
  1297.7 12.8 copy-start.8
  1297.7 12.8 copy-start.67
  1297.7 12.8 copy-start.85
  1324.9 267.7 %all-reduce.11.cloned.1.call-start = ((), (), s32[]{:S(2)}) async-start(), calls=%async_computation.12 | async-start | bytes 10747904 | tf_op jit(solution)/shard_map/psum | solution.py:578
  1343.9 106.5 %copy-start.48 = (bf16[1024,384]{0,1:T(8,128)(2,1)S(1)}, bf16[1024,384]{0,1:T(8,128)(2,1)}, u32[]{:S(2)}) copy-start(bf16[1024,384]{0,1:T(8,128)(2,1)} %pad_maximum_fusion.8) | copy-start | bytes 2359300
  1464.7 222.5 %reduce-scatter.8.cloned.1.call-start = ((), (), s32[]{:S(2)}) async-start(), calls=%async_computation.13 | async-start | bytes 7450624 | tf_op jit(solution)/shard_map/reduce_scatter | solution.py:635
  1495.6 100.8 %copy-start.74 = (f32[1024]{0:T(1024)S(1)}, f32[1024]{0:T(1024)}, u32[]{:S(2)}) copy-start(f32[1024]{0:T(1024)} %copy-done.73) | copy-start | bytes 12292
  1495.6 100.8 %copy-start.93 = (f32[32]{0:T(128)S(1)}, f32[32]{0:T(128)}, u32[]{:S(2)}) copy-start(f32[32]{0:T(128)} %copy-done.92) | copy-start | bytes 388
  1618.9 18.4 %slice-start.2 = ((s8[10485760]{0:T(1024)(128)(4,1)}), s8[4194304]{0:T(1024)(128)(4,1)S(1)}, s32[]{:S(2)}) async-start(s8[10485760]{0:T(1024)(128)(4,1)} %bitcast.262), calls=%async_computation.18 | async-start | bytes 8388608
  1618.9 18.4 %slice-start.3 = ((s8[10485760]{0:T(1024)(128)(4,1)}), s8[4194304]{0:T(1024)(128)(4,1)S(1)}, s32[]{:S(2)}) async-start(s8[10485760]{0:T(1024)(128)(4,1)} %bitcast.262), calls=%async_computation.19 | async-start | bytes 8388608
  1645.5 50.5 %copy-start.1 = (bf16[4,176,2048]{2,1,0:T(8,128)(2,1)S(1)}, bf16[4,176,2048]{2,1,0:T(8,128)(2,1)}, u32[]{:S(2)}) copy-start(bf16[4,176,2048]{2,1,0:T(8,128)(2,1)} %param.30) | copy-start | bytes 8650756
  (82 other events, 371.0 us)
Sparse Core Ops, SparseCore 0:
  10.8 125.3 all-gather.4
  138.3 44.9 all-gather.6
  185.5 35.0 all-gather.8
  230.9 109.6 all-reduce.6
  347.3 44.1 all-gather.10
  1182.8 108.1 all-reduce.8
  1294.9 83.9 reduce-scatter.9
  1381.9 66.4 reduce-scatter.11
  1464.8 127.7 all-reduce.10
  1617.7 69.4 reduce-scatter.7

commit v6 on v5

--- a/solution.py
+++ b/solution.py
@@ -471,8 +471,11 @@
         shared_back,
     )
     gate_part = gate_cols[:, :top_count]
-    feed_own = lax.psum_scatter(feed_part, "tensor", scatter_dimension=0, tiled=True).astype(
-        jnp.float32
+    feed_own = jnp.sum(
+        lax.all_to_all(
+            feed_part.reshape(tensor_size, tok_dev, D), "tensor", split_axis=0, concat_axis=0, tiled=True
+        ).astype(jnp.float32),
+        0,
     )
     reduced_back = lax.psum(
         jnp.concatenate([back_part, gate_cols.astype(jnp.bfloat16)], 1), "tensor"
@@ -488,9 +491,16 @@
     residual_grad = grad_seq_f + norm_back(residual_all, scale_two, gain_two, normed_two_grad)
     branch_grad = residual_grad.astype(jnp.bfloat16)
     shared_grads_in, branch_grad = lax.optimization_barrier((shared_grads_in, branch_grad))
-    shared_pack = lax.psum_scatter(
-        shared_grads_in, "dp", scatter_dimension=0, tiled=True
-    ).astype(jnp.float32)
+    shared_pack = jnp.sum(
+        lax.all_to_all(
+            shared_grads_in.reshape(dp_size, rows_dp, shared_grads_in.shape[1]),
+            "dp",
+            split_axis=0,
+            concat_axis=0,
+            tiled=True,
+        ).astype(jnp.float32),
+        0,
+    )
     output_grad_w_t = jnp.dot(branch_grad.T, mixed_all, preferred_element_type=jnp.float32)
     mixed_grad = (
         jnp.dot(branch_grad, output_weights_t, preferred_element_type=jnp.float32)

time: 1720 us -> 1720 us (level)
    all_to_all x0 -> x2, waiting for transfers between devices: none -> 102 us  [the longest x1 63.3 us: shards(): lax.all_to_all(feed_part.reshape(tensor_size, tok_dev, D), 'tensor', spli...]
    unnamed x12 -> x8, waiting for transfers between devices: 102 us -> 0.13 us
    unnamed x219 -> x221, local copies, waits for them, and re-layouts: 59.1 us -> 43.4 us
  transfers between devices with their start and end apart: 12 -> 12, of which waited for: 10 -> 10; matrix products, arithmetic and copies ran while one was open for 17% -> 16% of each run, Pallas kernels for 3% -> 3%
where the time goes in v6:
time: 1720 us; the launch traced here: 1700 us
  waiting for transfers between devices  812 us (47%)
  blocking collectives  236 us (14%)
  local copies, waits for them, and re-layouts  222 us (13%)
  matrix products  186 us (11%)
  other arithmetic  119 us (7%)
  Pallas kernels  86.9 us (5%)
  starting transfers between devices  23.3 us (1%)
    all_to_all x1, waiting for transfers between devices, shards(): lax.all_to_all(jnp.concatenate([expert_out.astype(jnp.bfloat16), row_grad...  245 us
    all_to_all x1, blocking collectives, shards(): lax.all_to_all(send_both, 'dp', split_axis=0, concat_axis=0, tiled=True)  236 us
    psum x1, waiting for transfers between devices, shards(): lax.psum(attn_part.astype(jnp.bfloat16), 'tensor').astype(jnp.float32)  108 us
    psum x1, waiting for transfers between devices, shards(): lax.psum(jnp.concatenate([normed_grad_part, latent_grad_part], 1).astype(...  98 us
    psum x1, waiting for transfers between devices, shards(): lax.psum(jnp.concatenate([back_part, gate_cols.astype(jnp.bfloat16)], 1),...  81 us
    all_to_all x1, waiting for transfers between devices, shards(): lax.all_to_all(feed_part.reshape(tensor_size, tok_dev, D), 'tensor', spli...  63.3 us
    all_to_all x1, waiting for transfers between devices, shards(): lax.all_to_all(jnp.broadcast_to(out_grad[None], (tensor_size,) + out_grad...  53.9 us
    pallas_call x1, Pallas kernels, dispatch_rows(): pl.pallas_call(dispatch_kernel, out_shape=jax.ShapeDtypeStruct((slots, 2...  50.5 us
  transfers between devices with their start and end apart: 12, of which 10 were waited for; matrix products, arithmetic and copies ran while one was open for 16% of the time, Pallas kernels for 3%

profile of v6, /device:TPU:0, one launch (start us, length us, event | category | flops | bytes accessed | tf_op | source)
XLA Modules:
  0.0 1702.6 jit_solution(12561806740869269672)
XLA Ops:
  20.1 7.8 all-to-all-start
  30.6 53.9 %all-to-all-done = bf16[8,128,2048]{1,2,0:T(8,128)(2,1)} async-done(((bf16[8,128,2048]{1,2,0:T(8,128)(2,1)}), bf16[8,128,2048]{1,2,0:T(8,128)(2,1)}, u32[]{:S(2)}, u32[]{:S(2)}) %all-to-all-start) | async-done | bytes 4194336 | tf_op jit(solution)/shard_map/all_to_all | solution.py:292
  89.4 46.8 %all-gather.5.cloned.1.call-done = bf16[1024,2048]{0,1:T(8,128)(2,1)} async-done(((bf16[128,2048]{0,1:T(8,128)(2,1)}), bf16[1024,2048]{0,1:T(8,128)(2,1)}) %all-gather.5.cloned.1.call-update) | async-done | bytes 4194320 | tf_op jit(solution)/shard_map/all_gather | solution.py:291
  139.3 44.1 %all-gather.7.cloned.1.call-done = bf16[2048,1090]{0,1:T(8,128)(2,1)} async-done(((bf16[128,1090]{0,1:T(8,128)(2,1)}), bf16[2048,1090]{0,1:T(8,128)(2,1)}) %all-gather.7.cloned.1.call-update) | async-done | bytes 4464656 | tf_op jit(solution)/shard_map/all_gather | solution.py:272
  232.4 108.2 %all-reduce.7.cloned.1.call-done = bf16[1024,2048]{0,1:T(8,128)(2,1)} async-done(((bf16[1024,2048]{0,1:T(8,128)(2,1)}), bf16[1024,2048]{0,1:T(8,128)(2,1)}) %all-reduce.7.cloned.1.call-update) | async-done | bytes 4194320 | tf_op jit(solution)/shard_map/psum | solution.py:363
  350.6 8.1 scatter_custom_fusion.tok_ref
  371.5 7.8 pad_maximum_fusion.1
  379.3 12.6 copy.224.both_hbm
  396.8 8.1 scatter_custom_fusion.1
  412.2 50.5 %shard_map.297 = bf16[2560,32,128]{2,1,0:T(8,128)(2,1)} custom-call(s32[2560]{0:T(1024)} %copy-done.63, bf16[1024,32,128]{2,1,0:T(8,128)(2,1)} %copy.224.both_hbm, f32[2,2560,1,128]{3,2,1,0:T(1,128)} %broadcast_in_dim.76.col_ref), custom_call_target="tpu_custom_call" | custom-call | flops 5242880 | bytes 41943040 | tf_op jit(solution)/shard_map/pallas_call | solution.py:120
  462.8 236.3 %all_to_all.25 = bf16[16,4,40,32,128]{4,3,2,1,0:T(8,128)(2,1)} all-to-all(bf16[16,4,40,32,128]{4,3,2,1,0:T(8,128)(2,1)} %bitcast.252), channel_id=1, replica_groups=mesh['dp'=16,'tensor'=8] {'dp'}, dimensions={0} | all-to-all | bytes 41943040 | tf_op jit(solution)/shard_map/all_to_all | solution.py:399
  699.1 31.3 %reshape.522 = bf16[16,4,40,4096]{3,2,1,0:T(8,128)(2,1)} reshape(bf16[16,4,40,32,128]{4,3,2,1,0:T(8,128)(2,1)} %all_to_all.25) | data formatting | bytes 41943040 | tf_op jit(solution)/shard_map/reshape | solution.py:400
  730.4 17.1 %fusion.164 = (bf16[16,4,40,2048]{3,2,1,0:T(8,128)(2,1)}, bf16[16,4,40,2048]{3,2,1,0:T(8,128)(2,1)}) fusion(bf16[16,4,40,4096]{3,2,1,0:T(8,128)(2,1)} %reshape.522), kind=kLoop, calls=%fused_computation.290 | loop fusion | bytes 41943040 | tf_op jit(solution)/shard_map/slice | solution.py:401
  747.5 8.8 fusion.12
  756.4 8.7 fusion.4
  765.0 11.3 fusion.43
  776.4 12.4 fusion.33
  794.3 12.3 fusion.1
  806.5 10.4 pad_maximum_fusion
  824.4 19.0 %copy.177 = bf16[16,4,40,32,128]{4,3,2,1,0:T(8,128)(2,1)} copy(bf16[16,4,40,32,128]{4,3,2,0,1:T(8,128)(2,1)} %bitcast.254) | data formatting | bytes 41943040 | tf_op jit(solution)/shard_map/reshape | solution.py:434
  884.8 244.8 %all-to-all-done.2 = bf16[16,4,40,32,128]{4,3,2,1,0:T(8,128)(2,1)} async-done(((bf16[16,4,40,32,128]{4,3,2,1,0:T(8,128)(2,1)}), bf16[16,4,40,32,128]{4,3,2,1,0:T(8,128)(2,1)}, u32[]{:S(2)}, u32[]{:S(2)}) %all-to-all-start.2) | async-done | bytes 20971552 | tf_op jit(solution)/shard_map/all_to_all | solution.py:431
  1133.1 36.4 %shard_map.298 = (bf16[1024,16,128]{2,1,0:T(8,128)(2,1)}, bf16[1024,16,128]{2,1,0:T(8,128)(2,1)}, f32[1024,1,128]{2,1,0:T(1,128)}) custom-call(s32[2048]{0:T(1024)} %multiply_add_fusion.slot_ref, bf16[2560,32,128]{2,1,0:T(8,128)(2,1)} %bitcast.36.table_hbm, f32[2,1024,1,128]{3,2,1,0:T(1,128)} %broadcast_in_dim.77.gate_ref, ...), custom_call_target="tpu_custom_call" | custom-call | flops 33554432 | bytes 46137344 | tf_op jit(solution)/shard_map/pallas_call | solution.py:191
  1204.8 63.3 %all-to-all-done.3 = bf16[8,128,2048]{2,1,0:T(8,128)(2,1)} async-done(((bf16[8,128,2048]{2,1,0:T(8,128)(2,1)}), bf16[8,128,2048]{2,1,0:T(8,128)(2,1)}, u32[]{:S(2)}, u32[]{:S(2)}) %all-to-all-start.3) | async-done | bytes 4194336 | tf_op jit(solution)/shard_map/all_to_all | solution.py:475
  1272.2 81.0 %all-reduce.9.cloned.1.call-done = bf16[1024,2050]{0,1:T(8,128)(2,1)} async-done(((bf16[1024,2050]{0,1:T(8,128)(2,1)}), bf16[1024,2050]{0,1:T(8,128)(2,1)}) %all-reduce.9.cloned.1.call-update) | async-done | bytes 4198416 | tf_op jit(solution)/shard_map/psum | solution.py:480
  1359.9 10.5 multiply_reduce_fusion
  1372.3 8.1 fusion.163
  1407.4 38.4 %all-to-all-done.4 = bf16[16,128,1056]{1,2,0:T(8,128)(2,1)} async-done(((bf16[16,128,1056]{1,2,0:T(8,128)(2,1)}), bf16[16,128,1056]{1,2,0:T(8,128)(2,1)}, u32[]{:S(2)}, u32[]{:S(2)}) %all-to-all-start.4) | async-done | bytes 4325408 | tf_op jit(solution)/shard_map/all_to_all | solution.py:495
  1453.2 10.7 pad_maximum_fusion.3
  1494.2 98.0 %all-reduce.11.cloned.1.call-done = bf16[1024,2624]{0,1:T(8,128)(2,1)} async-done(((bf16[1024,2624]{0,1:T(8,128)(2,1)}), bf16[1024,2624]{0,1:T(8,128)(2,1)}) %all-reduce.11.cloned.1.call-update) | async-done | bytes 5373968 | tf_op jit(solution)/shard_map/psum | solution.py:588
  1618.4 9.1 fusion.20
  1627.5 9.3 fusion.23
  1653.3 33.5 %reduce-scatter.2.cloned.1.call-done = f32[128,849]{0,1:T(8,128)} async-done(((f32[2048,849]{0,1:T(8,128)}), f32[128,849]{0,1:T(8,128)}) %reduce-scatter.2.cloned.1.call-update) | async-done | bytes 434704 | tf_op jit(solution)/shard_map/reduce_scatter | solution.py:645
  (422 shorter events, 327.5 us)
Async XLA Ops:
  7.2 757.8 %copy-start = (bf16[4,176,2048]{2,1,0:T(8,128)(2,1)S(1)}, bf16[4,176,2048]{2,1,0:T(8,128)(2,1)}, u32[]{:S(2)}) copy-start(bf16[4,176,2048]{2,1,0:T(8,128)(2,1)} %param.30) | copy-start | bytes 8650756
  7.2 128.9 %all-gather.5.cloned.1.call-start = ((), (), s32[]{:S(2)}) async-start(), calls=%async_computation.6 | async-start | bytes 4718592 | tf_op jit(solution)/shard_map/all_gather | solution.py:291
  9.5 173.9 %all-gather.7.cloned.1.call-start = ((), (), s32[]{:S(2)}) async-start(), calls=%async_computation.7 | async-start | bytes 4769792 | tf_op jit(solution)/shard_map/all_gather | solution.py:272
  20.1 64.5 %all-to-all-start = ((bf16[8,128,2048]{1,2,0:T(8,128)(2,1)}), bf16[8,128,2048]{1,2,0:T(8,128)(2,1)}, u32[]{:S(2)}, u32[]{:S(2)}) async-start(bf16[8,128,2048]{1,2,0:T(8,128)(2,1)} %broadcast_in_dim.62), calls=%async_computation | async-start | bytes 8388608 | tf_op jit(solution)/shard_map/all_to_all | solution.py:292
  27.9 197.8 %all-gather.9.cloned.1.call-start = ((), (), s32[]{:S(2)}) async-start(), calls=%async_computation.8 | async-start | bytes 1427456 | tf_op jit(solution)/shard_map/all_gather | solution.py:285
  28.7 311.9 %all-reduce.7.cloned.1.call-start = ((), (), s32[]{:S(2)}) async-start(), calls=%async_computation.9 | async-start | bytes 8388608 | tf_op jit(solution)/shard_map/psum | solution.py:363
  29.4 185.9 %copy-start.93 = (f32[32]{0:T(128)}, f32[32]{0:T(128)S(1)}, u32[]{:S(2)}) copy-start(f32[32]{0:T(128)S(1)} %multiply_power_fusion) | copy-start | bytes 388
  29.4 185.8 %copy-start.74 = (f32[1024]{0:T(1024)}, f32[1024]{0:T(1024)S(1)}, u32[]{:S(2)}) copy-start(f32[1024]{0:T(1024)S(1)} %iota_convert_fusion) | copy-start | bytes 12292
  139.3 55.9 %copy-start.72 = (f32[1024]{0:T(1024)}, f32[1024]{0:T(1024)S(1)}, u32[]{:S(2)}) copy-start(f32[1024]{0:T(1024)S(1)} %add_rsqrt_fusion.2) | copy-start | bytes 12292
  192.4 16.6 copy-start.80
  211.6 12.8 copy-start.14
  230.5 232.3 %all-gather.11.cloned.1.call-start = ((), (), s32[]{:S(2)}) async-start(), calls=%async_computation.10 | async-start | bytes 4595712 | tf_op jit(solution)/shard_map/all_gather | solution.py:394
  232.4 114.8 %copy-start.59 = (s32[1024,2]{0,1:T(2,128)S(1)}, s32[1024,2]{0,1:T(2,128)}, u32[]{:S(2)}) copy-start(s32[1024,2]{0,1:T(2,128)} %param.19) | copy-start | bytes 24580
  730.4 17.1 %copy-start.27 = (bf16[4,176,2048]{2,1,0:T(8,128)(2,1)S(1)}, bf16[4,176,2048]{2,1,0:T(8,128)(2,1)}, u32[]{:S(2)}) copy-start(bf16[4,176,2048]{2,1,0:T(8,128)(2,1)} %param.29) | copy-start | bytes 8650756
  843.4 286.1 %all-to-all-start.2 = ((bf16[16,4,40,32,128]{4,3,2,1,0:T(8,128)(2,1)}), bf16[16,4,40,32,128]{4,3,2,1,0:T(8,128)(2,1)}, u32[]{:S(2)}, u32[]{:S(2)}) async-start(bf16[16,4,40,32,128]{4,3,2,1,0:T(8,128)(2,1)} %copy.177), calls=%async_computation.2 | async-start | bytes 41943040 | tf_op jit(solution)/shard_map/all_to_all | solution.py:431
  848.9 504.3 %all-reduce.9.cloned.1.call-start = ((), (), s32[]{:S(2)}) async-start(), calls=%async_computation.11 | async-start | bytes 8421376 | tf_op jit(solution)/shard_map/psum | solution.py:480
  849.6 14.6 slice-start.7
  1189.8 78.4 %all-to-all-start.3 = ((bf16[8,128,2048]{2,1,0:T(8,128)(2,1)}), bf16[8,128,2048]{2,1,0:T(8,128)(2,1)}, u32[]{:S(2)}, u32[]{:S(2)}) async-start(bf16[8,128,2048]{2,1,0:T(8,128)(2,1)} %reshape_reshape.3), calls=%async_computation.3 | async-start | bytes 8388608 | tf_op jit(solution)/shard_map/all_to_all | solution.py:475
  1272.2 87.6 %copy-start.60 = (s32[1024,2]{0,1:T(2,128)S(1)}, s32[1024,2]{0,1:T(2,128)}, u32[]{:S(2)}) copy-start(s32[1024,2]{0,1:T(2,128)} %param.19) | copy-start | bytes 24580
  1272.2 87.6 %copy-start.35 = (bf16[2048,321]{0,1:T(8,128)(2,1)S(1)}, bf16[2048,321]{0,1:T(8,128)(2,1)}, u32[]{:S(2)}) copy-start(bf16[2048,321]{0,1:T(8,128)(2,1)} %all-gather.9.cloned.1.call-done) | copy-start | bytes 3944452
  1272.2 87.6 %copy-start.62 = (f32[2048,1]{0,1:T(1,128)S(1)}, f32[2048,1]{0,1:T(1,128)}, u32[]{:S(2)}) copy-start(f32[2048,1]{0,1:T(1,128)} %copy-done.61) | copy-start | bytes 24580
  1359.8 12.5 copy-start.8
  1359.9 20.5 %slice-start.2 = ((s8[4325376]{0:T(1024)(128)(4,1)}), s8[4194304]{0:T(1024)(128)(4,1)S(1)}, s32[]{:S(2)}) async-start(s8[4325376]{0:T(1024)(128)(4,1)} %bitcast.261), calls=%async_computation.16 | async-start | bytes 8388608
  1383.2 62.6 %all-to-all-start.4 = ((bf16[16,128,1056]{1,2,0:T(8,128)(2,1)}), bf16[16,128,1056]{1,2,0:T(8,128)(2,1)}, u32[]{:S(2)}, u32[]{:S(2)}) async-start(bf16[16,128,1056]{1,2,0:T(8,128)(2,1)} %copy_bitcast_fusion), calls=%async_computation.4 | async-start | bytes 8650752 | tf_op jit(solution)/shard_map/all_to_all | solution.py:495
  1387.7 204.5 %all-reduce.11.cloned.1.call-start = ((), (), s32[]{:S(2)}) async-start(), calls=%async_computation.12 | async-start | bytes 10747904 | tf_op jit(solution)/shard_map/psum | solution.py:588
  1406.6 42.8 %copy-start.49 = (bf16[1024,384]{0,1:T(8,128)(2,1)S(1)}, bf16[1024,384]{0,1:T(8,128)(2,1)}, u32[]{:S(2)}) copy-start(bf16[1024,384]{0,1:T(8,128)(2,1)} %pad_maximum_fusion.8) | copy-start | bytes 2359300
  1463.9 222.9 %reduce-scatter.2.cloned.1.call-start = ((), (), s32[]{:S(2)}) async-start(), calls=%async_computation.13 | async-start | bytes 7450624 | tf_op jit(solution)/shard_map/reduce_scatter | solution.py:645
  1494.2 101.9 %copy-start.75 = (f32[1024]{0:T(1024)S(1)}, f32[1024]{0:T(1024)}, u32[]{:S(2)}) copy-start(f32[1024]{0:T(1024)} %copy-done.74) | copy-start | bytes 12292
  1494.2 101.9 %copy-start.94 = (f32[32]{0:T(128)S(1)}, f32[32]{0:T(128)}, u32[]{:S(2)}) copy-start(f32[32]{0:T(128)} %copy-done.93) | copy-start | bytes 388
  1618.4 18.4 %slice-start.4 = ((s8[10485760]{0:T(1024)(128)(4,1)}), s8[4194304]{0:T(1024)(128)(4,1)S(1)}, s32[]{:S(2)}) async-start(s8[10485760]{0:T(1024)(128)(4,1)} %bitcast.265), calls=%async_computation.18 | async-start | bytes 8388608
  1618.4 18.4 %slice-start.5 = ((s8[10485760]{0:T(1024)(128)(4,1)}), s8[4194304]{0:T(1024)(128)(4,1)S(1)}, s32[]{:S(2)}) async-start(s8[10485760]{0:T(1024)(128)(4,1)} %bitcast.265), calls=%async_computation.19 | async-start | bytes 8388608
  1645.3 50.2 %copy-start.1 = (bf16[4,176,2048]{2,1,0:T(8,128)(2,1)S(1)}, bf16[4,176,2048]{2,1,0:T(8,128)(2,1)}, u32[]{:S(2)}) copy-start(bf16[4,176,2048]{2,1,0:T(8,128)(2,1)} %param.30) | copy-start | bytes 8650756
  (85 other events, 411.8 us)
Sparse Core Ops, SparseCore 0:
  10.8 125.3 all-gather.4
  138.3 44.9 all-gather.6
  185.5 35.0 all-gather.8
  230.6 109.9 all-reduce.6
  347.3 44.0 all-gather.10
  1182.6 170.4 all-reduce.8
  1464.0 128.1 all-reduce.10
  1617.2 69.4 reduce-scatter.1

commit v7 on v6

--- a/solution.py
+++ b/solution.py
@@ -141,39 +141,40 @@
 
 
 def combine_kernel(
-    slot_ref, table_hbm, gate_ref, grad_ref, shared_out_ref, shared_back_ref,
-    feed_ref, back_ref, part_ref, picked, sems,
+    slot_ref, out_hbm, back_hbm, gate_ref, grad_ref, shared_out_ref, shared_back_ref,
+    feed_ref, back_ref, part_ref, picked_out, picked_back, sems,
 ):
-    top = picked.shape[0]
-    block = picked.shape[1]
-    tile_rows = grad_ref.shape[1]
-    last = table_hbm.shape[0] - 1
+    top = picked_out.shape[0]
+    block = picked_out.shape[1]
+    last = out_hbm.shape[0] - 1
     base = pl.program_id(0) * block
 
     def start(r, carry):
         for k in range(top):
             slot = jnp.clip(slot_ref[(base + r) * top + k], 0, last)
-            pltpu.make_async_copy(table_hbm.at[slot], picked.at[k, r], sems.at[k, r]).start()
+            pltpu.make_async_copy(out_hbm.at[slot], picked_out.at[k, r], sems.at[0, k, r]).start()
+            pltpu.make_async_copy(back_hbm.at[slot], picked_back.at[k, r], sems.at[1, k, r]).start()
         return carry
 
-    lax.fori_loop(0, block, start, 0)
+    lax.fori_loop(0, block, start, 0, unroll=2)
 
     def finish(r, carry):
         for k in range(top):
-            pltpu.make_async_copy(table_hbm.at[0], picked.at[k, r], sems.at[k, r]).wait()
+            pltpu.make_async_copy(out_hbm.at[0], picked_out.at[k, r], sems.at[0, k, r]).wait()
+            pltpu.make_async_copy(back_hbm.at[0], picked_back.at[k, r], sems.at[1, k, r]).wait()
         return carry
 
-    lax.fori_loop(0, block, finish, 0)
+    lax.fori_loop(0, block, finish, 0, unroll=2)
     grad = grad_ref[...].astype(jnp.float32)
     weighted = None
     backs = None
     lanes = lax.broadcasted_iota(jnp.int32, part_ref.shape, 2)
     parts = jnp.zeros(part_ref.shape, jnp.float32)
     for k in range(top):
-        out_k = picked[k, :, :tile_rows, :].astype(jnp.float32)
+        out_k = picked_out[k].astype(jnp.float32)
         term = gate_ref[k] * out_k
         weighted = term if weighted is None else weighted + term
-        back_k = picked[k, :, tile_rows:, :].astype(jnp.float32)
+        back_k = picked_back[k].astype(jnp.float32)
         backs = back_k if backs is None else backs + back_k
         dot_k = jnp.sum(jnp.sum(grad * out_k, 2, keepdims=True), 1, keepdims=True)
         parts = jnp.where(lanes == k, dot_k, parts)
@@ -182,7 +183,7 @@
     part_ref[...] = parts
 
 
-def combine_rows(slot_index, table, gate_values, grad, shared_out, shared_back, block=128):
+def combine_rows(slot_index, out_table, back_table, gate_values, grad, shared_out, shared_back, block=128):
     tokens, top = gate_values.shape
     width = grad.shape[1]
     tile_rows = width // 128
@@ -200,6 +201,7 @@
             grid=(tokens // block,),
             in_specs=[
                 pl.BlockSpec(memory_space=pl.ANY),
+                pl.BlockSpec(memory_space=pl.ANY),
                 pl.BlockSpec((top, block, 1, 128), lambda i, s: (0, i, 0, 0)),
                 row_spec,
                 row_spec,
@@ -207,8 +209,9 @@
             ],
             out_specs=[row_spec, row_spec, pl.BlockSpec((block, 1, 128), lambda i, s: (i, 0, 0))],
             scratch_shapes=[
-                pltpu.VMEM((top, block, 2 * tile_rows, 128), table.dtype),
-                pltpu.SemaphoreType.DMA((top, block)),
+                pltpu.VMEM((top, block, tile_rows, 128), out_table.dtype),
+                pltpu.VMEM((top, block, tile_rows, 128), back_table.dtype),
+                pltpu.SemaphoreType.DMA((2, top, block)),
             ],
         ),
         cost_estimate=pl.CostEstimate(
@@ -218,7 +221,8 @@
         ),
     )(
         slot_index.reshape(-1),
-        table.reshape(table.shape[0], 2 * tile_rows, 128),
+        out_table,
+        back_table,
         gates,
         grad.reshape(tokens, tile_rows, 128),
         shared_out.reshape(tokens, tile_rows, 128),
@@ -409,6 +413,13 @@
     expert_out = jnp.einsum(
         "sjcf,jfd->sjcd", expert_act, expert_down, preferred_element_type=jnp.float32
     )
+    back_out = lax.all_to_all(
+        expert_out.astype(jnp.bfloat16).reshape(dp_size, exp_dev, capacity, tile_rows, 128),
+        "dp",
+        split_axis=0,
+        concat_axis=0,
+        tiled=True,
+    )
     act_grad = jnp.einsum(
         "sjcd,jfd->sjcf", recv_grads, expert_down, preferred_element_type=jnp.float32
     )
@@ -428,10 +439,10 @@
     row_grads = row_grads + jnp.einsum(
         "sjcf,jfd->sjcd", up_low_grad, expert_up, preferred_element_type=jnp.float32
     )
-    back_both = lax.all_to_all(
-        jnp.concatenate(
-            [expert_out.astype(jnp.bfloat16), row_grads.astype(jnp.bfloat16)], -1
-        ).reshape(dp_size, exp_dev, capacity, 2 * tile_rows, 128),
+    grads_low = row_grads.astype(jnp.bfloat16).reshape(dp_size, exp_dev, capacity, tile_rows, 128)
+    back_out, grads_low = lax.optimization_barrier((back_out, grads_low))
+    back_grads = lax.all_to_all(
+        grads_low,
         "dp",
         split_axis=0,
         concat_axis=0,
@@ -464,7 +475,8 @@
     table_rows = experts * capacity
     feed_part, back_part, gate_cols = combine_rows(
         slot_index.reshape(seq_len, top_count),
-        back_both.reshape(table_rows, 2 * tile_rows, 128),
+        back_out.reshape(table_rows, tile_rows, 128),
+        back_grads.reshape(table_rows, tile_rows, 128),
         gate_values,
         grad_seq,
         shared_out,

time: 1720 us -> 1710 us (level)
  waiting for transfers between devices: 812 us -> 777 us
  local copies, waits for them, and re-layouts: 222 us -> 243 us
    all_to_all x1 -> x2, waiting for transfers between devices: 245 us -> 209 us  [the longest x1 105 us: shards(): lax.all_to_all(grads_low, 'dp', split_axis=0, concat_axis=0, tiled=True)]
    unnamed x221 -> x232, local copies, waits for them, and re-layouts: 43.4 us -> 61.9 us
  transfers between devices with their start and end apart: 12 -> 13, of which waited for: 10 -> 11; matrix products, arithmetic and copies ran while one was open for 16% -> 17% of each run, Pallas kernels for 3% -> 3%
where the time goes in v7:
time: 1710 us; the launch traced here: 1690 us
  waiting for transfers between devices  777 us (45%)
  local copies, waits for them, and re-layouts  243 us (14%)
  blocking collectives  237 us (14%)
  matrix products  187 us (11%)
  other arithmetic  107 us (6%)
  Pallas kernels  94.9 us (6%)
  starting transfers between devices  28.4 us (2%)
    all_to_all x1, blocking collectives, shards(): lax.all_to_all(send_both, 'dp', split_axis=0, concat_axis=0, tiled=True)  237 us
    psum x1, waiting for transfers between devices, shards(): lax.psum(attn_part.astype(jnp.bfloat16), 'tensor').astype(jnp.float32)  108 us
    all_to_all x1, waiting for transfers between devices, shards(): lax.all_to_all(grads_low, 'dp', split_axis=0, concat_axis=0, tiled=True)  105 us
    all_to_all x1, waiting for transfers between devices, shards(): lax.all_to_all(expert_out.astype(jnp.bfloat16).reshape(dp_size, exp_dev,...  104 us
    psum x1, waiting for transfers between devices, shards(): lax.psum(jnp.concatenate([normed_grad_part, latent_grad_part], 1).astype(...  99.3 us
    psum x1, waiting for transfers between devices, shards(): lax.psum(jnp.concatenate([back_part, gate_cols.astype(jnp.bfloat16)], 1),...  81 us
    all_to_all x1, waiting for transfers between devices, shards(): lax.all_to_all(feed_part.reshape(tensor_size, tok_dev, D), 'tensor', spli...  62.5 us
    unnamed x232, local copies, waits for them, and re-layouts  61.9 us
  transfers between devices with their start and end apart: 13, of which 11 were waited for; matrix products, arithmetic and copies ran while one was open for 17% of the time, Pallas kernels for 3%

profile of v7, /device:TPU:0, one launch (start us, length us, event | category | flops | bytes accessed | tf_op | source)
XLA Modules:
  0.0 1691.4 jit_solution(12609145417859870154)
XLA Ops:
  30.9 53.7 %all-to-all-done = bf16[8,128,2048]{1,2,0:T(8,128)(2,1)} async-done(((bf16[8,128,2048]{1,2,0:T(8,128)(2,1)}), bf16[8,128,2048]{1,2,0:T(8,128)(2,1)}, u32[]{:S(2)}, u32[]{:S(2)}) %all-to-all-start) | async-done | bytes 4194336 | tf_op jit(solution)/shard_map/all_to_all | solution.py:296
  89.4 46.8 %all-gather.5.cloned.1.call-done = bf16[1024,2048]{0,1:T(8,128)(2,1)} async-done(((bf16[128,2048]{0,1:T(8,128)(2,1)}), bf16[1024,2048]{0,1:T(8,128)(2,1)}) %all-gather.5.cloned.1.call-update) | async-done | bytes 4194320 | tf_op jit(solution)/shard_map/all_gather | solution.py:295
  139.3 44.1 %all-gather.7.cloned.1.call-done = bf16[2048,1090]{0,1:T(8,128)(2,1)} async-done(((bf16[128,1090]{0,1:T(8,128)(2,1)}), bf16[2048,1090]{0,1:T(8,128)(2,1)}) %all-gather.7.cloned.1.call-update) | async-done | bytes 4464656 | tf_op jit(solution)/shard_map/all_gather | solution.py:276
  233.0 108.1 %all-reduce.7.cloned.1.call-done = bf16[1024,2048]{0,1:T(8,128)(2,1)} async-done(((bf16[1024,2048]{0,1:T(8,128)(2,1)}), bf16[1024,2048]{0,1:T(8,128)(2,1)}) %all-reduce.7.cloned.1.call-update) | async-done | bytes 4194320 | tf_op jit(solution)/shard_map/psum | solution.py:367
  351.0 8.1 scatter_custom_fusion.tok_ref
  389.2 12.5 copy.228.both_hbm
  408.9 50.2 %shard_map.297 = bf16[2560,32,128]{2,1,0:T(8,128)(2,1)} custom-call(s32[2560]{0:T(1024)} %copy-done.67, bf16[1024,32,128]{2,1,0:T(8,128)(2,1)} %copy.228.both_hbm, f32[2,2560,1,128]{3,2,1,0:T(1,128)} %broadcast_in_dim.76.col_ref), custom_call_target="tpu_custom_call" | custom-call | flops 5242880 | bytes 41943040 | tf_op jit(solution)/shard_map/pallas_call | solution.py:120
  459.2 236.8 %all_to_all.30 = bf16[16,4,40,32,128]{4,3,2,1,0:T(8,128)(2,1)} all-to-all(bf16[16,4,40,32,128]{4,3,2,1,0:T(8,128)(2,1)} %bitcast.258), channel_id=1, replica_groups=mesh['dp'=16,'tensor'=8] {'dp'}, dimensions={0} | all-to-all | bytes 41943040 | tf_op jit(solution)/shard_map/all_to_all | solution.py:403
  696.0 31.3 %reshape.530 = bf16[16,4,40,4096]{3,2,1,0:T(8,128)(2,1)} reshape(bf16[16,4,40,32,128]{4,3,2,1,0:T(8,128)(2,1)} %all_to_all.30) | data formatting | bytes 41943040 | tf_op jit(solution)/shard_map/reshape | solution.py:404
  727.3 16.8 fusion.163
  744.1 8.8 fusion.11
  752.9 8.7 fusion.9
  761.6 11.4 fusion.41
  779.9 11.9 copy.237
  791.8 11.2 copy.180
  808.1 9.9 fusion.32
  818.1 15.1 add_convert_fusion
  833.2 11.9 copy.238
  845.1 103.9 %all-to-all-done.2 = bf16[16,4,40,16,128]{4,3,2,1,0:T(8,128)(2,1)} async-done(((bf16[16,4,40,16,128]{4,3,2,1,0:T(8,128)(2,1)}), bf16[16,4,40,16,128]{4,3,2,1,0:T(8,128)(2,1)}, u32[]{:S(2)}, u32[]{:S(2)}) %all-to-all-start.2) | async-done | bytes 10485792 | tf_op jit(solution)/shard_map/all_to_all | solution.py:416
  949.0 11.2 copy.181
  1001.2 104.9 %all-to-all-done.3 = bf16[16,4,40,16,128]{4,3,2,1,0:T(8,128)(2,1)} async-done(((bf16[16,4,40,16,128]{4,3,2,1,0:T(8,128)(2,1)}), bf16[16,4,40,16,128]{4,3,2,1,0:T(8,128)(2,1)}, u32[]{:S(2)}, u32[]{:S(2)}) %all-to-all-start.3) | async-done | bytes 10485792 | tf_op jit(solution)/shard_map/all_to_all | solution.py:444
  1109.6 44.8 %shard_map.298 = (bf16[1024,16,128]{2,1,0:T(8,128)(2,1)}, bf16[1024,16,128]{2,1,0:T(8,128)(2,1)}, f32[1024,1,128]{2,1,0:T(1,128)}) custom-call(s32[2048]{0:T(1024)} %multiply_add_fusion.slot_ref, bf16[2560,16,128]{2,1,0:T(8,128)(2,1)} %bitcast.36.out_hbm, bf16[2560,16,128]{2,1,0:T(8,128)(2,1)} %bitcast.37.back_hbm, ...), custom_call_target="tpu_custom_call" | custom-call | flops 33554432 | bytes 46137344 | tf_op jit(solution)/shard_map/pallas_call | solution.py:192
  1189.3 62.5 %all-to-all-done.4 = bf16[8,128,2048]{2,1,0:T(8,128)(2,1)} async-done(((bf16[8,128,2048]{2,1,0:T(8,128)(2,1)}), bf16[8,128,2048]{2,1,0:T(8,128)(2,1)}, u32[]{:S(2)}, u32[]{:S(2)}) %all-to-all-start.4) | async-done | bytes 4194336 | tf_op jit(solution)/shard_map/all_to_all | solution.py:487
  1255.8 81.0 %all-reduce.9.cloned.1.call-done = bf16[1024,2050]{0,1:T(8,128)(2,1)} async-done(((bf16[1024,2050]{0,1:T(8,128)(2,1)}), bf16[1024,2050]{0,1:T(8,128)(2,1)}) %all-reduce.9.cloned.1.call-update) | async-done | bytes 4198416 | tf_op jit(solution)/shard_map/psum | solution.py:492
  1343.4 10.5 multiply_reduce_fusion
  1355.8 8.1 fusion.162
  1393.2 39.5 %all-to-all-done.5 = bf16[16,128,1056]{1,2,0:T(8,128)(2,1)} async-done(((bf16[16,128,1056]{1,2,0:T(8,128)(2,1)}), bf16[16,128,1056]{1,2,0:T(8,128)(2,1)}, u32[]{:S(2)}, u32[]{:S(2)}) %all-to-all-start.5) | async-done | bytes 4325408 | tf_op jit(solution)/shard_map/all_to_all | solution.py:507
  1440.2 10.7 pad_maximum_fusion.2
  1480.0 99.3 %all-reduce.11.cloned.1.call-done = bf16[1024,2624]{0,1:T(8,128)(2,1)} async-done(((bf16[1024,2624]{0,1:T(8,128)(2,1)}), bf16[1024,2624]{0,1:T(8,128)(2,1)}) %all-reduce.11.cloned.1.call-update) | async-done | bytes 5373968 | tf_op jit(solution)/shard_map/psum | solution.py:600
  1607.2 9.1 fusion.19
  1616.3 9.3 fusion.22
  1642.0 33.5 %reduce-scatter.2.cloned.1.call-done = f32[128,849]{0,1:T(8,128)} async-done(((f32[2048,849]{0,1:T(8,128)}), f32[128,849]{0,1:T(8,128)}) %reduce-scatter.2.cloned.1.call-update) | async-done | bytes 434704 | tf_op jit(solution)/shard_map/reduce_scatter | solution.py:657
  (435 shorter events, 349.2 us)
Async XLA Ops:
  7.2 754.4 %copy-start = (bf16[4,176,2048]{2,1,0:T(8,128)(2,1)S(1)}, bf16[4,176,2048]{2,1,0:T(8,128)(2,1)}, u32[]{:S(2)}) copy-start(bf16[4,176,2048]{2,1,0:T(8,128)(2,1)} %param.31) | copy-start | bytes 8650756
  7.2 128.9 %all-gather.5.cloned.1.call-start = ((), (), s32[]{:S(2)}) async-start(), calls=%async_computation.7 | async-start | bytes 4718592 | tf_op jit(solution)/shard_map/all_gather | solution.py:295
  9.5 173.9 %all-gather.7.cloned.1.call-start = ((), (), s32[]{:S(2)}) async-start(), calls=%async_computation.8 | async-start | bytes 4769792 | tf_op jit(solution)/shard_map/all_gather | solution.py:276
  20.1 64.5 %all-to-all-start = ((bf16[8,128,2048]{1,2,0:T(8,128)(2,1)}), bf16[8,128,2048]{1,2,0:T(8,128)(2,1)}, u32[]{:S(2)}, u32[]{:S(2)}) async-start(bf16[8,128,2048]{1,2,0:T(8,128)(2,1)} %broadcast_in_dim.62), calls=%async_computation | async-start | bytes 8388608 | tf_op jit(solution)/shard_map/all_to_all | solution.py:296
  27.9 198.4 %all-gather.9.cloned.1.call-start = ((), (), s32[]{:S(2)}) async-start(), calls=%async_computation.9 | async-start | bytes 1427456 | tf_op jit(solution)/shard_map/all_gather | solution.py:289
  28.7 312.4 %all-reduce.7.cloned.1.call-start = ((), (), s32[]{:S(2)}) async-start(), calls=%async_computation.10 | async-start | bytes 8388608 | tf_op jit(solution)/shard_map/psum | solution.py:367
  29.4 186.4 %copy-start.98 = (f32[32]{0:T(128)}, f32[32]{0:T(128)S(1)}, u32[]{:S(2)}) copy-start(f32[32]{0:T(128)S(1)} %multiply_power_fusion) | copy-start | bytes 388
  29.4 186.4 %copy-start.79 = (f32[1024]{0:T(1024)}, f32[1024]{0:T(1024)S(1)}, u32[]{:S(2)}) copy-start(f32[1024]{0:T(1024)S(1)} %iota_convert_fusion) | copy-start | bytes 12292
  139.3 48.4 %copy-start.77 = (f32[1024]{0:T(1024)}, f32[1024]{0:T(1024)S(1)}, u32[]{:S(2)}) copy-start(f32[1024]{0:T(1024)S(1)} %add_rsqrt_fusion.2) | copy-start | bytes 12292
  193.2 16.4 copy-start.74
  193.3 16.3 copy-start.85
  212.2 12.8 copy-start.16
  231.1 228.1 %all-gather.11.cloned.1.call-start = ((), (), s32[]{:S(2)}) async-start(), calls=%async_computation.11 | async-start | bytes 4595712 | tf_op jit(solution)/shard_map/all_gather | solution.py:398
  233.0 114.6 %copy-start.63 = (s32[1024,2]{0,1:T(2,128)S(1)}, s32[1024,2]{0,1:T(2,128)}, u32[]{:S(2)}) copy-start(s32[1024,2]{0,1:T(2,128)} %param.19) | copy-start | bytes 24580
  727.3 16.8 copy-start.30
  803.0 146.0 %all-to-all-start.2 = ((bf16[16,4,40,16,128]{4,3,2,1,0:T(8,128)(2,1)}), bf16[16,4,40,16,128]{4,3,2,1,0:T(8,128)(2,1)}, u32[]{:S(2)}, u32[]{:S(2)}) async-start(bf16[16,4,40,16,128]{4,3,2,1,0:T(8,128)(2,1)} %copy.180), calls=%async_computation.2 | async-start | bytes 20971520 | tf_op jit(solution)/shard_map/all_to_all | solution.py:416
  960.2 145.9 %all-to-all-start.3 = ((bf16[16,4,40,16,128]{4,3,2,1,0:T(8,128)(2,1)}), bf16[16,4,40,16,128]{4,3,2,1,0:T(8,128)(2,1)}, u32[]{:S(2)}, u32[]{:S(2)}) async-start(bf16[16,4,40,16,128]{4,3,2,1,0:T(8,128)(2,1)} %copy.181), calls=%async_computation.3 | async-start | bytes 20971520 | tf_op jit(solution)/shard_map/all_to_all | solution.py:444
  965.2 371.5 %all-reduce.9.cloned.1.call-start = ((), (), s32[]{:S(2)}) async-start(), calls=%async_computation.12 | async-start | bytes 8421376 | tf_op jit(solution)/shard_map/psum | solution.py:492
  965.9 14.8 slice-start.7
  1173.8 78.0 %all-to-all-start.4 = ((bf16[8,128,2048]{2,1,0:T(8,128)(2,1)}), bf16[8,128,2048]{2,1,0:T(8,128)(2,1)}, u32[]{:S(2)}, u32[]{:S(2)}) async-start(bf16[8,128,2048]{2,1,0:T(8,128)(2,1)} %reshape_reshape.3), calls=%async_computation.4 | async-start | bytes 8388608 | tf_op jit(solution)/shard_map/all_to_all | solution.py:487
  1255.8 87.5 %copy-start.64 = (s32[1024,2]{0,1:T(2,128)S(1)}, s32[1024,2]{0,1:T(2,128)}, u32[]{:S(2)}) copy-start(s32[1024,2]{0,1:T(2,128)} %param.19) | copy-start | bytes 24580
  1255.8 87.5 %copy-start.38 = (bf16[2048,321]{0,1:T(8,128)(2,1)S(1)}, bf16[2048,321]{0,1:T(8,128)(2,1)}, u32[]{:S(2)}) copy-start(bf16[2048,321]{0,1:T(8,128)(2,1)} %all-gather.9.cloned.1.call-done) | copy-start | bytes 3944452
  1255.8 87.5 %copy-start.66 = (f32[2048,1]{0,1:T(1,128)S(1)}, f32[2048,1]{0,1:T(1,128)}, u32[]{:S(2)}) copy-start(f32[2048,1]{0,1:T(1,128)} %copy-done.65) | copy-start | bytes 24580
  1343.3 12.5 copy-start.9
  1343.3 24.0 %slice-start.2 = ((s8[4325376]{0:T(1024)(128)(4,1)}), s8[4194304]{0:T(1024)(128)(4,1)S(1)}, s32[]{:S(2)}) async-start(s8[4325376]{0:T(1024)(128)(4,1)} %bitcast.269), calls=%async_computation.17 | async-start | bytes 8388608
  1370.2 62.5 %all-to-all-start.5 = ((bf16[16,128,1056]{1,2,0:T(8,128)(2,1)}), bf16[16,128,1056]{1,2,0:T(8,128)(2,1)}, u32[]{:S(2)}, u32[]{:S(2)}) async-start(bf16[16,128,1056]{1,2,0:T(8,128)(2,1)} %copy_bitcast_fusion), calls=%async_computation.5 | async-start | bytes 8650752 | tf_op jit(solution)/shard_map/all_to_all | solution.py:507
  1375.3 204.1 %all-reduce.11.cloned.1.call-start = ((), (), s32[]{:S(2)}) async-start(), calls=%async_computation.13 | async-start | bytes 10747904 | tf_op jit(solution)/shard_map/psum | solution.py:600
  1392.4 44.0 %copy-start.52 = (bf16[1024,384]{0,1:T(8,128)(2,1)S(1)}, bf16[1024,384]{0,1:T(8,128)(2,1)}, u32[]{:S(2)}) copy-start(bf16[1024,384]{0,1:T(8,128)(2,1)} %pad_maximum_fusion.7) | copy-start | bytes 2359300
  1450.9 224.6 %reduce-scatter.2.cloned.1.call-start = ((), (), s32[]{:S(2)}) async-start(), calls=%async_computation.14 | async-start | bytes 7450624 | tf_op jit(solution)/shard_map/reduce_scatter | solution.py:657
  1607.1 18.4 %slice-start.4 = ((s8[10485760]{0:T(1024)(128)(4,1)}), s8[4194304]{0:T(1024)(128)(4,1)S(1)}, s32[]{:S(2)}) async-start(s8[10485760]{0:T(1024)(128)(4,1)} %bitcast.273), calls=%async_computation.19 | async-start | bytes 8388608
  1607.1 18.4 %slice-start.5 = ((s8[10485760]{0:T(1024)(128)(4,1)}), s8[4194304]{0:T(1024)(128)(4,1)S(1)}, s32[]{:S(2)}) async-start(s8[10485760]{0:T(1024)(128)(4,1)} %bitcast.273), calls=%async_computation.20 | async-start | bytes 8388608
  1634.1 50.2 %copy-start.1 = (bf16[4,176,2048]{2,1,0:T(8,128)(2,1)S(1)}, bf16[4,176,2048]{2,1,0:T(8,128)(2,1)}, u32[]{:S(2)}) copy-start(bf16[4,176,2048]{2,1,0:T(8,128)(2,1)} %param.31) | copy-start | bytes 8650756
  (91 other events, 434.6 us)
Sparse Core Ops, SparseCore 0:
  10.8 125.3 all-gather.4
  138.3 44.9 all-gather.6
  185.5 35.0 all-gather.8
  231.2 109.8 all-reduce.6
  347.7 44.0 all-gather.10
  1166.6 170.1 all-reduce.8
  1451.0 128.2 all-reduce.10
  1606.0 69.4 reduce-scatter.1

commit v8 on v7

--- a/solution.py
+++ b/solution.py
@@ -293,14 +293,11 @@
     shared_local = jnp.concatenate([shared_gate, shared_up, shared_down.T], 1)
 
     hidden_all = lax.all_gather(hidden, "tensor", axis=0, tiled=True)
+    grad_blocks = jnp.broadcast_to(out_grad[None], (tensor_size,) + out_grad.shape)
+    grad_blocks, hidden_all = lax.optimization_barrier((grad_blocks, hidden_all))
     grad_seq = lax.all_to_all(
-        jnp.broadcast_to(out_grad[None], (tensor_size,) + out_grad.shape),
-        "tensor",
-        split_axis=0,
-        concat_axis=0,
-        tiled=True,
+        grad_blocks, "tensor", split_axis=0, concat_axis=0, tiled=True
     ).reshape(tensor_size * tok_dev, D)
-    grad_seq, hidden_all = lax.optimization_barrier((grad_seq, hidden_all))
     hidden_all_f = hidden_all.astype(jnp.float32)
     scale_one_all = norm_scale(hidden_all_f)
     gain_one = attn_gains.astype(jnp.float32)

time: 1710 us -> 1720 us (level)
    all_gather x1, waiting for transfers between devices: 46.8 us -> 71.6 us  [shards(): hidden_all = lax.all_gather(hidden, 'tensor', axis=0, tiled=True)]
    reshape x3 -> x1, local copies, waits for them, and re-layouts: 24.3 us -> 6.42 us  [shards(): grad_seq = lax.all_to_all(grad_blocks, 'tensor', split_axis=0, concat_axi...]
    unnamed x232 -> x206, local copies, waits for them, and re-layouts: 61.9 us -> 62.9 us
where the time goes in v8:
time: 1720 us; the launch traced here: 1700 us
  waiting for transfers between devices  785 us (46%)
  blocking collectives  238 us (14%)
  local copies, waits for them, and re-layouts  236 us (14%)
  matrix products  191 us (11%)
  other arithmetic  107 us (6%)
  Pallas kernels  95.5 us (6%)
  starting transfers between devices  32.8 us (2%)
    all_to_all x1, blocking collectives, shards(): lax.all_to_all(send_both, 'dp', split_axis=0, concat_axis=0, tiled=True)  238 us
    all_to_all x1, waiting for transfers between devices, shards(): lax.all_to_all(grads_low, 'dp', split_axis=0, concat_axis=0, tiled=True)  110 us
    psum x1, waiting for transfers between devices, shards(): lax.psum(attn_part.astype(jnp.bfloat16), 'tensor').astype(jnp.float32)  108 us
    all_to_all x1, waiting for transfers between devices, shards(): lax.all_to_all(expert_out.astype(jnp.bfloat16).reshape(dp_size, exp_dev,...  104 us
    psum x1, waiting for transfers between devices, shards(): lax.psum(jnp.concatenate([normed_grad_part, latent_grad_part], 1).astype(...  97.6 us
    psum x1, waiting for transfers between devices, shards(): lax.psum(jnp.concatenate([back_part, gate_cols.astype(jnp.bfloat16)], 1),...  79.6 us
    all_gather x1, waiting for transfers between devices, shards(): hidden_all = lax.all_gather(hidden, 'tensor', axis=0, tiled=True)  71.6 us
    unnamed x206, local copies, waits for them, and re-layouts  62.9 us
  transfers between devices with their start and end apart: 13, of which 11 were waited for; matrix products, arithmetic and copies ran while one was open for 17% of the time, Pallas kernels for 3%

profile of v8, /device:TPU:0, one launch (start us, length us, event | category | flops | bytes accessed | tf_op | source)
XLA Modules:
  0.0 1702.6 jit_solution(13763316346183313866)
XLA Ops:
  19.9 71.6 %all-gather.5.cloned.1.call-done = bf16[1024,2048]{0,1:T(8,128)(2,1)} async-done(((bf16[128,2048]{0,1:T(8,128)(2,1)}), bf16[1024,2048]{0,1:T(8,128)(2,1)}) %all-gather.5.cloned.1.call-update) | async-done | bytes 4194320 | tf_op jit(solution)/shard_map/all_gather | solution.py:295
  96.2 42.5 %all-gather.7.cloned.1.call-done = bf16[2048,1090]{0,1:T(8,128)(2,1)} async-done(((bf16[128,1090]{0,1:T(8,128)(2,1)}), bf16[2048,1090]{0,1:T(8,128)(2,1)}) %all-gather.7.cloned.1.call-update) | async-done | bytes 4464656 | tf_op jit(solution)/shard_map/all_gather | solution.py:276
  188.2 108.3 %all-reduce.7.cloned.1.call-done = bf16[1024,2048]{0,1:T(8,128)(2,1)} async-done(((bf16[1024,2048]{0,1:T(8,128)(2,1)}), bf16[1024,2048]{0,1:T(8,128)(2,1)}) %all-reduce.7.cloned.1.call-update) | async-done | bytes 4194320 | tf_op jit(solution)/shard_map/psum | solution.py:364
  320.2 43.0 %all-to-all-done = bf16[8,128,2048]{2,1,0:T(8,128)(2,1)} async-done(((bf16[8,128,2048]{2,1,0:T(8,128)(2,1)}), bf16[8,128,2048]{2,1,0:T(8,128)(2,1)}, u32[]{:S(2)}, u32[]{:S(2)}) %all-to-all-start) | async-done | bytes 4194336 | tf_op jit(solution)/shard_map/all_to_all | solution.py:298
  396.1 8.2 pad_maximum_fusion.both_hbm
  411.5 50.7 %shard_map.297 = bf16[2560,32,128]{2,1,0:T(8,128)(2,1)} custom-call(s32[2560]{0:T(1024)} %copy-done.61, bf16[1024,32,128]{2,1,0:T(8,128)(2,1)} %pad_maximum_fusion.both_hbm, f32[2,2560,1,128]{3,2,1,0:T(1,128)} %broadcast_in_dim.76.col_ref), custom_call_target="tpu_custom_call" | custom-call | flops 5242880 | bytes 41943040 | tf_op jit(solution)/shard_map/pallas_call | solution.py:120
  462.3 238.3 %all_to_all.30 = bf16[16,4,40,32,128]{4,3,2,1,0:T(8,128)(2,1)} all-to-all(bf16[16,4,40,32,128]{4,3,2,1,0:T(8,128)(2,1)} %bitcast.256), channel_id=1, replica_groups=mesh['dp'=16,'tensor'=8] {'dp'}, dimensions={0} | all-to-all | bytes 41943040 | tf_op jit(solution)/shard_map/all_to_all | solution.py:400
  700.6 31.3 %reshape.526 = bf16[16,4,40,4096]{3,2,1,0:T(8,128)(2,1)} reshape(bf16[16,4,40,32,128]{4,3,2,1,0:T(8,128)(2,1)} %all_to_all.30) | data formatting | bytes 41943040 | tf_op jit(solution)/shard_map/reshape | solution.py:401
  731.9 16.7 fusion.163
  748.6 8.8 fusion.11
  757.5 8.6 fusion.9
  766.1 11.3 fusion.41
  784.5 11.9 copy.231
  796.4 11.2 copy.174
  812.8 9.9 fusion.32
  822.6 15.1 add_convert_fusion
  837.7 12.0 copy.232
  849.7 104.0 %all-to-all-done.2 = bf16[16,4,40,16,128]{4,3,2,1,0:T(8,128)(2,1)} async-done(((bf16[16,4,40,16,128]{4,3,2,1,0:T(8,128)(2,1)}), bf16[16,4,40,16,128]{4,3,2,1,0:T(8,128)(2,1)}, u32[]{:S(2)}, u32[]{:S(2)}) %all-to-all-start.2) | async-done | bytes 10485792 | tf_op jit(solution)/shard_map/all_to_all | solution.py:413
  953.6 11.1 copy.175
  1000.9 109.7 %all-to-all-done.3 = bf16[16,4,40,16,128]{4,3,2,1,0:T(8,128)(2,1)} async-done(((bf16[16,4,40,16,128]{4,3,2,1,0:T(8,128)(2,1)}), bf16[16,4,40,16,128]{4,3,2,1,0:T(8,128)(2,1)}, u32[]{:S(2)}, u32[]{:S(2)}) %all-to-all-start.3) | async-done | bytes 10485792 | tf_op jit(solution)/shard_map/all_to_all | solution.py:441
  1114.2 44.8 %shard_map.298 = (bf16[1024,16,128]{2,1,0:T(8,128)(2,1)}, bf16[1024,16,128]{2,1,0:T(8,128)(2,1)}, f32[1024,1,128]{2,1,0:T(1,128)}) custom-call(s32[2048]{0:T(1024)} %multiply_add_fusion.slot_ref, bf16[2560,16,128]{2,1,0:T(8,128)(2,1)} %bitcast.36.out_hbm, bf16[2560,16,128]{2,1,0:T(8,128)(2,1)} %bitcast.37.back_hbm, ...), custom_call_target="tpu_custom_call" | custom-call | flops 33554432 | bytes 46137344 | tf_op jit(solution)/shard_map/pallas_call | solution.py:192
  1178.3 12.2 all-to-all-start.4
  1209.3 55.6 %all-to-all-done.4 = bf16[8,128,2048]{2,1,0:T(8,128)(2,1)} async-done(((bf16[8,128,2048]{2,1,0:T(8,128)(2,1)}), bf16[8,128,2048]{2,1,0:T(8,128)(2,1)}, u32[]{:S(2)}, u32[]{:S(2)}) %all-to-all-start.4) | async-done | bytes 4194336 | tf_op jit(solution)/shard_map/all_to_all | solution.py:484
  1269.0 79.6 %all-reduce.9.cloned.1.call-done = bf16[1024,2050]{0,1:T(8,128)(2,1)} async-done(((bf16[1024,2050]{0,1:T(8,128)(2,1)}), bf16[1024,2050]{0,1:T(8,128)(2,1)}) %all-reduce.9.cloned.1.call-update) | async-done | bytes 4198416 | tf_op jit(solution)/shard_map/psum | solution.py:489
  1355.3 8.4 multiply_reduce_fusion
  1363.7 9.1 fusion.162
  1404.4 40.0 %all-to-all-done.5 = bf16[16,128,1056]{1,2,0:T(8,128)(2,1)} async-done(((bf16[16,128,1056]{1,2,0:T(8,128)(2,1)}), bf16[16,128,1056]{1,2,0:T(8,128)(2,1)}, u32[]{:S(2)}, u32[]{:S(2)}) %all-to-all-start.5) | async-done | bytes 4325408 | tf_op jit(solution)/shard_map/all_to_all | solution.py:504
  1451.8 10.7 pad_maximum_fusion.2
  1492.9 97.6 %all-reduce.11.cloned.1.call-done = bf16[1024,2624]{0,1:T(8,128)(2,1)} async-done(((bf16[1024,2624]{0,1:T(8,128)(2,1)}), bf16[1024,2624]{0,1:T(8,128)(2,1)}) %all-reduce.11.cloned.1.call-update) | async-done | bytes 5373968 | tf_op jit(solution)/shard_map/psum | solution.py:597
  1618.3 9.1 fusion.19
  1627.4 9.3 fusion.22
  1653.2 33.5 %reduce-scatter.2.cloned.1.call-done = f32[128,849]{0,1:T(8,128)} async-done(((f32[2048,849]{0,1:T(8,128)}), f32[128,849]{0,1:T(8,128)}) %reduce-scatter.2.cloned.1.call-update) | async-done | bytes 434704 | tf_op jit(solution)/shard_map/reduce_scatter | solution.py:654
  (407 shorter events, 351.7 us)
Async XLA Ops:
  7.2 758.9 %copy-start = (bf16[4,176,2048]{2,1,0:T(8,128)(2,1)S(1)}, bf16[4,176,2048]{2,1,0:T(8,128)(2,1)}, u32[]{:S(2)}) copy-start(bf16[4,176,2048]{2,1,0:T(8,128)(2,1)} %param.31) | copy-start | bytes 8650756
  7.2 84.3 %all-gather.5.cloned.1.call-start = ((), (), s32[]{:S(2)}) async-start(), calls=%async_computation.7 | async-start | bytes 4718592 | tf_op jit(solution)/shard_map/all_gather | solution.py:295
  9.5 129.3 %all-gather.7.cloned.1.call-start = ((), (), s32[]{:S(2)}) async-start(), calls=%async_computation.8 | async-start | bytes 4769792 | tf_op jit(solution)/shard_map/all_gather | solution.py:276
  16.2 165.5 %all-gather.9.cloned.1.call-start = ((), (), s32[]{:S(2)}) async-start(), calls=%async_computation.9 | async-start | bytes 1427456 | tf_op jit(solution)/shard_map/all_gather | solution.py:289
  17.8 278.7 %all-reduce.7.cloned.1.call-start = ((), (), s32[]{:S(2)}) async-start(), calls=%async_computation.10 | async-start | bytes 8388608 | tf_op jit(solution)/shard_map/psum | solution.py:364
  17.9 153.4 %copy-start.70 = (f32[1024]{0:T(1024)}, f32[1024]{0:T(1024)S(1)}, u32[]{:S(2)}) copy-start(f32[1024]{0:T(1024)S(1)} %iota_convert_fusion) | copy-start | bytes 12292
  17.9 153.4 %copy-start.88 = (f32[32]{0:T(128)}, f32[32]{0:T(128)S(1)}, u32[]{:S(2)}) copy-start(f32[32]{0:T(128)S(1)} %multiply_power_fusion) | copy-start | bytes 388
  96.2 46.9 %copy-start.68 = (f32[1024]{0:T(1024)}, f32[1024]{0:T(1024)S(1)}, u32[]{:S(2)}) copy-start(f32[1024]{0:T(1024)S(1)} %add_rsqrt_fusion.2) | copy-start | bytes 12292
  148.6 16.4 copy-start.65
  148.7 16.3 copy-start.76
  167.6 12.8 copy-start.15
  186.5 275.7 %all-gather.11.cloned.1.call-start = ((), (), s32[]{:S(2)}) async-start(), calls=%async_computation.11 | async-start | bytes 4595712 | tf_op jit(solution)/shard_map/all_gather | solution.py:395
  303.1 60.1 %all-to-all-start = ((bf16[8,128,2048]{2,1,0:T(8,128)(2,1)}), bf16[8,128,2048]{2,1,0:T(8,128)(2,1)}, u32[]{:S(2)}, u32[]{:S(2)}) async-start(bf16[8,128,2048]{2,1,0:T(8,128)(2,1)} %broadcast_in_dim.62), calls=%async_computation | async-start | bytes 8388608 | tf_op jit(solution)/shard_map/all_to_all | solution.py:298
  319.3 49.6 %copy-start.61 = (s32[2560]{0:T(1024)}, s32[2560]{0:T(1024)S(1)}, u32[]{:S(2)}) copy-start(s32[2560]{0:T(1024)S(1)} %scatter_custom_fusion.tok_ref) | copy-start | bytes 30724
  320.2 55.6 %copy-start.59 = (f32[2048,1]{0,1:T(1,128)}, f32[2048,1]{0,1:T(1,128)S(1)}, u32[]{:S(2)}) copy-start(f32[2048,1]{0,1:T(1,128)S(1)} %slice_convert_fusion.1) | copy-start | bytes 24580
  731.9 16.7 copy-start.28
  807.6 146.0 %all-to-all-start.2 = ((bf16[16,4,40,16,128]{4,3,2,1,0:T(8,128)(2,1)}), bf16[16,4,40,16,128]{4,3,2,1,0:T(8,128)(2,1)}, u32[]{:S(2)}, u32[]{:S(2)}) async-start(bf16[16,4,40,16,128]{4,3,2,1,0:T(8,128)(2,1)} %copy.174), calls=%async_computation.2 | async-start | bytes 20971520 | tf_op jit(solution)/shard_map/all_to_all | solution.py:413
  964.8 145.9 %all-to-all-start.3 = ((bf16[16,4,40,16,128]{4,3,2,1,0:T(8,128)(2,1)}), bf16[16,4,40,16,128]{4,3,2,1,0:T(8,128)(2,1)}, u32[]{:S(2)}, u32[]{:S(2)}) async-start(bf16[16,4,40,16,128]{4,3,2,1,0:T(8,128)(2,1)} %copy.175), calls=%async_computation.3 | async-start | bytes 20971520 | tf_op jit(solution)/shard_map/all_to_all | solution.py:441
  969.8 378.8 %all-reduce.9.cloned.1.call-start = ((), (), s32[]{:S(2)}) async-start(), calls=%async_computation.12 | async-start | bytes 8421376 | tf_op jit(solution)/shard_map/psum | solution.py:489
  1178.3 12.3 copy-start.46
  1178.3 12.3 copy-start.48
  1178.3 86.6 %all-to-all-start.4 = ((bf16[8,128,2048]{2,1,0:T(8,128)(2,1)}), bf16[8,128,2048]{2,1,0:T(8,128)(2,1)}, u32[]{:S(2)}, u32[]{:S(2)}) async-start(bf16[8,128,2048]{2,1,0:T(8,128)(2,1)} %reshape_reshape.4), calls=%async_computation.4 | async-start | bytes 8388608 | tf_op jit(solution)/shard_map/all_to_all | solution.py:484
  1269.0 86.2 %copy-start.58 = (s32[1024,2]{0,1:T(2,128)S(1)}, s32[1024,2]{0,1:T(2,128)}, u32[]{:S(2)}) copy-start(s32[1024,2]{0,1:T(2,128)} %param.19) | copy-start | bytes 24580
  1269.0 86.2 %copy-start.36 = (bf16[2048,321]{0,1:T(8,128)(2,1)S(1)}, bf16[2048,321]{0,1:T(8,128)(2,1)}, u32[]{:S(2)}) copy-start(bf16[2048,321]{0,1:T(8,128)(2,1)} %all-gather.9.cloned.1.call-done) | copy-start | bytes 3944452
  1269.0 86.2 %copy-start.60 = (f32[2048,1]{0,1:T(1,128)S(1)}, f32[2048,1]{0,1:T(1,128)}, u32[]{:S(2)}) copy-start(f32[2048,1]{0,1:T(1,128)} %copy-done.59) | copy-start | bytes 24580
  1381.4 63.0 %all-to-all-start.5 = ((bf16[16,128,1056]{1,2,0:T(8,128)(2,1)}), bf16[16,128,1056]{1,2,0:T(8,128)(2,1)}, u32[]{:S(2)}, u32[]{:S(2)}) async-start(bf16[16,128,1056]{1,2,0:T(8,128)(2,1)} %copy_bitcast_fusion), calls=%async_computation.5 | async-start | bytes 8650752 | tf_op jit(solution)/shard_map/all_to_all | solution.py:504
  1386.4 204.1 %all-reduce.11.cloned.1.call-start = ((), (), s32[]{:S(2)}) async-start(), calls=%async_computation.13 | async-start | bytes 10747904 | tf_op jit(solution)/shard_map/psum | solution.py:597
  1403.6 44.4 %copy-start.50 = (bf16[1024,384]{0,1:T(8,128)(2,1)S(1)}, bf16[1024,384]{0,1:T(8,128)(2,1)}, u32[]{:S(2)}) copy-start(bf16[1024,384]{0,1:T(8,128)(2,1)} %pad_maximum_fusion.7) | copy-start | bytes 2359300
  1462.5 224.2 %reduce-scatter.2.cloned.1.call-start = ((), (), s32[]{:S(2)}) async-start(), calls=%async_computation.14 | async-start | bytes 7450624 | tf_op jit(solution)/shard_map/reduce_scatter | solution.py:654
  1618.3 18.4 %slice-start.2 = ((s8[10485760]{0:T(1024)(128)(4,1)}), s8[4194304]{0:T(1024)(128)(4,1)S(1)}, s32[]{:S(2)}) async-start(s8[10485760]{0:T(1024)(128)(4,1)} %bitcast.270), calls=%async_computation.17 | async-start | bytes 8388608
  1618.3 18.4 %slice-start.3 = ((s8[10485760]{0:T(1024)(128)(4,1)}), s8[4194304]{0:T(1024)(128)(4,1)S(1)}, s32[]{:S(2)}) async-start(s8[10485760]{0:T(1024)(128)(4,1)} %bitcast.270), calls=%async_computation.18 | async-start | bytes 8388608
  1645.3 50.2 %copy-start.1 = (bf16[4,176,2048]{2,1,0:T(8,128)(2,1)S(1)}, bf16[4,176,2048]{2,1,0:T(8,128)(2,1)}, u32[]{:S(2)}) copy-start(bf16[4,176,2048]{2,1,0:T(8,128)(2,1)} %param.31) | copy-start | bytes 8650756
  (78 other events, 361.9 us)
Sparse Core Ops, SparseCore 0:
  10.8 80.6 all-gather.4
  93.7 44.9 all-gather.6
  140.9 35.0 all-gather.8
  186.6 109.8 all-reduce.6
  303.2 82.2 all-gather.10
  1171.1 177.4 all-reduce.8
  1462.6 127.9 all-reduce.10
  1617.1 69.4 reduce-scatter.1

commit v9 on v8

--- a/solution.py
+++ b/solution.py
@@ -298,6 +298,9 @@
     grad_seq = lax.all_to_all(
         grad_blocks, "tensor", split_axis=0, concat_axis=0, tiled=True
     ).reshape(tensor_size * tok_dev, D)
+    grad_seq, query_weights, latent_weights = lax.optimization_barrier(
+        (grad_seq, query_weights, latent_weights)
+    )
     hidden_all_f = hidden_all.astype(jnp.float32)
     scale_one_all = norm_scale(hidden_all_f)
     gain_one = attn_gains.astype(jnp.float32)

time: 1720 us -> 1700 us (0.988)
    all_to_all x1, waiting for transfers between devices: 43 us -> 0.01 us  [shards(): lax.all_to_all(grad_blocks, 'tensor', split_axis=0, concat_axis=0, tiled=...]
    all_gather x1, waiting for transfers between devices: 42.5 us -> 70.8 us  [shards(): first_all = lax.all_gather(first_pack, 'dp', axis=0, tiled=True)]
    reshape x0 -> x2, local copies, waits for them, and re-layouts: none -> 19.5 us  [the longest x1 12.5 us: dispatch_rows(): both = jnp.concatenate([rows, grads], 1).reshape(count, 2 * tile_rows, 128)]
    unnamed x206 -> x240, local copies, waits for them, and re-layouts: 62.9 us -> 59.3 us
  transfers between devices with their start and end apart: 13 -> 13, of which waited for: 11 -> 10; matrix products, arithmetic and copies ran while one was open for 17% -> 18% of each run, Pallas kernels for 3% -> 3%
where the time goes in v9:
time: 1700 us; the launch traced here: 1690 us
  waiting for transfers between devices  775 us (46%)
  local copies, waits for them, and re-layouts  246 us (14%)
  blocking collectives  236 us (14%)
  matrix products  183 us (11%)
  other arithmetic  107 us (6%)
  Pallas kernels  94.6 us (6%)
  starting transfers between devices  25.5 us (2%)
  between operations  17 us (1%)
    all_to_all x1, blocking collectives, shards(): lax.all_to_all(send_both, 'dp', split_axis=0, concat_axis=0, tiled=True)  236 us
    psum x1, waiting for transfers between devices, shards(): lax.psum(attn_part.astype(jnp.bfloat16), 'tensor').astype(jnp.float32)  107 us
    all_to_all x1, waiting for transfers between devices, shards(): lax.all_to_all(grads_low, 'dp', split_axis=0, concat_axis=0, tiled=True)  105 us
    all_to_all x1, waiting for transfers between devices, shards(): lax.all_to_all(expert_out.astype(jnp.bfloat16).reshape(dp_size, exp_dev,...  104 us
    psum x1, waiting for transfers between devices, shards(): lax.psum(jnp.concatenate([normed_grad_part, latent_grad_part], 1).astype(...  99.1 us
    psum x1, waiting for transfers between devices, shards(): lax.psum(jnp.concatenate([back_part, gate_cols.astype(jnp.bfloat16)], 1),...  79.5 us
    all_gather x1, waiting for transfers between devices, shards(): hidden_all = lax.all_gather(hidden, 'tensor', axis=0, tiled=True)  74 us
    all_gather x1, waiting for transfers between devices, shards(): first_all = lax.all_gather(first_pack, 'dp', axis=0, tiled=True)  70.8 us
  transfers between devices with their start and end apart: 13, of which 10 were waited for; matrix products, arithmetic and copies ran while one was open for 18% of the time, Pallas kernels for 3%

profile of v9, /device:TPU:0, one launch (start us, length us, event | category | flops | bytes accessed | tf_op | source)
XLA Modules:
  0.0 1686.1 jit_solution(2095115919696063712)
XLA Ops:
  17.5 74.0 %all-gather.5.cloned.1.call-done = bf16[1024,2048]{0,1:T(8,128)(2,1)} async-done(((bf16[128,2048]{0,1:T(8,128)(2,1)}), bf16[1024,2048]{0,1:T(8,128)(2,1)}) %all-gather.5.cloned.1.call-update) | async-done | bytes 4194320 | tf_op jit(solution)/shard_map/all_gather | solution.py:295
  104.8 70.8 %all-gather.7.cloned.1.call-done = bf16[2048,1090]{0,1:T(8,128)(2,1)} async-done(((bf16[128,1090]{0,1:T(8,128)(2,1)}), bf16[2048,1090]{0,1:T(8,128)(2,1)}) %all-gather.7.cloned.1.call-update) | async-done | bytes 4464656 | tf_op jit(solution)/shard_map/all_gather | solution.py:276
  231.4 106.8 %all-reduce.7.cloned.1.call-done = bf16[1024,2048]{0,1:T(8,128)(2,1)} async-done(((bf16[1024,2048]{0,1:T(8,128)(2,1)}), bf16[1024,2048]{0,1:T(8,128)(2,1)}) %all-reduce.7.cloned.1.call-update) | async-done | bytes 4194320 | tf_op jit(solution)/shard_map/psum | solution.py:367
  348.0 8.1 scatter_custom_fusion.tok_ref
  370.3 8.1 scatter_custom_fusion.1
  386.1 12.5 copy.228.both_hbm
  405.9 49.8 %shard_map.297 = bf16[2560,32,128]{2,1,0:T(8,128)(2,1)} custom-call(s32[2560]{0:T(1024)} %copy-done.72, bf16[1024,32,128]{2,1,0:T(8,128)(2,1)} %copy.228.both_hbm, f32[2,2560,1,128]{3,2,1,0:T(1,128)} %broadcast_in_dim.76.col_ref), custom_call_target="tpu_custom_call" | custom-call | flops 5242880 | bytes 41943040 | tf_op jit(solution)/shard_map/pallas_call | solution.py:120
  455.8 236.5 %all_to_all.30 = bf16[16,4,40,32,128]{4,3,2,1,0:T(8,128)(2,1)} all-to-all(bf16[16,4,40,32,128]{4,3,2,1,0:T(8,128)(2,1)} %bitcast.262), channel_id=1, replica_groups=mesh['dp'=16,'tensor'=8] {'dp'}, dimensions={0} | all-to-all | bytes 41943040 | tf_op jit(solution)/shard_map/all_to_all | solution.py:403
  692.2 31.4 %reshape.530 = bf16[16,4,40,4096]{3,2,1,0:T(8,128)(2,1)} reshape(bf16[16,4,40,32,128]{4,3,2,1,0:T(8,128)(2,1)} %all_to_all.30) | data formatting | bytes 41943040 | tf_op jit(solution)/shard_map/reshape | solution.py:404
  723.6 16.8 fusion.157
  740.4 8.8 fusion.11
  749.2 8.7 fusion.9
  757.9 11.4 fusion.41
  776.4 11.8 copy.237
  788.2 11.2 copy.180
  804.6 10.0 fusion.32
  814.6 15.1 add_convert_fusion
  829.7 12.0 copy.238
  841.7 103.8 %all-to-all-done.2 = bf16[16,4,40,16,128]{4,3,2,1,0:T(8,128)(2,1)} async-done(((bf16[16,4,40,16,128]{4,3,2,1,0:T(8,128)(2,1)}), bf16[16,4,40,16,128]{4,3,2,1,0:T(8,128)(2,1)}, u32[]{:S(2)}, u32[]{:S(2)}) %all-to-all-start.2) | async-done | bytes 10485792 | tf_op jit(solution)/shard_map/all_to_all | solution.py:416
  945.4 11.2 copy.181
  997.4 105.2 %all-to-all-done.3 = bf16[16,4,40,16,128]{4,3,2,1,0:T(8,128)(2,1)} async-done(((bf16[16,4,40,16,128]{4,3,2,1,0:T(8,128)(2,1)}), bf16[16,4,40,16,128]{4,3,2,1,0:T(8,128)(2,1)}, u32[]{:S(2)}, u32[]{:S(2)}) %all-to-all-start.3) | async-done | bytes 10485792 | tf_op jit(solution)/shard_map/all_to_all | solution.py:444
  1106.1 44.8 %shard_map.298 = (bf16[1024,16,128]{2,1,0:T(8,128)(2,1)}, bf16[1024,16,128]{2,1,0:T(8,128)(2,1)}, f32[1024,1,128]{2,1,0:T(1,128)}) custom-call(s32[2048]{0:T(1024)} %multiply_add_fusion.slot_ref, bf16[2560,16,128]{2,1,0:T(8,128)(2,1)} %bitcast.36.out_hbm, bf16[2560,16,128]{2,1,0:T(8,128)(2,1)} %bitcast.37.back_hbm, ...), custom_call_target="tpu_custom_call" | custom-call | flops 33554432 | bytes 46137344 | tf_op jit(solution)/shard_map/pallas_call | solution.py:192
  1186.0 63.9 %all-to-all-done.4 = bf16[8,128,2048]{2,1,0:T(8,128)(2,1)} async-done(((bf16[8,128,2048]{2,1,0:T(8,128)(2,1)}), bf16[8,128,2048]{2,1,0:T(8,128)(2,1)}, u32[]{:S(2)}, u32[]{:S(2)}) %all-to-all-start.4) | async-done | bytes 4194336 | tf_op jit(solution)/shard_map/all_to_all | solution.py:487
  1253.9 79.5 %all-reduce.9.cloned.1.call-done = bf16[1024,2050]{0,1:T(8,128)(2,1)} async-done(((bf16[1024,2050]{0,1:T(8,128)(2,1)}), bf16[1024,2050]{0,1:T(8,128)(2,1)}) %all-reduce.9.cloned.1.call-update) | async-done | bytes 4198416 | tf_op jit(solution)/shard_map/psum | solution.py:492
  1340.0 10.5 multiply_reduce_fusion
  1352.5 8.1 fusion.156
  1390.7 38.8 %all-to-all-done.5 = bf16[16,128,1056]{1,2,0:T(8,128)(2,1)} async-done(((bf16[16,128,1056]{1,2,0:T(8,128)(2,1)}), bf16[16,128,1056]{1,2,0:T(8,128)(2,1)}, u32[]{:S(2)}, u32[]{:S(2)}) %all-to-all-start.5) | async-done | bytes 4325408 | tf_op jit(solution)/shard_map/all_to_all | solution.py:507
  1436.9 10.9 pad_maximum_fusion.2
  1477.1 99.1 %all-reduce.11.cloned.1.call-done = bf16[1024,2624]{0,1:T(8,128)(2,1)} async-done(((bf16[1024,2624]{0,1:T(8,128)(2,1)}), bf16[1024,2624]{0,1:T(8,128)(2,1)}) %all-reduce.11.cloned.1.call-update) | async-done | bytes 5373968 | tf_op jit(solution)/shard_map/psum | solution.py:600
  1601.9 9.1 fusion.19
  1611.0 9.3 fusion.22
  1636.8 33.5 %reduce-scatter.2.cloned.1.call-done = f32[128,849]{0,1:T(8,128)} async-done(((f32[2048,849]{0,1:T(8,128)}), f32[128,849]{0,1:T(8,128)}) %reduce-scatter.2.cloned.1.call-update) | async-done | bytes 434704 | tf_op jit(solution)/shard_map/reduce_scatter | solution.py:657
  (445 shorter events, 338.1 us)
Async XLA Ops:
  7.2 750.7 %copy-start = (bf16[4,176,2048]{2,1,0:T(8,128)(2,1)S(1)}, bf16[4,176,2048]{2,1,0:T(8,128)(2,1)}, u32[]{:S(2)}) copy-start(bf16[4,176,2048]{2,1,0:T(8,128)(2,1)} %param.31) | copy-start | bytes 8650756
  7.2 84.3 %all-gather.5.cloned.1.call-start = ((), (), s32[]{:S(2)}) async-start(), calls=%async_computation.7 | async-start | bytes 4718592 | tf_op jit(solution)/shard_map/all_gather | solution.py:295
  9.5 166.2 %all-gather.7.cloned.1.call-start = ((), (), s32[]{:S(2)}) async-start(), calls=%async_computation.8 | async-start | bytes 4769792 | tf_op jit(solution)/shard_map/all_gather | solution.py:276
  94.1 99.5 %all-to-all-start = ((bf16[8,128,2048]{1,2,0:T(8,128)(2,1)}), bf16[8,128,2048]{1,2,0:T(8,128)(2,1)}, u32[]{:S(2)}, u32[]{:S(2)}) async-start(bf16[8,128,2048]{1,2,0:T(8,128)(2,1)} %broadcast_in_dim.62), calls=%async_computation | async-start | bytes 8388608 | tf_op jit(solution)/shard_map/all_to_all | solution.py:298
  98.8 125.7 %all-gather.9.cloned.1.call-start = ((), (), s32[]{:S(2)}) async-start(), calls=%async_computation.9 | async-start | bytes 1427456 | tf_op jit(solution)/shard_map/all_gather | solution.py:289
  99.5 238.6 %all-reduce.7.cloned.1.call-start = ((), (), s32[]{:S(2)}) async-start(), calls=%async_computation.10 | async-start | bytes 8388608 | tf_op jit(solution)/shard_map/psum | solution.py:367
  100.3 113.8 %copy-start.102 = (f32[32]{0:T(128)}, f32[32]{0:T(128)S(1)}, u32[]{:S(2)}) copy-start(f32[32]{0:T(128)S(1)} %multiply_power_fusion) | copy-start | bytes 388
  100.3 113.7 %copy-start.83 = (f32[1024]{0:T(1024)}, f32[1024]{0:T(1024)S(1)}, u32[]{:S(2)}) copy-start(f32[1024]{0:T(1024)S(1)} %iota_convert_fusion) | copy-start | bytes 12292
  104.8 86.2 %copy-start.81 = (f32[1024]{0:T(1024)}, f32[1024]{0:T(1024)S(1)}, u32[]{:S(2)}) copy-start(f32[1024]{0:T(1024)S(1)} %add_rsqrt_fusion.2) | copy-start | bytes 12292
  176.5 14.5 copy-start.66
  176.6 31.2 %copy-start.89 = (f32[512]{0:T(512)}, f32[512]{0:T(512)S(1)}, u32[]{:S(2)}) copy-start(f32[512]{0:T(512)S(1)} %reshape.501) | copy-start | bytes 6148
  210.4 12.8 copy-start.17
  229.3 226.5 %all-gather.11.cloned.1.call-start = ((), (), s32[]{:S(2)}) async-start(), calls=%async_computation.11 | async-start | bytes 4595712 | tf_op jit(solution)/shard_map/all_gather | solution.py:398
  231.4 113.2 %copy-start.68 = (s32[1024,2]{0,1:T(2,128)S(1)}, s32[1024,2]{0,1:T(2,128)}, u32[]{:S(2)}) copy-start(s32[1024,2]{0,1:T(2,128)} %param.19) | copy-start | bytes 24580
  723.6 16.8 copy-start.31
  799.4 146.0 %all-to-all-start.2 = ((bf16[16,4,40,16,128]{4,3,2,1,0:T(8,128)(2,1)}), bf16[16,4,40,16,128]{4,3,2,1,0:T(8,128)(2,1)}, u32[]{:S(2)}, u32[]{:S(2)}) async-start(bf16[16,4,40,16,128]{4,3,2,1,0:T(8,128)(2,1)} %copy.180), calls=%async_computation.2 | async-start | bytes 20971520 | tf_op jit(solution)/shard_map/all_to_all | solution.py:416
  956.7 145.9 %all-to-all-start.3 = ((bf16[16,4,40,16,128]{4,3,2,1,0:T(8,128)(2,1)}), bf16[16,4,40,16,128]{4,3,2,1,0:T(8,128)(2,1)}, u32[]{:S(2)}, u32[]{:S(2)}) async-start(bf16[16,4,40,16,128]{4,3,2,1,0:T(8,128)(2,1)} %copy.181), calls=%async_computation.3 | async-start | bytes 20971520 | tf_op jit(solution)/shard_map/all_to_all | solution.py:444
  961.7 371.7 %all-reduce.9.cloned.1.call-start = ((), (), s32[]{:S(2)}) async-start(), calls=%async_computation.12 | async-start | bytes 8421376 | tf_op jit(solution)/shard_map/psum | solution.py:492
  962.4 14.8 slice-start.7
  1170.3 79.6 %all-to-all-start.4 = ((bf16[8,128,2048]{2,1,0:T(8,128)(2,1)}), bf16[8,128,2048]{2,1,0:T(8,128)(2,1)}, u32[]{:S(2)}, u32[]{:S(2)}) async-start(bf16[8,128,2048]{2,1,0:T(8,128)(2,1)} %reshape_reshape.3), calls=%async_computation.4 | async-start | bytes 8388608 | tf_op jit(solution)/shard_map/all_to_all | solution.py:487
  1253.9 86.0 %copy-start.69 = (s32[1024,2]{0,1:T(2,128)S(1)}, s32[1024,2]{0,1:T(2,128)}, u32[]{:S(2)}) copy-start(s32[1024,2]{0,1:T(2,128)} %param.19) | copy-start | bytes 24580
  1253.9 86.1 %copy-start.41 = (bf16[2048,321]{0,1:T(8,128)(2,1)S(1)}, bf16[2048,321]{0,1:T(8,128)(2,1)}, u32[]{:S(2)}) copy-start(bf16[2048,321]{0,1:T(8,128)(2,1)} %all-gather.9.cloned.1.call-done) | copy-start | bytes 3944452
  1253.9 86.1 %copy-start.71 = (f32[2048,1]{0,1:T(1,128)S(1)}, f32[2048,1]{0,1:T(1,128)}, u32[]{:S(2)}) copy-start(f32[2048,1]{0,1:T(1,128)} %copy-done.70) | copy-start | bytes 24580
  1340.0 12.5 copy-start.10
  1340.0 24.0 %slice-start.2 = ((s8[4325376]{0:T(1024)(128)(4,1)}), s8[4194304]{0:T(1024)(128)(4,1)S(1)}, s32[]{:S(2)}) async-start(s8[4325376]{0:T(1024)(128)(4,1)} %bitcast.273), calls=%async_computation.17 | async-start | bytes 8388608
  1366.9 62.7 %all-to-all-start.5 = ((bf16[16,128,1056]{1,2,0:T(8,128)(2,1)}), bf16[16,128,1056]{1,2,0:T(8,128)(2,1)}, u32[]{:S(2)}, u32[]{:S(2)}) async-start(bf16[16,128,1056]{1,2,0:T(8,128)(2,1)} %copy_bitcast_fusion), calls=%async_computation.5 | async-start | bytes 8650752 | tf_op jit(solution)/shard_map/all_to_all | solution.py:507
  1371.7 204.4 %all-reduce.11.cloned.1.call-start = ((), (), s32[]{:S(2)}) async-start(), calls=%async_computation.13 | async-start | bytes 10747904 | tf_op jit(solution)/shard_map/psum | solution.py:600
  1389.0 44.3 %copy-start.47 = (bf16[2048,384]{0,1:T(8,128)(2,1)S(1)}, bf16[2048,384]{0,1:T(8,128)(2,1)}, u32[]{:S(2)}) copy-start(bf16[2048,384]{0,1:T(8,128)(2,1)} %slice.282) | copy-start | bytes 4718596
  1447.8 222.5 %reduce-scatter.2.cloned.1.call-start = ((), (), s32[]{:S(2)}) async-start(), calls=%async_computation.14 | async-start | bytes 7450624 | tf_op jit(solution)/shard_map/reduce_scatter | solution.py:657
  1601.9 18.4 %slice-start.4 = ((s8[10485760]{0:T(1024)(128)(4,1)}), s8[4194304]{0:T(1024)(128)(4,1)S(1)}, s32[]{:S(2)}) async-start(s8[10485760]{0:T(1024)(128)(4,1)} %bitcast.277), calls=%async_computation.19 | async-start | bytes 8388608
  1601.9 18.4 %slice-start.5 = ((s8[10485760]{0:T(1024)(128)(4,1)}), s8[4194304]{0:T(1024)(128)(4,1)S(1)}, s32[]{:S(2)}) async-start(s8[10485760]{0:T(1024)(128)(4,1)} %bitcast.277), calls=%async_computation.20 | async-start | bytes 8388608
  1628.8 50.2 %copy-start.1 = (bf16[4,176,2048]{2,1,0:T(8,128)(2,1)S(1)}, bf16[4,176,2048]{2,1,0:T(8,128)(2,1)}, u32[]{:S(2)}) copy-start(bf16[4,176,2048]{2,1,0:T(8,128)(2,1)} %param.31) | copy-start | bytes 8650756
  (95 other events, 447.8 us)
Sparse Core Ops, SparseCore 0:
  10.8 80.6 all-gather.4
  93.7 81.8 all-gather.6
  177.9 33.7 all-gather.8
  229.4 108.7 all-reduce.6
  344.8 44.0 all-gather.10
  1163.1 170.2 all-reduce.8
  1447.9 128.1 all-reduce.10
  1600.7 69.4 reduce-scatter.1

commit v10 on v9

--- a/solution.py
+++ b/solution.py
@@ -364,18 +364,8 @@
     attn_part = jnp.einsum(
         "tk,dk->td", mixed_all, output_weights_t, preferred_element_type=jnp.float32
     )
-    branch_all = lax.psum(attn_part.astype(jnp.bfloat16), "tensor").astype(jnp.float32)
-    shared_local, branch_all = lax.optimization_barrier((shared_local, branch_all))
-    residual_all = hidden_all_f + branch_all
-    residual_own = lax.dynamic_slice_in_dim(residual_all, start_row, tok_dev, 0)
-    scale_two = norm_scale(residual_all)
-    gain_two = second_gains.astype(jnp.float32)
-    normed_two = (residual_all * scale_two * gain_two).astype(jnp.bfloat16)
-    logits = jnp.dot(normed_two, router_weights, preferred_element_type=jnp.float32)
     top_count = routes.shape[1]
     chosen_hot = routes[:, :, None] == jnp.arange(experts)[None, None, :]
-    chosen_logits = jnp.sum(jnp.where(chosen_hot, logits[:, None, :], 0.0), -1)
-    gate_values = jax.nn.softmax(chosen_logits, axis=-1)
     assignments = seq_len * top_count
     flat_hot = chosen_hot.reshape(assignments, experts).astype(jnp.bfloat16)
     lower = (jnp.arange(assignments)[:, None] > jnp.arange(assignments)[None, :]).astype(jnp.bfloat16)
@@ -387,10 +377,23 @@
     slot_index = expert_ids * capacity + slot_pos
     token_ids = jnp.arange(seq_len * top_count) // top_count
     slot_token = jnp.full((experts * capacity,), seq_len, jnp.int32).at[slot_index].set(token_ids)
+    slot_valid = (slot_token < seq_len).astype(jnp.float32)
+    slot_index, slot_token, slot_valid, attn_part = lax.optimization_barrier(
+        (slot_index, slot_token, slot_valid, attn_part)
+    )
+    branch_all = lax.psum(attn_part.astype(jnp.bfloat16), "tensor").astype(jnp.float32)
+    shared_local, branch_all = lax.optimization_barrier((shared_local, branch_all))
+    residual_all = hidden_all_f + branch_all
+    residual_own = lax.dynamic_slice_in_dim(residual_all, start_row, tok_dev, 0)
+    scale_two = norm_scale(residual_all)
+    gain_two = second_gains.astype(jnp.float32)
+    normed_two = (residual_all * scale_two * gain_two).astype(jnp.bfloat16)
+    logits = jnp.dot(normed_two, router_weights, preferred_element_type=jnp.float32)
+    chosen_logits = jnp.sum(jnp.where(chosen_hot, logits[:, None, :], 0.0), -1)
+    gate_values = jax.nn.softmax(chosen_logits, axis=-1)
     slot_gate = (
         jnp.zeros((experts * capacity,), jnp.float32).at[slot_index].set(gate_values.reshape(-1))
     )
-    slot_valid = (slot_token < seq_len).astype(jnp.float32)
     tile_rows = D // 128
     send_both = dispatch_rows(slot_token, normed_two, grad_seq, slot_valid, slot_gate).reshape(
         dp_size, exp_dev, capacity, 2 * tile_rows, 128

time: 1700 us -> 1690 us (level)
    unnamed x240 -> x232, local copies, waits for them, and re-layouts: 59.3 us -> 60.9 us
where the time goes in v10:
time: 1690 us; the launch traced here: 1680 us
  waiting for transfers between devices  761 us (45%)
  local copies, waits for them, and re-layouts  256 us (15%)
  blocking collectives  237 us (14%)
  matrix products  183 us (11%)
  other arithmetic  107 us (6%)
  Pallas kernels  96.3 us (6%)
  starting transfers between devices  25.1 us (1%)
  between operations  17 us (1%)
    all_to_all x1, blocking collectives, shards(): lax.all_to_all(send_both, 'dp', split_axis=0, concat_axis=0, tiled=True)  237 us
    psum x1, waiting for transfers between devices, shards(): lax.psum(attn_part.astype(jnp.bfloat16), 'tensor').astype(jnp.float32)  107 us
    all_to_all x1, waiting for transfers between devices, shards(): lax.all_to_all(grads_low, 'dp', split_axis=0, concat_axis=0, tiled=True)  106 us
    all_to_all x1, waiting for transfers between devices, shards(): lax.all_to_all(expert_out.astype(jnp.bfloat16).reshape(dp_size, exp_dev,...  104 us
    psum x1, waiting for transfers between devices, shards(): lax.psum(jnp.concatenate([normed_grad_part, latent_grad_part], 1).astype(...  99.1 us
    psum x1, waiting for transfers between devices, shards(): lax.psum(jnp.concatenate([back_part, gate_cols.astype(jnp.bfloat16)], 1),...  79.5 us
    all_gather x1, waiting for transfers between devices, shards(): hidden_all = lax.all_gather(hidden, 'tensor', axis=0, tiled=True)  67 us
    all_to_all x1, waiting for transfers between devices, shards(): lax.all_to_all(feed_part.reshape(tensor_size, tok_dev, D), 'tensor', spli...  63.4 us
  transfers between devices with their start and end apart: 13, of which 10 were waited for; matrix products, arithmetic and copies ran while one was open for 18% of the time, Pallas kernels for 3%

profile of v10, /device:TPU:0, one launch (start us, length us, event | category | flops | bytes accessed | tf_op | source)
XLA Modules:
  0.0 1682.3 jit_solution(4951824039129692188)
XLA Ops:
  24.5 67.0 %all-gather.5.cloned.1.call-done = bf16[1024,2048]{0,1:T(8,128)(2,1)} async-done(((bf16[128,2048]{0,1:T(8,128)(2,1)}), bf16[1024,2048]{0,1:T(8,128)(2,1)}) %all-gather.5.cloned.1.call-update) | async-done | bytes 4194320 | tf_op jit(solution)/shard_map/all_gather | solution.py:295
  99.4 8.4 scatter_custom_fusion.tok_ref
  112.5 63.2 %all-gather.7.cloned.1.call-done = bf16[2048,1090]{0,1:T(8,128)(2,1)} async-done(((bf16[128,1090]{0,1:T(8,128)(2,1)}), bf16[2048,1090]{0,1:T(8,128)(2,1)}) %all-gather.7.cloned.1.call-update) | async-done | bytes 4464656 | tf_op jit(solution)/shard_map/all_gather | solution.py:276
  237.6 107.1 %all-reduce.7.cloned.1.call-done = bf16[1024,2048]{0,1:T(8,128)(2,1)} async-done(((bf16[1024,2048]{0,1:T(8,128)(2,1)}), bf16[1024,2048]{0,1:T(8,128)(2,1)}) %all-reduce.7.cloned.1.call-update) | async-done | bytes 4194320 | tf_op jit(solution)/shard_map/psum | solution.py:384
  365.2 8.1 scatter_custom_fusion.1
  381.2 12.5 copy.227.both_hbm
  401.0 51.5 %shard_map.297 = bf16[2560,32,128]{2,1,0:T(8,128)(2,1)} custom-call(s32[2560]{0:T(1024)} %copy-done.72, bf16[1024,32,128]{2,1,0:T(8,128)(2,1)} %copy.227.both_hbm, f32[2,2560,1,128]{3,2,1,0:T(1,128)} %broadcast_in_dim.79.col_ref), custom_call_target="tpu_custom_call" | custom-call | flops 5242880 | bytes 41943040 | tf_op jit(solution)/shard_map/pallas_call | solution.py:120
  452.6 236.5 %all_to_all.30 = bf16[16,4,40,32,128]{4,3,2,1,0:T(8,128)(2,1)} all-to-all(bf16[16,4,40,32,128]{4,3,2,1,0:T(8,128)(2,1)} %bitcast.262), channel_id=1, replica_groups=mesh['dp'=16,'tensor'=8] {'dp'}, dimensions={0} | all-to-all | bytes 41943040 | tf_op jit(solution)/shard_map/all_to_all | solution.py:406
  689.1 31.3 %reshape.530 = bf16[16,4,40,4096]{3,2,1,0:T(8,128)(2,1)} reshape(bf16[16,4,40,32,128]{4,3,2,1,0:T(8,128)(2,1)} %all_to_all.30) | data formatting | bytes 41943040 | tf_op jit(solution)/shard_map/reshape | solution.py:407
  720.4 16.8 %fusion.158 = (bf16[16,4,40,2048]{3,2,1,0:T(8,128)(2,1)}, bf16[16,4,40,2048]{3,2,1,0:T(8,128)(2,1)}) fusion(bf16[16,4,40,4096]{3,2,1,0:T(8,128)(2,1)} %reshape.530), kind=kLoop, calls=%fused_computation.283 | loop fusion | bytes 41943040 | tf_op jit(solution)/shard_map/slice | solution.py:409
  737.2 8.8 fusion.11
  746.0 8.7 fusion.9
  754.7 11.4 fusion.41
  773.3 11.8 copy.236
  785.1 11.2 copy.180
  801.4 9.9 fusion.32
  811.3 15.1 add_convert_fusion
  826.4 12.0 copy.237
  838.4 103.9 %all-to-all-done.2 = bf16[16,4,40,16,128]{4,3,2,1,0:T(8,128)(2,1)} async-done(((bf16[16,4,40,16,128]{4,3,2,1,0:T(8,128)(2,1)}), bf16[16,4,40,16,128]{4,3,2,1,0:T(8,128)(2,1)}, u32[]{:S(2)}, u32[]{:S(2)}) %all-to-all-start.2) | async-done | bytes 10485792 | tf_op jit(solution)/shard_map/all_to_all | solution.py:419
  942.3 11.2 copy.181
  993.4 105.8 %all-to-all-done.3 = bf16[16,4,40,16,128]{4,3,2,1,0:T(8,128)(2,1)} async-done(((bf16[16,4,40,16,128]{4,3,2,1,0:T(8,128)(2,1)}), bf16[16,4,40,16,128]{4,3,2,1,0:T(8,128)(2,1)}, u32[]{:S(2)}, u32[]{:S(2)}) %all-to-all-start.3) | async-done | bytes 10485792 | tf_op jit(solution)/shard_map/all_to_all | solution.py:447
  1102.8 44.8 %shard_map.298 = (bf16[1024,16,128]{2,1,0:T(8,128)(2,1)}, bf16[1024,16,128]{2,1,0:T(8,128)(2,1)}, f32[1024,1,128]{2,1,0:T(1,128)}) custom-call(s32[2048]{0:T(1024)} %copy-done.78, bf16[2560,16,128]{2,1,0:T(8,128)(2,1)} %bitcast.36.out_hbm, bf16[2560,16,128]{2,1,0:T(8,128)(2,1)} %bitcast.37.back_hbm, f32[2,1024,1,128]{3,2,1,0:T(1,128)} %broadcast_in_dim.80.gate_ref, ...), custom_call_target="tpu_custom_call" | custom-call | flops 33554432 | bytes 46137344 | tf_op jit(solution)/shard_map/pallas_call | solution.py:192
  1182.7 63.4 %all-to-all-done.4 = bf16[8,128,2048]{2,1,0:T(8,128)(2,1)} async-done(((bf16[8,128,2048]{2,1,0:T(8,128)(2,1)}), bf16[8,128,2048]{2,1,0:T(8,128)(2,1)}, u32[]{:S(2)}, u32[]{:S(2)}) %all-to-all-start.4) | async-done | bytes 4194336 | tf_op jit(solution)/shard_map/all_to_all | solution.py:490
  1250.1 79.5 %all-reduce.9.cloned.1.call-done = bf16[1024,2050]{0,1:T(8,128)(2,1)} async-done(((bf16[1024,2050]{0,1:T(8,128)(2,1)}), bf16[1024,2050]{0,1:T(8,128)(2,1)}) %all-reduce.9.cloned.1.call-update) | async-done | bytes 4198416 | tf_op jit(solution)/shard_map/psum | solution.py:495
  1336.2 10.5 multiply_reduce_fusion
  1348.7 8.1 fusion.157
  1386.9 38.8 %all-to-all-done.5 = bf16[16,128,1056]{1,2,0:T(8,128)(2,1)} async-done(((bf16[16,128,1056]{1,2,0:T(8,128)(2,1)}), bf16[16,128,1056]{1,2,0:T(8,128)(2,1)}, u32[]{:S(2)}, u32[]{:S(2)}) %all-to-all-start.5) | async-done | bytes 4325408 | tf_op jit(solution)/shard_map/all_to_all | solution.py:510
  1433.1 10.9 pad_maximum_fusion.2
  1473.3 99.1 %all-reduce.11.cloned.1.call-done = bf16[1024,2624]{0,1:T(8,128)(2,1)} async-done(((bf16[1024,2624]{0,1:T(8,128)(2,1)}), bf16[1024,2624]{0,1:T(8,128)(2,1)}) %all-reduce.11.cloned.1.call-update) | async-done | bytes 5373968 | tf_op jit(solution)/shard_map/psum | solution.py:603
  1598.1 9.1 fusion.19
  1607.2 9.3 fusion.22
  1633.0 33.5 %reduce-scatter.2.cloned.1.call-done = f32[128,849]{0,1:T(8,128)} async-done(((f32[2048,849]{0,1:T(8,128)}), f32[128,849]{0,1:T(8,128)}) %reduce-scatter.2.cloned.1.call-update) | async-done | bytes 434704 | tf_op jit(solution)/shard_map/reduce_scatter | solution.py:660
  (439 shorter events, 346.4 us)
Async XLA Ops:
  7.2 747.5 %copy-start = (bf16[4,176,2048]{2,1,0:T(8,128)(2,1)S(1)}, bf16[4,176,2048]{2,1,0:T(8,128)(2,1)}, u32[]{:S(2)}) copy-start(bf16[4,176,2048]{2,1,0:T(8,128)(2,1)} %param.31) | copy-start | bytes 8650756
  7.2 84.3 %all-gather.5.cloned.1.call-start = ((), (), s32[]{:S(2)}) async-start(), calls=%async_computation.7 | async-start | bytes 4718592 | tf_op jit(solution)/shard_map/all_gather | solution.py:295
  9.5 166.2 %all-gather.7.cloned.1.call-start = ((), (), s32[]{:S(2)}) async-start(), calls=%async_computation.8 | async-start | bytes 4769792 | tf_op jit(solution)/shard_map/all_gather | solution.py:276
  16.2 208.6 %all-gather.9.cloned.1.call-start = ((), (), s32[]{:S(2)}) async-start(), calls=%async_computation.9 | async-start | bytes 1427456 | tf_op jit(solution)/shard_map/all_gather | solution.py:289
  94.1 99.6 %all-to-all-start = ((bf16[8,128,2048]{1,2,0:T(8,128)(2,1)}), bf16[8,128,2048]{1,2,0:T(8,128)(2,1)}, u32[]{:S(2)}, u32[]{:S(2)}) async-start(bf16[8,128,2048]{1,2,0:T(8,128)(2,1)} %broadcast_in_dim.64), calls=%async_computation | async-start | bytes 8388608 | tf_op jit(solution)/shard_map/all_to_all | solution.py:298
  98.8 246.0 %all-reduce.7.cloned.1.call-start = ((), (), s32[]{:S(2)}) async-start(), calls=%async_computation.10 | async-start | bytes 8388608 | tf_op jit(solution)/shard_map/psum | solution.py:384
  107.8 74.9 %copy-start.72 = (s32[2560]{0:T(1024)}, s32[2560]{0:T(1024)S(1)}, u32[]{:S(2)}) copy-start(s32[2560]{0:T(1024)S(1)} %scatter_custom_fusion.tok_ref) | copy-start | bytes 30724
  107.8 106.5 %copy-start.99 = (f32[32]{0:T(128)}, f32[32]{0:T(128)S(1)}, u32[]{:S(2)}) copy-start(f32[32]{0:T(128)S(1)} %multiply_power_fusion) | copy-start | bytes 388
  107.9 106.5 %copy-start.85 = (f32[1024]{0:T(1024)}, f32[1024]{0:T(1024)S(1)}, u32[]{:S(2)}) copy-start(f32[1024]{0:T(1024)S(1)} %iota_convert_fusion) | copy-start | bytes 12292
  107.9 244.1 %copy-start.78 = (s32[2048]{0:T(1024)}, s32[2048]{0:T(1024)S(1)}, u32[]{:S(2)}) copy-start(s32[2048]{0:T(1024)S(1)} %multiply_add_fusion.slot_ref) | copy-start | bytes 24580
  112.5 78.6 %copy-start.83 = (f32[1024]{0:T(1024)}, f32[1024]{0:T(1024)S(1)}, u32[]{:S(2)}) copy-start(f32[1024]{0:T(1024)S(1)} %add_rsqrt_fusion.2) | copy-start | bytes 12292
  176.6 14.5 copy-start.66
  176.7 31.5 %copy-start.91 = (f32[512]{0:T(512)}, f32[512]{0:T(512)S(1)}, u32[]{:S(2)}) copy-start(f32[512]{0:T(512)S(1)} %reshape.501) | copy-start | bytes 6148
  210.7 12.8 copy-start.17
  236.0 216.6 %all-gather.11.cloned.1.call-start = ((), (), s32[]{:S(2)}) async-start(), calls=%async_computation.11 | async-start | bytes 4595712 | tf_op jit(solution)/shard_map/all_gather | solution.py:401
  720.4 16.8 %copy-start.33 = (bf16[4,176,2048]{2,1,0:T(8,128)(2,1)S(1)}, bf16[4,176,2048]{2,1,0:T(8,128)(2,1)}, u32[]{:S(2)}) copy-start(bf16[4,176,2048]{2,1,0:T(8,128)(2,1)} %param.29) | copy-start | bytes 8650756
  796.3 146.0 %all-to-all-start.2 = ((bf16[16,4,40,16,128]{4,3,2,1,0:T(8,128)(2,1)}), bf16[16,4,40,16,128]{4,3,2,1,0:T(8,128)(2,1)}, u32[]{:S(2)}, u32[]{:S(2)}) async-start(bf16[16,4,40,16,128]{4,3,2,1,0:T(8,128)(2,1)} %copy.180), calls=%async_computation.2 | async-start | bytes 20971520 | tf_op jit(solution)/shard_map/all_to_all | solution.py:419
  953.5 145.8 %all-to-all-start.3 = ((bf16[16,4,40,16,128]{4,3,2,1,0:T(8,128)(2,1)}), bf16[16,4,40,16,128]{4,3,2,1,0:T(8,128)(2,1)}, u32[]{:S(2)}, u32[]{:S(2)}) async-start(bf16[16,4,40,16,128]{4,3,2,1,0:T(8,128)(2,1)} %copy.181), calls=%async_computation.3 | async-start | bytes 20971520 | tf_op jit(solution)/shard_map/all_to_all | solution.py:447
  958.4 371.2 %all-reduce.9.cloned.1.call-start = ((), (), s32[]{:S(2)}) async-start(), calls=%async_computation.12 | async-start | bytes 8421376 | tf_op jit(solution)/shard_map/psum | solution.py:495
  958.5 14.7 slice-start.7
  1167.0 79.1 %all-to-all-start.4 = ((bf16[8,128,2048]{2,1,0:T(8,128)(2,1)}), bf16[8,128,2048]{2,1,0:T(8,128)(2,1)}, u32[]{:S(2)}, u32[]{:S(2)}) async-start(bf16[8,128,2048]{2,1,0:T(8,128)(2,1)} %reshape_reshape.3), calls=%async_computation.4 | async-start | bytes 8388608 | tf_op jit(solution)/shard_map/all_to_all | solution.py:490
  1250.1 86.0 %copy-start.69 = (s32[1024,2]{0,1:T(2,128)S(1)}, s32[1024,2]{0,1:T(2,128)}, u32[]{:S(2)}) copy-start(s32[1024,2]{0,1:T(2,128)} %param.19) | copy-start | bytes 24580
  1250.1 86.1 %copy-start.41 = (bf16[2048,321]{0,1:T(8,128)(2,1)S(1)}, bf16[2048,321]{0,1:T(8,128)(2,1)}, u32[]{:S(2)}) copy-start(bf16[2048,321]{0,1:T(8,128)(2,1)} %all-gather.9.cloned.1.call-done) | copy-start | bytes 3944452
  1250.1 86.1 %copy-start.71 = (f32[2048,1]{0,1:T(1,128)S(1)}, f32[2048,1]{0,1:T(1,128)}, u32[]{:S(2)}) copy-start(f32[2048,1]{0,1:T(1,128)} %copy-done.70) | copy-start | bytes 24580
  1336.2 24.0 %slice-start.2 = ((s8[4325376]{0:T(1024)(128)(4,1)}), s8[4194304]{0:T(1024)(128)(4,1)S(1)}, s32[]{:S(2)}) async-start(s8[4325376]{0:T(1024)(128)(4,1)} %bitcast.273), calls=%async_computation.17 | async-start | bytes 8388608
  1363.1 62.7 %all-to-all-start.5 = ((bf16[16,128,1056]{1,2,0:T(8,128)(2,1)}), bf16[16,128,1056]{1,2,0:T(8,128)(2,1)}, u32[]{:S(2)}, u32[]{:S(2)}) async-start(bf16[16,128,1056]{1,2,0:T(8,128)(2,1)} %copy_bitcast_fusion), calls=%async_computation.5 | async-start | bytes 8650752 | tf_op jit(solution)/shard_map/all_to_all | solution.py:510
  1367.9 204.4 %all-reduce.11.cloned.1.call-start = ((), (), s32[]{:S(2)}) async-start(), calls=%async_computation.13 | async-start | bytes 10747904 | tf_op jit(solution)/shard_map/psum | solution.py:603
  1385.2 44.3 %copy-start.47 = (bf16[2048,384]{0,1:T(8,128)(2,1)S(1)}, bf16[2048,384]{0,1:T(8,128)(2,1)}, u32[]{:S(2)}) copy-start(bf16[2048,384]{0,1:T(8,128)(2,1)} %slice.282) | copy-start | bytes 4718596
  1444.0 222.5 %reduce-scatter.2.cloned.1.call-start = ((), (), s32[]{:S(2)}) async-start(), calls=%async_computation.14 | async-start | bytes 7450624 | tf_op jit(solution)/shard_map/reduce_scatter | solution.py:660
  1598.1 18.4 %slice-start.4 = ((s8[10485760]{0:T(1024)(128)(4,1)}), s8[4194304]{0:T(1024)(128)(4,1)S(1)}, s32[]{:S(2)}) async-start(s8[10485760]{0:T(1024)(128)(4,1)} %bitcast.277), calls=%async_computation.19 | async-start | bytes 8388608
  1598.1 18.4 %slice-start.5 = ((s8[10485760]{0:T(1024)(128)(4,1)}), s8[4194304]{0:T(1024)(128)(4,1)S(1)}, s32[]{:S(2)}) async-start(s8[10485760]{0:T(1024)(128)(4,1)} %bitcast.277), calls=%async_computation.20 | async-start | bytes 8388608
  1625.1 50.2 %copy-start.1 = (bf16[4,176,2048]{2,1,0:T(8,128)(2,1)S(1)}, bf16[4,176,2048]{2,1,0:T(8,128)(2,1)}, u32[]{:S(2)}) copy-start(bf16[4,176,2048]{2,1,0:T(8,128)(2,1)} %param.31) | copy-start | bytes 8650756
  (91 other events, 434.2 us)
Sparse Core Ops, SparseCore 0:
  10.8 80.6 all-gather.4
  93.7 81.9 all-gather.6
  177.9 33.7 all-gather.8
  236.1 108.6 all-reduce.6
  351.3 44.3 all-gather.10
  1159.7 169.8 all-reduce.8
  1444.1 128.1 all-reduce.10
  1597.0 69.4 reduce-scatter.1

commit v11 on v10

--- a/solution.py
+++ b/solution.py
@@ -87,27 +87,39 @@
 
 
 def dispatch_kernel(tok_ref, both_hbm, col_ref, out_ref, both_buf, sems):
-    block = both_buf.shape[0]
-    tile_rows = both_buf.shape[1] // 2
+    block = both_buf.shape[1]
+    tile_rows = both_buf.shape[2] // 2
     last = both_hbm.shape[0] - 1
-    base = pl.program_id(0) * block
-
-    def start(r, carry):
-        tok = jnp.minimum(tok_ref[base + r], last)
-        pltpu.make_async_copy(both_hbm.at[tok], both_buf.at[r], sems.at[r]).start()
+    step = pl.program_id(0)
+    steps = pl.num_programs(0)
+
+    def fetch(index, slot):
+        def start(r, carry):
+            tok = jnp.minimum(tok_ref[index * block + r], last)
+            pltpu.make_async_copy(both_hbm.at[tok], both_buf.at[slot, r], sems.at[slot, r]).start()
+            return carry
+
+        lax.fori_loop(0, block, start, 0, unroll=4)
+
+    @pl.when(step == 0)
+    def _():
+        fetch(0, 0)
+
+    @pl.when(step + 1 < steps)
+    def _():
+        fetch(step + 1, (step + 1) % 2)
+
+    slot = step % 2
+
+    def finish(r, carry):
+        pltpu.make_async_copy(both_hbm.at[0], both_buf.at[slot, r], sems.at[slot, r]).wait()
         return carry
 
-    lax.fori_loop(0, block, start, 0, unroll=4)
-
-    def finish(r, carry):
-        pltpu.make_async_copy(both_hbm.at[0], both_buf.at[r], sems.at[r]).wait()
-        return carry
-
     lax.fori_loop(0, block, finish, 0, unroll=4)
-    rows = both_buf[:, :tile_rows, :]
+    rows = both_buf[slot, :, :tile_rows, :]
     out_ref[:, :tile_rows, :] = jnp.where(col_ref[0] > 0, rows, jnp.zeros_like(rows))
     out_ref[:, tile_rows:, :] = (
-        both_buf[:, tile_rows:, :].astype(jnp.float32) * col_ref[1]
+        both_buf[slot, :, tile_rows:, :].astype(jnp.float32) * col_ref[1]
     ).astype(out_ref.dtype)
 
 
@@ -129,10 +141,11 @@
             ],
             out_specs=pl.BlockSpec((block, 2 * tile_rows, 128), lambda i, tok: (i, 0, 0)),
             scratch_shapes=[
-                pltpu.VMEM((block, 2 * tile_rows, 128), rows.dtype),
-                pltpu.SemaphoreType.DMA((block,)),
+                pltpu.VMEM((2, block, 2 * tile_rows, 128), rows.dtype),
+                pltpu.SemaphoreType.DMA((2, block)),
             ],
         ),
+        compiler_params=pltpu.CompilerParams(dimension_semantics=("arbitrary",)),
         cost_estimate=pl.CostEstimate(
             flops=slots * width, transcendentals=0, bytes_accessed=4 * slots * 2 * width
         ),

time: 1690 us -> 1680 us (level)
  transfers between devices with their start and end apart: 13 -> 13, of which waited for: 10 -> 10; matrix products, arithmetic and copies ran while one was open for 18% -> 18% of each run, Pallas kernels for 3% -> 2%
where the time goes in v11:
time: 1680 us; the launch traced here: 1670 us
  waiting for transfers between devices  762 us (45%)
  local copies, waits for them, and re-layouts  256 us (15%)
  blocking collectives  237 us (14%)
  matrix products  183 us (11%)
  other arithmetic  107 us (6%)
  Pallas kernels  81.1 us (5%)
  starting transfers between devices  25.1 us (1%)
  between operations  17 us (1%)
    all_to_all x1, blocking collectives, shards(): lax.all_to_all(send_both, 'dp', split_axis=0, concat_axis=0, tiled=True)  237 us
    psum x1, waiting for transfers between devices, shards(): lax.psum(attn_part.astype(jnp.bfloat16), 'tensor').astype(jnp.float32)  107 us
    all_to_all x1, waiting for transfers between devices, shards(): lax.all_to_all(grads_low, 'dp', split_axis=0, concat_axis=0, tiled=True)  106 us
    all_to_all x1, waiting for transfers between devices, shards(): lax.all_to_all(expert_out.astype(jnp.bfloat16).reshape(dp_size, exp_dev,...  104 us
    psum x1, waiting for transfers between devices, shards(): lax.psum(jnp.concatenate([normed_grad_part, latent_grad_part], 1).astype(...  99.1 us
    psum x1, waiting for transfers between devices, shards(): lax.psum(jnp.concatenate([back_part, gate_cols.astype(jnp.bfloat16)], 1),...  79.7 us
    all_gather x1, waiting for transfers between devices, shards(): hidden_all = lax.all_gather(hidden, 'tensor', axis=0, tiled=True)  67 us
    all_to_all x1, waiting for transfers between devices, shards(): lax.all_to_all(feed_part.reshape(tensor_size, tok_dev, D), 'tensor', spli...  63.4 us
  transfers between devices with their start and end apart: 13, of which 10 were waited for; matrix products, arithmetic and copies ran while one was open for 18% of the time, Pallas kernels for 2%

profile of v11, /device:TPU:0, one launch (start us, length us, event | category | flops | bytes accessed | tf_op | source)
XLA Modules:
  0.0 1667.3 jit_solution(16801388873410125966)
XLA Ops:
  24.5 67.0 %all-gather.5.cloned.1.call-done = bf16[1024,2048]{0,1:T(8,128)(2,1)} async-done(((bf16[128,2048]{0,1:T(8,128)(2,1)}), bf16[1024,2048]{0,1:T(8,128)(2,1)}) %all-gather.5.cloned.1.call-update) | async-done | bytes 4194320 | tf_op jit(solution)/shard_map/all_gather | solution.py:308
  99.4 8.4 scatter_custom_fusion.tok_ref
  112.5 63.2 %all-gather.7.cloned.1.call-done = bf16[2048,1090]{0,1:T(8,128)(2,1)} async-done(((bf16[128,1090]{0,1:T(8,128)(2,1)}), bf16[2048,1090]{0,1:T(8,128)(2,1)}) %all-gather.7.cloned.1.call-update) | async-done | bytes 4464656 | tf_op jit(solution)/shard_map/all_gather | solution.py:289
  237.6 107.1 %all-reduce.7.cloned.1.call-done = bf16[1024,2048]{0,1:T(8,128)(2,1)} async-done(((bf16[1024,2048]{0,1:T(8,128)(2,1)}), bf16[1024,2048]{0,1:T(8,128)(2,1)}) %all-reduce.7.cloned.1.call-update) | async-done | bytes 4194320 | tf_op jit(solution)/shard_map/psum | solution.py:397
  365.2 8.1 scatter_custom_fusion.1
  381.2 12.5 copy.227.both_hbm
  401.0 36.4 %shard_map.297 = bf16[2560,32,128]{2,1,0:T(8,128)(2,1)} custom-call(s32[2560]{0:T(1024)} %copy-done.72, bf16[1024,32,128]{2,1,0:T(8,128)(2,1)} %copy.227.both_hbm, f32[2,2560,1,128]{3,2,1,0:T(1,128)} %broadcast_in_dim.79.col_ref), custom_call_target="tpu_custom_call" | custom-call | flops 5242880 | bytes 41943040 | tf_op jit(solution)/shard_map/pallas_call | solution.py:132
  437.4 236.5 %all_to_all.30 = bf16[16,4,40,32,128]{4,3,2,1,0:T(8,128)(2,1)} all-to-all(bf16[16,4,40,32,128]{4,3,2,1,0:T(8,128)(2,1)} %bitcast.262), channel_id=1, replica_groups=mesh['dp'=16,'tensor'=8] {'dp'}, dimensions={0} | all-to-all | bytes 41943040 | tf_op jit(solution)/shard_map/all_to_all | solution.py:419
  673.9 31.3 %reshape.530 = bf16[16,4,40,4096]{3,2,1,0:T(8,128)(2,1)} reshape(bf16[16,4,40,32,128]{4,3,2,1,0:T(8,128)(2,1)} %all_to_all.30) | data formatting | bytes 41943040 | tf_op jit(solution)/shard_map/reshape | solution.py:420
  705.2 16.8 %fusion.158 = (bf16[16,4,40,2048]{3,2,1,0:T(8,128)(2,1)}, bf16[16,4,40,2048]{3,2,1,0:T(8,128)(2,1)}) fusion(bf16[16,4,40,4096]{3,2,1,0:T(8,128)(2,1)} %reshape.530), kind=kLoop, calls=%fused_computation.283 | loop fusion | bytes 41943040 | tf_op jit(solution)/shard_map/slice | solution.py:422
  722.1 8.8 fusion.11
  730.9 8.7 fusion.9
  739.5 11.4 fusion.41
  758.1 11.8 copy.236
  769.9 11.2 copy.180
  786.3 9.9 fusion.32
  796.2 15.1 add_convert_fusion
  811.2 12.0 copy.237
  823.2 103.9 %all-to-all-done.2 = bf16[16,4,40,16,128]{4,3,2,1,0:T(8,128)(2,1)} async-done(((bf16[16,4,40,16,128]{4,3,2,1,0:T(8,128)(2,1)}), bf16[16,4,40,16,128]{4,3,2,1,0:T(8,128)(2,1)}, u32[]{:S(2)}, u32[]{:S(2)}) %all-to-all-start.2) | async-done | bytes 10485792 | tf_op jit(solution)/shard_map/all_to_all | solution.py:432
  927.1 11.2 copy.181
  978.3 105.8 %all-to-all-done.3 = bf16[16,4,40,16,128]{4,3,2,1,0:T(8,128)(2,1)} async-done(((bf16[16,4,40,16,128]{4,3,2,1,0:T(8,128)(2,1)}), bf16[16,4,40,16,128]{4,3,2,1,0:T(8,128)(2,1)}, u32[]{:S(2)}, u32[]{:S(2)}) %all-to-all-start.3) | async-done | bytes 10485792 | tf_op jit(solution)/shard_map/all_to_all | solution.py:460
  1087.6 44.8 %shard_map.298 = (bf16[1024,16,128]{2,1,0:T(8,128)(2,1)}, bf16[1024,16,128]{2,1,0:T(8,128)(2,1)}, f32[1024,1,128]{2,1,0:T(1,128)}) custom-call(s32[2048]{0:T(1024)} %copy-done.78, bf16[2560,16,128]{2,1,0:T(8,128)(2,1)} %bitcast.36.out_hbm, bf16[2560,16,128]{2,1,0:T(8,128)(2,1)} %bitcast.37.back_hbm, f32[2,1024,1,128]{3,2,1,0:T(1,128)} %broadcast_in_dim.80.gate_ref, ...), custom_call_target="tpu_custom_call" | custom-call | flops 33554432 | bytes 46137344 | tf_op jit(solution)/shard_map/pallas_call | solution.py:205
  1167.5 63.4 %all-to-all-done.4 = bf16[8,128,2048]{2,1,0:T(8,128)(2,1)} async-done(((bf16[8,128,2048]{2,1,0:T(8,128)(2,1)}), bf16[8,128,2048]{2,1,0:T(8,128)(2,1)}, u32[]{:S(2)}, u32[]{:S(2)}) %all-to-all-start.4) | async-done | bytes 4194336 | tf_op jit(solution)/shard_map/all_to_all | solution.py:503
  1234.9 79.7 %all-reduce.9.cloned.1.call-done = bf16[1024,2050]{0,1:T(8,128)(2,1)} async-done(((bf16[1024,2050]{0,1:T(8,128)(2,1)}), bf16[1024,2050]{0,1:T(8,128)(2,1)}) %all-reduce.9.cloned.1.call-update) | async-done | bytes 4198416 | tf_op jit(solution)/shard_map/psum | solution.py:508
  1321.2 10.5 multiply_reduce_fusion
  1333.7 8.1 fusion.157
  1371.9 38.8 %all-to-all-done.5 = bf16[16,128,1056]{1,2,0:T(8,128)(2,1)} async-done(((bf16[16,128,1056]{1,2,0:T(8,128)(2,1)}), bf16[16,128,1056]{1,2,0:T(8,128)(2,1)}, u32[]{:S(2)}, u32[]{:S(2)}) %all-to-all-start.5) | async-done | bytes 4325408 | tf_op jit(solution)/shard_map/all_to_all | solution.py:523
  1418.1 10.9 pad_maximum_fusion.2
  1458.2 99.1 %all-reduce.11.cloned.1.call-done = bf16[1024,2624]{0,1:T(8,128)(2,1)} async-done(((bf16[1024,2624]{0,1:T(8,128)(2,1)}), bf16[1024,2624]{0,1:T(8,128)(2,1)}) %all-reduce.11.cloned.1.call-update) | async-done | bytes 5373968 | tf_op jit(solution)/shard_map/psum | solution.py:616
  1583.1 9.1 fusion.19
  1592.2 9.3 fusion.22
  1618.0 33.5 %reduce-scatter.2.cloned.1.call-done = f32[128,849]{0,1:T(8,128)} async-done(((f32[2048,849]{0,1:T(8,128)}), f32[128,849]{0,1:T(8,128)}) %reduce-scatter.2.cloned.1.call-update) | async-done | bytes 434704 | tf_op jit(solution)/shard_map/reduce_scatter | solution.py:673
  (439 shorter events, 346.4 us)
Async XLA Ops:
  7.2 732.4 %copy-start = (bf16[4,176,2048]{2,1,0:T(8,128)(2,1)S(1)}, bf16[4,176,2048]{2,1,0:T(8,128)(2,1)}, u32[]{:S(2)}) copy-start(bf16[4,176,2048]{2,1,0:T(8,128)(2,1)} %param.31) | copy-start | bytes 8650756
  7.2 84.3 %all-gather.5.cloned.1.call-start = ((), (), s32[]{:S(2)}) async-start(), calls=%async_computation.7 | async-start | bytes 4718592 | tf_op jit(solution)/shard_map/all_gather | solution.py:308
  9.5 166.2 %all-gather.7.cloned.1.call-start = ((), (), s32[]{:S(2)}) async-start(), calls=%async_computation.8 | async-start | bytes 4769792 | tf_op jit(solution)/shard_map/all_gather | solution.py:289
  16.2 208.6 %all-gather.9.cloned.1.call-start = ((), (), s32[]{:S(2)}) async-start(), calls=%async_computation.9 | async-start | bytes 1427456 | tf_op jit(solution)/shard_map/all_gather | solution.py:302
  94.1 99.6 %all-to-all-start = ((bf16[8,128,2048]{1,2,0:T(8,128)(2,1)}), bf16[8,128,2048]{1,2,0:T(8,128)(2,1)}, u32[]{:S(2)}, u32[]{:S(2)}) async-start(bf16[8,128,2048]{1,2,0:T(8,128)(2,1)} %broadcast_in_dim.64), calls=%async_computation | async-start | bytes 8388608 | tf_op jit(solution)/shard_map/all_to_all | solution.py:311
  98.8 246.0 %all-reduce.7.cloned.1.call-start = ((), (), s32[]{:S(2)}) async-start(), calls=%async_computation.10 | async-start | bytes 8388608 | tf_op jit(solution)/shard_map/psum | solution.py:397
  107.8 74.9 %copy-start.72 = (s32[2560]{0:T(1024)}, s32[2560]{0:T(1024)S(1)}, u32[]{:S(2)}) copy-start(s32[2560]{0:T(1024)S(1)} %scatter_custom_fusion.tok_ref) | copy-start | bytes 30724
  107.8 106.5 %copy-start.99 = (f32[32]{0:T(128)}, f32[32]{0:T(128)S(1)}, u32[]{:S(2)}) copy-start(f32[32]{0:T(128)S(1)} %multiply_power_fusion) | copy-start | bytes 388
  107.9 106.5 %copy-start.85 = (f32[1024]{0:T(1024)}, f32[1024]{0:T(1024)S(1)}, u32[]{:S(2)}) copy-start(f32[1024]{0:T(1024)S(1)} %iota_convert_fusion) | copy-start | bytes 12292
  107.9 244.1 %copy-start.78 = (s32[2048]{0:T(1024)}, s32[2048]{0:T(1024)S(1)}, u32[]{:S(2)}) copy-start(s32[2048]{0:T(1024)S(1)} %multiply_add_fusion.slot_ref) | copy-start | bytes 24580
  112.5 78.6 %copy-start.83 = (f32[1024]{0:T(1024)}, f32[1024]{0:T(1024)S(1)}, u32[]{:S(2)}) copy-start(f32[1024]{0:T(1024)S(1)} %add_rsqrt_fusion.2) | copy-start | bytes 12292
  176.6 14.5 copy-start.66
  176.7 31.5 %copy-start.91 = (f32[512]{0:T(512)}, f32[512]{0:T(512)S(1)}, u32[]{:S(2)}) copy-start(f32[512]{0:T(512)S(1)} %reshape.501) | copy-start | bytes 6148
  210.7 12.8 copy-start.17
  236.0 201.4 %all-gather.11.cloned.1.call-start = ((), (), s32[]{:S(2)}) async-start(), calls=%async_computation.11 | async-start | bytes 4595712 | tf_op jit(solution)/shard_map/all_gather | solution.py:414
  705.2 16.8 %copy-start.33 = (bf16[4,176,2048]{2,1,0:T(8,128)(2,1)S(1)}, bf16[4,176,2048]{2,1,0:T(8,128)(2,1)}, u32[]{:S(2)}) copy-start(bf16[4,176,2048]{2,1,0:T(8,128)(2,1)} %param.29) | copy-start | bytes 8650756
  781.2 146.0 %all-to-all-start.2 = ((bf16[16,4,40,16,128]{4,3,2,1,0:T(8,128)(2,1)}), bf16[16,4,40,16,128]{4,3,2,1,0:T(8,128)(2,1)}, u32[]{:S(2)}, u32[]{:S(2)}) async-start(bf16[16,4,40,16,128]{4,3,2,1,0:T(8,128)(2,1)} %copy.180), calls=%async_computation.2 | async-start | bytes 20971520 | tf_op jit(solution)/shard_map/all_to_all | solution.py:432
  938.3 145.8 %all-to-all-start.3 = ((bf16[16,4,40,16,128]{4,3,2,1,0:T(8,128)(2,1)}), bf16[16,4,40,16,128]{4,3,2,1,0:T(8,128)(2,1)}, u32[]{:S(2)}, u32[]{:S(2)}) async-start(bf16[16,4,40,16,128]{4,3,2,1,0:T(8,128)(2,1)} %copy.181), calls=%async_computation.3 | async-start | bytes 20971520 | tf_op jit(solution)/shard_map/all_to_all | solution.py:460
  943.2 371.4 %all-reduce.9.cloned.1.call-start = ((), (), s32[]{:S(2)}) async-start(), calls=%async_computation.12 | async-start | bytes 8421376 | tf_op jit(solution)/shard_map/psum | solution.py:508
  943.3 14.7 slice-start.7
  1151.8 79.1 %all-to-all-start.4 = ((bf16[8,128,2048]{2,1,0:T(8,128)(2,1)}), bf16[8,128,2048]{2,1,0:T(8,128)(2,1)}, u32[]{:S(2)}, u32[]{:S(2)}) async-start(bf16[8,128,2048]{2,1,0:T(8,128)(2,1)} %reshape_reshape.3), calls=%async_computation.4 | async-start | bytes 8388608 | tf_op jit(solution)/shard_map/all_to_all | solution.py:503
  1234.9 86.2 %copy-start.69 = (s32[1024,2]{0,1:T(2,128)S(1)}, s32[1024,2]{0,1:T(2,128)}, u32[]{:S(2)}) copy-start(s32[1024,2]{0,1:T(2,128)} %param.19) | copy-start | bytes 24580
  1234.9 86.2 %copy-start.41 = (bf16[2048,321]{0,1:T(8,128)(2,1)S(1)}, bf16[2048,321]{0,1:T(8,128)(2,1)}, u32[]{:S(2)}) copy-start(bf16[2048,321]{0,1:T(8,128)(2,1)} %all-gather.9.cloned.1.call-done) | copy-start | bytes 3944452
  1234.9 86.2 %copy-start.71 = (f32[2048,1]{0,1:T(1,128)S(1)}, f32[2048,1]{0,1:T(1,128)}, u32[]{:S(2)}) copy-start(f32[2048,1]{0,1:T(1,128)} %copy-done.70) | copy-start | bytes 24580
  1321.2 24.0 %slice-start.2 = ((s8[4325376]{0:T(1024)(128)(4,1)}), s8[4194304]{0:T(1024)(128)(4,1)S(1)}, s32[]{:S(2)}) async-start(s8[4325376]{0:T(1024)(128)(4,1)} %bitcast.273), calls=%async_computation.17 | async-start | bytes 8388608
  1348.0 62.7 %all-to-all-start.5 = ((bf16[16,128,1056]{1,2,0:T(8,128)(2,1)}), bf16[16,128,1056]{1,2,0:T(8,128)(2,1)}, u32[]{:S(2)}, u32[]{:S(2)}) async-start(bf16[16,128,1056]{1,2,0:T(8,128)(2,1)} %copy_bitcast_fusion), calls=%async_computation.5 | async-start | bytes 8650752 | tf_op jit(solution)/shard_map/all_to_all | solution.py:523
  1352.9 204.4 %all-reduce.11.cloned.1.call-start = ((), (), s32[]{:S(2)}) async-start(), calls=%async_computation.13 | async-start | bytes 10747904 | tf_op jit(solution)/shard_map/psum | solution.py:616
  1370.2 44.3 %copy-start.47 = (bf16[2048,384]{0,1:T(8,128)(2,1)S(1)}, bf16[2048,384]{0,1:T(8,128)(2,1)}, u32[]{:S(2)}) copy-start(bf16[2048,384]{0,1:T(8,128)(2,1)} %slice.282) | copy-start | bytes 4718596
  1429.0 222.5 %reduce-scatter.2.cloned.1.call-start = ((), (), s32[]{:S(2)}) async-start(), calls=%async_computation.14 | async-start | bytes 7450624 | tf_op jit(solution)/shard_map/reduce_scatter | solution.py:673
  1583.1 18.4 %slice-start.4 = ((s8[10485760]{0:T(1024)(128)(4,1)}), s8[4194304]{0:T(1024)(128)(4,1)S(1)}, s32[]{:S(2)}) async-start(s8[10485760]{0:T(1024)(128)(4,1)} %bitcast.277), calls=%async_computation.19 | async-start | bytes 8388608
  1583.1 18.4 %slice-start.5 = ((s8[10485760]{0:T(1024)(128)(4,1)}), s8[4194304]{0:T(1024)(128)(4,1)S(1)}, s32[]{:S(2)}) async-start(s8[10485760]{0:T(1024)(128)(4,1)} %bitcast.277), calls=%async_computation.20 | async-start | bytes 8388608
  1610.0 50.2 %copy-start.1 = (bf16[4,176,2048]{2,1,0:T(8,128)(2,1)S(1)}, bf16[4,176,2048]{2,1,0:T(8,128)(2,1)}, u32[]{:S(2)}) copy-start(bf16[4,176,2048]{2,1,0:T(8,128)(2,1)} %param.31) | copy-start | bytes 8650756
  (91 other events, 434.2 us)
Sparse Core Ops, SparseCore 0:
  10.8 80.6 all-gather.4
  93.7 81.9 all-gather.6
  177.9 33.7 all-gather.8
  236.1 108.6 all-reduce.6
  351.3 44.3 all-gather.10
  1144.6 169.9 all-reduce.8
  1429.1 128.1 all-reduce.10
  1581.9 69.4 reduce-scatter.1

commit v12 on v11

--- a/solution.py
+++ b/solution.py
@@ -157,24 +157,40 @@
     slot_ref, out_hbm, back_hbm, gate_ref, grad_ref, shared_out_ref, shared_back_ref,
     feed_ref, back_ref, part_ref, picked_out, picked_back, sems,
 ):
-    top = picked_out.shape[0]
-    block = picked_out.shape[1]
+    top = picked_out.shape[1]
+    block = picked_out.shape[2]
     last = out_hbm.shape[0] - 1
-    base = pl.program_id(0) * block
-
-    def start(r, carry):
-        for k in range(top):
-            slot = jnp.clip(slot_ref[(base + r) * top + k], 0, last)
-            pltpu.make_async_copy(out_hbm.at[slot], picked_out.at[k, r], sems.at[0, k, r]).start()
-            pltpu.make_async_copy(back_hbm.at[slot], picked_back.at[k, r], sems.at[1, k, r]).start()
-        return carry
-
-    lax.fori_loop(0, block, start, 0, unroll=2)
+    step = pl.program_id(0)
+    steps = pl.num_programs(0)
+
+    def fetch(index, buf):
+        def start(r, carry):
+            for k in range(top):
+                slot = jnp.clip(slot_ref[(index * block + r) * top + k], 0, last)
+                pltpu.make_async_copy(
+                    out_hbm.at[slot], picked_out.at[buf, k, r], sems.at[buf, 0, k, r]
+                ).start()
+                pltpu.make_async_copy(
+                    back_hbm.at[slot], picked_back.at[buf, k, r], sems.at[buf, 1, k, r]
+                ).start()
+            return carry
+
+        lax.fori_loop(0, block, start, 0, unroll=2)
+
+    @pl.when(step == 0)
+    def _():
+        fetch(0, 0)
+
+    @pl.when(step + 1 < steps)
+    def _():
+        fetch(step + 1, (step + 1) % 2)
+
+    now = step % 2
 
     def finish(r, carry):
         for k in range(top):
-            pltpu.make_async_copy(out_hbm.at[0], picked_out.at[k, r], sems.at[0, k, r]).wait()
-            pltpu.make_async_copy(back_hbm.at[0], picked_back.at[k, r], sems.at[1, k, r]).wait()
+            pltpu.make_async_copy(out_hbm.at[0], picked_out.at[now, k, r], sems.at[now, 0, k, r]).wait()
+            pltpu.make_async_copy(back_hbm.at[0], picked_back.at[now, k, r], sems.at[now, 1, k, r]).wait()
         return carry
 
     lax.fori_loop(0, block, finish, 0, unroll=2)
@@ -184,10 +200,10 @@
     lanes = lax.broadcasted_iota(jnp.int32, part_ref.shape, 2)
     parts = jnp.zeros(part_ref.shape, jnp.float32)
     for k in range(top):
-        out_k = picked_out[k].astype(jnp.float32)
+        out_k = picked_out[now, k].astype(jnp.float32)
         term = gate_ref[k] * out_k
         weighted = term if weighted is None else weighted + term
-        back_k = picked_back[k].astype(jnp.float32)
+        back_k = picked_back[now, k].astype(jnp.float32)
         backs = back_k if backs is None else backs + back_k
         dot_k = jnp.sum(jnp.sum(grad * out_k, 2, keepdims=True), 1, keepdims=True)
         parts = jnp.where(lanes == k, dot_k, parts)
@@ -222,11 +238,12 @@
             ],
             out_specs=[row_spec, row_spec, pl.BlockSpec((block, 1, 128), lambda i, s: (i, 0, 0))],
             scratch_shapes=[
-                pltpu.VMEM((top, block, tile_rows, 128), out_table.dtype),
-                pltpu.VMEM((top, block, tile_rows, 128), back_table.dtype),
-                pltpu.SemaphoreType.DMA((2, top, block)),
+                pltpu.VMEM((2, top, block, tile_rows, 128), out_table.dtype),
+                pltpu.VMEM((2, top, block, tile_rows, 128), back_table.dtype),
+                pltpu.SemaphoreType.DMA((2, 2, top, block)),
             ],
         ),
+        compiler_params=pltpu.CompilerParams(dimension_semantics=("arbitrary",)),
         cost_estimate=pl.CostEstimate(
             flops=8 * tokens * top * width,
             transcendentals=0,

time: 1680 us -> 1670 us (level)
  no operation moved by 1% of the time
where the time goes in v12:
time: 1670 us; the launch traced here: 1660 us
  waiting for transfers between devices  762 us (46%)
  local copies, waits for them, and re-layouts  256 us (15%)
  blocking collectives  237 us (14%)
  matrix products  183 us (11%)
  other arithmetic  107 us (6%)
  Pallas kernels  78.3 us (5%)
  starting transfers between devices  25.1 us (2%)
  between operations  17 us (1%)
    all_to_all x1, blocking collectives, shards(): lax.all_to_all(send_both, 'dp', split_axis=0, concat_axis=0, tiled=True)  237 us
    psum x1, waiting for transfers between devices, shards(): lax.psum(attn_part.astype(jnp.bfloat16), 'tensor').astype(jnp.float32)  107 us
    all_to_all x1, waiting for transfers between devices, shards(): lax.all_to_all(grads_low, 'dp', split_axis=0, concat_axis=0, tiled=True)  106 us
    all_to_all x1, waiting for transfers between devices, shards(): lax.all_to_all(expert_out.astype(jnp.bfloat16).reshape(dp_size, exp_dev,...  104 us
    psum x1, waiting for transfers between devices, shards(): lax.psum(jnp.concatenate([normed_grad_part, latent_grad_part], 1).astype(...  99.1 us
    psum x1, waiting for transfers between devices, shards(): lax.psum(jnp.concatenate([back_part, gate_cols.astype(jnp.bfloat16)], 1),...  79.7 us
    all_gather x1, waiting for transfers between devices, shards(): hidden_all = lax.all_gather(hidden, 'tensor', axis=0, tiled=True)  67 us
    all_to_all x1, waiting for transfers between devices, shards(): lax.all_to_all(feed_part.reshape(tensor_size, tok_dev, D), 'tensor', spli...  63.4 us
  transfers between devices with their start and end apart: 13, of which 10 were waited for; matrix products, arithmetic and copies ran while one was open for 18% of the time, Pallas kernels for 2%

profile of v12, /device:TPU:0, one launch (start us, length us, event | category | flops | bytes accessed | tf_op | source)
XLA Modules:
  0.0 1664.4 jit_solution(7552754341848952538)
XLA Ops:
  24.5 67.0 %all-gather.5.cloned.1.call-done = bf16[1024,2048]{0,1:T(8,128)(2,1)} async-done(((bf16[128,2048]{0,1:T(8,128)(2,1)}), bf16[1024,2048]{0,1:T(8,128)(2,1)}) %all-gather.5.cloned.1.call-update) | async-done | bytes 4194320 | tf_op jit(solution)/shard_map/all_gather | solution.py:325
  99.4 8.4 scatter_custom_fusion.tok_ref
  112.5 63.2 %all-gather.7.cloned.1.call-done = bf16[2048,1090]{0,1:T(8,128)(2,1)} async-done(((bf16[128,1090]{0,1:T(8,128)(2,1)}), bf16[2048,1090]{0,1:T(8,128)(2,1)}) %all-gather.7.cloned.1.call-update) | async-done | bytes 4464656 | tf_op jit(solution)/shard_map/all_gather | solution.py:306
  237.6 107.1 %all-reduce.7.cloned.1.call-done = bf16[1024,2048]{0,1:T(8,128)(2,1)} async-done(((bf16[1024,2048]{0,1:T(8,128)(2,1)}), bf16[1024,2048]{0,1:T(8,128)(2,1)}) %all-reduce.7.cloned.1.call-update) | async-done | bytes 4194320 | tf_op jit(solution)/shard_map/psum | solution.py:414
  365.2 8.1 scatter_custom_fusion.1
  381.2 12.5 copy.227.both_hbm
  401.0 35.3 %shard_map.297 = bf16[2560,32,128]{2,1,0:T(8,128)(2,1)} custom-call(s32[2560]{0:T(1024)} %copy-done.72, bf16[1024,32,128]{2,1,0:T(8,128)(2,1)} %copy.227.both_hbm, f32[2,2560,1,128]{3,2,1,0:T(1,128)} %broadcast_in_dim.79.col_ref), custom_call_target="tpu_custom_call" | custom-call | flops 5242880 | bytes 41943040 | tf_op jit(solution)/shard_map/pallas_call | solution.py:132
  436.4 236.5 %all_to_all.30 = bf16[16,4,40,32,128]{4,3,2,1,0:T(8,128)(2,1)} all-to-all(bf16[16,4,40,32,128]{4,3,2,1,0:T(8,128)(2,1)} %bitcast.262), channel_id=1, replica_groups=mesh['dp'=16,'tensor'=8] {'dp'}, dimensions={0} | all-to-all | bytes 41943040 | tf_op jit(solution)/shard_map/all_to_all | solution.py:436
  672.9 31.3 %reshape.530 = bf16[16,4,40,4096]{3,2,1,0:T(8,128)(2,1)} reshape(bf16[16,4,40,32,128]{4,3,2,1,0:T(8,128)(2,1)} %all_to_all.30) | data formatting | bytes 41943040 | tf_op jit(solution)/shard_map/reshape | solution.py:437
  704.2 16.8 %fusion.158 = (bf16[16,4,40,2048]{3,2,1,0:T(8,128)(2,1)}, bf16[16,4,40,2048]{3,2,1,0:T(8,128)(2,1)}) fusion(bf16[16,4,40,4096]{3,2,1,0:T(8,128)(2,1)} %reshape.530), kind=kLoop, calls=%fused_computation.283 | loop fusion | bytes 41943040 | tf_op jit(solution)/shard_map/slice | solution.py:439
  721.0 8.8 fusion.11
  729.9 8.7 fusion.9
  738.5 11.4 fusion.41
  757.1 11.8 copy.236
  768.9 11.2 copy.180
  785.3 9.9 fusion.32
  795.2 15.1 add_convert_fusion
  810.2 12.0 copy.237
  822.2 103.9 %all-to-all-done.2 = bf16[16,4,40,16,128]{4,3,2,1,0:T(8,128)(2,1)} async-done(((bf16[16,4,40,16,128]{4,3,2,1,0:T(8,128)(2,1)}), bf16[16,4,40,16,128]{4,3,2,1,0:T(8,128)(2,1)}, u32[]{:S(2)}, u32[]{:S(2)}) %all-to-all-start.2) | async-done | bytes 10485792 | tf_op jit(solution)/shard_map/all_to_all | solution.py:449
  926.1 11.2 copy.181
  977.3 105.8 %all-to-all-done.3 = bf16[16,4,40,16,128]{4,3,2,1,0:T(8,128)(2,1)} async-done(((bf16[16,4,40,16,128]{4,3,2,1,0:T(8,128)(2,1)}), bf16[16,4,40,16,128]{4,3,2,1,0:T(8,128)(2,1)}, u32[]{:S(2)}, u32[]{:S(2)}) %all-to-all-start.3) | async-done | bytes 10485792 | tf_op jit(solution)/shard_map/all_to_all | solution.py:477
  1086.6 42.9 %shard_map.298 = (bf16[1024,16,128]{2,1,0:T(8,128)(2,1)}, bf16[1024,16,128]{2,1,0:T(8,128)(2,1)}, f32[1024,1,128]{2,1,0:T(1,128)}) custom-call(s32[2048]{0:T(1024)} %copy-done.78, bf16[2560,16,128]{2,1,0:T(8,128)(2,1)} %bitcast.36.out_hbm, bf16[2560,16,128]{2,1,0:T(8,128)(2,1)} %bitcast.37.back_hbm, f32[2,1024,1,128]{3,2,1,0:T(1,128)} %broadcast_in_dim.80.gate_ref, ...), custom_call_target="tpu_custom_call" | custom-call | flops 33554432 | bytes 46137344 | tf_op jit(solution)/shard_map/pallas_call | solution.py:221
  1164.7 63.4 %all-to-all-done.4 = bf16[8,128,2048]{2,1,0:T(8,128)(2,1)} async-done(((bf16[8,128,2048]{2,1,0:T(8,128)(2,1)}), bf16[8,128,2048]{2,1,0:T(8,128)(2,1)}, u32[]{:S(2)}, u32[]{:S(2)}) %all-to-all-start.4) | async-done | bytes 4194336 | tf_op jit(solution)/shard_map/all_to_all | solution.py:520
  1232.1 79.7 %all-reduce.9.cloned.1.call-done = bf16[1024,2050]{0,1:T(8,128)(2,1)} async-done(((bf16[1024,2050]{0,1:T(8,128)(2,1)}), bf16[1024,2050]{0,1:T(8,128)(2,1)}) %all-reduce.9.cloned.1.call-update) | async-done | bytes 4198416 | tf_op jit(solution)/shard_map/psum | solution.py:525
  1318.4 10.5 multiply_reduce_fusion
  1330.8 8.1 fusion.157
  1369.0 38.8 %all-to-all-done.5 = bf16[16,128,1056]{1,2,0:T(8,128)(2,1)} async-done(((bf16[16,128,1056]{1,2,0:T(8,128)(2,1)}), bf16[16,128,1056]{1,2,0:T(8,128)(2,1)}, u32[]{:S(2)}, u32[]{:S(2)}) %all-to-all-start.5) | async-done | bytes 4325408 | tf_op jit(solution)/shard_map/all_to_all | solution.py:540
  1415.2 10.9 pad_maximum_fusion.2
  1455.4 99.1 %all-reduce.11.cloned.1.call-done = bf16[1024,2624]{0,1:T(8,128)(2,1)} async-done(((bf16[1024,2624]{0,1:T(8,128)(2,1)}), bf16[1024,2624]{0,1:T(8,128)(2,1)}) %all-reduce.11.cloned.1.call-update) | async-done | bytes 5373968 | tf_op jit(solution)/shard_map/psum | solution.py:633
  1580.3 9.1 fusion.19
  1589.4 9.3 fusion.22
  1615.1 33.4 %reduce-scatter.2.cloned.1.call-done = f32[128,849]{0,1:T(8,128)} async-done(((f32[2048,849]{0,1:T(8,128)}), f32[128,849]{0,1:T(8,128)}) %reduce-scatter.2.cloned.1.call-update) | async-done | bytes 434704 | tf_op jit(solution)/shard_map/reduce_scatter | solution.py:690
  (439 shorter events, 346.4 us)
Async XLA Ops:
  7.2 731.3 %copy-start = (bf16[4,176,2048]{2,1,0:T(8,128)(2,1)S(1)}, bf16[4,176,2048]{2,1,0:T(8,128)(2,1)}, u32[]{:S(2)}) copy-start(bf16[4,176,2048]{2,1,0:T(8,128)(2,1)} %param.31) | copy-start | bytes 8650756
  7.2 84.3 %all-gather.5.cloned.1.call-start = ((), (), s32[]{:S(2)}) async-start(), calls=%async_computation.7 | async-start | bytes 4718592 | tf_op jit(solution)/shard_map/all_gather | solution.py:325
  9.5 166.2 %all-gather.7.cloned.1.call-start = ((), (), s32[]{:S(2)}) async-start(), calls=%async_computation.8 | async-start | bytes 4769792 | tf_op jit(solution)/shard_map/all_gather | solution.py:306
  16.2 208.6 %all-gather.9.cloned.1.call-start = ((), (), s32[]{:S(2)}) async-start(), calls=%async_computation.9 | async-start | bytes 1427456 | tf_op jit(solution)/shard_map/all_gather | solution.py:319
  94.1 99.6 %all-to-all-start = ((bf16[8,128,2048]{1,2,0:T(8,128)(2,1)}), bf16[8,128,2048]{1,2,0:T(8,128)(2,1)}, u32[]{:S(2)}, u32[]{:S(2)}) async-start(bf16[8,128,2048]{1,2,0:T(8,128)(2,1)} %broadcast_in_dim.64), calls=%async_computation | async-start | bytes 8388608 | tf_op jit(solution)/shard_map/all_to_all | solution.py:328
  98.8 246.0 %all-reduce.7.cloned.1.call-start = ((), (), s32[]{:S(2)}) async-start(), calls=%async_computation.10 | async-start | bytes 8388608 | tf_op jit(solution)/shard_map/psum | solution.py:414
  107.8 74.9 %copy-start.72 = (s32[2560]{0:T(1024)}, s32[2560]{0:T(1024)S(1)}, u32[]{:S(2)}) copy-start(s32[2560]{0:T(1024)S(1)} %scatter_custom_fusion.tok_ref) | copy-start | bytes 30724
  107.8 106.5 %copy-start.99 = (f32[32]{0:T(128)}, f32[32]{0:T(128)S(1)}, u32[]{:S(2)}) copy-start(f32[32]{0:T(128)S(1)} %multiply_power_fusion) | copy-start | bytes 388
  107.9 106.5 %copy-start.85 = (f32[1024]{0:T(1024)}, f32[1024]{0:T(1024)S(1)}, u32[]{:S(2)}) copy-start(f32[1024]{0:T(1024)S(1)} %iota_convert_fusion) | copy-start | bytes 12292
  107.9 244.1 %copy-start.78 = (s32[2048]{0:T(1024)}, s32[2048]{0:T(1024)S(1)}, u32[]{:S(2)}) copy-start(s32[2048]{0:T(1024)S(1)} %multiply_add_fusion.slot_ref) | copy-start | bytes 24580
  112.5 78.6 %copy-start.83 = (f32[1024]{0:T(1024)}, f32[1024]{0:T(1024)S(1)}, u32[]{:S(2)}) copy-start(f32[1024]{0:T(1024)S(1)} %add_rsqrt_fusion.2) | copy-start | bytes 12292
  176.6 14.5 copy-start.66
  176.7 31.5 %copy-start.91 = (f32[512]{0:T(512)}, f32[512]{0:T(512)S(1)}, u32[]{:S(2)}) copy-start(f32[512]{0:T(512)S(1)} %reshape.501) | copy-start | bytes 6148
  210.7 12.8 copy-start.17
  236.0 200.4 %all-gather.11.cloned.1.call-start = ((), (), s32[]{:S(2)}) async-start(), calls=%async_computation.11 | async-start | bytes 4595712 | tf_op jit(solution)/shard_map/all_gather | solution.py:431
  704.2 16.8 %copy-start.33 = (bf16[4,176,2048]{2,1,0:T(8,128)(2,1)S(1)}, bf16[4,176,2048]{2,1,0:T(8,128)(2,1)}, u32[]{:S(2)}) copy-start(bf16[4,176,2048]{2,1,0:T(8,128)(2,1)} %param.29) | copy-start | bytes 8650756
  780.1 146.0 %all-to-all-start.2 = ((bf16[16,4,40,16,128]{4,3,2,1,0:T(8,128)(2,1)}), bf16[16,4,40,16,128]{4,3,2,1,0:T(8,128)(2,1)}, u32[]{:S(2)}, u32[]{:S(2)}) async-start(bf16[16,4,40,16,128]{4,3,2,1,0:T(8,128)(2,1)} %copy.180), calls=%async_computation.2 | async-start | bytes 20971520 | tf_op jit(solution)/shard_map/all_to_all | solution.py:449
  937.3 145.8 %all-to-all-start.3 = ((bf16[16,4,40,16,128]{4,3,2,1,0:T(8,128)(2,1)}), bf16[16,4,40,16,128]{4,3,2,1,0:T(8,128)(2,1)}, u32[]{:S(2)}, u32[]{:S(2)}) async-start(bf16[16,4,40,16,128]{4,3,2,1,0:T(8,128)(2,1)} %copy.181), calls=%async_computation.3 | async-start | bytes 20971520 | tf_op jit(solution)/shard_map/all_to_all | solution.py:477
  942.2 369.5 %all-reduce.9.cloned.1.call-start = ((), (), s32[]{:S(2)}) async-start(), calls=%async_computation.12 | async-start | bytes 8421376 | tf_op jit(solution)/shard_map/psum | solution.py:525
  942.3 14.7 slice-start.7
  1149.0 79.1 %all-to-all-start.4 = ((bf16[8,128,2048]{2,1,0:T(8,128)(2,1)}), bf16[8,128,2048]{2,1,0:T(8,128)(2,1)}, u32[]{:S(2)}, u32[]{:S(2)}) async-start(bf16[8,128,2048]{2,1,0:T(8,128)(2,1)} %reshape_reshape.3), calls=%async_computation.4 | async-start | bytes 8388608 | tf_op jit(solution)/shard_map/all_to_all | solution.py:520
  1232.1 86.2 %copy-start.69 = (s32[1024,2]{0,1:T(2,128)S(1)}, s32[1024,2]{0,1:T(2,128)}, u32[]{:S(2)}) copy-start(s32[1024,2]{0,1:T(2,128)} %param.19) | copy-start | bytes 24580
  1232.1 86.2 %copy-start.41 = (bf16[2048,321]{0,1:T(8,128)(2,1)S(1)}, bf16[2048,321]{0,1:T(8,128)(2,1)}, u32[]{:S(2)}) copy-start(bf16[2048,321]{0,1:T(8,128)(2,1)} %all-gather.9.cloned.1.call-done) | copy-start | bytes 3944452
  1232.1 86.2 %copy-start.71 = (f32[2048,1]{0,1:T(1,128)S(1)}, f32[2048,1]{0,1:T(1,128)}, u32[]{:S(2)}) copy-start(f32[2048,1]{0,1:T(1,128)} %copy-done.70) | copy-start | bytes 24580
  1318.4 24.0 %slice-start.2 = ((s8[4325376]{0:T(1024)(128)(4,1)}), s8[4194304]{0:T(1024)(128)(4,1)S(1)}, s32[]{:S(2)}) async-start(s8[4325376]{0:T(1024)(128)(4,1)} %bitcast.273), calls=%async_computation.17 | async-start | bytes 8388608
  1345.2 62.7 %all-to-all-start.5 = ((bf16[16,128,1056]{1,2,0:T(8,128)(2,1)}), bf16[16,128,1056]{1,2,0:T(8,128)(2,1)}, u32[]{:S(2)}, u32[]{:S(2)}) async-start(bf16[16,128,1056]{1,2,0:T(8,128)(2,1)} %copy_bitcast_fusion), calls=%async_computation.5 | async-start | bytes 8650752 | tf_op jit(solution)/shard_map/all_to_all | solution.py:540
  1350.1 204.4 %all-reduce.11.cloned.1.call-start = ((), (), s32[]{:S(2)}) async-start(), calls=%async_computation.13 | async-start | bytes 10747904 | tf_op jit(solution)/shard_map/psum | solution.py:633
  1367.3 44.3 %copy-start.47 = (bf16[2048,384]{0,1:T(8,128)(2,1)S(1)}, bf16[2048,384]{0,1:T(8,128)(2,1)}, u32[]{:S(2)}) copy-start(bf16[2048,384]{0,1:T(8,128)(2,1)} %slice.282) | copy-start | bytes 4718596
  1426.1 222.5 %reduce-scatter.2.cloned.1.call-start = ((), (), s32[]{:S(2)}) async-start(), calls=%async_computation.14 | async-start | bytes 7450624 | tf_op jit(solution)/shard_map/reduce_scatter | solution.py:690
  1580.3 18.4 %slice-start.4 = ((s8[10485760]{0:T(1024)(128)(4,1)}), s8[4194304]{0:T(1024)(128)(4,1)S(1)}, s32[]{:S(2)}) async-start(s8[10485760]{0:T(1024)(128)(4,1)} %bitcast.277), calls=%async_computation.19 | async-start | bytes 8388608
  1580.3 18.4 %slice-start.5 = ((s8[10485760]{0:T(1024)(128)(4,1)}), s8[4194304]{0:T(1024)(128)(4,1)S(1)}, s32[]{:S(2)}) async-start(s8[10485760]{0:T(1024)(128)(4,1)} %bitcast.277), calls=%async_computation.20 | async-start | bytes 8388608
  1607.2 50.2 %copy-start.1 = (bf16[4,176,2048]{2,1,0:T(8,128)(2,1)S(1)}, bf16[4,176,2048]{2,1,0:T(8,128)(2,1)}, u32[]{:S(2)}) copy-start(bf16[4,176,2048]{2,1,0:T(8,128)(2,1)} %param.31) | copy-start | bytes 8650756
  (91 other events, 434.2 us)
Sparse Core Ops, SparseCore 0:
  10.8 80.6 all-gather.4
  93.7 81.9 all-gather.6
  177.9 33.7 all-gather.8
  236.1 108.6 all-reduce.6
  351.3 44.3 all-gather.10
  1141.7 169.9 all-reduce.8
  1426.2 128.1 all-reduce.10
  1579.1 69.4 reduce-scatter.1

commit v13 on v12

--- a/solution.py
+++ b/solution.py
@@ -408,8 +408,11 @@
     token_ids = jnp.arange(seq_len * top_count) // top_count
     slot_token = jnp.full((experts * capacity,), seq_len, jnp.int32).at[slot_index].set(token_ids)
     slot_valid = (slot_token < seq_len).astype(jnp.float32)
-    slot_index, slot_token, slot_valid, attn_part = lax.optimization_barrier(
-        (slot_index, slot_token, slot_valid, attn_part)
+    slot_assign = jnp.zeros((experts * capacity,), jnp.int32).at[slot_index].set(
+        jnp.arange(assignments, dtype=jnp.int32)
+    )
+    slot_index, slot_token, slot_valid, slot_assign, attn_part = lax.optimization_barrier(
+        (slot_index, slot_token, slot_valid, slot_assign, attn_part)
     )
     branch_all = lax.psum(attn_part.astype(jnp.bfloat16), "tensor").astype(jnp.float32)
     shared_local, branch_all = lax.optimization_barrier((shared_local, branch_all))
@@ -421,9 +424,7 @@
     logits = jnp.dot(normed_two, router_weights, preferred_element_type=jnp.float32)
     chosen_logits = jnp.sum(jnp.where(chosen_hot, logits[:, None, :], 0.0), -1)
     gate_values = jax.nn.softmax(chosen_logits, axis=-1)
-    slot_gate = (
-        jnp.zeros((experts * capacity,), jnp.float32).at[slot_index].set(gate_values.reshape(-1))
-    )
+    slot_gate = jnp.take(gate_values.reshape(-1), slot_assign) * slot_valid
     tile_rows = D // 128
     send_both = dispatch_rows(slot_token, normed_two, grad_seq, slot_valid, slot_gate).reshape(
         dp_size, exp_dev, capacity, 2 * tile_rows, 128

time: 1670 us -> 1680 us (level)
    unnamed x232 -> x230, local copies, waits for them, and re-layouts: 60.9 us -> 60.9 us
  transfers between devices with their start and end apart: 13 -> 13, of which waited for: 10 -> 10; matrix products, arithmetic and copies ran while one was open for 18% -> 19% of each run, Pallas kernels for 2% -> 2%
where the time goes in v13:
time: 1680 us; the launch traced here: 1670 us
  waiting for transfers between devices  753 us (45%)
  local copies, waits for them, and re-layouts  270 us (16%)
  blocking collectives  237 us (14%)
  matrix products  183 us (11%)
  other arithmetic  107 us (6%)
  Pallas kernels  78.5 us (5%)
  starting transfers between devices  25.1 us (1%)
  between operations  17 us (1%)
    all_to_all x1, blocking collectives, shards(): lax.all_to_all(send_both, 'dp', split_axis=0, concat_axis=0, tiled=True)  237 us
    psum x1, waiting for transfers between devices, shards(): lax.psum(attn_part.astype(jnp.bfloat16), 'tensor').astype(jnp.float32)  107 us
    all_to_all x1, waiting for transfers between devices, shards(): lax.all_to_all(grads_low, 'dp', split_axis=0, concat_axis=0, tiled=True)  106 us
    all_to_all x1, waiting for transfers between devices, shards(): lax.all_to_all(expert_out.astype(jnp.bfloat16).reshape(dp_size, exp_dev,...  104 us
    psum x1, waiting for transfers between devices, shards(): lax.psum(jnp.concatenate([normed_grad_part, latent_grad_part], 1).astype(...  99.1 us
    psum x1, waiting for transfers between devices, shards(): lax.psum(jnp.concatenate([back_part, gate_cols.astype(jnp.bfloat16)], 1),...  79.6 us
    all_gather x1, waiting for transfers between devices, shards(): hidden_all = lax.all_gather(hidden, 'tensor', axis=0, tiled=True)  67 us
    all_to_all x1, waiting for transfers between devices, shards(): lax.all_to_all(feed_part.reshape(tensor_size, tok_dev, D), 'tensor', spli...  63.3 us
  transfers between devices with their start and end apart: 13, of which 10 were waited for; matrix products, arithmetic and copies ran while one was open for 19% of the time, Pallas kernels for 2%

profile of v13, /device:TPU:0, one launch (start us, length us, event | category | flops | bytes accessed | tf_op | source)
XLA Modules:
  0.0 1670.1 jit_solution(12418162667839842999)
XLA Ops:
  24.5 67.0 %all-gather.5.cloned.1.call-done = bf16[1024,2048]{0,1:T(8,128)(2,1)} async-done(((bf16[128,2048]{0,1:T(8,128)(2,1)}), bf16[1024,2048]{0,1:T(8,128)(2,1)}) %all-gather.5.cloned.1.call-update) | async-done | bytes 4194320 | tf_op jit(solution)/shard_map/all_gather | solution.py:325
  107.5 8.4 scatter_custom_fusion.1
  121.0 54.7 %all-gather.7.cloned.1.call-done = bf16[2048,1090]{0,1:T(8,128)(2,1)} async-done(((bf16[128,1090]{0,1:T(8,128)(2,1)}), bf16[2048,1090]{0,1:T(8,128)(2,1)}) %all-gather.7.cloned.1.call-update) | async-done | bytes 4464656 | tf_op jit(solution)/shard_map/all_gather | solution.py:306
  237.6 107.0 %all-reduce.7.cloned.1.call-done = bf16[1024,2048]{0,1:T(8,128)(2,1)} async-done(((bf16[1024,2048]{0,1:T(8,128)(2,1)}), bf16[1024,2048]{0,1:T(8,128)(2,1)}) %all-reduce.7.cloned.1.call-update) | async-done | bytes 4194320 | tf_op jit(solution)/shard_map/psum | solution.py:417
  365.1 13.6 gather_fusion
  386.6 12.5 copy.227.both_hbm
  406.4 35.6 %shard_map.297 = bf16[2560,32,128]{2,1,0:T(8,128)(2,1)} custom-call(s32[2560]{0:T(1024)} %copy-done.72, bf16[1024,32,128]{2,1,0:T(8,128)(2,1)} %copy.227.both_hbm, f32[2,2560,1,128]{3,2,1,0:T(1,128)} %broadcast_in_dim.86.col_ref), custom_call_target="tpu_custom_call" | custom-call | flops 5242880 | bytes 41943040 | tf_op jit(solution)/shard_map/pallas_call | solution.py:132
  442.0 236.5 %all_to_all.30 = bf16[16,4,40,32,128]{4,3,2,1,0:T(8,128)(2,1)} all-to-all(bf16[16,4,40,32,128]{4,3,2,1,0:T(8,128)(2,1)} %bitcast.262), channel_id=1, replica_groups=mesh['dp'=16,'tensor'=8] {'dp'}, dimensions={0} | all-to-all | bytes 41943040 | tf_op jit(solution)/shard_map/all_to_all | solution.py:437
  678.6 31.3 %reshape.543 = bf16[16,4,40,4096]{3,2,1,0:T(8,128)(2,1)} reshape(bf16[16,4,40,32,128]{4,3,2,1,0:T(8,128)(2,1)} %all_to_all.30) | data formatting | bytes 41943040 | tf_op jit(solution)/shard_map/reshape | solution.py:438
  709.9 16.8 %fusion.158 = (bf16[16,4,40,2048]{3,2,1,0:T(8,128)(2,1)}, bf16[16,4,40,2048]{3,2,1,0:T(8,128)(2,1)}) fusion(bf16[16,4,40,4096]{3,2,1,0:T(8,128)(2,1)} %reshape.543), kind=kLoop, calls=%fused_computation.286 | loop fusion | bytes 41943040 | tf_op jit(solution)/shard_map/slice | solution.py:440
  726.6 8.8 fusion.11
  735.5 8.7 fusion.9
  744.1 11.4 fusion.41
  762.7 11.8 copy.236
  774.5 11.2 copy.180
  790.9 9.9 fusion.32
  800.8 15.1 add_convert_fusion
  815.9 12.0 copy.237
  827.8 103.9 %all-to-all-done.2 = bf16[16,4,40,16,128]{4,3,2,1,0:T(8,128)(2,1)} async-done(((bf16[16,4,40,16,128]{4,3,2,1,0:T(8,128)(2,1)}), bf16[16,4,40,16,128]{4,3,2,1,0:T(8,128)(2,1)}, u32[]{:S(2)}, u32[]{:S(2)}) %all-to-all-start.2) | async-done | bytes 10485792 | tf_op jit(solution)/shard_map/all_to_all | solution.py:450
  931.7 11.2 copy.181
  982.9 105.8 %all-to-all-done.3 = bf16[16,4,40,16,128]{4,3,2,1,0:T(8,128)(2,1)} async-done(((bf16[16,4,40,16,128]{4,3,2,1,0:T(8,128)(2,1)}), bf16[16,4,40,16,128]{4,3,2,1,0:T(8,128)(2,1)}, u32[]{:S(2)}, u32[]{:S(2)}) %all-to-all-start.3) | async-done | bytes 10485792 | tf_op jit(solution)/shard_map/all_to_all | solution.py:478
  1092.3 42.9 %shard_map.298 = (bf16[1024,16,128]{2,1,0:T(8,128)(2,1)}, bf16[1024,16,128]{2,1,0:T(8,128)(2,1)}, f32[1024,1,128]{2,1,0:T(1,128)}) custom-call(s32[2048]{0:T(1024)} %multiply_add_fusion.slot_ref, bf16[2560,16,128]{2,1,0:T(8,128)(2,1)} %bitcast.36.out_hbm, bf16[2560,16,128]{2,1,0:T(8,128)(2,1)} %bitcast.37.back_hbm, ...), custom_call_target="tpu_custom_call" | custom-call | flops 33554432 | bytes 46137344 | tf_op jit(solution)/shard_map/pallas_call | solution.py:221
  1170.3 63.3 %all-to-all-done.4 = bf16[8,128,2048]{2,1,0:T(8,128)(2,1)} async-done(((bf16[8,128,2048]{2,1,0:T(8,128)(2,1)}), bf16[8,128,2048]{2,1,0:T(8,128)(2,1)}, u32[]{:S(2)}, u32[]{:S(2)}) %all-to-all-start.4) | async-done | bytes 4194336 | tf_op jit(solution)/shard_map/all_to_all | solution.py:521
  1237.7 79.6 %all-reduce.9.cloned.1.call-done = bf16[1024,2050]{0,1:T(8,128)(2,1)} async-done(((bf16[1024,2050]{0,1:T(8,128)(2,1)}), bf16[1024,2050]{0,1:T(8,128)(2,1)}) %all-reduce.9.cloned.1.call-update) | async-done | bytes 4198416 | tf_op jit(solution)/shard_map/psum | solution.py:526
  1323.9 10.5 multiply_reduce_fusion
  1336.4 8.1 fusion.157
  1374.6 38.8 %all-to-all-done.5 = bf16[16,128,1056]{1,2,0:T(8,128)(2,1)} async-done(((bf16[16,128,1056]{1,2,0:T(8,128)(2,1)}), bf16[16,128,1056]{1,2,0:T(8,128)(2,1)}, u32[]{:S(2)}, u32[]{:S(2)}) %all-to-all-start.5) | async-done | bytes 4325408 | tf_op jit(solution)/shard_map/all_to_all | solution.py:541
  1420.7 10.9 pad_maximum_fusion.2
  1460.9 99.1 %all-reduce.11.cloned.1.call-done = bf16[1024,2624]{0,1:T(8,128)(2,1)} async-done(((bf16[1024,2624]{0,1:T(8,128)(2,1)}), bf16[1024,2624]{0,1:T(8,128)(2,1)}) %all-reduce.11.cloned.1.call-update) | async-done | bytes 5373968 | tf_op jit(solution)/shard_map/psum | solution.py:634
  1585.9 9.1 fusion.19
  1595.0 9.3 fusion.22
  1620.8 33.5 %reduce-scatter.2.cloned.1.call-done = f32[128,849]{0,1:T(8,128)} async-done(((f32[2048,849]{0,1:T(8,128)}), f32[128,849]{0,1:T(8,128)}) %reduce-scatter.2.cloned.1.call-update) | async-done | bytes 434704 | tf_op jit(solution)/shard_map/reduce_scatter | solution.py:691
  (441 shorter events, 355.1 us)
Async XLA Ops:
  7.2 736.9 %copy-start = (bf16[4,176,2048]{2,1,0:T(8,128)(2,1)S(1)}, bf16[4,176,2048]{2,1,0:T(8,128)(2,1)}, u32[]{:S(2)}) copy-start(bf16[4,176,2048]{2,1,0:T(8,128)(2,1)} %param.31) | copy-start | bytes 8650756
  7.2 84.3 %all-gather.5.cloned.1.call-start = ((), (), s32[]{:S(2)}) async-start(), calls=%async_computation.7 | async-start | bytes 4718592 | tf_op jit(solution)/shard_map/all_gather | solution.py:325
  9.5 166.2 %all-gather.7.cloned.1.call-start = ((), (), s32[]{:S(2)}) async-start(), calls=%async_computation.8 | async-start | bytes 4769792 | tf_op jit(solution)/shard_map/all_gather | solution.py:306
  16.2 208.6 %all-gather.9.cloned.1.call-start = ((), (), s32[]{:S(2)}) async-start(), calls=%async_computation.9 | async-start | bytes 1427456 | tf_op jit(solution)/shard_map/all_gather | solution.py:319
  94.1 99.5 %all-to-all-start = ((bf16[8,128,2048]{1,2,0:T(8,128)(2,1)}), bf16[8,128,2048]{1,2,0:T(8,128)(2,1)}, u32[]{:S(2)}, u32[]{:S(2)}) async-start(bf16[8,128,2048]{1,2,0:T(8,128)(2,1)} %broadcast_in_dim.70), calls=%async_computation | async-start | bytes 8388608 | tf_op jit(solution)/shard_map/all_to_all | solution.py:328
  98.8 245.8 %all-reduce.7.cloned.1.call-start = ((), (), s32[]{:S(2)}) async-start(), calls=%async_computation.10 | async-start | bytes 8388608 | tf_op jit(solution)/shard_map/psum | solution.py:417
  107.5 75.2 %copy-start.72 = (s32[2560]{0:T(1024)}, s32[2560]{0:T(1024)S(1)}, u32[]{:S(2)}) copy-start(s32[2560]{0:T(1024)S(1)} %scatter_custom_fusion.tok_ref) | copy-start | bytes 30724
  115.9 98.4 %copy-start.98 = (f32[32]{0:T(128)}, f32[32]{0:T(128)S(1)}, u32[]{:S(2)}) copy-start(f32[32]{0:T(128)S(1)} %multiply_power_fusion) | copy-start | bytes 388
  115.9 98.4 %copy-start.84 = (f32[1024]{0:T(1024)}, f32[1024]{0:T(1024)S(1)}, u32[]{:S(2)}) copy-start(f32[1024]{0:T(1024)S(1)} %iota_convert_fusion) | copy-start | bytes 12292
  121.0 70.1 %copy-start.82 = (f32[1024]{0:T(1024)}, f32[1024]{0:T(1024)S(1)}, u32[]{:S(2)}) copy-start(f32[1024]{0:T(1024)S(1)} %add_rsqrt_fusion.2) | copy-start | bytes 12292
  176.6 14.5 copy-start.66
  176.6 31.4 %copy-start.90 = (f32[512]{0:T(512)}, f32[512]{0:T(512)S(1)}, u32[]{:S(2)}) copy-start(f32[512]{0:T(512)S(1)} %reshape.506) | copy-start | bytes 6148
  210.7 12.8 copy-start.17
  235.9 206.1 %all-gather.11.cloned.1.call-start = ((), (), s32[]{:S(2)}) async-start(), calls=%async_computation.11 | async-start | bytes 4595712 | tf_op jit(solution)/shard_map/all_gather | solution.py:432
  709.8 16.8 %copy-start.33 = (bf16[4,176,2048]{2,1,0:T(8,128)(2,1)S(1)}, bf16[4,176,2048]{2,1,0:T(8,128)(2,1)}, u32[]{:S(2)}) copy-start(bf16[4,176,2048]{2,1,0:T(8,128)(2,1)} %param.29) | copy-start | bytes 8650756
  785.7 146.0 %all-to-all-start.2 = ((bf16[16,4,40,16,128]{4,3,2,1,0:T(8,128)(2,1)}), bf16[16,4,40,16,128]{4,3,2,1,0:T(8,128)(2,1)}, u32[]{:S(2)}, u32[]{:S(2)}) async-start(bf16[16,4,40,16,128]{4,3,2,1,0:T(8,128)(2,1)} %copy.180), calls=%async_computation.2 | async-start | bytes 20971520 | tf_op jit(solution)/shard_map/all_to_all | solution.py:450
  942.9 145.8 %all-to-all-start.3 = ((bf16[16,4,40,16,128]{4,3,2,1,0:T(8,128)(2,1)}), bf16[16,4,40,16,128]{4,3,2,1,0:T(8,128)(2,1)}, u32[]{:S(2)}, u32[]{:S(2)}) async-start(bf16[16,4,40,16,128]{4,3,2,1,0:T(8,128)(2,1)} %copy.181), calls=%async_computation.3 | async-start | bytes 20971520 | tf_op jit(solution)/shard_map/all_to_all | solution.py:478
  947.8 369.5 %all-reduce.9.cloned.1.call-start = ((), (), s32[]{:S(2)}) async-start(), calls=%async_computation.12 | async-start | bytes 8421376 | tf_op jit(solution)/shard_map/psum | solution.py:526
  947.9 14.7 slice-start.7
  1154.6 79.1 %all-to-all-start.4 = ((bf16[8,128,2048]{2,1,0:T(8,128)(2,1)}), bf16[8,128,2048]{2,1,0:T(8,128)(2,1)}, u32[]{:S(2)}, u32[]{:S(2)}) async-start(bf16[8,128,2048]{2,1,0:T(8,128)(2,1)} %reshape_reshape.3), calls=%async_computation.4 | async-start | bytes 8388608 | tf_op jit(solution)/shard_map/all_to_all | solution.py:521
  1237.7 86.1 %copy-start.69 = (s32[1024,2]{0,1:T(2,128)S(1)}, s32[1024,2]{0,1:T(2,128)}, u32[]{:S(2)}) copy-start(s32[1024,2]{0,1:T(2,128)} %param.19) | copy-start | bytes 24580
  1237.7 86.2 %copy-start.41 = (bf16[2048,321]{0,1:T(8,128)(2,1)S(1)}, bf16[2048,321]{0,1:T(8,128)(2,1)}, u32[]{:S(2)}) copy-start(bf16[2048,321]{0,1:T(8,128)(2,1)} %all-gather.9.cloned.1.call-done) | copy-start | bytes 3944452
  1237.7 86.2 %copy-start.71 = (f32[2048,1]{0,1:T(1,128)S(1)}, f32[2048,1]{0,1:T(1,128)}, u32[]{:S(2)}) copy-start(f32[2048,1]{0,1:T(1,128)} %copy-done.70) | copy-start | bytes 24580
  1323.9 12.5 copy-start.10
  1323.9 24.0 %slice-start.2 = ((s8[4325376]{0:T(1024)(128)(4,1)}), s8[4194304]{0:T(1024)(128)(4,1)S(1)}, s32[]{:S(2)}) async-start(s8[4325376]{0:T(1024)(128)(4,1)} %bitcast.273), calls=%async_computation.17 | async-start | bytes 8388608
  1350.7 62.7 %all-to-all-start.5 = ((bf16[16,128,1056]{1,2,0:T(8,128)(2,1)}), bf16[16,128,1056]{1,2,0:T(8,128)(2,1)}, u32[]{:S(2)}, u32[]{:S(2)}) async-start(bf16[16,128,1056]{1,2,0:T(8,128)(2,1)} %copy_bitcast_fusion), calls=%async_computation.5 | async-start | bytes 8650752 | tf_op jit(solution)/shard_map/all_to_all | solution.py:541
  1355.6 204.4 %all-reduce.11.cloned.1.call-start = ((), (), s32[]{:S(2)}) async-start(), calls=%async_computation.13 | async-start | bytes 10747904 | tf_op jit(solution)/shard_map/psum | solution.py:634
  1372.9 44.3 %copy-start.47 = (bf16[2048,384]{0,1:T(8,128)(2,1)S(1)}, bf16[2048,384]{0,1:T(8,128)(2,1)}, u32[]{:S(2)}) copy-start(bf16[2048,384]{0,1:T(8,128)(2,1)} %slice.284) | copy-start | bytes 4718596
  1431.7 222.6 %reduce-scatter.2.cloned.1.call-start = ((), (), s32[]{:S(2)}) async-start(), calls=%async_computation.14 | async-start | bytes 7450624 | tf_op jit(solution)/shard_map/reduce_scatter | solution.py:691
  1585.9 18.4 %slice-start.4 = ((s8[10485760]{0:T(1024)(128)(4,1)}), s8[4194304]{0:T(1024)(128)(4,1)S(1)}, s32[]{:S(2)}) async-start(s8[10485760]{0:T(1024)(128)(4,1)} %bitcast.277), calls=%async_computation.19 | async-start | bytes 8388608
  1585.9 18.4 %slice-start.5 = ((s8[10485760]{0:T(1024)(128)(4,1)}), s8[4194304]{0:T(1024)(128)(4,1)S(1)}, s32[]{:S(2)}) async-start(s8[10485760]{0:T(1024)(128)(4,1)} %bitcast.277), calls=%async_computation.20 | async-start | bytes 8388608
  1612.9 50.2 %copy-start.1 = (bf16[4,176,2048]{2,1,0:T(8,128)(2,1)S(1)}, bf16[4,176,2048]{2,1,0:T(8,128)(2,1)}, u32[]{:S(2)}) copy-start(bf16[4,176,2048]{2,1,0:T(8,128)(2,1)} %param.31) | copy-start | bytes 8650756
  (90 other events, 422.5 us)
Sparse Core Ops, SparseCore 0:
  10.8 80.6 all-gather.4
  93.7 81.9 all-gather.6
  177.9 33.7 all-gather.8
  236.1 108.4 all-reduce.6
  351.2 44.1 all-gather.10
  1147.4 169.8 all-reduce.8
  1431.8 128.1 all-reduce.10
  1584.8 69.4 reduce-scatter.1

commit v14 on v12

--- a/solution.py
+++ b/solution.py
@@ -123,7 +123,7 @@
     ).astype(out_ref.dtype)
 
 
-def dispatch_rows(slot_token, rows, grads, valid, gate, block=128):
+def dispatch_rows(slot_token, rows, grads, valid, gate, block=256):
     slots = slot_token.shape[0]
     count, width = rows.shape
     tile_rows = width // 128

time: 1670 us -> 1670 us (level)
  no operation moved by 1% of the time
where the time goes in v14:
time: 1670 us; the launch traced here: 1660 us
  waiting for transfers between devices  762 us (46%)
  local copies, waits for them, and re-layouts  256 us (15%)
  blocking collectives  237 us (14%)
  matrix products  183 us (11%)
  other arithmetic  107 us (6%)
  Pallas kernels  77.1 us (5%)
  starting transfers between devices  25.1 us (2%)
  between operations  17 us (1%)
    all_to_all x1, blocking collectives, shards(): lax.all_to_all(send_both, 'dp', split_axis=0, concat_axis=0, tiled=True)  237 us
    psum x1, waiting for transfers between devices, shards(): lax.psum(attn_part.astype(jnp.bfloat16), 'tensor').astype(jnp.float32)  107 us
    all_to_all x1, waiting for transfers between devices, shards(): lax.all_to_all(grads_low, 'dp', split_axis=0, concat_axis=0, tiled=True)  106 us
    all_to_all x1, waiting for transfers between devices, shards(): lax.all_to_all(expert_out.astype(jnp.bfloat16).reshape(dp_size, exp_dev,...  104 us
    psum x1, waiting for transfers between devices, shards(): lax.psum(jnp.concatenate([normed_grad_part, latent_grad_part], 1).astype(...  99.1 us
    psum x1, waiting for transfers between devices, shards(): lax.psum(jnp.concatenate([back_part, gate_cols.astype(jnp.bfloat16)], 1),...  79.7 us
    all_gather x1, waiting for transfers between devices, shards(): hidden_all = lax.all_gather(hidden, 'tensor', axis=0, tiled=True)  67 us
    all_to_all x1, waiting for transfers between devices, shards(): lax.all_to_all(feed_part.reshape(tensor_size, tok_dev, D), 'tensor', spli...  63.4 us
  transfers between devices with their start and end apart: 13, of which 10 were waited for; matrix products, arithmetic and copies ran while one was open for 18% of the time, Pallas kernels for 2%

profile of v14, /device:TPU:0, one launch (start us, length us, event | category | flops | bytes accessed | tf_op | source)
XLA Modules:
  0.0 1663.3 jit_solution(17048154206183540512)
XLA Ops:
  24.5 67.0 %all-gather.5.cloned.1.call-done = bf16[1024,2048]{0,1:T(8,128)(2,1)} async-done(((bf16[128,2048]{0,1:T(8,128)(2,1)}), bf16[1024,2048]{0,1:T(8,128)(2,1)}) %all-gather.5.cloned.1.call-update) | async-done | bytes 4194320 | tf_op jit(solution)/shard_map/all_gather | solution.py:325
  99.4 8.4 scatter_custom_fusion.tok_ref
  112.5 63.2 %all-gather.7.cloned.1.call-done = bf16[2048,1090]{0,1:T(8,128)(2,1)} async-done(((bf16[128,1090]{0,1:T(8,128)(2,1)}), bf16[2048,1090]{0,1:T(8,128)(2,1)}) %all-gather.7.cloned.1.call-update) | async-done | bytes 4464656 | tf_op jit(solution)/shard_map/all_gather | solution.py:306
  237.6 107.1 %all-reduce.7.cloned.1.call-done = bf16[1024,2048]{0,1:T(8,128)(2,1)} async-done(((bf16[1024,2048]{0,1:T(8,128)(2,1)}), bf16[1024,2048]{0,1:T(8,128)(2,1)}) %all-reduce.7.cloned.1.call-update) | async-done | bytes 4194320 | tf_op jit(solution)/shard_map/psum | solution.py:414
  365.2 8.1 scatter_custom_fusion.1
  381.2 12.5 copy.227.both_hbm
  401.0 34.2 %shard_map.297 = bf16[2560,32,128]{2,1,0:T(8,128)(2,1)} custom-call(s32[2560]{0:T(1024)} %copy-done.72, bf16[1024,32,128]{2,1,0:T(8,128)(2,1)} %copy.227.both_hbm, f32[2,2560,1,128]{3,2,1,0:T(1,128)} %broadcast_in_dim.79.col_ref), custom_call_target="tpu_custom_call" | custom-call | flops 5242880 | bytes 41943040 | tf_op jit(solution)/shard_map/pallas_call | solution.py:132
  435.2 236.5 %all_to_all.30 = bf16[16,4,40,32,128]{4,3,2,1,0:T(8,128)(2,1)} all-to-all(bf16[16,4,40,32,128]{4,3,2,1,0:T(8,128)(2,1)} %bitcast.262), channel_id=1, replica_groups=mesh['dp'=16,'tensor'=8] {'dp'}, dimensions={0} | all-to-all | bytes 41943040 | tf_op jit(solution)/shard_map/all_to_all | solution.py:436
  671.7 31.3 %reshape.530 = bf16[16,4,40,4096]{3,2,1,0:T(8,128)(2,1)} reshape(bf16[16,4,40,32,128]{4,3,2,1,0:T(8,128)(2,1)} %all_to_all.30) | data formatting | bytes 41943040 | tf_op jit(solution)/shard_map/reshape | solution.py:437
  703.0 16.8 %fusion.158 = (bf16[16,4,40,2048]{3,2,1,0:T(8,128)(2,1)}, bf16[16,4,40,2048]{3,2,1,0:T(8,128)(2,1)}) fusion(bf16[16,4,40,4096]{3,2,1,0:T(8,128)(2,1)} %reshape.530), kind=kLoop, calls=%fused_computation.283 | loop fusion | bytes 41943040 | tf_op jit(solution)/shard_map/slice | solution.py:439
  719.9 8.8 fusion.11
  728.7 8.7 fusion.9
  737.3 11.4 fusion.41
  755.9 11.8 copy.236
  767.7 11.2 copy.180
  784.1 9.9 fusion.32
  794.0 15.1 add_convert_fusion
  809.1 12.0 copy.237
  821.0 103.9 %all-to-all-done.2 = bf16[16,4,40,16,128]{4,3,2,1,0:T(8,128)(2,1)} async-done(((bf16[16,4,40,16,128]{4,3,2,1,0:T(8,128)(2,1)}), bf16[16,4,40,16,128]{4,3,2,1,0:T(8,128)(2,1)}, u32[]{:S(2)}, u32[]{:S(2)}) %all-to-all-start.2) | async-done | bytes 10485792 | tf_op jit(solution)/shard_map/all_to_all | solution.py:449
  924.9 11.2 copy.181
  976.1 105.8 %all-to-all-done.3 = bf16[16,4,40,16,128]{4,3,2,1,0:T(8,128)(2,1)} async-done(((bf16[16,4,40,16,128]{4,3,2,1,0:T(8,128)(2,1)}), bf16[16,4,40,16,128]{4,3,2,1,0:T(8,128)(2,1)}, u32[]{:S(2)}, u32[]{:S(2)}) %all-to-all-start.3) | async-done | bytes 10485792 | tf_op jit(solution)/shard_map/all_to_all | solution.py:477
  1085.5 42.9 %shard_map.298 = (bf16[1024,16,128]{2,1,0:T(8,128)(2,1)}, bf16[1024,16,128]{2,1,0:T(8,128)(2,1)}, f32[1024,1,128]{2,1,0:T(1,128)}) custom-call(s32[2048]{0:T(1024)} %copy-done.78, bf16[2560,16,128]{2,1,0:T(8,128)(2,1)} %bitcast.36.out_hbm, bf16[2560,16,128]{2,1,0:T(8,128)(2,1)} %bitcast.37.back_hbm, f32[2,1024,1,128]{3,2,1,0:T(1,128)} %broadcast_in_dim.80.gate_ref, ...), custom_call_target="tpu_custom_call" | custom-call | flops 33554432 | bytes 46137344 | tf_op jit(solution)/shard_map/pallas_call | solution.py:221
  1163.5 63.4 %all-to-all-done.4 = bf16[8,128,2048]{2,1,0:T(8,128)(2,1)} async-done(((bf16[8,128,2048]{2,1,0:T(8,128)(2,1)}), bf16[8,128,2048]{2,1,0:T(8,128)(2,1)}, u32[]{:S(2)}, u32[]{:S(2)}) %all-to-all-start.4) | async-done | bytes 4194336 | tf_op jit(solution)/shard_map/all_to_all | solution.py:520
  1230.9 79.7 %all-reduce.9.cloned.1.call-done = bf16[1024,2050]{0,1:T(8,128)(2,1)} async-done(((bf16[1024,2050]{0,1:T(8,128)(2,1)}), bf16[1024,2050]{0,1:T(8,128)(2,1)}) %all-reduce.9.cloned.1.call-update) | async-done | bytes 4198416 | tf_op jit(solution)/shard_map/psum | solution.py:525
  1317.2 10.5 multiply_reduce_fusion
  1329.6 8.1 fusion.157
  1367.9 38.8 %all-to-all-done.5 = bf16[16,128,1056]{1,2,0:T(8,128)(2,1)} async-done(((bf16[16,128,1056]{1,2,0:T(8,128)(2,1)}), bf16[16,128,1056]{1,2,0:T(8,128)(2,1)}, u32[]{:S(2)}, u32[]{:S(2)}) %all-to-all-start.5) | async-done | bytes 4325408 | tf_op jit(solution)/shard_map/all_to_all | solution.py:540
  1414.0 10.9 pad_maximum_fusion.2
  1454.2 99.1 %all-reduce.11.cloned.1.call-done = bf16[1024,2624]{0,1:T(8,128)(2,1)} async-done(((bf16[1024,2624]{0,1:T(8,128)(2,1)}), bf16[1024,2624]{0,1:T(8,128)(2,1)}) %all-reduce.11.cloned.1.call-update) | async-done | bytes 5373968 | tf_op jit(solution)/shard_map/psum | solution.py:633
  1579.1 9.1 fusion.19
  1588.2 9.3 fusion.22
  1614.0 33.5 %reduce-scatter.2.cloned.1.call-done = f32[128,849]{0,1:T(8,128)} async-done(((f32[2048,849]{0,1:T(8,128)}), f32[128,849]{0,1:T(8,128)}) %reduce-scatter.2.cloned.1.call-update) | async-done | bytes 434704 | tf_op jit(solution)/shard_map/reduce_scatter | solution.py:690
  (439 shorter events, 346.4 us)
Async XLA Ops:
  7.2 730.2 %copy-start = (bf16[4,176,2048]{2,1,0:T(8,128)(2,1)S(1)}, bf16[4,176,2048]{2,1,0:T(8,128)(2,1)}, u32[]{:S(2)}) copy-start(bf16[4,176,2048]{2,1,0:T(8,128)(2,1)} %param.31) | copy-start | bytes 8650756
  7.2 84.3 %all-gather.5.cloned.1.call-start = ((), (), s32[]{:S(2)}) async-start(), calls=%async_computation.7 | async-start | bytes 4718592 | tf_op jit(solution)/shard_map/all_gather | solution.py:325
  9.5 166.2 %all-gather.7.cloned.1.call-start = ((), (), s32[]{:S(2)}) async-start(), calls=%async_computation.8 | async-start | bytes 4769792 | tf_op jit(solution)/shard_map/all_gather | solution.py:306
  16.2 208.6 %all-gather.9.cloned.1.call-start = ((), (), s32[]{:S(2)}) async-start(), calls=%async_computation.9 | async-start | bytes 1427456 | tf_op jit(solution)/shard_map/all_gather | solution.py:319
  94.1 99.6 %all-to-all-start = ((bf16[8,128,2048]{1,2,0:T(8,128)(2,1)}), bf16[8,128,2048]{1,2,0:T(8,128)(2,1)}, u32[]{:S(2)}, u32[]{:S(2)}) async-start(bf16[8,128,2048]{1,2,0:T(8,128)(2,1)} %broadcast_in_dim.64), calls=%async_computation | async-start | bytes 8388608 | tf_op jit(solution)/shard_map/all_to_all | solution.py:328
  98.8 246.0 %all-reduce.7.cloned.1.call-start = ((), (), s32[]{:S(2)}) async-start(), calls=%async_computation.10 | async-start | bytes 8388608 | tf_op jit(solution)/shard_map/psum | solution.py:414
  107.8 74.9 %copy-start.72 = (s32[2560]{0:T(1024)}, s32[2560]{0:T(1024)S(1)}, u32[]{:S(2)}) copy-start(s32[2560]{0:T(1024)S(1)} %scatter_custom_fusion.tok_ref) | copy-start | bytes 30724
  107.8 106.5 %copy-start.99 = (f32[32]{0:T(128)}, f32[32]{0:T(128)S(1)}, u32[]{:S(2)}) copy-start(f32[32]{0:T(128)S(1)} %multiply_power_fusion) | copy-start | bytes 388
  107.9 106.5 %copy-start.85 = (f32[1024]{0:T(1024)}, f32[1024]{0:T(1024)S(1)}, u32[]{:S(2)}) copy-start(f32[1024]{0:T(1024)S(1)} %iota_convert_fusion) | copy-start | bytes 12292
  107.9 244.1 %copy-start.78 = (s32[2048]{0:T(1024)}, s32[2048]{0:T(1024)S(1)}, u32[]{:S(2)}) copy-start(s32[2048]{0:T(1024)S(1)} %multiply_add_fusion.slot_ref) | copy-start | bytes 24580
  112.5 78.6 %copy-start.83 = (f32[1024]{0:T(1024)}, f32[1024]{0:T(1024)S(1)}, u32[]{:S(2)}) copy-start(f32[1024]{0:T(1024)S(1)} %add_rsqrt_fusion.2) | copy-start | bytes 12292
  176.6 14.5 copy-start.66
  176.7 31.5 %copy-start.91 = (f32[512]{0:T(512)}, f32[512]{0:T(512)S(1)}, u32[]{:S(2)}) copy-start(f32[512]{0:T(512)S(1)} %reshape.501) | copy-start | bytes 6148
  210.7 12.8 copy-start.17
  236.0 199.2 %all-gather.11.cloned.1.call-start = ((), (), s32[]{:S(2)}) async-start(), calls=%async_computation.11 | async-start | bytes 4595712 | tf_op jit(solution)/shard_map/all_gather | solution.py:431
  703.0 16.8 %copy-start.33 = (bf16[4,176,2048]{2,1,0:T(8,128)(2,1)S(1)}, bf16[4,176,2048]{2,1,0:T(8,128)(2,1)}, u32[]{:S(2)}) copy-start(bf16[4,176,2048]{2,1,0:T(8,128)(2,1)} %param.29) | copy-start | bytes 8650756
  779.0 146.0 %all-to-all-start.2 = ((bf16[16,4,40,16,128]{4,3,2,1,0:T(8,128)(2,1)}), bf16[16,4,40,16,128]{4,3,2,1,0:T(8,128)(2,1)}, u32[]{:S(2)}, u32[]{:S(2)}) async-start(bf16[16,4,40,16,128]{4,3,2,1,0:T(8,128)(2,1)} %copy.180), calls=%async_computation.2 | async-start | bytes 20971520 | tf_op jit(solution)/shard_map/all_to_all | solution.py:449
  936.1 145.8 %all-to-all-start.3 = ((bf16[16,4,40,16,128]{4,3,2,1,0:T(8,128)(2,1)}), bf16[16,4,40,16,128]{4,3,2,1,0:T(8,128)(2,1)}, u32[]{:S(2)}, u32[]{:S(2)}) async-start(bf16[16,4,40,16,128]{4,3,2,1,0:T(8,128)(2,1)} %copy.181), calls=%async_computation.3 | async-start | bytes 20971520 | tf_op jit(solution)/shard_map/all_to_all | solution.py:477
  941.0 369.5 %all-reduce.9.cloned.1.call-start = ((), (), s32[]{:S(2)}) async-start(), calls=%async_computation.12 | async-start | bytes 8421376 | tf_op jit(solution)/shard_map/psum | solution.py:525
  941.1 14.7 slice-start.7
  1147.8 79.1 %all-to-all-start.4 = ((bf16[8,128,2048]{2,1,0:T(8,128)(2,1)}), bf16[8,128,2048]{2,1,0:T(8,128)(2,1)}, u32[]{:S(2)}, u32[]{:S(2)}) async-start(bf16[8,128,2048]{2,1,0:T(8,128)(2,1)} %reshape_reshape.3), calls=%async_computation.4 | async-start | bytes 8388608 | tf_op jit(solution)/shard_map/all_to_all | solution.py:520
  1230.9 86.2 %copy-start.69 = (s32[1024,2]{0,1:T(2,128)S(1)}, s32[1024,2]{0,1:T(2,128)}, u32[]{:S(2)}) copy-start(s32[1024,2]{0,1:T(2,128)} %param.19) | copy-start | bytes 24580
  1230.9 86.2 %copy-start.41 = (bf16[2048,321]{0,1:T(8,128)(2,1)S(1)}, bf16[2048,321]{0,1:T(8,128)(2,1)}, u32[]{:S(2)}) copy-start(bf16[2048,321]{0,1:T(8,128)(2,1)} %all-gather.9.cloned.1.call-done) | copy-start | bytes 3944452
  1230.9 86.2 %copy-start.71 = (f32[2048,1]{0,1:T(1,128)S(1)}, f32[2048,1]{0,1:T(1,128)}, u32[]{:S(2)}) copy-start(f32[2048,1]{0,1:T(1,128)} %copy-done.70) | copy-start | bytes 24580
  1317.2 24.0 %slice-start.2 = ((s8[4325376]{0:T(1024)(128)(4,1)}), s8[4194304]{0:T(1024)(128)(4,1)S(1)}, s32[]{:S(2)}) async-start(s8[4325376]{0:T(1024)(128)(4,1)} %bitcast.273), calls=%async_computation.17 | async-start | bytes 8388608
  1344.0 62.7 %all-to-all-start.5 = ((bf16[16,128,1056]{1,2,0:T(8,128)(2,1)}), bf16[16,128,1056]{1,2,0:T(8,128)(2,1)}, u32[]{:S(2)}, u32[]{:S(2)}) async-start(bf16[16,128,1056]{1,2,0:T(8,128)(2,1)} %copy_bitcast_fusion), calls=%async_computation.5 | async-start | bytes 8650752 | tf_op jit(solution)/shard_map/all_to_all | solution.py:540
  1348.9 204.4 %all-reduce.11.cloned.1.call-start = ((), (), s32[]{:S(2)}) async-start(), calls=%async_computation.13 | async-start | bytes 10747904 | tf_op jit(solution)/shard_map/psum | solution.py:633
  1366.1 44.3 %copy-start.47 = (bf16[2048,384]{0,1:T(8,128)(2,1)S(1)}, bf16[2048,384]{0,1:T(8,128)(2,1)}, u32[]{:S(2)}) copy-start(bf16[2048,384]{0,1:T(8,128)(2,1)} %slice.282) | copy-start | bytes 4718596
  1424.9 222.5 %reduce-scatter.2.cloned.1.call-start = ((), (), s32[]{:S(2)}) async-start(), calls=%async_computation.14 | async-start | bytes 7450624 | tf_op jit(solution)/shard_map/reduce_scatter | solution.py:690
  1579.1 18.4 %slice-start.4 = ((s8[10485760]{0:T(1024)(128)(4,1)}), s8[4194304]{0:T(1024)(128)(4,1)S(1)}, s32[]{:S(2)}) async-start(s8[10485760]{0:T(1024)(128)(4,1)} %bitcast.277), calls=%async_computation.19 | async-start | bytes 8388608
  1579.1 18.4 %slice-start.5 = ((s8[10485760]{0:T(1024)(128)(4,1)}), s8[4194304]{0:T(1024)(128)(4,1)S(1)}, s32[]{:S(2)}) async-start(s8[10485760]{0:T(1024)(128)(4,1)} %bitcast.277), calls=%async_computation.20 | async-start | bytes 8388608
  1606.0 50.2 %copy-start.1 = (bf16[4,176,2048]{2,1,0:T(8,128)(2,1)S(1)}, bf16[4,176,2048]{2,1,0:T(8,128)(2,1)}, u32[]{:S(2)}) copy-start(bf16[4,176,2048]{2,1,0:T(8,128)(2,1)} %param.31) | copy-start | bytes 8650756
  (91 other events, 434.2 us)
Sparse Core Ops, SparseCore 0:
  10.8 80.6 all-gather.4
  93.7 81.9 all-gather.6
  177.9 33.7 all-gather.8
  236.1 108.6 all-reduce.6
  351.3 44.3 all-gather.10
  1140.6 169.9 all-reduce.8
  1425.1 128.1 all-reduce.10
  1577.9 69.4 reduce-scatter.1

commit v15 on v14

--- a/solution.py
+++ b/solution.py
@@ -175,7 +175,7 @@
                 ).start()
             return carry
 
-        lax.fori_loop(0, block, start, 0, unroll=2)
+        lax.fori_loop(0, block, start, 0, unroll=4)
 
     @pl.when(step == 0)
     def _():
@@ -193,7 +193,7 @@
             pltpu.make_async_copy(back_hbm.at[0], picked_back.at[now, k, r], sems.at[now, 1, k, r]).wait()
         return carry
 
-    lax.fori_loop(0, block, finish, 0, unroll=2)
+    lax.fori_loop(0, block, finish, 0, unroll=4)
     grad = grad_ref[...].astype(jnp.float32)
     weighted = None
     backs = None

time: 1670 us -> 1670 us (level)
  no operation moved by 1% of the time
where the time goes in v15:
time: 1670 us; the launch traced here: 1660 us
  waiting for transfers between devices  761 us (46%)
  local copies, waits for them, and re-layouts  256 us (15%)
  blocking collectives  237 us (14%)
  matrix products  183 us (11%)
  other arithmetic  107 us (6%)
  Pallas kernels  74.5 us (4%)
  starting transfers between devices  25.1 us (2%)
  between operations  17 us (1%)
    all_to_all x1, blocking collectives, shards(): lax.all_to_all(send_both, 'dp', split_axis=0, concat_axis=0, tiled=True)  237 us
    psum x1, waiting for transfers between devices, shards(): lax.psum(attn_part.astype(jnp.bfloat16), 'tensor').astype(jnp.float32)  107 us
    all_to_all x1, waiting for transfers between devices, shards(): lax.all_to_all(grads_low, 'dp', split_axis=0, concat_axis=0, tiled=True)  106 us
    all_to_all x1, waiting for transfers between devices, shards(): lax.all_to_all(expert_out.astype(jnp.bfloat16).reshape(dp_size, exp_dev,...  104 us
    psum x1, waiting for transfers between devices, shards(): lax.psum(jnp.concatenate([normed_grad_part, latent_grad_part], 1).astype(...  99.1 us
    psum x1, waiting for transfers between devices, shards(): lax.psum(jnp.concatenate([back_part, gate_cols.astype(jnp.bfloat16)], 1),...  79.5 us
    all_gather x1, waiting for transfers between devices, shards(): hidden_all = lax.all_gather(hidden, 'tensor', axis=0, tiled=True)  67 us
    all_to_all x1, waiting for transfers between devices, shards(): lax.all_to_all(feed_part.reshape(tensor_size, tok_dev, D), 'tensor', spli...  63.4 us
  transfers between devices with their start and end apart: 13, of which 10 were waited for; matrix products, arithmetic and copies ran while one was open for 18% of the time, Pallas kernels for 2%

profile of v15, /device:TPU:0, one launch (start us, length us, event | category | flops | bytes accessed | tf_op | source)
XLA Modules:
  0.0 1660.6 jit_solution(17868887471697872793)
XLA Ops:
  24.5 67.0 %all-gather.5.cloned.1.call-done = bf16[1024,2048]{0,1:T(8,128)(2,1)} async-done(((bf16[128,2048]{0,1:T(8,128)(2,1)}), bf16[1024,2048]{0,1:T(8,128)(2,1)}) %all-gather.5.cloned.1.call-update) | async-done | bytes 4194320 | tf_op jit(solution)/shard_map/all_gather | solution.py:325
  99.4 8.4 scatter_custom_fusion.tok_ref
  112.5 63.2 %all-gather.7.cloned.1.call-done = bf16[2048,1090]{0,1:T(8,128)(2,1)} async-done(((bf16[128,1090]{0,1:T(8,128)(2,1)}), bf16[2048,1090]{0,1:T(8,128)(2,1)}) %all-gather.7.cloned.1.call-update) | async-done | bytes 4464656 | tf_op jit(solution)/shard_map/all_gather | solution.py:306
  237.6 107.1 %all-reduce.7.cloned.1.call-done = bf16[1024,2048]{0,1:T(8,128)(2,1)} async-done(((bf16[1024,2048]{0,1:T(8,128)(2,1)}), bf16[1024,2048]{0,1:T(8,128)(2,1)}) %all-reduce.7.cloned.1.call-update) | async-done | bytes 4194320 | tf_op jit(solution)/shard_map/psum | solution.py:414
  365.2 8.1 scatter_custom_fusion.1
  381.2 12.5 copy.227.both_hbm
  401.0 35.1 %shard_map.297 = bf16[2560,32,128]{2,1,0:T(8,128)(2,1)} custom-call(s32[2560]{0:T(1024)} %copy-done.72, bf16[1024,32,128]{2,1,0:T(8,128)(2,1)} %copy.227.both_hbm, f32[2,2560,1,128]{3,2,1,0:T(1,128)} %broadcast_in_dim.79.col_ref), custom_call_target="tpu_custom_call" | custom-call | flops 5242880 | bytes 41943040 | tf_op jit(solution)/shard_map/pallas_call | solution.py:132
  436.2 236.5 %all_to_all.30 = bf16[16,4,40,32,128]{4,3,2,1,0:T(8,128)(2,1)} all-to-all(bf16[16,4,40,32,128]{4,3,2,1,0:T(8,128)(2,1)} %bitcast.262), channel_id=1, replica_groups=mesh['dp'=16,'tensor'=8] {'dp'}, dimensions={0} | all-to-all | bytes 41943040 | tf_op jit(solution)/shard_map/all_to_all | solution.py:436
  672.7 31.3 %reshape.530 = bf16[16,4,40,4096]{3,2,1,0:T(8,128)(2,1)} reshape(bf16[16,4,40,32,128]{4,3,2,1,0:T(8,128)(2,1)} %all_to_all.30) | data formatting | bytes 41943040 | tf_op jit(solution)/shard_map/reshape | solution.py:437
  704.0 16.8 %fusion.158 = (bf16[16,4,40,2048]{3,2,1,0:T(8,128)(2,1)}, bf16[16,4,40,2048]{3,2,1,0:T(8,128)(2,1)}) fusion(bf16[16,4,40,4096]{3,2,1,0:T(8,128)(2,1)} %reshape.530), kind=kLoop, calls=%fused_computation.283 | loop fusion | bytes 41943040 | tf_op jit(solution)/shard_map/slice | solution.py:439
  720.8 8.8 fusion.11
  729.6 8.7 fusion.9
  738.3 11.4 fusion.41
  756.9 11.8 copy.236
  768.7 11.2 copy.180
  785.0 9.9 fusion.32
  794.9 15.1 add_convert_fusion
  810.0 12.0 copy.237
  821.9 103.9 %all-to-all-done.2 = bf16[16,4,40,16,128]{4,3,2,1,0:T(8,128)(2,1)} async-done(((bf16[16,4,40,16,128]{4,3,2,1,0:T(8,128)(2,1)}), bf16[16,4,40,16,128]{4,3,2,1,0:T(8,128)(2,1)}, u32[]{:S(2)}, u32[]{:S(2)}) %all-to-all-start.2) | async-done | bytes 10485792 | tf_op jit(solution)/shard_map/all_to_all | solution.py:449
  925.9 11.2 copy.181
  977.0 105.8 %all-to-all-done.3 = bf16[16,4,40,16,128]{4,3,2,1,0:T(8,128)(2,1)} async-done(((bf16[16,4,40,16,128]{4,3,2,1,0:T(8,128)(2,1)}), bf16[16,4,40,16,128]{4,3,2,1,0:T(8,128)(2,1)}, u32[]{:S(2)}, u32[]{:S(2)}) %all-to-all-start.3) | async-done | bytes 10485792 | tf_op jit(solution)/shard_map/all_to_all | solution.py:477
  1086.4 39.4 %shard_map.298 = (bf16[1024,16,128]{2,1,0:T(8,128)(2,1)}, bf16[1024,16,128]{2,1,0:T(8,128)(2,1)}, f32[1024,1,128]{2,1,0:T(1,128)}) custom-call(s32[2048]{0:T(1024)} %copy-done.78, bf16[2560,16,128]{2,1,0:T(8,128)(2,1)} %bitcast.36.out_hbm, bf16[2560,16,128]{2,1,0:T(8,128)(2,1)} %bitcast.37.back_hbm, f32[2,1024,1,128]{3,2,1,0:T(1,128)} %broadcast_in_dim.80.gate_ref, ...), custom_call_target="tpu_custom_call" | custom-call | flops 33554432 | bytes 46137344 | tf_op jit(solution)/shard_map/pallas_call | solution.py:221
  1160.9 63.4 %all-to-all-done.4 = bf16[8,128,2048]{2,1,0:T(8,128)(2,1)} async-done(((bf16[8,128,2048]{2,1,0:T(8,128)(2,1)}), bf16[8,128,2048]{2,1,0:T(8,128)(2,1)}, u32[]{:S(2)}, u32[]{:S(2)}) %all-to-all-start.4) | async-done | bytes 4194336 | tf_op jit(solution)/shard_map/all_to_all | solution.py:520
  1228.3 79.5 %all-reduce.9.cloned.1.call-done = bf16[1024,2050]{0,1:T(8,128)(2,1)} async-done(((bf16[1024,2050]{0,1:T(8,128)(2,1)}), bf16[1024,2050]{0,1:T(8,128)(2,1)}) %all-reduce.9.cloned.1.call-update) | async-done | bytes 4198416 | tf_op jit(solution)/shard_map/psum | solution.py:525
  1314.5 10.5 multiply_reduce_fusion
  1326.9 8.1 fusion.157
  1365.2 38.8 %all-to-all-done.5 = bf16[16,128,1056]{1,2,0:T(8,128)(2,1)} async-done(((bf16[16,128,1056]{1,2,0:T(8,128)(2,1)}), bf16[16,128,1056]{1,2,0:T(8,128)(2,1)}, u32[]{:S(2)}, u32[]{:S(2)}) %all-to-all-start.5) | async-done | bytes 4325408 | tf_op jit(solution)/shard_map/all_to_all | solution.py:540
  1411.3 10.9 pad_maximum_fusion.2
  1451.5 99.1 %all-reduce.11.cloned.1.call-done = bf16[1024,2624]{0,1:T(8,128)(2,1)} async-done(((bf16[1024,2624]{0,1:T(8,128)(2,1)}), bf16[1024,2624]{0,1:T(8,128)(2,1)}) %all-reduce.11.cloned.1.call-update) | async-done | bytes 5373968 | tf_op jit(solution)/shard_map/psum | solution.py:633
  1576.4 9.1 fusion.19
  1585.5 9.3 fusion.22
  1611.3 33.5 %reduce-scatter.2.cloned.1.call-done = f32[128,849]{0,1:T(8,128)} async-done(((f32[2048,849]{0,1:T(8,128)}), f32[128,849]{0,1:T(8,128)}) %reduce-scatter.2.cloned.1.call-update) | async-done | bytes 434704 | tf_op jit(solution)/shard_map/reduce_scatter | solution.py:690
  (439 shorter events, 346.3 us)
Async XLA Ops:
  7.2 731.1 %copy-start = (bf16[4,176,2048]{2,1,0:T(8,128)(2,1)S(1)}, bf16[4,176,2048]{2,1,0:T(8,128)(2,1)}, u32[]{:S(2)}) copy-start(bf16[4,176,2048]{2,1,0:T(8,128)(2,1)} %param.31) | copy-start | bytes 8650756
  7.2 84.3 %all-gather.5.cloned.1.call-start = ((), (), s32[]{:S(2)}) async-start(), calls=%async_computation.7 | async-start | bytes 4718592 | tf_op jit(solution)/shard_map/all_gather | solution.py:325
  9.5 166.2 %all-gather.7.cloned.1.call-start = ((), (), s32[]{:S(2)}) async-start(), calls=%async_computation.8 | async-start | bytes 4769792 | tf_op jit(solution)/shard_map/all_gather | solution.py:306
  16.2 208.6 %all-gather.9.cloned.1.call-start = ((), (), s32[]{:S(2)}) async-start(), calls=%async_computation.9 | async-start | bytes 1427456 | tf_op jit(solution)/shard_map/all_gather | solution.py:319
  94.1 99.6 %all-to-all-start = ((bf16[8,128,2048]{1,2,0:T(8,128)(2,1)}), bf16[8,128,2048]{1,2,0:T(8,128)(2,1)}, u32[]{:S(2)}, u32[]{:S(2)}) async-start(bf16[8,128,2048]{1,2,0:T(8,128)(2,1)} %broadcast_in_dim.64), calls=%async_computation | async-start | bytes 8388608 | tf_op jit(solution)/shard_map/all_to_all | solution.py:328
  98.8 246.0 %all-reduce.7.cloned.1.call-start = ((), (), s32[]{:S(2)}) async-start(), calls=%async_computation.10 | async-start | bytes 8388608 | tf_op jit(solution)/shard_map/psum | solution.py:414
  107.8 74.9 %copy-start.72 = (s32[2560]{0:T(1024)}, s32[2560]{0:T(1024)S(1)}, u32[]{:S(2)}) copy-start(s32[2560]{0:T(1024)S(1)} %scatter_custom_fusion.tok_ref) | copy-start | bytes 30724
  107.8 106.5 %copy-start.99 = (f32[32]{0:T(128)}, f32[32]{0:T(128)S(1)}, u32[]{:S(2)}) copy-start(f32[32]{0:T(128)S(1)} %multiply_power_fusion) | copy-start | bytes 388
  107.9 106.5 %copy-start.85 = (f32[1024]{0:T(1024)}, f32[1024]{0:T(1024)S(1)}, u32[]{:S(2)}) copy-start(f32[1024]{0:T(1024)S(1)} %iota_convert_fusion) | copy-start | bytes 12292
  107.9 244.1 %copy-start.78 = (s32[2048]{0:T(1024)}, s32[2048]{0:T(1024)S(1)}, u32[]{:S(2)}) copy-start(s32[2048]{0:T(1024)S(1)} %multiply_add_fusion.slot_ref) | copy-start | bytes 24580
  112.5 78.6 %copy-start.83 = (f32[1024]{0:T(1024)}, f32[1024]{0:T(1024)S(1)}, u32[]{:S(2)}) copy-start(f32[1024]{0:T(1024)S(1)} %add_rsqrt_fusion.2) | copy-start | bytes 12292
  176.6 14.5 copy-start.66
  176.7 31.5 %copy-start.91 = (f32[512]{0:T(512)}, f32[512]{0:T(512)S(1)}, u32[]{:S(2)}) copy-start(f32[512]{0:T(512)S(1)} %reshape.501) | copy-start | bytes 6148
  210.7 12.8 copy-start.17
  236.0 200.2 %all-gather.11.cloned.1.call-start = ((), (), s32[]{:S(2)}) async-start(), calls=%async_computation.11 | async-start | bytes 4595712 | tf_op jit(solution)/shard_map/all_gather | solution.py:431
  704.0 16.8 %copy-start.33 = (bf16[4,176,2048]{2,1,0:T(8,128)(2,1)S(1)}, bf16[4,176,2048]{2,1,0:T(8,128)(2,1)}, u32[]{:S(2)}) copy-start(bf16[4,176,2048]{2,1,0:T(8,128)(2,1)} %param.29) | copy-start | bytes 8650756
  779.9 146.0 %all-to-all-start.2 = ((bf16[16,4,40,16,128]{4,3,2,1,0:T(8,128)(2,1)}), bf16[16,4,40,16,128]{4,3,2,1,0:T(8,128)(2,1)}, u32[]{:S(2)}, u32[]{:S(2)}) async-start(bf16[16,4,40,16,128]{4,3,2,1,0:T(8,128)(2,1)} %copy.180), calls=%async_computation.2 | async-start | bytes 20971520 | tf_op jit(solution)/shard_map/all_to_all | solution.py:449
  937.1 145.8 %all-to-all-start.3 = ((bf16[16,4,40,16,128]{4,3,2,1,0:T(8,128)(2,1)}), bf16[16,4,40,16,128]{4,3,2,1,0:T(8,128)(2,1)}, u32[]{:S(2)}, u32[]{:S(2)}) async-start(bf16[16,4,40,16,128]{4,3,2,1,0:T(8,128)(2,1)} %copy.181), calls=%async_computation.3 | async-start | bytes 20971520 | tf_op jit(solution)/shard_map/all_to_all | solution.py:477
  942.0 365.9 %all-reduce.9.cloned.1.call-start = ((), (), s32[]{:S(2)}) async-start(), calls=%async_computation.12 | async-start | bytes 8421376 | tf_op jit(solution)/shard_map/psum | solution.py:525
  942.1 14.7 slice-start.7
  1145.2 79.1 %all-to-all-start.4 = ((bf16[8,128,2048]{2,1,0:T(8,128)(2,1)}), bf16[8,128,2048]{2,1,0:T(8,128)(2,1)}, u32[]{:S(2)}, u32[]{:S(2)}) async-start(bf16[8,128,2048]{2,1,0:T(8,128)(2,1)} %reshape_reshape.3), calls=%async_computation.4 | async-start | bytes 8388608 | tf_op jit(solution)/shard_map/all_to_all | solution.py:520
  1228.3 86.1 %copy-start.69 = (s32[1024,2]{0,1:T(2,128)S(1)}, s32[1024,2]{0,1:T(2,128)}, u32[]{:S(2)}) copy-start(s32[1024,2]{0,1:T(2,128)} %param.19) | copy-start | bytes 24580
  1228.3 86.1 %copy-start.41 = (bf16[2048,321]{0,1:T(8,128)(2,1)S(1)}, bf16[2048,321]{0,1:T(8,128)(2,1)}, u32[]{:S(2)}) copy-start(bf16[2048,321]{0,1:T(8,128)(2,1)} %all-gather.9.cloned.1.call-done) | copy-start | bytes 3944452
  1228.3 86.1 %copy-start.71 = (f32[2048,1]{0,1:T(1,128)S(1)}, f32[2048,1]{0,1:T(1,128)}, u32[]{:S(2)}) copy-start(f32[2048,1]{0,1:T(1,128)} %copy-done.70) | copy-start | bytes 24580
  1314.5 24.0 %slice-start.2 = ((s8[4325376]{0:T(1024)(128)(4,1)}), s8[4194304]{0:T(1024)(128)(4,1)S(1)}, s32[]{:S(2)}) async-start(s8[4325376]{0:T(1024)(128)(4,1)} %bitcast.273), calls=%async_computation.17 | async-start | bytes 8388608
  1341.3 62.7 %all-to-all-start.5 = ((bf16[16,128,1056]{1,2,0:T(8,128)(2,1)}), bf16[16,128,1056]{1,2,0:T(8,128)(2,1)}, u32[]{:S(2)}, u32[]{:S(2)}) async-start(bf16[16,128,1056]{1,2,0:T(8,128)(2,1)} %copy_bitcast_fusion), calls=%async_computation.5 | async-start | bytes 8650752 | tf_op jit(solution)/shard_map/all_to_all | solution.py:540
  1346.2 204.4 %all-reduce.11.cloned.1.call-start = ((), (), s32[]{:S(2)}) async-start(), calls=%async_computation.13 | async-start | bytes 10747904 | tf_op jit(solution)/shard_map/psum | solution.py:633
  1363.4 44.3 %copy-start.47 = (bf16[2048,384]{0,1:T(8,128)(2,1)S(1)}, bf16[2048,384]{0,1:T(8,128)(2,1)}, u32[]{:S(2)}) copy-start(bf16[2048,384]{0,1:T(8,128)(2,1)} %slice.282) | copy-start | bytes 4718596
  1422.2 222.5 %reduce-scatter.2.cloned.1.call-start = ((), (), s32[]{:S(2)}) async-start(), calls=%async_computation.14 | async-start | bytes 7450624 | tf_op jit(solution)/shard_map/reduce_scatter | solution.py:690
  1576.4 18.4 %slice-start.4 = ((s8[10485760]{0:T(1024)(128)(4,1)}), s8[4194304]{0:T(1024)(128)(4,1)S(1)}, s32[]{:S(2)}) async-start(s8[10485760]{0:T(1024)(128)(4,1)} %bitcast.277), calls=%async_computation.19 | async-start | bytes 8388608
  1576.4 18.4 %slice-start.5 = ((s8[10485760]{0:T(1024)(128)(4,1)}), s8[4194304]{0:T(1024)(128)(4,1)S(1)}, s32[]{:S(2)}) async-start(s8[10485760]{0:T(1024)(128)(4,1)} %bitcast.277), calls=%async_computation.20 | async-start | bytes 8388608
  1603.3 50.2 %copy-start.1 = (bf16[4,176,2048]{2,1,0:T(8,128)(2,1)S(1)}, bf16[4,176,2048]{2,1,0:T(8,128)(2,1)}, u32[]{:S(2)}) copy-start(bf16[4,176,2048]{2,1,0:T(8,128)(2,1)} %param.31) | copy-start | bytes 8650756
  (91 other events, 434.2 us)
Sparse Core Ops, SparseCore 0:
  10.8 80.6 all-gather.4
  93.7 81.9 all-gather.6
  177.9 33.7 all-gather.8
  236.1 108.6 all-reduce.6
  351.3 44.3 all-gather.10
  1138.0 169.8 all-reduce.8
  1422.4 128.1 all-reduce.10
  1575.2 69.4 reduce-scatter.1
